TPU v7x, 128 devices: a whole 4x4x4 slice. The times are simulated.
128 devices in a mesh: blk: 16 (over y, z_lo, core), col: 8 (over x, z_hi).
Axes of the slice: x: 4, y: 4, z: 4 (z_hi: 2, z_lo: 2; z = z_hi * 2 + z_lo), core: 2. Of those that a mesh axis runs over, the one named last changes fastest.
Arguments:
- three_index: float32 [4096, 12, 4096], P('blk', None, 'col'), may hold values from -6 to 6
- coefficients: float32 [4096, 1024], P('col', 'blk'), may hold values from -0.0078125 to 0.0078125
Outputs:
- exchange_matrix: float32 [4096, 4096], P(('blk', 'col'))
All inputs are finite; a program needn't handle non-finite values.
Results may differ from a plain program's by a relative error of at most 0.000065.
Values sent between devices are 32-bit elements; how exact they have to be, the bound alone decides.
No kernel may reach another device: no remote copies, remote signals or barrier semaphores. Data moves between devices by JAX's collectives and lax.ppermute only.
A program may use at most 128 MiB of HBM per device.

v0:
```python
import jax
import jax.numpy as jnp
from jax import lax
from jax.sharding import PartitionSpec as P


def passed_along(block, axis, distance):
    devices = range(lax.axis_size(axis))
    route = [((i - distance) % len(devices), i) for i in devices]
    return lax.ppermute(block, axis, route)


def gram_tile(own_block, other_block):
    return lax.dot_general(
        own_block,
        other_block,
        (((1,), (1,)), ((), ())),
        precision=lax.Precision.HIGHEST,
        preferred_element_type=jnp.float32,
    )


def on_device(three_index, coefficients):
    row_count = three_index.shape[0]
    aux_count = three_index.shape[1]
    flattened = three_index.reshape(row_count * aux_count, three_index.shape[2])
    partial_x = jnp.dot(
        flattened,
        lax.all_gather(coefficients, "blk", axis=1, tiled=True),
        precision=lax.Precision.HIGHEST,
        preferred_element_type=jnp.float32,
    )
    partial_x = partial_x.reshape(row_count, aux_count, partial_x.shape[1])
    half_x = lax.psum_scatter(partial_x, "col", scatter_dimension=2, tiled=True)
    own_block = half_x.reshape(row_count, aux_count * half_x.shape[2])
    cycle_length = lax.axis_size("blk")
    cycle_place = lax.axis_index("blk")

    def place_tile(exchange_part, block_tile, block_index):
        column = jnp.mod(block_index, cycle_length) * row_count
        return lax.dynamic_update_slice(exchange_part, block_tile, (jnp.int32(0), column))

    exchange_part = jnp.zeros((row_count, row_count * cycle_length), jnp.float32)
    exchange_part = place_tile(exchange_part, gram_tile(own_block, own_block), cycle_place)

    def advance(step_index, carry):
        moving, exchange_part = carry
        moving = passed_along(moving, "blk", 1)
        exchange_part = place_tile(
            exchange_part, gram_tile(own_block, moving), cycle_place - step_index
        )
        return (moving, exchange_part)

    moving, exchange_part = lax.fori_loop(1, cycle_length, advance, (own_block, exchange_part))
    return lax.psum_scatter(exchange_part, "col", scatter_dimension=0, tiled=True)


def solution(mesh):
    return jax.shard_map(
        on_device,
        mesh=mesh,
        in_specs=(P("blk", None, "col"), P("col", "blk")),
        out_specs=P(("blk", "col"), None),
        check_vma=False,
    )
```

profile of v0, /device:TPU:0, one launch (start us, length us, event | category | flops | bytes accessed | tf_op | source)
XLA Modules:
  0.0 700.3 jit_solution(17133692003925320395)
XLA Ops:
  7.3 38.1 %all-gather.2.cloned.1.call-done = f32[512,1024]{0,1:T(8,128)} async-done(((f32[512,64]{0,1:T(8,128)}), f32[512,1024]{0,1:T(8,128)}) %all-gather.2.cloned.1.call-update) | async-done | bytes 2097168 | tf_op jit(solution)/shard_map/all_gather | solution.py:29
  45.4 24.8 %fusion = f32[256,12,1024]{2,0,1:T(8,128)} fusion(f32[256,12,512]{2,0,1:T(8,128)} %param.4, f32[512,1024]{0,1:T(8,128)} %all-gather.2.cloned.1.call-done), kind=kOutput, calls=%fused_computation.1 | convolution fusion | flops 19327352832 | bytes 20971520 | tf_op jit(solution)/shard_map/dot_general | solution.py:27
  70.5 152.1 %reduce-scatter.3.cloned.1.call-done = f32[256,12,128]{2,0,1:T(8,128)} async-done(((f32[256,12,1024]{2,0,1:T(8,128)}), f32[256,12,128]{2,0,1:T(8,128)}) %reduce-scatter.3.cloned.1.call-update) | async-done | bytes 1572880 | tf_op jit(solution)/shard_map/reduce_scatter | solution.py:34
  222.6 1.9 copy.3
  225.0 1.2 copy.9
  227.5 1.4 fusion.2
  229.0 1.9 copy-done
  230.9 383.0 %while.17 = (s32[]{:T(128)}, f32[256,1536]{1,0:T(8,128)}, f32[256,4096]{1,0:T(8,128)}, f32[256,1536]{1,0:T(8,128)S(1)}, s32[]{:T(128)}, /*index=5*/s32[]{:T(128)...) while((s32[]{:T(128)}, f32[256,1536]{1,0:T(8,128)}, f32[256,4096]{1,0:T(8,128)}, ...), condition=%wide.region_2.3_spmd, body=%wide.region_1.2_spmd.sunk | while | flops 1207959552 | bytes 12845376 | solution.py:54
  230.9 22.2 %collective-permute-done = f32[256,1536]{1,0:T(8,128)S(1)} collective-permute-done((f32[256,1536]{1,0:T(8,128)}, f32[256,1536]{1,0:T(8,128)S(1)}, u32[]{:S(2)}, u32[]{:S(2)}) %collective-permute-start) | collective-permute-done | bytes 1572896 | tf_op jit(solution)/shard_map/while/body/eval_jaxpr/ppermute | solution.py:10
  253.1 1.2 copy.15
  254.3 2.2 convolution_dynamic-update-slice_fusion.2
  256.4 22.2 %collective-permute-done = f32[256,1536]{1,0:T(8,128)S(1)} collective-permute-done((f32[256,1536]{1,0:T(8,128)}, f32[256,1536]{1,0:T(8,128)S(1)}, u32[]{:S(2)}, u32[]{:S(2)}) %collective-permute-start) | collective-permute-done | bytes 1572896 | tf_op jit(solution)/shard_map/while/body/eval_jaxpr/ppermute | solution.py:10
  278.6 1.2 copy.15
  279.8 2.2 convolution_dynamic-update-slice_fusion.2
  281.9 22.2 %collective-permute-done = f32[256,1536]{1,0:T(8,128)S(1)} collective-permute-done((f32[256,1536]{1,0:T(8,128)}, f32[256,1536]{1,0:T(8,128)S(1)}, u32[]{:S(2)}, u32[]{:S(2)}) %collective-permute-start) | collective-permute-done | bytes 1572896 | tf_op jit(solution)/shard_map/while/body/eval_jaxpr/ppermute | solution.py:10
  304.1 1.2 copy.15
  305.3 2.2 convolution_dynamic-update-slice_fusion.2
  307.5 22.2 %collective-permute-done = f32[256,1536]{1,0:T(8,128)S(1)} collective-permute-done((f32[256,1536]{1,0:T(8,128)}, f32[256,1536]{1,0:T(8,128)S(1)}, u32[]{:S(2)}, u32[]{:S(2)}) %collective-permute-start) | collective-permute-done | bytes 1572896 | tf_op jit(solution)/shard_map/while/body/eval_jaxpr/ppermute | solution.py:10
  329.6 1.2 copy.15
  330.8 2.2 convolution_dynamic-update-slice_fusion.2
  333.0 22.2 %collective-permute-done = f32[256,1536]{1,0:T(8,128)S(1)} collective-permute-done((f32[256,1536]{1,0:T(8,128)}, f32[256,1536]{1,0:T(8,128)S(1)}, u32[]{:S(2)}, u32[]{:S(2)}) %collective-permute-start) | collective-permute-done | bytes 1572896 | tf_op jit(solution)/shard_map/while/body/eval_jaxpr/ppermute | solution.py:10
  355.2 1.2 copy.15
  356.3 2.2 convolution_dynamic-update-slice_fusion.2
  358.5 22.2 %collective-permute-done = f32[256,1536]{1,0:T(8,128)S(1)} collective-permute-done((f32[256,1536]{1,0:T(8,128)}, f32[256,1536]{1,0:T(8,128)S(1)}, u32[]{:S(2)}, u32[]{:S(2)}) %collective-permute-start) | collective-permute-done | bytes 1572896 | tf_op jit(solution)/shard_map/while/body/eval_jaxpr/ppermute | solution.py:10
  380.7 1.2 copy.15
  381.9 2.2 convolution_dynamic-update-slice_fusion.2
  384.0 22.2 %collective-permute-done = f32[256,1536]{1,0:T(8,128)S(1)} collective-permute-done((f32[256,1536]{1,0:T(8,128)}, f32[256,1536]{1,0:T(8,128)S(1)}, u32[]{:S(2)}, u32[]{:S(2)}) %collective-permute-start) | collective-permute-done | bytes 1572896 | tf_op jit(solution)/shard_map/while/body/eval_jaxpr/ppermute | solution.py:10
  406.2 1.2 copy.15
  407.4 2.2 convolution_dynamic-update-slice_fusion.2
  409.5 22.2 %collective-permute-done = f32[256,1536]{1,0:T(8,128)S(1)} collective-permute-done((f32[256,1536]{1,0:T(8,128)}, f32[256,1536]{1,0:T(8,128)S(1)}, u32[]{:S(2)}, u32[]{:S(2)}) %collective-permute-start) | collective-permute-done | bytes 1572896 | tf_op jit(solution)/shard_map/while/body/eval_jaxpr/ppermute | solution.py:10
  431.7 1.2 copy.15
  432.9 2.2 convolution_dynamic-update-slice_fusion.2
  435.1 22.2 %collective-permute-done = f32[256,1536]{1,0:T(8,128)S(1)} collective-permute-done((f32[256,1536]{1,0:T(8,128)}, f32[256,1536]{1,0:T(8,128)S(1)}, u32[]{:S(2)}, u32[]{:S(2)}) %collective-permute-start) | collective-permute-done | bytes 1572896 | tf_op jit(solution)/shard_map/while/body/eval_jaxpr/ppermute | solution.py:10
  457.2 1.2 copy.15
  458.4 2.2 convolution_dynamic-update-slice_fusion.2
  460.6 22.2 %collective-permute-done = f32[256,1536]{1,0:T(8,128)S(1)} collective-permute-done((f32[256,1536]{1,0:T(8,128)}, f32[256,1536]{1,0:T(8,128)S(1)}, u32[]{:S(2)}, u32[]{:S(2)}) %collective-permute-start) | collective-permute-done | bytes 1572896 | tf_op jit(solution)/shard_map/while/body/eval_jaxpr/ppermute | solution.py:10
  484.0 2.2 convolution_dynamic-update-slice_fusion.2
  486.2 22.2 %collective-permute-done = f32[256,1536]{1,0:T(8,128)S(1)} collective-permute-done((f32[256,1536]{1,0:T(8,128)}, f32[256,1536]{1,0:T(8,128)S(1)}, u32[]{:S(2)}, u32[]{:S(2)}) %collective-permute-start) | collective-permute-done | bytes 1572896 | tf_op jit(solution)/shard_map/while/body/eval_jaxpr/ppermute | solution.py:10
  509.5 2.2 convolution_dynamic-update-slice_fusion.2
  511.7 22.2 %collective-permute-done = f32[256,1536]{1,0:T(8,128)S(1)} collective-permute-done((f32[256,1536]{1,0:T(8,128)}, f32[256,1536]{1,0:T(8,128)S(1)}, u32[]{:S(2)}, u32[]{:S(2)}) %collective-permute-start) | collective-permute-done | bytes 1572896 | tf_op jit(solution)/shard_map/while/body/eval_jaxpr/ppermute | solution.py:10
  535.1 2.2 convolution_dynamic-update-slice_fusion.2
  537.3 22.2 %collective-permute-done = f32[256,1536]{1,0:T(8,128)S(1)} collective-permute-done((f32[256,1536]{1,0:T(8,128)}, f32[256,1536]{1,0:T(8,128)S(1)}, u32[]{:S(2)}, u32[]{:S(2)}) %collective-permute-start) | collective-permute-done | bytes 1572896 | tf_op jit(solution)/shard_map/while/body/eval_jaxpr/ppermute | solution.py:10
  560.6 2.2 convolution_dynamic-update-slice_fusion.2
  562.8 22.2 %collective-permute-done = f32[256,1536]{1,0:T(8,128)S(1)} collective-permute-done((f32[256,1536]{1,0:T(8,128)}, f32[256,1536]{1,0:T(8,128)S(1)}, u32[]{:S(2)}, u32[]{:S(2)}) %collective-permute-start) | collective-permute-done | bytes 1572896 | tf_op jit(solution)/shard_map/while/body/eval_jaxpr/ppermute | solution.py:10
  586.1 2.2 convolution_dynamic-update-slice_fusion.2
  588.4 22.2 %collective-permute-done = f32[256,1536]{1,0:T(8,128)S(1)} collective-permute-done((f32[256,1536]{1,0:T(8,128)}, f32[256,1536]{1,0:T(8,128)S(1)}, u32[]{:S(2)}, u32[]{:S(2)}) %collective-permute-start) | collective-permute-done | bytes 1572896 | tf_op jit(solution)/shard_map/while/body/eval_jaxpr/ppermute | solution.py:10
  611.7 2.2 convolution_dynamic-update-slice_fusion.2
  613.9 79.8 %reduce-scatter.5.cloned.1.call-done = f32[32,4096]{1,0:T(8,128)} async-done(((f32[256,4096]{1,0:T(8,128)}), f32[32,4096]{1,0:T(8,128)}) %reduce-scatter.5.cloned.1.call-update) | async-done | bytes 524304 | tf_op jit(solution)/shard_map/reduce_scatter | solution.py:55
  (32 shorter events, 9.9 us)
Async XLA Ops:
  6.5 38.9 %all-gather.2.cloned.1.call-start = ((), (), s32[]{:S(2)}) async-start(), calls=%async_computation.2 | async-start | bytes 2228224 | tf_op jit(solution)/shard_map/all_gather | solution.py:29
  7.3 215.3 %reduce-scatter.3.cloned.1.call-start = ((), (), s32[]{:S(2)}) async-start(), calls=%async_computation.3 | async-start | bytes 14155776 | tf_op jit(solution)/shard_map/reduce_scatter | solution.py:34
  70.3 623.5 %reduce-scatter.5.cloned.1.call-start = ((), (), s32[]{:S(2)}) async-start(), calls=%async_computation.4 | async-start | bytes 4718592 | tf_op jit(solution)/shard_map/reduce_scatter | solution.py:55
  226.1 1.4 copy-start.1
  229.0 1.9 copy-start
  230.9 22.2 %collective-permute-start = (f32[256,1536]{1,0:T(8,128)}, f32[256,1536]{1,0:T(8,128)S(1)}, u32[]{:S(2)}, u32[]{:S(2)}) collective-permute-start(f32[256,1536]{1,0:T(8,128)} %get-tuple-element.197), channel_id=1, source_target_pairs={{120,0},{0,8},{8,16},{16,24},{24,32},{32,40},{40,48},{48,56},{56,6... | collective-permute-start | bytes 4718600 | tf_op jit(solution)/shard_map/while/body/eval_jaxpr/ppermute | solution.py:10
  256.4 22.2 %collective-permute-start = (f32[256,1536]{1,0:T(8,128)}, f32[256,1536]{1,0:T(8,128)S(1)}, u32[]{:S(2)}, u32[]{:S(2)}) collective-permute-start(f32[256,1536]{1,0:T(8,128)} %get-tuple-element.197), channel_id=1, source_target_pairs={{120,0},{0,8},{8,16},{16,24},{24,32},{32,40},{40,48},{48,56},{56,6... | collective-permute-start | bytes 4718600 | tf_op jit(solution)/shard_map/while/body/eval_jaxpr/ppermute | solution.py:10
  281.9 22.2 %collective-permute-start = (f32[256,1536]{1,0:T(8,128)}, f32[256,1536]{1,0:T(8,128)S(1)}, u32[]{:S(2)}, u32[]{:S(2)}) collective-permute-start(f32[256,1536]{1,0:T(8,128)} %get-tuple-element.197), channel_id=1, source_target_pairs={{120,0},{0,8},{8,16},{16,24},{24,32},{32,40},{40,48},{48,56},{56,6... | collective-permute-start | bytes 4718600 | tf_op jit(solution)/shard_map/while/body/eval_jaxpr/ppermute | solution.py:10
  307.5 22.2 %collective-permute-start = (f32[256,1536]{1,0:T(8,128)}, f32[256,1536]{1,0:T(8,128)S(1)}, u32[]{:S(2)}, u32[]{:S(2)}) collective-permute-start(f32[256,1536]{1,0:T(8,128)} %get-tuple-element.197), channel_id=1, source_target_pairs={{120,0},{0,8},{8,16},{16,24},{24,32},{32,40},{40,48},{48,56},{56,6... | collective-permute-start | bytes 4718600 | tf_op jit(solution)/shard_map/while/body/eval_jaxpr/ppermute | solution.py:10
  333.0 22.2 %collective-permute-start = (f32[256,1536]{1,0:T(8,128)}, f32[256,1536]{1,0:T(8,128)S(1)}, u32[]{:S(2)}, u32[]{:S(2)}) collective-permute-start(f32[256,1536]{1,0:T(8,128)} %get-tuple-element.197), channel_id=1, source_target_pairs={{120,0},{0,8},{8,16},{16,24},{24,32},{32,40},{40,48},{48,56},{56,6... | collective-permute-start | bytes 4718600 | tf_op jit(solution)/shard_map/while/body/eval_jaxpr/ppermute | solution.py:10
  358.5 22.2 %collective-permute-start = (f32[256,1536]{1,0:T(8,128)}, f32[256,1536]{1,0:T(8,128)S(1)}, u32[]{:S(2)}, u32[]{:S(2)}) collective-permute-start(f32[256,1536]{1,0:T(8,128)} %get-tuple-element.197), channel_id=1, source_target_pairs={{120,0},{0,8},{8,16},{16,24},{24,32},{32,40},{40,48},{48,56},{56,6... | collective-permute-start | bytes 4718600 | tf_op jit(solution)/shard_map/while/body/eval_jaxpr/ppermute | solution.py:10
  384.0 22.2 %collective-permute-start = (f32[256,1536]{1,0:T(8,128)}, f32[256,1536]{1,0:T(8,128)S(1)}, u32[]{:S(2)}, u32[]{:S(2)}) collective-permute-start(f32[256,1536]{1,0:T(8,128)} %get-tuple-element.197), channel_id=1, source_target_pairs={{120,0},{0,8},{8,16},{16,24},{24,32},{32,40},{40,48},{48,56},{56,6... | collective-permute-start | bytes 4718600 | tf_op jit(solution)/shard_map/while/body/eval_jaxpr/ppermute | solution.py:10
  409.5 22.2 %collective-permute-start = (f32[256,1536]{1,0:T(8,128)}, f32[256,1536]{1,0:T(8,128)S(1)}, u32[]{:S(2)}, u32[]{:S(2)}) collective-permute-start(f32[256,1536]{1,0:T(8,128)} %get-tuple-element.197), channel_id=1, source_target_pairs={{120,0},{0,8},{8,16},{16,24},{24,32},{32,40},{40,48},{48,56},{56,6... | collective-permute-start | bytes 4718600 | tf_op jit(solution)/shard_map/while/body/eval_jaxpr/ppermute | solution.py:10
  435.1 22.2 %collective-permute-start = (f32[256,1536]{1,0:T(8,128)}, f32[256,1536]{1,0:T(8,128)S(1)}, u32[]{:S(2)}, u32[]{:S(2)}) collective-permute-start(f32[256,1536]{1,0:T(8,128)} %get-tuple-element.197), channel_id=1, source_target_pairs={{120,0},{0,8},{8,16},{16,24},{24,32},{32,40},{40,48},{48,56},{56,6... | collective-permute-start | bytes 4718600 | tf_op jit(solution)/shard_map/while/body/eval_jaxpr/ppermute | solution.py:10
  460.6 22.2 %collective-permute-start = (f32[256,1536]{1,0:T(8,128)}, f32[256,1536]{1,0:T(8,128)S(1)}, u32[]{:S(2)}, u32[]{:S(2)}) collective-permute-start(f32[256,1536]{1,0:T(8,128)} %get-tuple-element.197), channel_id=1, source_target_pairs={{120,0},{0,8},{8,16},{16,24},{24,32},{32,40},{40,48},{48,56},{56,6... | collective-permute-start | bytes 4718600 | tf_op jit(solution)/shard_map/while/body/eval_jaxpr/ppermute | solution.py:10
  486.2 22.2 %collective-permute-start = (f32[256,1536]{1,0:T(8,128)}, f32[256,1536]{1,0:T(8,128)S(1)}, u32[]{:S(2)}, u32[]{:S(2)}) collective-permute-start(f32[256,1536]{1,0:T(8,128)} %get-tuple-element.197), channel_id=1, source_target_pairs={{120,0},{0,8},{8,16},{16,24},{24,32},{32,40},{40,48},{48,56},{56,6... | collective-permute-start | bytes 4718600 | tf_op jit(solution)/shard_map/while/body/eval_jaxpr/ppermute | solution.py:10
  511.7 22.2 %collective-permute-start = (f32[256,1536]{1,0:T(8,128)}, f32[256,1536]{1,0:T(8,128)S(1)}, u32[]{:S(2)}, u32[]{:S(2)}) collective-permute-start(f32[256,1536]{1,0:T(8,128)} %get-tuple-element.197), channel_id=1, source_target_pairs={{120,0},{0,8},{8,16},{16,24},{24,32},{32,40},{40,48},{48,56},{56,6... | collective-permute-start | bytes 4718600 | tf_op jit(solution)/shard_map/while/body/eval_jaxpr/ppermute | solution.py:10
  537.3 22.2 %collective-permute-start = (f32[256,1536]{1,0:T(8,128)}, f32[256,1536]{1,0:T(8,128)S(1)}, u32[]{:S(2)}, u32[]{:S(2)}) collective-permute-start(f32[256,1536]{1,0:T(8,128)} %get-tuple-element.197), channel_id=1, source_target_pairs={{120,0},{0,8},{8,16},{16,24},{24,32},{32,40},{40,48},{48,56},{56,6... | collective-permute-start | bytes 4718600 | tf_op jit(solution)/shard_map/while/body/eval_jaxpr/ppermute | solution.py:10
  562.8 22.2 %collective-permute-start = (f32[256,1536]{1,0:T(8,128)}, f32[256,1536]{1,0:T(8,128)S(1)}, u32[]{:S(2)}, u32[]{:S(2)}) collective-permute-start(f32[256,1536]{1,0:T(8,128)} %get-tuple-element.197), channel_id=1, source_target_pairs={{120,0},{0,8},{8,16},{16,24},{24,32},{32,40},{40,48},{48,56},{56,6... | collective-permute-start | bytes 4718600 | tf_op jit(solution)/shard_map/while/body/eval_jaxpr/ppermute | solution.py:10
  588.4 22.2 %collective-permute-start = (f32[256,1536]{1,0:T(8,128)}, f32[256,1536]{1,0:T(8,128)S(1)}, u32[]{:S(2)}, u32[]{:S(2)}) collective-permute-start(f32[256,1536]{1,0:T(8,128)} %get-tuple-element.197), channel_id=1, source_target_pairs={{120,0},{0,8},{8,16},{16,24},{24,32},{32,40},{40,48},{48,56},{56,6... | collective-permute-start | bytes 4718600 | tf_op jit(solution)/shard_map/while/body/eval_jaxpr/ppermute | solution.py:10
Sparse Core Ops, SparseCore 0:
  9.1 36.3 all-gather.1
  70.4 152.1 reduce-scatter.2
  614.0 79.6 reduce-scatter.4
where the time goes:
time: 700 us
  waiting for transfers between devices  603 us (86%)
  matrix products  59.2 us (8%)
  local copies, waits for them, and re-layouts  24.4 us (3%)
  between operations  13.2 us (2%)
    ppermute x15, waiting for transfers between devices, passed_along(): return lax.ppermute(block, axis, route)  332 us
    reduce_scatter x1, waiting for transfers between devices, on_device(): half_x = lax.psum_scatter(partial_x, 'col', scatter_dimension=2, tiled=True)  152 us
    reduce_scatter x1, waiting for transfers between devices, on_device(): lax.psum_scatter(exchange_part, 'col', scatter_dimension=0, tiled=True)  79.8 us
    all_gather x1, waiting for transfers between devices, on_device(): lax.all_gather(coefficients, 'blk', axis=1, tiled=True)  38.1 us
    dot_general x16, matrix products, gram_tile(): lax.dot_general(own_block, other_block, (((1,), (1,)), ((), ())), precisi...  34.4 us
    dot_general x1, matrix products, on_device(): jnp.dot(flattened, lax.all_gather(coefficients, 'blk', axis=1, tiled=True...  24.8 us
    while x15, local copies, waits for them, and re-layouts  17.6 us
  transfers between devices with their start and end apart: 18, of which 18 were waited for; matrix products, arithmetic and copies ran while one was open for 0% of the time, Pallas kernels for 0%

commit v1 on v0

v1 whole, which is shorter than its diff:
```python
import jax
import jax.numpy as jnp
from jax import lax
from jax.sharding import PartitionSpec as P

Y, ZL, CORES, X, ZH = 4, 2, 2, 4, 2
HIGH = lax.Precision.HIGH
X_GROUPS = [[x * ZH + zh for x in range(X)] for zh in range(ZH)]


def block_of(y, zl, core):
    return ((y % Y) * ZL + zl % ZL) * CORES + core % CORES


def upper(y):
    return (y % Y) // 2


def next_row(y, zl, core):
    return y + 1, zl, core


def next_across(y, zl, core):
    return y + 1, 1 - zl, (core + zl + upper(y)) % 2


def previous_row(y, zl, core):
    return y - 1, zl, (core + upper(y)) % 2


def places():
    return [(y, zl, core) for y in range(Y) for zl in range(ZL) for core in range(CORES)]


def fetched(value, source_of):
    route = [(block_of(*source_of(*at)), block_of(*at)) for at in places()]
    return lax.ppermute(value, "blk", route)


def delivered(value, target_of):
    route = [(block_of(*at), block_of(*target_of(*at))) for at in places()]
    return lax.ppermute(value, "blk", route)


def other_core(y, zl, core):
    return y, zl, 1 - core


def over_to_across(y, zl, core):
    return y, 1 - zl, (core + zl + upper(y)) % 2


def product(left, right):
    return lax.dot_general(
        left, right, (((1,), (1,)), ((), ())), precision=HIGH, preferred_element_type=jnp.float32
    )


def all_orbitals(coefficients):
    mine = coefficients.T
    x = lax.axis_index("col") // ZH
    ring = {}
    for step in range(1, X):
        route = [(((t + step) % X) * ZH + zh, t * ZH + zh) for t in range(X) for zh in range(ZH)]
        ring[step] = lax.ppermute(mine, "col", route)
    order = [ring[1], ring[2], ring[3], mine]
    twice = jnp.stack(order + order[:3])
    by_x = lax.dynamic_slice(twice, (X - 1 - x, 0, 0), (X,) + mine.shape)
    joined = by_x.transpose(1, 0, 2).reshape(mine.shape[0], X * mine.shape[1])
    return lax.all_gather(joined, "blk", axis=0, tiled=True)


def on_device(three_index, coefficients):
    rows, aux, _ = three_index.shape
    by_aux = three_index.transpose(1, 0, 2)
    blk, col = lax.axis_index("blk"), lax.axis_index("col")
    y, zl, core = blk // (ZL * CORES), (blk // CORES) % ZL, blk % CORES
    zh = col % ZH
    swap_zh = [(x * ZH + 1 - h, x * ZH + h) for x in range(X) for h in range(ZH)]

    orbitals = all_orbitals(coefficients)
    half = orbitals.shape[0] // ZH
    kept = lax.dynamic_slice(orbitals, (zh * half, 0), (half, orbitals.shape[1]))
    sent = lax.dynamic_slice(orbitals, ((1 - zh) * half, 0), (half, orbitals.shape[1]))

    tiles = None
    for chunk in range(aux // X):
        part = lax.all_to_all(
            by_aux[X * chunk : X * (chunk + 1)],
            "col",
            split_axis=0,
            concat_axis=2,
            tiled=True,
            axis_index_groups=X_GROUPS,
        )[0]
        arrived = lax.ppermute(product(part, sent), "col", swap_zh)
        own = product(part, kept) + arrived
        other = fetched(own, other_core)
        below = fetched(own, next_row)
        above = fetched(own, previous_row)
        across = fetched(below, over_to_across)
        pair = jnp.concatenate([own, other])
        terms = (
            product(own, pair),
            product(below, pair),
            product(across, jnp.concatenate([pair, below])),
            product(above, jnp.concatenate([below, across])),
        )
        tiles = terms if tiles is None else tuple(a + b for a, b in zip(tiles, terms))

    own_t, below_t, across_t, above_t = tiles
    flip = lambda t: t.T
    cut = lambda t, k: t[:, k * rows : (k + 1) * rows]
    slabs = [
        own_t, flip(cut(below_t, 0)), flip(cut(across_t, 0)),
        flip(cut(below_t, 1)), flip(cut(across_t, 1)),
        below_t, flip(cut(across_t, 2)), flip(cut(above_t, 0)),
        across_t, flip(cut(above_t, 1)),
        above_t,
    ]
    whole = jnp.concatenate(slabs, axis=1)
    shares = lax.axis_size("col")
    split = whole.reshape(shares, rows // shares, whole.shape[1])
    summed = lax.all_to_all(split, "col", split_axis=0, concat_axis=0, tiled=True).sum(0)

    def span(first, count):
        return summed[:, first * rows : (first + count) * rows]

    def columns(at):
        other_at = other_core(*at)
        return {"own": at, "other": other_at, "below": next_row(*at),
                "across": next_across(*at), "above": previous_row(*at)}

    here = (y, zl, core)
    partner = other_core(*here)
    of_below = (y - 1, zl, core)
    of_across = (y - 1, 1 - zl, (core + (1 - zl) + upper(y - 1)) % 2)
    of_above = (y + 1, zl, (core + upper(y + 1)) % 2)
    arrivals = [
        (span(0, 4), here, ("own", "other", "below", "across")),
        (delivered(span(4, 2), other_core), partner, ("below", "across")),
        (delivered(span(6, 4), next_row), of_below, ("own", "other", "across", "above")),
        (delivered(span(10, 4), next_across), of_across, ("own", "other", "below", "above")),
        (delivered(span(14, 2), previous_row), of_above, ("below", "across")),
    ]
    result = jnp.zeros(summed.shape, jnp.float32)
    for slab, source, names in arrivals:
        at = columns(source)
        for k, name in enumerate(names):
            column = block_of(*at[name]) * rows
            piece = slab[:, k * rows : (k + 1) * rows]
            result = lax.dynamic_update_slice(result, piece, (jnp.int32(0), column))
    return result


def solution(mesh):
    return jax.shard_map(
        on_device,
        mesh=mesh,
        in_specs=(P("blk", None, "col"), P("col", "blk")),
        out_specs=P(("blk", "col"), None),
        check_vma=False,
    )
```

time: 700 us -> 316 us (0.45)
  waiting for transfers between devices: 603 us -> 128 us
  blocking collectives: 0 us -> 58.5 us
  starting transfers between devices: 0.3 us -> 36.5 us
  matrix products: 59.2 us -> 45.4 us
    ppermute x15 -> x22, waiting for transfers between devices: 332 us -> 58.6 us  [the longest x12 45.3 us: fetched(): return lax.ppermute(value, 'blk', route)]
    reduce_scatter x2 -> x0, waiting for transfers between devices: 232 us -> none  [the longest x1 152 us: on_device(): half_x = lax.psum_scatter(partial_x, 'col', scatter_dimension=2, tiled=True)]
    all_to_all x0 -> x2, waiting for transfers between devices: none -> 69.5 us  [the longest x1 58.7 us: on_device(): lax.all_to_all(split, 'col', split_axis=0, concat_axis=0, tiled=True).sum(0)]
    all_to_all x0 -> x2, blocking collectives: none -> 58.5 us  [on_device(): lax.all_to_all(by_aux[X * chunk:X * (chunk + 1)], 'col', split_axis=0, co...]
    all_gather x1, waiting for transfers between devices: 38.1 us -> 0.02 us  [all_orbitals(): return lax.all_gather(joined, 'blk', axis=0, tiled=True)]
    ppermute x15 -> x22, starting transfers between devices: 0.04 us -> 28.3 us  [the longest x12 10.3 us: fetched(): return lax.ppermute(value, 'blk', route)]
    while x16 -> x0, local copies, waits for them, and re-layouts: 18 us -> none
    unnamed x5 -> x46, local copies, waits for them, and re-layouts: 4.04 us -> 20.5 us
  transfers between devices with their start and end apart: 18 -> 25, of which waited for: 18 -> 13; matrix products, arithmetic and copies ran while one was open for 0% -> 20% of each run, Pallas kernels for 0% -> 0%
where the time goes in v1:
time: 316 us; the launch traced here: 315 us
  waiting for transfers between devices  128 us (41%)
  blocking collectives  58.5 us (19%)
  matrix products  45.4 us (14%)
  starting transfers between devices  36.5 us (12%)
  local copies, waits for them, and re-layouts  29.4 us (9%)
  between operations  14.6 us (5%)
    all_to_all x1, waiting for transfers between devices, on_device(): lax.all_to_all(split, 'col', split_axis=0, concat_axis=0, tiled=True).sum(0)  58.7 us
    all_to_all x2, blocking collectives, on_device(): lax.all_to_all(by_aux[X * chunk:X * (chunk + 1)], 'col', split_axis=0, co...  58.5 us
    dot_general x18, matrix products, product(): lax.dot_general(left, right, (((1,), (1,)), ((), ())), precision=HIGH, pr...  45.4 us
    ppermute x12, waiting for transfers between devices, fetched(): return lax.ppermute(value, 'blk', route)  45.3 us
    unnamed x46, local copies, waits for them, and re-layouts  20.5 us
    all_to_all x1, waiting for transfers between devices, on_device(): lax.all_to_all(by_aux[X * chunk:X * (chunk + 1)], 'col', split_axis=0, co...  10.8 us
    ppermute x12, starting transfers between devices, fetched(): return lax.ppermute(value, 'blk', route)  10.3 us
    ppermute x3, waiting for transfers between devices, all_orbitals(): ring[step] = lax.ppermute(mine, 'col', route)  7.77 us
  transfers between devices with their start and end apart: 25, of which 13 were waited for; matrix products, arithmetic and copies ran while one was open for 20% of the time, Pallas kernels for 0%

profile of v1, /device:TPU:0, one launch (start us, length us, event | category | flops | bytes accessed | tf_op | source)
XLA Modules:
  0.0 315.0 jit_solution(5301982362706362559)
XLA Ops:
  6.5 2.8 collective-permute-start
  11.1 4.2 %collective-permute-done = f32[64,512]{1,0:T(8,128)S(1)} collective-permute-done((f32[64,512]{1,0:T(8,128)}, f32[64,512]{1,0:T(8,128)S(1)}, u32[]{:S(2)}, u32[]{:S(2)}) %collective-permute-start) | collective-permute-done | bytes 131104 | tf_op jit(solution)/shard_map/ppermute | solution.py:65
  15.3 2.2 collective-permute-done.1
  17.5 1.4 collective-permute-done.2
  20.8 6.6 %copy.14 = f32[256,12,512]{0,2,1:T(8,128)} copy(f32[256,12,512]{2,0,1:T(8,128)} %param.2) | data formatting | bytes 12582912 | tf_op args[0]
  27.3 4.8 %fusion.100 = (f32[4,256,512]{1,2,0:T(8,128)}, f32[4,256,512]{1,2,0:T(8,128)S(1)}, f32[4,256,512]{1,2,0:T(8,128)S(1)}) fusion(f32[12,256,512]{1,2,0:T(8,128)} %bitcast.86), kind=kLoop, calls=%fused_computation.122 | loop fusion | bytes 12582912 | tf_op jit(solution)/shard_map/slice | solution.py:89
  32.2 29.8 %all_to_all.50 = f32[4,256,512]{1,2,0:T(8,128)} all-to-all(f32[4,256,512]{1,2,0:T(8,128)S(1)} %get-tuple-element.6), channel_id=1, replica_groups={{0,2,4,6},{1,3,5,7},{8,10,12,14},{9,11,13,15},{16,18,20,22},{17,19,21,2..., dimensions={0} | all-to-all | bytes 4194304 | tf_op jit(solution)/shard_map/all_to_all | solution.py:88
  62.0 28.7 %all_to_all.51 = f32[4,256,512]{1,2,0:T(8,128)} all-to-all(f32[4,256,512]{1,2,0:T(8,128)S(1)} %get-tuple-element.7), channel_id=1, replica_groups={{0,2,4,6},{1,3,5,7},{8,10,12,14},{9,11,13,15},{16,18,20,22},{17,19,21,2..., dimensions={0} | all-to-all | bytes 4194304 | tf_op jit(solution)/shard_map/all_to_all | solution.py:88
  90.7 3.6 %all-to-all-start = ((f32[4,256,512]{1,2,0:T(8,128)}), f32[4,256,512]{1,2,0:T(8,128)S(1)}, u32[]{:S(2)}, u32[]{:S(2)}) async-start(f32[4,256,512]{1,2,0:T(8,128)} %get-tuple-element.5), calls=%async_computation | async-start | bytes 4194304 | tf_op jit(solution)/shard_map/all_to_all | solution.py:88
  94.3 4.8 %fusion.51 = f32[256,512]{1,0:T(8,128)S(1)} fusion(f32[256,2048]{0,1:T(8,128)} %bitcast.91, f32[1024,2048]{1,0:T(8,128)} %all-gather.2.cloned.1.call-done, s32[]{:T(128)S(6)} %select_n.280), kind=kOutput, calls=%fused_computation.37 | convolution fusion | flops 1610612736 | bytes 6815748 | tf_op jit(solution)/shard_map/dot_general | solution.py:54
  99.2 3.9 %collective-permute-start.7 = (f32[256,512]{1,0:T(8,128)S(1)}, f32[256,512]{1,0:T(8,128)}, u32[]{:S(2)}, u32[]{:S(2)}) collective-permute-start(f32[256,512]{1,0:T(8,128)S(1)} %fusion.51), channel_id=1, source_target_pairs={{1,0},{0,1},{3,2},{2,3},{5,4},{4,5},{7,6},{6,7},{9,8},{8,9},{11,10... | collective-permute-start | bytes 1572872 | tf_op jit(solution)/shard_map/ppermute | solution.py:96
  103.1 4.9 %fusion.48 = f32[256,512]{1,0:T(8,128)} fusion(f32[256,2048]{0,1:T(8,128)S(1)} %bitcast.89, f32[1024,2048]{1,0:T(8,128)} %all-gather.2.cloned.1.call-done, s32[]{:T(128)S(6)} %select_n.280), kind=kOutput, calls=%fused_computation.36 | convolution fusion | flops 1610612736 | bytes 6815748 | tf_op jit(solution)/shard_map/dot_general | solution.py:54
  108.0 10.8 %all-to-all-done = f32[4,256,512]{1,2,0:T(8,128)S(1)} async-done(((f32[4,256,512]{1,2,0:T(8,128)}), f32[4,256,512]{1,2,0:T(8,128)S(1)}, u32[]{:S(2)}, u32[]{:S(2)}) %all-to-all-start) | async-done | bytes 2097184 | tf_op jit(solution)/shard_map/all_to_all | solution.py:88
  118.8 4.2 %fusion.45 = f32[256,512]{1,0:T(8,128)S(1)} fusion(f32[256,2048]{0,1:T(8,128)S(1)} %bitcast.87, f32[1024,2048]{1,0:T(8,128)} %all-gather.2.cloned.1.call-done, s32[]{:T(128)S(6)} %select_n.280), kind=kOutput, calls=%fused_computation.35 | convolution fusion | flops 1610612736 | bytes 6815748 | tf_op jit(solution)/shard_map/dot_general | solution.py:54
  123.0 3.5 %collective-permute-start.3 = (f32[256,512]{1,0:T(8,128)S(1)}, f32[256,512]{1,0:T(8,128)S(1)}, u32[]{:S(2)}, u32[]{:S(2)}) collective-permute-start(f32[256,512]{1,0:T(8,128)S(1)} %fusion.45), channel_id=1, source_target_pairs={{1,0},{0,1},{3,2},{2,3},{5,4},{4,5},{7,6},{6,7},{9,8},{8,9},{11,10... | collective-permute-start | bytes 1572872 | tf_op jit(solution)/shard_map/ppermute | solution.py:96
  126.5 4.2 %fusion.58 = f32[256,512]{1,0:T(8,128)S(1)} fusion(f32[256,512]{1,0:T(8,128)} %collective-permute-done.7, f32[256,2048]{0,1:T(8,128)S(1)} %bitcast.92, f32[1024,2048]{1,0:T(8,128)} %all-gather.2.cloned.1.call-done, s32[]{:T(128)S(6)} %select_n.279), kind=kOutput, calls=%fused_computation.45 | convolution fusion | flops 1610743808 | bytes 7340036 | tf_op jit(solution)/shard_map/dot_general | solution.py:54
  130.8 3.8 %collective-permute-start.11 = (f32[256,512]{1,0:T(8,128)S(1)}, f32[256,512]{1,0:T(8,128)S(1)}, u32[]{:S(2)}, u32[]{:S(2)}) collective-permute-start(f32[256,512]{1,0:T(8,128)S(1)} %fusion.58), channel_id=1, source_target_pairs={{32,0},{40,8},{48,16},{56,24},{64,32},{72,40},{80,48},{88,56},{96,... | collective-permute-start | bytes 1572872 | tf_op jit(solution)/shard_map/ppermute | solution.py:37
  134.6 5.1 %fusion.61 = f32[256,512]{1,0:T(8,128)} fusion(f32[256,512]{1,0:T(8,128)} %collective-permute-done.5, f32[256,2048]{0,1:T(8,128)S(1)} %bitcast.90, f32[1024,2048]{1,0:T(8,128)} %all-gather.2.cloned.1.call-done, s32[]{:T(128)S(6)} %select_n.279), kind=kOutput, calls=%fused_computation.46 | convolution fusion | flops 1610743808 | bytes 7340036 | tf_op jit(solution)/shard_map/dot_general | solution.py:54
  140.6 1.9 fusion.64
  143.1 3.8 %collective-permute-done.11 = f32[256,512]{1,0:T(8,128)S(1)} collective-permute-done((f32[256,512]{1,0:T(8,128)S(1)}, f32[256,512]{1,0:T(8,128)S(1)}, u32[]{:S(2)}, u32[]{:S(2)}) %collective-permute-start.11) | collective-permute-done | bytes 524320 | tf_op jit(solution)/shard_map/ppermute | solution.py:37
  148.7 9.5 %collective-permute-done.10 = f32[256,512]{1,0:T(8,128)S(1)} collective-permute-done((f32[256,512]{1,0:T(8,128)}, f32[256,512]{1,0:T(8,128)S(1)}, u32[]{:S(2)}, u32[]{:S(2)}) %collective-permute-start.10) | collective-permute-done | bytes 524320 | tf_op jit(solution)/shard_map/ppermute | solution.py:37
  158.2 1.9 fusion.67
  160.1 8.5 %collective-permute-done.9 = f32[256,512]{1,0:T(8,128)S(1)} collective-permute-done((f32[256,512]{1,0:T(8,128)S(1)}, f32[256,512]{1,0:T(8,128)S(1)}, u32[]{:S(2)}, u32[]{:S(2)}) %collective-permute-start.9) | collective-permute-done | bytes 524320 | tf_op jit(solution)/shard_map/ppermute | solution.py:37
  170.3 1.7 fusion.70
  172.8 1.9 collective-permute-start.12
  174.8 2.0 fusion.68
  176.8 1.5 fusion.55
  179.2 8.1 %collective-permute-done.14 = f32[256,512]{1,0:T(8,128)} collective-permute-done((f32[256,512]{1,0:T(8,128)}, f32[256,512]{1,0:T(8,128)}, u32[]{:S(2)}, u32[]{:S(2)}) %collective-permute-start.14) | collective-permute-done | bytes 524320 | tf_op jit(solution)/shard_map/ppermute | solution.py:37
  188.2 2.1 fusion.24
  190.3 8.2 %collective-permute-done.13 = f32[256,512]{1,0:T(8,128)} collective-permute-done((f32[256,512]{1,0:T(8,128)}, f32[256,512]{1,0:T(8,128)}, u32[]{:S(2)}, u32[]{:S(2)}) %collective-permute-start.13) | collective-permute-done | bytes 524320 | tf_op jit(solution)/shard_map/ppermute | solution.py:37
  198.5 2.4 fusion.18
  200.8 7.3 %collective-permute-done.12 = f32[256,512]{1,0:T(8,128)} collective-permute-done((f32[256,512]{1,0:T(8,128)S(1)}, f32[256,512]{1,0:T(8,128)}, u32[]{:S(2)}, u32[]{:S(2)}) %collective-permute-start.12) | collective-permute-done | bytes 524320 | tf_op jit(solution)/shard_map/ppermute | solution.py:37
  208.1 1.9 fusion.33
  210.9 1.1 copy.28
  212.8 1.1 copy.29
  215.3 1.9 constant_dynamic-update-slice_fusion.4
  217.2 1.1 copy.30
  218.3 2.0 fusion.78
  220.3 1.8 fusion.74
  222.2 1.8 fusion.57
  228.5 4.6 %all-to-all-start.3 = ((f32[8,32,4096]{2,1,0:T(8,128)}), f32[8,32,4096]{2,1,0:T(8,128)}, u32[]{:S(2)}, u32[]{:S(2)}) async-start(f32[8,32,4096]{2,1,0:T(8,128)} %bitcast.35), calls=%async_computation.3 | async-start | bytes 8388608 | tf_op jit(solution)/shard_map/all_to_all | solution.py:124
  233.7 58.7 %all-to-all-done.3 = f32[8,32,4096]{2,1,0:T(8,128)} async-done(((f32[8,32,4096]{2,1,0:T(8,128)}), f32[8,32,4096]{2,1,0:T(8,128)}, u32[]{:S(2)}, u32[]{:S(2)}) %all-to-all-start.3) | async-done | bytes 4194336 | tf_op jit(solution)/shard_map/all_to_all | solution.py:124
  292.4 2.4 reduce_sum.9
  295.0 1.2 collective-permute-start.19
  296.2 1.9 collective-permute-start.20
  298.1 2.8 collective-permute-start.21
  301.1 3.4 %collective-permute-done.19 = f32[32,1024]{1,0:T(8,128)S(1)} collective-permute-done((f32[32,1024]{1,0:T(8,128)S(1)}, f32[32,1024]{1,0:T(8,128)S(1)}, u32[]{:S(2)}, u32[]{:S(2)}) %collective-permute-start.19) | collective-permute-done | bytes 131104 | tf_op jit(solution)/shard_map/ppermute | solution.py:42
  304.5 2.1 collective-permute-done.20
  (101 shorter events, 20.6 us)
Async XLA Ops:
  6.5 87.8 %all-gather.2.cloned.1.call-start = ((), (), s32[]{:S(2)}) async-start(), calls=%async_computation.4 | async-start | bytes 8912896 | tf_op jit(solution)/shard_map/all_gather | solution.py:70
  6.5 8.7 %collective-permute-start = (f32[64,512]{1,0:T(8,128)}, f32[64,512]{1,0:T(8,128)S(1)}, u32[]{:S(2)}, u32[]{:S(2)}) collective-permute-start(f32[64,512]{1,0:T(8,128)} %bitcast.94), channel_id=1, source_target_pairs={{2,0},{3,1},{4,2},{5,3},{6,4},{7,5},{0,6},{1,7},{10,8},{11,9},{12,... | collective-permute-start | bytes 393224 | tf_op jit(solution)/shard_map/ppermute | solution.py:65
  9.4 8.1 %collective-permute-start.1 = (f32[64,512]{1,0:T(8,128)}, f32[64,512]{1,0:T(8,128)S(1)}, u32[]{:S(2)}, u32[]{:S(2)}) collective-permute-start(f32[64,512]{1,0:T(8,128)} %bitcast.95), channel_id=1, source_target_pairs={{4,0},{5,1},{6,2},{7,3},{0,4},{1,5},{2,6},{3,7},{12,8},{13,9},{14,... | collective-permute-start | bytes 393224 | tf_op jit(solution)/shard_map/ppermute | solution.py:65
  10.2 8.7 %collective-permute-start.2 = (f32[64,512]{1,0:T(8,128)}, f32[64,512]{1,0:T(8,128)S(1)}, u32[]{:S(2)}, u32[]{:S(2)}) collective-permute-start(f32[64,512]{1,0:T(8,128)} %bitcast.96), channel_id=1, source_target_pairs={{6,0},{7,1},{0,2},{1,3},{2,4},{3,5},{4,6},{5,7},{14,8},{15,9},{8,1... | collective-permute-start | bytes 393224 | tf_op jit(solution)/shard_map/ppermute | solution.py:65
  90.7 28.1 %all-to-all-start = ((f32[4,256,512]{1,2,0:T(8,128)}), f32[4,256,512]{1,2,0:T(8,128)S(1)}, u32[]{:S(2)}, u32[]{:S(2)}) async-start(f32[4,256,512]{1,2,0:T(8,128)} %get-tuple-element.5), calls=%async_computation | async-start | bytes 4194304 | tf_op jit(solution)/shard_map/all_to_all | solution.py:88
  94.3 8.7 %copy-start = (f32[4,256,512]{1,2,0:T(8,128)S(1)}, f32[4,256,512]{1,2,0:T(8,128)}, u32[]{:S(2)}) copy-start(f32[4,256,512]{1,2,0:T(8,128)} %all_to_all.51) | copy-start | bytes 6291460
  99.2 27.3 %collective-permute-start.7 = (f32[256,512]{1,0:T(8,128)S(1)}, f32[256,512]{1,0:T(8,128)}, u32[]{:S(2)}, u32[]{:S(2)}) collective-permute-start(f32[256,512]{1,0:T(8,128)S(1)} %fusion.51), channel_id=1, source_target_pairs={{1,0},{0,1},{3,2},{2,3},{5,4},{4,5},{7,6},{6,7},{9,8},{8,9},{11,10... | collective-permute-start | bytes 1572872 | tf_op jit(solution)/shard_map/ppermute | solution.py:96
  108.0 26.6 %collective-permute-start.5 = (f32[256,512]{1,0:T(8,128)}, f32[256,512]{1,0:T(8,128)}, u32[]{:S(2)}, u32[]{:S(2)}) collective-permute-start(f32[256,512]{1,0:T(8,128)} %fusion.48), channel_id=1, source_target_pairs={{1,0},{0,1},{3,2},{2,3},{5,4},{4,5},{7,6},{6,7},{9,8},{8,9},{11,10... | collective-permute-start | bytes 1572872 | tf_op jit(solution)/shard_map/ppermute | solution.py:96
  118.8 7.7 %copy-start.2 = (f32[4,256,512]{1,2,0:T(8,128)S(1)}, f32[4,256,512]{1,2,0:T(8,128)}, u32[]{:S(2)}) copy-start(f32[4,256,512]{1,2,0:T(8,128)} %all_to_all.50) | copy-start | bytes 6291460
  118.8 21.8 %slice-start = ((s8[8388608]{0:T(1024)(128)(4,1)}), s8[4194304]{0:T(1024)(128)(4,1)S(1)}, s32[]{:S(2)}) async-start(s8[8388608]{0:T(1024)(128)(4,1)} %bitcast.84), calls=%async_computation.5 | async-start | bytes 8388608
  122.9 11.7 %copy-start.1 = (f32[4,256,512]{1,2,0:T(8,128)S(1)}, f32[4,256,512]{1,2,0:T(8,128)}, u32[]{:S(2)}) copy-start(f32[4,256,512]{1,2,0:T(8,128)} %all_to_all.51) | copy-start | bytes 6291460
  123.0 17.6 %slice-start.1 = ((s8[8388608]{0:T(1024)(128)(4,1)}), s8[4194304]{0:T(1024)(128)(4,1)S(1)}, s32[]{:S(2)}) async-start(s8[8388608]{0:T(1024)(128)(4,1)} %bitcast.84), calls=%async_computation.6 | async-start | bytes 8388608
  123.0 17.6 %collective-permute-start.3 = (f32[256,512]{1,0:T(8,128)S(1)}, f32[256,512]{1,0:T(8,128)S(1)}, u32[]{:S(2)}, u32[]{:S(2)}) collective-permute-start(f32[256,512]{1,0:T(8,128)S(1)} %fusion.45), channel_id=1, source_target_pairs={{1,0},{0,1},{3,2},{2,3},{5,4},{4,5},{7,6},{6,7},{9,8},{8,9},{11,10... | collective-permute-start | bytes 1572872 | tf_op jit(solution)/shard_map/ppermute | solution.py:96
  130.7 12.1 %collective-permute-start.8 = (f32[256,512]{1,0:T(8,128)S(1)}, f32[256,512]{1,0:T(8,128)S(1)}, u32[]{:S(2)}, u32[]{:S(2)}) collective-permute-start(f32[256,512]{1,0:T(8,128)S(1)} %fusion.58), channel_id=1, source_target_pairs={{8,0},{0,8},{24,16},{16,24},{40,32},{32,40},{56,48},{48,56},{72,64... | collective-permute-start | bytes 1572872 | tf_op jit(solution)/shard_map/ppermute | solution.py:37
  130.8 16.1 %collective-permute-start.11 = (f32[256,512]{1,0:T(8,128)S(1)}, f32[256,512]{1,0:T(8,128)S(1)}, u32[]{:S(2)}, u32[]{:S(2)}) collective-permute-start(f32[256,512]{1,0:T(8,128)S(1)} %fusion.58), channel_id=1, source_target_pairs={{32,0},{40,8},{48,16},{56,24},{64,32},{72,40},{80,48},{88,56},{96,... | collective-permute-start | bytes 1572872 | tf_op jit(solution)/shard_map/ppermute | solution.py:37
  139.7 8.8 %collective-permute-start.6 = (f32[256,512]{1,0:T(8,128)}, f32[256,512]{1,0:T(8,128)S(1)}, u32[]{:S(2)}, u32[]{:S(2)}) collective-permute-start(f32[256,512]{1,0:T(8,128)} %fusion.61), channel_id=1, source_target_pairs={{8,0},{0,8},{24,16},{16,24},{40,32},{32,40},{56,48},{48,56},{72,64... | collective-permute-start | bytes 1572872 | tf_op jit(solution)/shard_map/ppermute | solution.py:37
  139.7 18.5 %collective-permute-start.10 = (f32[256,512]{1,0:T(8,128)}, f32[256,512]{1,0:T(8,128)S(1)}, u32[]{:S(2)}, u32[]{:S(2)}) collective-permute-start(f32[256,512]{1,0:T(8,128)} %fusion.61), channel_id=1, source_target_pairs={{32,0},{40,8},{48,16},{56,24},{64,32},{72,40},{80,48},{88,56},{96,... | collective-permute-start | bytes 1572872 | tf_op jit(solution)/shard_map/ppermute | solution.py:37
  142.5 17.6 %collective-permute-start.4 = (f32[256,512]{1,0:T(8,128)S(1)}, f32[256,512]{1,0:T(8,128)S(1)}, u32[]{:S(2)}, u32[]{:S(2)}) collective-permute-start(f32[256,512]{1,0:T(8,128)S(1)} %fusion.64), channel_id=1, source_target_pairs={{8,0},{0,8},{24,16},{16,24},{40,32},{32,40},{56,48},{48,56},{72,64... | collective-permute-start | bytes 1572872 | tf_op jit(solution)/shard_map/ppermute | solution.py:37
  142.8 26.6 %copy-start.3 = (f32[256,512]{1,0:T(8,128)}, f32[256,512]{1,0:T(8,128)S(1)}, u32[]{:S(2)}) copy-start(f32[256,512]{1,0:T(8,128)S(1)} %collective-permute-done.8) | copy-start | bytes 1572868
  142.8 25.9 %collective-permute-start.9 = (f32[256,512]{1,0:T(8,128)S(1)}, f32[256,512]{1,0:T(8,128)S(1)}, u32[]{:S(2)}, u32[]{:S(2)}) collective-permute-start(f32[256,512]{1,0:T(8,128)S(1)} %fusion.64), channel_id=1, source_target_pairs={{32,0},{40,8},{48,16},{56,24},{64,32},{72,40},{80,48},{88,56},{96,... | collective-permute-start | bytes 1572872 | tf_op jit(solution)/shard_map/ppermute | solution.py:37
  146.9 22.5 %copy-start.7 = (f32[256,512]{1,0:T(8,128)}, f32[256,512]{1,0:T(8,128)S(1)}, u32[]{:S(2)}) copy-start(f32[256,512]{1,0:T(8,128)S(1)} %collective-permute-done.11) | copy-start | bytes 1572868
  146.9 71.4 %collective-permute-start.17 = (f32[256,512]{1,0:T(8,128)S(1)}, f32[256,512]{1,0:T(8,128)}, u32[]{:S(2)}, u32[]{:S(2)}) collective-permute-start(f32[256,512]{1,0:T(8,128)S(1)} %fusion.58), channel_id=1, source_target_pairs={{96,0},{104,8},{112,16},{120,24},{0,32},{8,40},{16,48},{24,56},{40... | collective-permute-start | bytes 1572872 | tf_op jit(solution)/shard_map/ppermute | solution.py:37
  148.4 21.0 %copy-start.5 = (f32[256,512]{1,0:T(8,128)}, f32[256,512]{1,0:T(8,128)S(1)}, u32[]{:S(2)}) copy-start(f32[256,512]{1,0:T(8,128)S(1)} %collective-permute-done.6) | copy-start | bytes 1572868
  148.5 71.9 %collective-permute-start.16 = (f32[256,512]{1,0:T(8,128)}, f32[256,512]{1,0:T(8,128)}, u32[]{:S(2)}, u32[]{:S(2)}) collective-permute-start(f32[256,512]{1,0:T(8,128)} %fusion.61), channel_id=1, source_target_pairs={{96,0},{104,8},{112,16},{120,24},{0,32},{8,40},{16,48},{24,56},{40... | collective-permute-start | bytes 1572872 | tf_op jit(solution)/shard_map/ppermute | solution.py:37
  158.2 1.9 copy-start.8
  169.3 0.8 copy-start.6
  170.1 18.1 %copy-start.4 = (f32[256,512]{1,0:T(8,128)S(1)}, f32[256,512]{1,0:T(8,128)}, u32[]{:S(2)}) copy-start(f32[256,512]{1,0:T(8,128)} %copy-done.3) | copy-start | bytes 1572868
  172.0 15.2 %collective-permute-start.14 = (f32[256,512]{1,0:T(8,128)}, f32[256,512]{1,0:T(8,128)}, u32[]{:S(2)}, u32[]{:S(2)}) collective-permute-start(f32[256,512]{1,0:T(8,128)} %copy-done.7), channel_id=1, source_target_pairs={{16,0},{24,8},{8,16},{0,24},{48,32},{56,40},{40,48},{32,56},{88,64... | collective-permute-start | bytes 1572872 | tf_op jit(solution)/shard_map/ppermute | solution.py:37
  172.4 26.1 %collective-permute-start.13 = (f32[256,512]{1,0:T(8,128)}, f32[256,512]{1,0:T(8,128)}, u32[]{:S(2)}, u32[]{:S(2)}) collective-permute-start(f32[256,512]{1,0:T(8,128)} %copy-done.8), channel_id=1, source_target_pairs={{16,0},{24,8},{8,16},{0,24},{48,32},{56,40},{40,48},{32,56},{88,64... | collective-permute-start | bytes 1572872 | tf_op jit(solution)/shard_map/ppermute | solution.py:37
  172.8 35.3 %collective-permute-start.12 = (f32[256,512]{1,0:T(8,128)S(1)}, f32[256,512]{1,0:T(8,128)}, u32[]{:S(2)}, u32[]{:S(2)}) collective-permute-start(f32[256,512]{1,0:T(8,128)S(1)} %collective-permute-done.9), channel_id=1, source_target_pairs={{16,0},{24,8},{8,16},{0,24},{48,32},{56,40},{40,48},{32,56},{88,64... | collective-permute-start | bytes 1572872 | tf_op jit(solution)/shard_map/ppermute | solution.py:37
  187.2 34.9 %collective-permute-start.15 = (f32[256,512]{1,0:T(8,128)S(1)}, f32[256,512]{1,0:T(8,128)}, u32[]{:S(2)}, u32[]{:S(2)}) collective-permute-start(f32[256,512]{1,0:T(8,128)S(1)} %fusion.64), channel_id=1, source_target_pairs={{96,0},{104,8},{112,16},{120,24},{0,32},{8,40},{16,48},{24,56},{40... | collective-permute-start | bytes 1572872 | tf_op jit(solution)/shard_map/ppermute | solution.py:37
  210.0 10.3 %copy-start.9 = (f32[256,512]{1,0:T(8,128)S(1)}, f32[256,512]{1,0:T(8,128)}, u32[]{:S(2)}) copy-start(f32[256,512]{1,0:T(8,128)} %copy-done.8) | copy-start | bytes 1572868
  228.5 63.9 %all-to-all-start.3 = ((f32[8,32,4096]{2,1,0:T(8,128)}), f32[8,32,4096]{2,1,0:T(8,128)}, u32[]{:S(2)}, u32[]{:S(2)}) async-start(f32[8,32,4096]{2,1,0:T(8,128)} %bitcast.35), calls=%async_computation.3 | async-start | bytes 8388608 | tf_op jit(solution)/shard_map/all_to_all | solution.py:124
  294.9 6.2 %collective-permute-start.18 = (f32[32,512]{1,0:T(8,128)S(1)}, f32[32,512]{1,0:T(8,128)S(1)}, u32[]{:S(2)}, u32[]{:S(2)}) collective-permute-start(f32[32,512]{1,0:T(8,128)S(1)} %get-tuple-element.12), channel_id=1, source_target_pairs={{0,8},{8,0},{16,24},{24,16},{32,40},{40,32},{48,56},{56,48},{64,72... | collective-permute-start | bytes 196616 | tf_op jit(solution)/shard_map/ppermute | solution.py:42
  295.0 9.5 %collective-permute-start.19 = (f32[32,1024]{1,0:T(8,128)S(1)}, f32[32,1024]{1,0:T(8,128)S(1)}, u32[]{:S(2)}, u32[]{:S(2)}) collective-permute-start(f32[32,1024]{1,0:T(8,128)S(1)} %get-tuple-element.14), channel_id=1, source_target_pairs={{0,32},{8,40},{16,48},{24,56},{32,64},{40,72},{48,80},{56,88},{64,... | collective-permute-start | bytes 393224 | tf_op jit(solution)/shard_map/ppermute | solution.py:42
  296.2 10.5 %collective-permute-start.20 = (f32[32,1024]{1,0:T(8,128)S(1)}, f32[32,1024]{1,0:T(8,128)S(1)}, u32[]{:S(2)}, u32[]{:S(2)}) collective-permute-start(f32[32,1024]{1,0:T(8,128)S(1)} %get-tuple-element.13), channel_id=1, source_target_pairs={{0,48},{8,56},{16,40},{24,32},{32,80},{40,88},{48,72},{56,64},{64,... | collective-permute-start | bytes 393224 | tf_op jit(solution)/shard_map/ppermute | solution.py:42
  298.1 8.6 %collective-permute-start.21 = (f32[32,512]{1,0:T(8,128)S(1)}, f32[32,512]{1,0:T(8,128)S(1)}, u32[]{:S(2)}, u32[]{:S(2)}) collective-permute-start(f32[32,512]{1,0:T(8,128)S(1)} %get-tuple-element.11), channel_id=1, source_target_pairs={{0,96},{8,104},{16,112},{24,120},{32,0},{40,8},{48,16},{56,24},{64... | collective-permute-start | bytes 196616 | tf_op jit(solution)/shard_map/ppermute | solution.py:42
  306.8 0.8 copy-start.10
Sparse Core Ops, SparseCore 0:
  20.9 52.3 all-gather.1

commit v2 on v0

v2 whole, which is shorter than its diff:
```python
import functools

import jax
import jax.numpy as jnp
import numpy as np
from jax import lax
from jax.experimental import pallas as pl
from jax.experimental.pallas import tpu as pltpu
from jax.sharding import PartitionSpec as P

Y, ZL, CORES, X, ZH = 4, 2, 2, 4, 2
X_GROUPS = [[x * ZH + zh for x in range(X)] for zh in range(ZH)]
OWN, OTHER, BELOW, ABOVE, ACROSS = range(5)
EARLY = [(OWN, OWN), (OWN, OTHER), (OWN, BELOW), (OTHER, BELOW),
         (BELOW, OWN), (BELOW, OTHER), (BELOW, ABOVE), (ABOVE, BELOW)]
LATE = [(OWN, ACROSS), (OTHER, ACROSS), (BELOW, ACROSS), (ABOVE, ACROSS),
        (ACROSS, OWN), (ACROSS, OTHER), (ACROSS, BELOW), (ACROSS, ABOVE)]


def block_of(y, zl, core):
    return ((y % Y) * ZL + zl % ZL) * CORES + core % CORES


def upper(y):
    return (y % Y) // 2


def itself(y, zl, core):
    return y, zl, core


def other_core(y, zl, core):
    return y, zl, 1 - core


def next_row(y, zl, core):
    return y + 1, zl, core


def previous_row(y, zl, core):
    return y - 1, zl, (core + upper(y)) % 2


def next_across(y, zl, core):
    return y + 1, 1 - zl, (core + zl + upper(y)) % 2


def over_to_across(y, zl, core):
    return y, 1 - zl, (core + zl + upper(y)) % 2


RELATED = [itself, other_core, next_row, previous_row, next_across]


def places():
    return [(y, zl, core) for y in range(Y) for zl in range(ZL) for core in range(CORES)]


def fetched(value, source_of):
    route = [(block_of(*source_of(*at)), block_of(*at)) for at in places()]
    return lax.ppermute(value, "blk", route)


def delivered(value, target_of):
    route = [(block_of(*at), block_of(*target_of(*at))) for at in places()]
    return lax.ppermute(value, "blk", route)


def column_table():
    table = np.zeros((len(places()), len(EARLY) + len(LATE)), np.int32)
    slot = 0
    for tiles in (EARLY, LATE):
        for row in range(5):
            for left, right in tiles:
                if left != row:
                    continue
                for at in places():
                    target = block_of(*RELATED[row](*at))
                    table[target, slot] = block_of(*RELATED[right](*at))
                slot += 1
    return table


def high_and_low(value):
    high = value.astype(jnp.bfloat16)
    return high, (value - high.astype(jnp.float32)).astype(jnp.bfloat16)


def dot(left, right):
    return lax.dot_general(
        left, right, (((1,), (1,)), ((), ())), preferred_element_type=jnp.float32
    )


def transform_kernel(place, part, orbitals, out, high, low):
    width = part.shape[-1]

    @pl.when(pl.program_id(0) == 0)
    def _():
        for x in range(X):
            high[:, x * width : (x + 1) * width], low[:, x * width : (x + 1) * width] = (
                high_and_low(part[x, 0])
            )

    total = jnp.zeros(out.shape, jnp.float32)
    for x in range(X):
        slot = lax.rem(x - place[0] + X, X)
        block = orbitals[:, pl.ds(slot, 1)]
        c_high, c_low = high_and_low(block.reshape(out.shape[1], width))
        b_high = high[:, x * width : (x + 1) * width]
        b_low = low[:, x * width : (x + 1) * width]
        total += dot(b_high, c_high) + (dot(b_high, c_low) + dot(b_low, c_high))
    out[...] = total


def transformed(part, index, orbitals, place, half):
    rows, width = part.shape[2:]
    blocks, _, each, _ = orbitals.shape
    steps, run = 2, blocks // 4
    columns = run * each
    return pl.pallas_call(
        transform_kernel,
        grid_spec=pltpu.PrefetchScalarGridSpec(
            num_scalar_prefetch=1,
            grid=(steps,),
            in_specs=[
                pl.BlockSpec((X, 1, rows, width), lambda j, s: (0, index, 0, 0)),
                pl.BlockSpec((run, X, each, width), lambda j, s: (s[1] * 2 + j, 0, 0, 0)),
            ],
            out_specs=pl.BlockSpec((rows, columns), lambda j, s: (0, j)),
            scratch_shapes=[pltpu.VMEM((rows, X * width), jnp.bfloat16)] * 2,
        ),
        out_shape=jax.ShapeDtypeStruct((rows, steps * columns), jnp.float32),
        compiler_params=pltpu.CompilerParams(vmem_limit_bytes=32 << 20),
        cost_estimate=pl.CostEstimate(
            flops=6 * rows * X * width * steps * columns, bytes_accessed=8 << 20, transcendentals=0
        ),
        name="transform",
    )(jnp.stack([place, half]), part, orbitals)


def gram_kernel(count, more, left_of, right_of, *refs):
    blocks, refs = refs[:count], refs[count:]
    if more:
        so_far, refs = refs[0], refs[1:]
    out, lefts, rights = refs
    depth = blocks[0].shape[1]
    step = pl.program_id(0)

    @pl.when(step == 0)
    def _():
        for k, block in enumerate(blocks):
            high, low = high_and_low(block[...])
            for ref, order in ((lefts, (high, high, low)), (rights, (high, low, high))):
                for piece, value in enumerate(order):
                    ref[k, :, piece * depth : (piece + 1) * depth] = value

    tile = dot(lefts[left_of[step]], rights[right_of[step]]).reshape(out.shape)
    out[...] = so_far[...] + tile if more else tile


def gram(blocks, pairs, shares, so_far):
    rows, depth = blocks[0].shape
    count = len(blocks)
    tiles = len(pairs)
    more = so_far is not None
    whole = pl.BlockSpec((rows, depth), lambda t, *s: (0, 0))
    tile = pl.BlockSpec((shares, 1, rows // shares, rows), lambda t, *s: (0, t, 0, 0))
    shape = jax.ShapeDtypeStruct((shares, tiles, rows // shares, rows), jnp.float32)
    order = np.array(pairs, np.int32)
    return pl.pallas_call(
        functools.partial(gram_kernel, count, more),
        grid_spec=pltpu.PrefetchScalarGridSpec(
            num_scalar_prefetch=2,
            grid=(tiles,),
            in_specs=[whole] * count + [tile] * more,
            out_specs=tile,
            scratch_shapes=[pltpu.VMEM((count, rows, 3 * depth), jnp.bfloat16)] * 2,
        ),
        out_shape=shape,
        input_output_aliases={2 + count: 0} if more else {},
        compiler_params=pltpu.CompilerParams(vmem_limit_bytes=32 << 20),
        cost_estimate=pl.CostEstimate(
            flops=6 * tiles * rows * rows * depth, bytes_accessed=6 << 20, transcendentals=0
        ),
        name="gram",
    )(order[:, 0], order[:, 1], *blocks, *([so_far] if more else []))


def assemble_kernel(table, *refs):
    *groups, out = refs
    slot = 0
    for group in groups:
        for k in range(group.shape[0]):
            width = group.shape[2]
            at = pl.multiple_of(table[slot] * width, width)
            out[:, pl.ds(at, width)] = group[k]
            slot += 1


def assembled(table, groups, columns):
    return pl.pallas_call(
        assemble_kernel,
        in_specs=[pl.BlockSpec(memory_space=pltpu.SMEM)]
        + [pl.BlockSpec(memory_space=pltpu.VMEM)] * len(groups),
        out_specs=pl.BlockSpec(memory_space=pltpu.VMEM),
        out_shape=jax.ShapeDtypeStruct((groups[0].shape[1], columns), jnp.float32),
        cost_estimate=pl.CostEstimate(flops=0, bytes_accessed=1 << 20, transcendentals=0),
        name="assemble",
    )(table, *groups)


def all_orbitals(coefficients):
    mine = coefficients.T
    ring = [mine]
    for step in range(1, X):
        route = [(((t + step) % X) * ZH + zh, t * ZH + zh) for t in range(X) for zh in range(ZH)]
        ring.append(lax.ppermute(mine, "col", route))
    return lax.all_gather(jnp.stack(ring), "blk", axis=0, tiled=False)


def on_device(three_index, coefficients):
    rows, aux, width = three_index.shape
    by_aux = three_index.transpose(1, 0, 2)
    blk, col = lax.axis_index("blk"), lax.axis_index("col")
    place, zh = col // ZH, col % ZH
    swap_zh = [(x * ZH + 1 - h, x * ZH + h) for x in range(X) for h in range(ZH)]
    shares = lax.axis_size("col")

    def over_x(part):
        moved = lax.all_to_all(
            part, "col", split_axis=0, concat_axis=0, tiled=True, axis_index_groups=X_GROUPS
        )
        return moved.reshape(X, part.shape[0] // X, rows, width)

    cut = aux - X
    parts = [over_x(by_aux[:cut]), over_x(by_aux[cut:])]
    orbitals = all_orbitals(coefficients)
    chunks = [(part, k) for part in parts for k in range(part.shape[1])]

    early = late = None
    for part, k in chunks:
        arrived = lax.ppermute(transformed(part, k, orbitals, place, 1 - zh), "col", swap_zh)
        own = transformed(part, k, orbitals, place, zh) + arrived
        other = fetched(own, other_core)
        below = fetched(own, next_row)
        above = fetched(own, previous_row)
        across = fetched(below, over_to_across)
        early = gram([own, other, below, above], EARLY, shares, early)
        late = gram([own, other, below, above, across], LATE, shares, late)

    def sent_home(tiles, pairs):
        summed = lax.all_to_all(tiles, "col", split_axis=0, concat_axis=0, tiled=True).sum(0)
        groups = []
        first = 0
        for row, target_of in enumerate(RELATED):
            count = sum(left == row for left, _ in pairs)
            if count:
                group = summed[first : first + count]
                groups.append(delivered(group, target_of) if row else group)
            first += count
        return groups

    groups = sent_home(early, EARLY) + sent_home(late, LATE)
    table = lax.dynamic_slice(jnp.asarray(column_table()), (blk, 0), (1, 16))[0]
    return assembled(table, groups, rows * lax.axis_size("blk"))


def solution(mesh):
    return jax.shard_map(
        on_device,
        mesh=mesh,
        in_specs=(P("blk", None, "col"), P("col", "blk")),
        out_specs=P(("blk", "col"), None),
        check_vma=False,
    )
```

time: 700 us -> 307 us (0.44)
  waiting for transfers between devices: 603 us -> 140 us
  Pallas kernels: 0 us -> 71.6 us
  matrix products: 59.2 us -> 0 us
  starting transfers between devices: 0.3 us -> 52.4 us
    ppermute x15 -> x25, waiting for transfers between devices: 332 us -> 59.3 us  [the longest x12 49.2 us: fetched(): return lax.ppermute(value, 'blk', route)]
    reduce_scatter x2 -> x0, waiting for transfers between devices: 232 us -> none  [the longest x1 152 us: on_device(): half_x = lax.psum_scatter(partial_x, 'col', scatter_dimension=2, tiled=True)]
    all_to_all x0 -> x4, waiting for transfers between devices: none -> 80.5 us  [the longest x2 54.8 us: over_x(): lax.all_to_all(part, 'col', split_axis=0, concat_axis=0, tiled=True, axis...]
    pallas_call x0 -> x13, Pallas kernels: none -> 71.6 us  [the longest x6 44.6 us: gram(): pl.pallas_call(functools.partial(gram_kernel, count, more), grid_spec=plt...]
    dot_general x17 -> x0, matrix products: 59.2 us -> none  [the longest x16 34.4 us: gram_tile(): lax.dot_general(own_block, other_block, (((1,), (1,)), ((), ())), precisi...]
    all_gather x1, waiting for transfers between devices: 38.1 us -> 0.01 us  [all_orbitals(): return lax.all_gather(jnp.stack(ring), 'blk', axis=0, tiled=False)]
    ppermute x15 -> x25, starting transfers between devices: 0.04 us -> 32 us  [the longest x12 12.8 us: fetched(): return lax.ppermute(value, 'blk', route)]
    all_to_all x0 -> x4, starting transfers between devices: none -> 20.4 us  [the longest x2 11.9 us: sent_home(): lax.all_to_all(tiles, 'col', split_axis=0, concat_axis=0, tiled=True).sum(0)]
  transfers between devices with their start and end apart: 18 -> 30, of which waited for: 18 -> 15; matrix products, arithmetic and copies ran while one was open for 0% -> 5% of each run, Pallas kernels for 0% -> 20%
where the time goes in v2:
time: 307 us; the launch traced here: 306 us
  waiting for transfers between devices  140 us (46%)
  Pallas kernels  71.6 us (23%)
  starting transfers between devices  52.4 us (17%)
  local copies, waits for them, and re-layouts  21.8 us (7%)
  between operations  13.8 us (4%)
  other arithmetic  6.13 us (2%)
    all_to_all x2, waiting for transfers between devices, over_x(): lax.all_to_all(part, 'col', split_axis=0, concat_axis=0, tiled=True, axis...  54.8 us
    ppermute x12, waiting for transfers between devices, fetched(): return lax.ppermute(value, 'blk', route)  49.2 us
    pallas_call x6, Pallas kernels, gram(): pl.pallas_call(functools.partial(gram_kernel, count, more), grid_spec=plt...  44.6 us
    all_to_all x2, waiting for transfers between devices, sent_home(): lax.all_to_all(tiles, 'col', split_axis=0, concat_axis=0, tiled=True).sum(0)  25.8 us
    pallas_call x6, Pallas kernels, transformed(): pl.pallas_call(transform_kernel, grid_spec=pltpu.PrefetchScalarGridSpec(n...  25.1 us
    ppermute x12, starting transfers between devices, fetched(): return lax.ppermute(value, 'blk', route)  12.8 us
    all_to_all x2, starting transfers between devices, sent_home(): lax.all_to_all(tiles, 'col', split_axis=0, concat_axis=0, tiled=True).sum(0)  11.9 us
    unnamed x60, local copies, waits for them, and re-layouts  11.6 us
  transfers between devices with their start and end apart: 30, of which 15 were waited for; matrix products, arithmetic and copies ran while one was open for 5% of the time, Pallas kernels for 20%

profile of v2, /device:TPU:0, one launch (start us, length us, event | category | flops | bytes accessed | tf_op | source)
XLA Modules:
  0.0 305.6 jit_solution(18068996222846710460)
XLA Ops:
  6.5 2.8 collective-permute-start
  11.1 4.2 %collective-permute-done = f32[64,512]{1,0:T(8,128)S(1)} collective-permute-done((f32[64,512]{1,0:T(8,128)}, f32[64,512]{1,0:T(8,128)S(1)}, u32[]{:S(2)}, u32[]{:S(2)}) %collective-permute-start) | collective-permute-done | bytes 131104 | tf_op jit(solution)/shard_map/ppermute | solution.py:218
  15.3 2.2 collective-permute-done.1
  17.5 1.4 collective-permute-done.2
  18.9 1.7 pad_maximum_fusion
  20.6 4.6 %slice.45 = f32[8,256,512]{2,1,0:T(8,128)} slice(f32[12,256,512]{2,1,0:T(8,128)} %bitcast.23), slice={[0:8], [0:256], [0:512]} | slice | bytes 8388608 | tf_op jit(solution)/shard_map/slice | solution.py:237
  25.2 4.8 %all-to-all-start.1 = ((f32[8,256,512]{2,1,0:T(8,128)}), f32[8,256,512]{2,1,0:T(8,128)}, u32[]{:S(2)}, u32[]{:S(2)}) async-start(f32[8,256,512]{2,1,0:T(8,128)} %slice.45), calls=%async_computation.1 | async-start | bytes 8388608 | tf_op jit(solution)/shard_map/all_to_all | solution.py:231
  30.0 3.1 %slice.44 = f32[4,256,512]{2,1,0:T(8,128)} slice(f32[12,256,512]{2,1,0:T(8,128)} %bitcast.24), slice={[8:12], [0:256], [0:512]} | slice | bytes 4194304 | tf_op jit(solution)/shard_map/slice | solution.py:237
  33.2 46.0 %all-to-all-done.1 = f32[8,256,512]{2,1,0:T(8,128)} async-done(((f32[8,256,512]{2,1,0:T(8,128)}), f32[8,256,512]{2,1,0:T(8,128)}, u32[]{:S(2)}, u32[]{:S(2)}) %all-to-all-start.1) | async-done | bytes 4194336 | tf_op jit(solution)/shard_map/all_to_all | solution.py:231
  79.2 3.6 %all-to-all-start = ((f32[4,256,512]{2,1,0:T(8,128)}), f32[4,256,512]{2,1,0:T(8,128)S(1)}, u32[]{:S(2)}, u32[]{:S(2)}) async-start(f32[4,256,512]{2,1,0:T(8,128)} %slice.44), calls=%async_computation | async-start | bytes 4194304 | tf_op jit(solution)/shard_map/all_to_all | solution.py:231
  82.9 3.4 %copy-done = f32[64,64,512]{2,1,0:T(8,128)S(1)} copy-done((f32[64,64,512]{2,1,0:T(8,128)S(1)}, f32[64,64,512]{2,1,0:T(8,128)}, u32[]{:S(2)}) %copy-start) | copy-done | bytes 8388632
  86.3 4.6 %transform.11 = f32[256,512]{1,0:T(8,128)S(1)} custom-call(s32[2]{0:T(128)S(1)} %pad_add_fusion.1.place, f32[4,2,256,512]{3,2,1,0:T(8,128)} %bitcast.12.part, f32[16,4,64,512]{3,2,1,0:T(8,128)S(1)} %bitcast.15), custom_call_target="tpu_custom_call" | custom-call | flops 1610612736 | bytes 8388608 | tf_op jit(solution)/shard_map/transform/pallas_call | solution.py:121
  90.9 4.0 %collective-permute-start.11 = (f32[256,512]{1,0:T(8,128)S(1)}, f32[256,512]{1,0:T(8,128)}, u32[]{:S(2)}, u32[]{:S(2)}) collective-permute-start(f32[256,512]{1,0:T(8,128)S(1)} %transform.11), channel_id=1, source_target_pairs={{1,0},{0,1},{3,2},{2,3},{5,4},{4,5},{7,6},{6,7},{9,8},{8,9},{11,10... | collective-permute-start | bytes 1572872 | tf_op jit(solution)/shard_map/ppermute | solution.py:243
  94.9 4.7 %transform.9 = f32[256,512]{1,0:T(8,128)S(1)} custom-call(s32[2]{0:T(128)S(1)} %pad_add_fusion.1.place, f32[4,2,256,512]{3,2,1,0:T(8,128)} %bitcast.12.part, f32[16,4,64,512]{3,2,1,0:T(8,128)S(1)} %bitcast.16), custom_call_target="tpu_custom_call" | custom-call | flops 1610612736 | bytes 8388608 | tf_op jit(solution)/shard_map/transform/pallas_call | solution.py:121
  99.7 8.8 %all-to-all-done = f32[4,256,512]{2,1,0:T(8,128)S(1)} async-done(((f32[4,256,512]{2,1,0:T(8,128)}), f32[4,256,512]{2,1,0:T(8,128)S(1)}, u32[]{:S(2)}, u32[]{:S(2)}) %all-to-all-start) | async-done | bytes 2097184 | tf_op jit(solution)/shard_map/all_to_all | solution.py:231
  108.5 3.4 %copy-done.1 = f32[64,64,512]{2,1,0:T(8,128)S(1)} copy-done((f32[64,64,512]{2,1,0:T(8,128)S(1)}, f32[64,64,512]{2,1,0:T(8,128)}, u32[]{:S(2)}) %copy-start.1) | copy-done | bytes 8388632
  111.9 3.1 %transform.7 = f32[256,512]{1,0:T(8,128)S(1)} custom-call(s32[2]{0:T(128)S(1)} %pad_add_fusion.1.place, f32[4,1,256,512]{3,2,1,0:T(8,128)S(1)} %bitcast.21, f32[16,4,64,512]{3,2,1,0:T(8,128)S(1)} %bitcast.17), custom_call_target="tpu_custom_call" | custom-call | flops 1610612736 | bytes 8388608 | tf_op jit(solution)/shard_map/transform/pallas_call | solution.py:121
  114.9 4.0 %collective-permute-start.3 = (f32[256,512]{1,0:T(8,128)S(1)}, f32[256,512]{1,0:T(8,128)S(1)}, u32[]{:S(2)}, u32[]{:S(2)}) collective-permute-start(f32[256,512]{1,0:T(8,128)S(1)} %transform.7), channel_id=1, source_target_pairs={{1,0},{0,1},{3,2},{2,3},{5,4},{4,5},{7,6},{6,7},{9,8},{8,9},{11,10... | collective-permute-start | bytes 1572872 | tf_op jit(solution)/shard_map/ppermute | solution.py:243
  118.9 4.8 %transform.10 = f32[256,512]{1,0:T(8,128)S(1)} custom-call(s32[2]{0:T(128)S(1)} %pad_add_fusion.place, f32[4,2,256,512]{3,2,1,0:T(8,128)} %bitcast.12.part, f32[16,4,64,512]{3,2,1,0:T(8,128)S(1)} %bitcast.18), custom_call_target="tpu_custom_call" | custom-call | flops 1610612736 | bytes 8388608 | tf_op jit(solution)/shard_map/transform/pallas_call | solution.py:121
  123.7 1.1 add.21.refs_0_
  124.8 3.1 %collective-permute-start.13 = (f32[256,512]{1,0:T(8,128)S(1)}, f32[256,512]{1,0:T(8,128)S(1)}, u32[]{:S(2)}, u32[]{:S(2)}) collective-permute-start(f32[256,512]{1,0:T(8,128)S(1)} %add.21.refs_0_), channel_id=1, source_target_pairs={{32,0},{40,8},{48,16},{56,24},{64,32},{72,40},{80,48},{88,56},{96,... | collective-permute-start | bytes 1572872 | tf_op jit(solution)/shard_map/ppermute | solution.py:61
  127.9 4.8 %transform.8 = f32[256,512]{1,0:T(8,128)S(1)} custom-call(s32[2]{0:T(128)S(1)} %pad_add_fusion.place, f32[4,2,256,512]{3,2,1,0:T(8,128)} %bitcast.12.part, f32[16,4,64,512]{3,2,1,0:T(8,128)S(1)} %bitcast.19), custom_call_target="tpu_custom_call" | custom-call | flops 1610612736 | bytes 8388608 | tf_op jit(solution)/shard_map/transform/pallas_call | solution.py:121
  132.8 1.1 add.20.refs_0_
  134.0 3.3 %collective-permute-start.9 = (f32[256,512]{1,0:T(8,128)S(1)}, f32[256,512]{1,0:T(8,128)S(1)}, u32[]{:S(2)}, u32[]{:S(2)}) collective-permute-start(f32[256,512]{1,0:T(8,128)S(1)} %add.20.refs_0_), channel_id=1, source_target_pairs={{32,0},{40,8},{48,16},{56,24},{64,32},{72,40},{80,48},{88,56},{96,... | collective-permute-start | bytes 1572872 | tf_op jit(solution)/shard_map/ppermute | solution.py:61
  137.6 3.2 %transform.6 = f32[256,512]{1,0:T(8,128)S(1)} custom-call(s32[2]{0:T(128)S(1)} %pad_add_fusion.place, f32[4,1,256,512]{3,2,1,0:T(8,128)S(1)} %bitcast.22, f32[16,4,64,512]{3,2,1,0:T(8,128)S(1)} %bitcast.20), custom_call_target="tpu_custom_call" | custom-call | flops 1610612736 | bytes 8388608 | tf_op jit(solution)/shard_map/transform/pallas_call | solution.py:121
  140.9 3.2 %collective-permute-start.5 = (f32[256,512]{1,0:T(8,128)S(1)}, f32[256,512]{1,0:T(8,128)S(1)}, u32[]{:S(2)}, u32[]{:S(2)}) collective-permute-start(f32[256,512]{1,0:T(8,128)S(1)} %add.19.refs_0_), channel_id=1, source_target_pairs={{32,0},{40,8},{48,16},{56,24},{64,32},{72,40},{80,48},{88,56},{96,... | collective-permute-start | bytes 1572872 | tf_op jit(solution)/shard_map/ppermute | solution.py:61
  144.0 4.7 %collective-permute-done.14.refs_3_ = f32[256,512]{1,0:T(8,128)S(1)} collective-permute-done((f32[256,512]{1,0:T(8,128)S(1)}, f32[256,512]{1,0:T(8,128)S(1)}, u32[]{:S(2)}, u32[]{:S(2)}) %collective-permute-start.14) | collective-permute-done | bytes 524320 | tf_op jit(solution)/shard_map/ppermute | solution.py:61
  149.9 5.9 %gram.6.refs_4_ = f32[8,8,32,256]{3,2,1,0:T(8,128)} custom-call(s32[8]{0:T(128)S(1)} %copy-done.15, s32[8]{0:T(128)S(1)} %copy-done.16, f32[256,512]{1,0:T(8,128)S(1)} %add.21.refs_0_, f32[256,512]{1,0:T(8,128)S(1)} %collective-permute-done.12.refs_1_, f32[256,512]{1,0:T(8,128)S(1)} %collective-permute-done.13.refs_2_, ...), custom_call_target="tpu_custom_call" | custom-call | flops 1610612736 | bytes 6291456 | tf_op jit(solution)/shard_map/gram/pallas_call | solution.py:171
  155.8 4.2 %collective-permute-done.10.refs_3_ = f32[256,512]{1,0:T(8,128)S(1)} collective-permute-done((f32[256,512]{1,0:T(8,128)S(1)}, f32[256,512]{1,0:T(8,128)S(1)}, u32[]{:S(2)}, u32[]{:S(2)}) %collective-permute-start.10) | collective-permute-done | bytes 524320 | tf_op jit(solution)/shard_map/ppermute | solution.py:61
  160.0 8.1 %gram.7.refs_4_ = f32[8,8,32,256]{3,2,1,0:T(8,128)} custom-call(s32[8]{0:T(128)S(1)} %copy-done.15, s32[8]{0:T(128)S(1)} %copy-done.16, f32[256,512]{1,0:T(8,128)S(1)} %add.20.refs_0_, f32[256,512]{1,0:T(8,128)S(1)} %collective-permute-done.8.refs_1_, f32[256,512]{1,0:T(8,128)S(1)} %collective-permute-done.9.refs_2_, ...), custom_call_target="tpu_custom_call", output_to_operand_aliasing={{}: (6, {})} | custom-call | flops 1610612736 | bytes 6291456 | tf_op jit(solution)/shard_map/gram/pallas_call | solution.py:171
  168.2 2.6 collective-permute-done.6.refs_3_
  170.8 8.1 %gram.8 = f32[8,8,32,256]{3,2,1,0:T(8,128)} custom-call(s32[8]{0:T(128)S(1)} %copy-done.15, s32[8]{0:T(128)S(1)} %copy-done.16, f32[256,512]{1,0:T(8,128)S(1)} %add.19.refs_0_, f32[256,512]{1,0:T(8,128)S(1)} %collective-permute-done.4.refs_1_, f32[256,512]{1,0:T(8,128)S(1)} %collective-permute-done.5.refs_2_, ...), custom_call_target="tpu_custom_call", output_to_operand_aliasing={{}: (6, {})} | custom-call | flops 1610612736 | bytes 6291456 | tf_op jit(solution)/shard_map/gram/pallas_call | solution.py:171
  178.9 4.5 %all-to-all-start.2 = ((f32[8,8,32,256]{3,2,1,0:T(8,128)}), f32[8,8,32,256]{3,2,1,0:T(8,128)}, u32[]{:S(2)}, u32[]{:S(2)}) async-start(f32[8,8,32,256]{3,2,1,0:T(8,128)} %gram.8), calls=%async_computation.2 | async-start | bytes 4194304 | tf_op jit(solution)/shard_map/all_to_all | solution.py:253
  184.5 1.5 collective-permute-start.18
  186.0 33.9 %collective-permute-done.20.refs_4_ = f32[256,512]{1,0:T(8,128)S(1)} collective-permute-done((f32[256,512]{1,0:T(8,128)}, f32[256,512]{1,0:T(8,128)S(1)}, u32[]{:S(2)}, u32[]{:S(2)}) %collective-permute-start.20) | collective-permute-done | bytes 524320 | tf_op jit(solution)/shard_map/ppermute | solution.py:61
  224.1 6.0 %gram.9.refs_5_ = f32[8,8,32,256]{3,2,1,0:T(8,128)} custom-call(s32[8]{0:T(128)S(1)} %copy-done.13, s32[8]{0:T(128)S(1)} %copy-done.14, f32[256,512]{1,0:T(8,128)S(1)} %copy-done.12, f32[256,512]{1,0:T(8,128)S(1)} %copy-done.20, f32[256,512]{1,0:T(8,128)S(1)} %copy-done.18, f32[256,512]{1,0:T(8,128)S(1)} %copy-done.22, ...), custom_call_target="tpu_custom_call" | custom-call | flops 1610612736 | bytes 6291456 | tf_op jit(solution)/shard_map/gram/pallas_call | solution.py:171
  230.1 1.1 collective-permute-done.19.refs_4_
  231.1 8.2 %gram.10.refs_5_ = f32[8,8,32,256]{3,2,1,0:T(8,128)} custom-call(s32[8]{0:T(128)S(1)} %copy-done.13, s32[8]{0:T(128)S(1)} %copy-done.14, f32[256,512]{1,0:T(8,128)S(1)} %add.20.refs_0_, f32[256,512]{1,0:T(8,128)S(1)} %copy-done.6, f32[256,512]{1,0:T(8,128)S(1)} %collective-permute-done.9.refs_2_, ...), custom_call_target="tpu_custom_call", output_to_operand_aliasing={{}: (7, {})} | custom-call | flops 1610612736 | bytes 6291456 | tf_op jit(solution)/shard_map/gram/pallas_call | solution.py:171
  239.4 2.0 collective-permute-done.18.refs_4_
  241.3 8.2 %gram.11 = f32[8,8,32,256]{3,2,1,0:T(8,128)} custom-call(s32[8]{0:T(128)S(1)} %copy-done.13, s32[8]{0:T(128)S(1)} %copy-done.14, f32[256,512]{1,0:T(8,128)S(1)} %add.19.refs_0_, f32[256,512]{1,0:T(8,128)S(1)} %copy-done.8, f32[256,512]{1,0:T(8,128)S(1)} %collective-permute-done.5.refs_2_, f32[256,512]{1,0:T(8,128)S(1)} %copy-done.10, ...), custom_call_target="tpu_custom_call", output_to_operand_aliasing={{}: (7, {})} | custom-call | flops 1610612736 | bytes 6291456 | tf_op jit(solution)/shard_map/gram/pallas_call | solution.py:171
  249.6 7.4 %all-to-all-start.3 = ((f32[8,8,32,256]{3,2,1,0:T(8,128)}), f32[8,8,32,256]{3,2,1,0:T(8,128)S(1)}, u32[]{:S(2)}, u32[]{:S(2)}) async-start(f32[8,8,32,256]{3,2,1,0:T(8,128)} %gram.11), calls=%async_computation.3 | async-start | bytes 4194304 | tf_op jit(solution)/shard_map/all_to_all | solution.py:253
  257.0 1.8 reduce_sum.18
  259.5 3.2 %collective-permute-start.17 = (f32[1,32,256]{2,1,0:T(8,128)S(1)}, f32[1,32,256]{2,1,0:T(8,128)S(1)}, u32[]{:S(2)}, u32[]{:S(2)}) collective-permute-start(f32[1,32,256]{2,1,0:T(8,128)S(1)} %get-tuple-element.9), channel_id=1, source_target_pairs={{0,96},{8,104},{16,112},{24,120},{32,0},{40,8},{48,16},{56,24},{64... | collective-permute-start | bytes 98312 | tf_op jit(solution)/shard_map/ppermute | solution.py:66
  262.7 25.8 %all-to-all-done.3 = f32[8,8,32,256]{3,2,1,0:T(8,128)S(1)} async-done(((f32[8,8,32,256]{3,2,1,0:T(8,128)}), f32[8,8,32,256]{3,2,1,0:T(8,128)S(1)}, u32[]{:S(2)}, u32[]{:S(2)}) %all-to-all-start.3) | async-done | bytes 2097184 | tf_op jit(solution)/shard_map/all_to_all | solution.py:253
  289.5 3.2 %collective-permute-start.23 = (f32[1,32,256]{2,1,0:T(8,128)S(1)}, f32[1,32,256]{2,1,0:T(8,128)S(1)}, u32[]{:S(2)}, u32[]{:S(2)}) collective-permute-start(f32[1,32,256]{2,1,0:T(8,128)S(1)} %get-tuple-element.5), channel_id=1, source_target_pairs={{0,96},{8,104},{16,112},{24,120},{32,0},{40,8},{48,16},{56,24},{64... | collective-permute-start | bytes 98312 | tf_op jit(solution)/shard_map/ppermute | solution.py:66
  292.7 1.2 dynamic-slice_bitcast_fusion.table
  295.0 1.2 collective-permute-done.24.refs_8_
  296.8 2.0 assemble.1
  (101 shorter events, 12.3 us)
Async XLA Ops:
  6.5 76.3 %all-gather.3.cloned.1.call-start = ((), (), s32[]{:S(2)}) async-start(), calls=%async_computation.4 | async-start | bytes 8912896 | tf_op jit(solution)/shard_map/all_gather | solution.py:219
  6.5 8.7 %collective-permute-start = (f32[64,512]{1,0:T(8,128)}, f32[64,512]{1,0:T(8,128)S(1)}, u32[]{:S(2)}, u32[]{:S(2)}) collective-permute-start(f32[64,512]{1,0:T(8,128)} %bitcast.25), channel_id=1, source_target_pairs={{2,0},{3,1},{4,2},{5,3},{6,4},{7,5},{0,6},{1,7},{10,8},{11,9},{12,... | collective-permute-start | bytes 393224 | tf_op jit(solution)/shard_map/ppermute | solution.py:218
  9.4 8.1 %collective-permute-start.1 = (f32[64,512]{1,0:T(8,128)}, f32[64,512]{1,0:T(8,128)S(1)}, u32[]{:S(2)}, u32[]{:S(2)}) collective-permute-start(f32[64,512]{1,0:T(8,128)} %bitcast.26), channel_id=1, source_target_pairs={{4,0},{5,1},{6,2},{7,3},{0,4},{1,5},{2,6},{3,7},{12,8},{13,9},{14,... | collective-permute-start | bytes 393224 | tf_op jit(solution)/shard_map/ppermute | solution.py:218
  10.2 8.7 %collective-permute-start.2 = (f32[64,512]{1,0:T(8,128)}, f32[64,512]{1,0:T(8,128)S(1)}, u32[]{:S(2)}, u32[]{:S(2)}) collective-permute-start(f32[64,512]{1,0:T(8,128)} %bitcast.27), channel_id=1, source_target_pairs={{6,0},{7,1},{0,2},{1,3},{2,4},{3,5},{4,6},{5,7},{14,8},{15,9},{8,1... | collective-permute-start | bytes 393224 | tf_op jit(solution)/shard_map/ppermute | solution.py:218
  25.2 54.0 %all-to-all-start.1 = ((f32[8,256,512]{2,1,0:T(8,128)}), f32[8,256,512]{2,1,0:T(8,128)}, u32[]{:S(2)}, u32[]{:S(2)}) async-start(f32[8,256,512]{2,1,0:T(8,128)} %slice.45), calls=%async_computation.1 | async-start | bytes 8388608 | tf_op jit(solution)/shard_map/all_to_all | solution.py:231
  79.2 29.3 %all-to-all-start = ((f32[4,256,512]{2,1,0:T(8,128)}), f32[4,256,512]{2,1,0:T(8,128)S(1)}, u32[]{:S(2)}, u32[]{:S(2)}) async-start(f32[4,256,512]{2,1,0:T(8,128)} %slice.44), calls=%async_computation | async-start | bytes 4194304 | tf_op jit(solution)/shard_map/all_to_all | solution.py:231
  90.9 32.7 %collective-permute-start.11 = (f32[256,512]{1,0:T(8,128)S(1)}, f32[256,512]{1,0:T(8,128)}, u32[]{:S(2)}, u32[]{:S(2)}) collective-permute-start(f32[256,512]{1,0:T(8,128)S(1)} %transform.11), channel_id=1, source_target_pairs={{1,0},{0,1},{3,2},{2,3},{5,4},{4,5},{7,6},{6,7},{9,8},{8,9},{11,10... | collective-permute-start | bytes 1572872 | tf_op jit(solution)/shard_map/ppermute | solution.py:243
  99.5 33.3 %collective-permute-start.7 = (f32[256,512]{1,0:T(8,128)S(1)}, f32[256,512]{1,0:T(8,128)}, u32[]{:S(2)}, u32[]{:S(2)}) collective-permute-start(f32[256,512]{1,0:T(8,128)S(1)} %transform.9), channel_id=1, source_target_pairs={{1,0},{0,1},{3,2},{2,3},{5,4},{4,5},{7,6},{6,7},{9,8},{8,9},{11,10... | collective-permute-start | bytes 1572872 | tf_op jit(solution)/shard_map/ppermute | solution.py:243
  111.9 7.0 %copy-start.2 = (f32[64,64,512]{2,1,0:T(8,128)S(1)}, f32[64,64,512]{2,1,0:T(8,128)}, u32[]{:S(2)}) copy-start(f32[64,64,512]{2,1,0:T(8,128)} %all-gather.3.cloned.1.call-done) | copy-start | bytes 25165828
  114.9 22.4 %collective-permute-start.3 = (f32[256,512]{1,0:T(8,128)S(1)}, f32[256,512]{1,0:T(8,128)S(1)}, u32[]{:S(2)}, u32[]{:S(2)}) collective-permute-start(f32[256,512]{1,0:T(8,128)S(1)} %transform.7), channel_id=1, source_target_pairs={{1,0},{0,1},{3,2},{2,3},{5,4},{4,5},{7,6},{6,7},{9,8},{8,9},{11,10... | collective-permute-start | bytes 1572872 | tf_op jit(solution)/shard_map/ppermute | solution.py:243
  124.8 25.1 %copy-start.11 = (f32[256,512]{1,0:T(8,128)}, f32[256,512]{1,0:T(8,128)S(1)}, u32[]{:S(2)}) copy-start(f32[256,512]{1,0:T(8,128)S(1)} %add.21.refs_0_) | copy-start | bytes 1572868
  124.8 12.5 %collective-permute-start.13 = (f32[256,512]{1,0:T(8,128)S(1)}, f32[256,512]{1,0:T(8,128)S(1)}, u32[]{:S(2)}, u32[]{:S(2)}) collective-permute-start(f32[256,512]{1,0:T(8,128)S(1)} %add.21.refs_0_), channel_id=1, source_target_pairs={{32,0},{40,8},{48,16},{56,24},{64,32},{72,40},{80,48},{88,56},{96,... | collective-permute-start | bytes 1572872 | tf_op jit(solution)/shard_map/ppermute | solution.py:61
  132.7 8.2 %collective-permute-start.12 = (f32[256,512]{1,0:T(8,128)S(1)}, f32[256,512]{1,0:T(8,128)S(1)}, u32[]{:S(2)}, u32[]{:S(2)}) collective-permute-start(f32[256,512]{1,0:T(8,128)S(1)} %add.21.refs_0_), channel_id=1, source_target_pairs={{8,0},{0,8},{24,16},{16,24},{40,32},{32,40},{56,48},{48,56},{72,64... | collective-permute-start | bytes 1572872 | tf_op jit(solution)/shard_map/ppermute | solution.py:61
  132.7 16.0 %collective-permute-start.14 = (f32[256,512]{1,0:T(8,128)S(1)}, f32[256,512]{1,0:T(8,128)S(1)}, u32[]{:S(2)}, u32[]{:S(2)}) collective-permute-start(f32[256,512]{1,0:T(8,128)S(1)} %add.21.refs_0_), channel_id=1, source_target_pairs={{96,0},{104,8},{112,16},{120,24},{0,32},{8,40},{16,48},{24,56},{40... | collective-permute-start | bytes 1572872 | tf_op jit(solution)/shard_map/ppermute | solution.py:61
  134.0 15.9 %copy-start.15 = (s32[8]{0:T(128)S(1)}, s32[8]{0:T(128)}, u32[]{:S(2)}) copy-start(s32[8]{0:T(128)} %constant.49.clone.left_of) | copy-start | bytes 100
  134.0 15.9 %copy-start.16 = (s32[8]{0:T(128)S(1)}, s32[8]{0:T(128)}, u32[]{:S(2)}) copy-start(s32[8]{0:T(128)} %constant.50.clone.right_of) | copy-start | bytes 100
  134.0 15.6 %collective-permute-start.9 = (f32[256,512]{1,0:T(8,128)S(1)}, f32[256,512]{1,0:T(8,128)S(1)}, u32[]{:S(2)}, u32[]{:S(2)}) collective-permute-start(f32[256,512]{1,0:T(8,128)S(1)} %add.20.refs_0_), channel_id=1, source_target_pairs={{32,0},{40,8},{48,16},{56,24},{64,32},{72,40},{80,48},{88,56},{96,... | collective-permute-start | bytes 1572872 | tf_op jit(solution)/shard_map/ppermute | solution.py:61
  137.3 22.7 %collective-permute-start.10 = (f32[256,512]{1,0:T(8,128)S(1)}, f32[256,512]{1,0:T(8,128)S(1)}, u32[]{:S(2)}, u32[]{:S(2)}) collective-permute-start(f32[256,512]{1,0:T(8,128)S(1)} %add.20.refs_0_), channel_id=1, source_target_pairs={{96,0},{104,8},{112,16},{120,24},{0,32},{8,40},{16,48},{24,56},{40... | collective-permute-start | bytes 1572872 | tf_op jit(solution)/shard_map/ppermute | solution.py:61
  137.3 12.6 %copy-start.17 = (f32[256,512]{1,0:T(8,128)}, f32[256,512]{1,0:T(8,128)S(1)}, u32[]{:S(2)}) copy-start(f32[256,512]{1,0:T(8,128)S(1)} %collective-permute-done.13.refs_2_) | copy-start | bytes 1572868
  137.3 22.7 %collective-permute-start.8 = (f32[256,512]{1,0:T(8,128)S(1)}, f32[256,512]{1,0:T(8,128)S(1)}, u32[]{:S(2)}, u32[]{:S(2)}) collective-permute-start(f32[256,512]{1,0:T(8,128)S(1)} %add.20.refs_0_), channel_id=1, source_target_pairs={{8,0},{0,8},{24,16},{16,24},{40,32},{32,40},{56,48},{48,56},{72,64... | collective-permute-start | bytes 1572872 | tf_op jit(solution)/shard_map/ppermute | solution.py:61
  140.8 14.9 %copy-start.19 = (f32[256,512]{1,0:T(8,128)}, f32[256,512]{1,0:T(8,128)S(1)}, u32[]{:S(2)}) copy-start(f32[256,512]{1,0:T(8,128)S(1)} %collective-permute-done.12.refs_1_) | copy-start | bytes 1572868
  140.9 27.3 %collective-permute-start.5 = (f32[256,512]{1,0:T(8,128)S(1)}, f32[256,512]{1,0:T(8,128)S(1)}, u32[]{:S(2)}, u32[]{:S(2)}) collective-permute-start(f32[256,512]{1,0:T(8,128)S(1)} %add.19.refs_0_), channel_id=1, source_target_pairs={{32,0},{40,8},{48,16},{56,24},{64,32},{72,40},{80,48},{88,56},{96,... | collective-permute-start | bytes 1572872 | tf_op jit(solution)/shard_map/ppermute | solution.py:61
  148.8 7.0 %copy-start.21 = (f32[256,512]{1,0:T(8,128)}, f32[256,512]{1,0:T(8,128)S(1)}, u32[]{:S(2)}) copy-start(f32[256,512]{1,0:T(8,128)S(1)} %collective-permute-done.14.refs_3_) | copy-start | bytes 1572868
  148.8 19.4 %collective-permute-start.4 = (f32[256,512]{1,0:T(8,128)S(1)}, f32[256,512]{1,0:T(8,128)S(1)}, u32[]{:S(2)}, u32[]{:S(2)}) collective-permute-start(f32[256,512]{1,0:T(8,128)S(1)} %add.19.refs_0_), channel_id=1, source_target_pairs={{8,0},{0,8},{24,16},{16,24},{40,32},{32,40},{56,48},{48,56},{72,64... | collective-permute-start | bytes 1572872 | tf_op jit(solution)/shard_map/ppermute | solution.py:61
  149.6 21.2 %collective-permute-start.6 = (f32[256,512]{1,0:T(8,128)S(1)}, f32[256,512]{1,0:T(8,128)S(1)}, u32[]{:S(2)}, u32[]{:S(2)}) collective-permute-start(f32[256,512]{1,0:T(8,128)S(1)} %add.19.refs_0_), channel_id=1, source_target_pairs={{96,0},{104,8},{112,16},{120,24},{0,32},{8,40},{16,48},{24,56},{40... | collective-permute-start | bytes 1572872 | tf_op jit(solution)/shard_map/ppermute | solution.py:61
  160.0 8.1 %copy-start.3 = (f32[256,512]{1,0:T(8,128)}, f32[256,512]{1,0:T(8,128)S(1)}, u32[]{:S(2)}) copy-start(f32[256,512]{1,0:T(8,128)S(1)} %collective-permute-done.10.refs_3_) | copy-start | bytes 1572868
  160.0 8.1 %copy-start.5 = (f32[256,512]{1,0:T(8,128)}, f32[256,512]{1,0:T(8,128)S(1)}, u32[]{:S(2)}) copy-start(f32[256,512]{1,0:T(8,128)S(1)} %collective-permute-done.8.refs_1_) | copy-start | bytes 1572868
  168.2 10.7 %copy-start.7 = (f32[256,512]{1,0:T(8,128)}, f32[256,512]{1,0:T(8,128)S(1)}, u32[]{:S(2)}) copy-start(f32[256,512]{1,0:T(8,128)S(1)} %collective-permute-done.4.refs_1_) | copy-start | bytes 1572868
  170.8 8.1 %copy-start.9 = (f32[256,512]{1,0:T(8,128)}, f32[256,512]{1,0:T(8,128)S(1)}, u32[]{:S(2)}) copy-start(f32[256,512]{1,0:T(8,128)S(1)} %collective-permute-done.6.refs_3_) | copy-start | bytes 1572868
  178.9 41.0 %copy-start.13 = (s32[8]{0:T(128)S(1)}, s32[8]{0:T(128)}, u32[]{:S(2)}) copy-start(s32[8]{0:T(128)} %constant.51.clone.left_of) | copy-start | bytes 100
  178.9 41.0 %copy-start.14 = (s32[8]{0:T(128)S(1)}, s32[8]{0:T(128)}, u32[]{:S(2)}) copy-start(s32[8]{0:T(128)} %constant.52.clone.right_of) | copy-start | bytes 100
  178.9 70.6 %all-to-all-start.2 = ((f32[8,8,32,256]{3,2,1,0:T(8,128)}), f32[8,8,32,256]{3,2,1,0:T(8,128)}, u32[]{:S(2)}, u32[]{:S(2)}) async-start(f32[8,8,32,256]{3,2,1,0:T(8,128)} %gram.8), calls=%async_computation.2 | async-start | bytes 4194304 | tf_op jit(solution)/shard_map/all_to_all | solution.py:253
  183.4 47.7 %copy-start.4 = (f32[256,512]{1,0:T(8,128)S(1)}, f32[256,512]{1,0:T(8,128)}, u32[]{:S(2)}) copy-start(f32[256,512]{1,0:T(8,128)} %copy-done.3) | copy-start | bytes 1572868
  183.5 47.7 %copy-start.6 = (f32[256,512]{1,0:T(8,128)S(1)}, f32[256,512]{1,0:T(8,128)}, u32[]{:S(2)}) copy-start(f32[256,512]{1,0:T(8,128)} %copy-done.5) | copy-start | bytes 1572868
  183.5 36.4 %collective-permute-start.20 = (f32[256,512]{1,0:T(8,128)}, f32[256,512]{1,0:T(8,128)S(1)}, u32[]{:S(2)}, u32[]{:S(2)}) collective-permute-start(f32[256,512]{1,0:T(8,128)} %copy-done.17), channel_id=1, source_target_pairs={{16,0},{24,8},{8,16},{0,24},{48,32},{56,40},{40,48},{32,56},{88,64... | collective-permute-start | bytes 1572872 | tf_op jit(solution)/shard_map/ppermute | solution.py:61
  183.8 47.3 %collective-permute-start.19 = (f32[256,512]{1,0:T(8,128)S(1)}, f32[256,512]{1,0:T(8,128)S(1)}, u32[]{:S(2)}, u32[]{:S(2)}) collective-permute-start(f32[256,512]{1,0:T(8,128)S(1)} %collective-permute-done.9.refs_2_), channel_id=1, source_target_pairs={{16,0},{24,8},{8,16},{0,24},{48,32},{56,40},{40,48},{32,56},{88,64... | collective-permute-start | bytes 1572872 | tf_op jit(solution)/shard_map/ppermute | solution.py:61
  184.5 56.8 %collective-permute-start.18 = (f32[256,512]{1,0:T(8,128)S(1)}, f32[256,512]{1,0:T(8,128)S(1)}, u32[]{:S(2)}, u32[]{:S(2)}) collective-permute-start(f32[256,512]{1,0:T(8,128)S(1)} %collective-permute-done.5.refs_2_), channel_id=1, source_target_pairs={{16,0},{24,8},{8,16},{0,24},{48,32},{56,40},{40,48},{32,56},{88,64... | collective-permute-start | bytes 1572872 | tf_op jit(solution)/shard_map/ppermute | solution.py:61
  230.1 11.3 %copy-start.8 = (f32[256,512]{1,0:T(8,128)S(1)}, f32[256,512]{1,0:T(8,128)}, u32[]{:S(2)}) copy-start(f32[256,512]{1,0:T(8,128)} %copy-done.7) | copy-start | bytes 1572868
  230.1 11.3 %copy-start.10 = (f32[256,512]{1,0:T(8,128)S(1)}, f32[256,512]{1,0:T(8,128)}, u32[]{:S(2)}) copy-start(f32[256,512]{1,0:T(8,128)} %copy-done.9) | copy-start | bytes 1572868
  249.6 38.9 %all-to-all-start.3 = ((f32[8,8,32,256]{3,2,1,0:T(8,128)}), f32[8,8,32,256]{3,2,1,0:T(8,128)S(1)}, u32[]{:S(2)}, u32[]{:S(2)}) async-start(f32[8,8,32,256]{3,2,1,0:T(8,128)} %gram.11), calls=%async_computation.3 | async-start | bytes 4194304 | tf_op jit(solution)/shard_map/all_to_all | solution.py:253
  259.4 34.5 %collective-permute-start.16 = (f32[3,32,256]{2,1,0:T(8,128)S(1)}, f32[3,32,256]{2,1,0:T(8,128)S(1)}, u32[]{:S(2)}, u32[]{:S(2)}) collective-permute-start(f32[3,32,256]{2,1,0:T(8,128)S(1)} %get-tuple-element.11), channel_id=1, source_target_pairs={{0,32},{8,40},{16,48},{24,56},{32,64},{40,72},{48,80},{56,88},{64,... | collective-permute-start | bytes 294920 | tf_op jit(solution)/shard_map/ppermute | solution.py:66
  259.4 30.0 %collective-permute-start.15 = (f32[1,32,256]{2,1,0:T(8,128)S(1)}, f32[1,32,256]{2,1,0:T(8,128)S(1)}, u32[]{:S(2)}, u32[]{:S(2)}) collective-permute-start(f32[1,32,256]{2,1,0:T(8,128)S(1)} %get-tuple-element.10), channel_id=1, source_target_pairs={{0,8},{8,0},{16,24},{24,16},{32,40},{40,32},{48,56},{56,48},{64,72... | collective-permute-start | bytes 98312 | tf_op jit(solution)/shard_map/ppermute | solution.py:66
  259.5 29.9 %collective-permute-start.17 = (f32[1,32,256]{2,1,0:T(8,128)S(1)}, f32[1,32,256]{2,1,0:T(8,128)S(1)}, u32[]{:S(2)}, u32[]{:S(2)}) collective-permute-start(f32[1,32,256]{2,1,0:T(8,128)S(1)} %get-tuple-element.9), channel_id=1, source_target_pairs={{0,96},{8,104},{16,112},{24,120},{32,0},{40,8},{48,16},{56,24},{64... | collective-permute-start | bytes 98312 | tf_op jit(solution)/shard_map/ppermute | solution.py:66
  288.7 7.5 %collective-permute-start.24 = (f32[4,32,256]{2,1,0:T(8,128)S(1)}, f32[4,32,256]{2,1,0:T(8,128)S(1)}, u32[]{:S(2)}, u32[]{:S(2)}) collective-permute-start(f32[4,32,256]{2,1,0:T(8,128)S(1)} %slice.54), channel_id=1, source_target_pairs={{0,48},{8,56},{16,40},{24,32},{32,80},{40,88},{48,72},{56,64},{64,... | collective-permute-start | bytes 393224 | tf_op jit(solution)/shard_map/ppermute | solution.py:66
  289.4 4.6 %collective-permute-start.21 = (f32[1,32,256]{2,1,0:T(8,128)S(1)}, f32[1,32,256]{2,1,0:T(8,128)S(1)}, u32[]{:S(2)}, u32[]{:S(2)}) collective-permute-start(f32[1,32,256]{2,1,0:T(8,128)S(1)} %get-tuple-element.7), channel_id=1, source_target_pairs={{0,8},{8,0},{16,24},{24,16},{32,40},{40,32},{48,56},{56,48},{64,72... | collective-permute-start | bytes 98312 | tf_op jit(solution)/shard_map/ppermute | solution.py:66
  289.4 6.8 %copy-start.25 = (f32[1,32,256]{2,1,0:T(8,128)}, f32[1,32,256]{2,1,0:T(8,128)S(1)}, u32[]{:S(2)}) copy-start(f32[1,32,256]{2,1,0:T(8,128)S(1)} %collective-permute-done.15.refs_1_) | copy-start | bytes 98308
  289.4 5.6 %collective-permute-start.22 = (f32[1,32,256]{2,1,0:T(8,128)S(1)}, f32[1,32,256]{2,1,0:T(8,128)S(1)}, u32[]{:S(2)}, u32[]{:S(2)}) collective-permute-start(f32[1,32,256]{2,1,0:T(8,128)S(1)} %get-tuple-element.6), channel_id=1, source_target_pairs={{0,32},{8,40},{16,48},{24,56},{32,64},{40,72},{48,80},{56,88},{64,... | collective-permute-start | bytes 98312 | tf_op jit(solution)/shard_map/ppermute | solution.py:66
  289.5 5.5 %collective-permute-start.23 = (f32[1,32,256]{2,1,0:T(8,128)S(1)}, f32[1,32,256]{2,1,0:T(8,128)S(1)}, u32[]{:S(2)}, u32[]{:S(2)}) collective-permute-start(f32[1,32,256]{2,1,0:T(8,128)S(1)} %get-tuple-element.5), channel_id=1, source_target_pairs={{0,96},{8,104},{16,112},{24,120},{32,0},{40,8},{48,16},{56,24},{64... | collective-permute-start | bytes 98312 | tf_op jit(solution)/shard_map/ppermute | solution.py:66
  (12 other events, 25.2 us)
Sparse Core Ops, SparseCore 0:
  20.7 52.3 all-gather.2

commit v3 on v2

--- a/solution.py
+++ b/solution.py
@@ -131,7 +131,6 @@
             scratch_shapes=[pltpu.VMEM((rows, X * width), jnp.bfloat16)] * 2,
         ),
         out_shape=jax.ShapeDtypeStruct((rows, steps * columns), jnp.float32),
-        compiler_params=pltpu.CompilerParams(vmem_limit_bytes=32 << 20),
         cost_estimate=pl.CostEstimate(
             flops=6 * rows * X * width * steps * columns, bytes_accessed=8 << 20, transcendentals=0
         ),
@@ -145,46 +144,51 @@
         so_far, refs = refs[0], refs[1:]
     out, lefts, rights = refs
     depth = blocks[0].shape[1]
+    chunks = count // lefts.shape[0]
     step = pl.program_id(0)
 
     @pl.when(step == 0)
     def _():
         for k, block in enumerate(blocks):
             high, low = high_and_low(block[...])
+            at, first = k // chunks, k % chunks * 3
             for ref, order in ((lefts, (high, high, low)), (rights, (high, low, high))):
-                for piece, value in enumerate(order):
-                    ref[k, :, piece * depth : (piece + 1) * depth] = value
-
-    tile = dot(lefts[left_of[step]], rights[right_of[step]]).reshape(out.shape)
-    out[...] = so_far[...] + tile if more else tile
-
-
-def gram(blocks, pairs, shares, so_far):
-    rows, depth = blocks[0].shape
-    count = len(blocks)
-    tiles = len(pairs)
+                for piece, value in enumerate(order, first):
+                    ref[at, :, piece * depth : (piece + 1) * depth] = value
+
+    shares, together, part, width = out.shape
+    for k in range(together):
+        at = step * together + k
+        tile = dot(lefts[left_of[at]], rights[right_of[at]]).reshape(shares, part, width)
+        out[:, k] = so_far[:, k] + tile if more else tile
+
+
+def gram(blocks, pairs, shares, so_far=None):
+    rows, depth = blocks[0][0].shape
+    chunks = len(blocks[0])
+    flat = [chunk for block in blocks for chunk in block]
+    tiles, together = len(pairs), 2
     more = so_far is not None
     whole = pl.BlockSpec((rows, depth), lambda t, *s: (0, 0))
-    tile = pl.BlockSpec((shares, 1, rows // shares, rows), lambda t, *s: (0, t, 0, 0))
+    tile = pl.BlockSpec((shares, together, rows // shares, rows), lambda t, *s: (0, t, 0, 0))
     shape = jax.ShapeDtypeStruct((shares, tiles, rows // shares, rows), jnp.float32)
     order = np.array(pairs, np.int32)
     return pl.pallas_call(
-        functools.partial(gram_kernel, count, more),
+        functools.partial(gram_kernel, len(flat), more),
         grid_spec=pltpu.PrefetchScalarGridSpec(
             num_scalar_prefetch=2,
-            grid=(tiles,),
-            in_specs=[whole] * count + [tile] * more,
+            grid=(tiles // together,),
+            in_specs=[whole] * len(flat) + [tile] * more,
             out_specs=tile,
-            scratch_shapes=[pltpu.VMEM((count, rows, 3 * depth), jnp.bfloat16)] * 2,
+            scratch_shapes=[pltpu.VMEM((len(blocks), rows, 3 * chunks * depth), jnp.bfloat16)] * 2,
         ),
         out_shape=shape,
-        input_output_aliases={2 + count: 0} if more else {},
-        compiler_params=pltpu.CompilerParams(vmem_limit_bytes=32 << 20),
+        input_output_aliases={2 + len(flat): 0} if more else {},
         cost_estimate=pl.CostEstimate(
-            flops=6 * tiles * rows * rows * depth, bytes_accessed=6 << 20, transcendentals=0
+            flops=6 * tiles * rows * rows * chunks * depth, bytes_accessed=6 << 20, transcendentals=0
         ),
         name="gram",
-    )(order[:, 0], order[:, 1], *blocks, *([so_far] if more else []))
+    )(order[:, 0], order[:, 1], *flat, *([so_far] if more else []))
 
 
 def assemble_kernel(table, *refs):
@@ -210,13 +214,8 @@
     )(table, *groups)
 
 
-def all_orbitals(coefficients):
-    mine = coefficients.T
-    ring = [mine]
-    for step in range(1, X):
-        route = [(((t + step) % X) * ZH + zh, t * ZH + zh) for t in range(X) for zh in range(ZH)]
-        ring.append(lax.ppermute(mine, "col", route))
-    return lax.all_gather(jnp.stack(ring), "blk", axis=0, tiled=False)
+def together(*values):
+    return lax.optimization_barrier(values)
 
 
 def on_device(three_index, coefficients):
@@ -233,21 +232,51 @@
         )
         return moved.reshape(X, part.shape[0] // X, rows, width)
 
+    def to_other_half(value):
+        return lax.ppermute(value, "col", swap_zh)
+
     cut = aux - X
-    parts = [over_x(by_aux[:cut]), over_x(by_aux[cut:])]
-    orbitals = all_orbitals(coefficients)
-    chunks = [(part, k) for part in parts for k in range(part.shape[1])]
-
-    early = late = None
-    for part, k in chunks:
-        arrived = lax.ppermute(transformed(part, k, orbitals, place, 1 - zh), "col", swap_zh)
-        own = transformed(part, k, orbitals, place, zh) + arrived
-        other = fetched(own, other_core)
-        below = fetched(own, next_row)
-        above = fetched(own, previous_row)
-        across = fetched(below, over_to_across)
-        early = gram([own, other, below, above], EARLY, shares, early)
-        late = gram([own, other, below, above, across], LATE, shares, late)
+    ring = [coefficients.T]
+    for step in range(1, X):
+        route = [(((t + step) % X) * ZH + h, t * ZH + h) for t in range(X) for h in range(ZH)]
+        ring.append(lax.ppermute(ring[0], "col", route))
+    first, *ring = together(by_aux[:cut], *ring)
+    ring = jnp.stack(ring)
+    first_part = over_x(first)
+    orbitals = lax.all_gather(ring, "blk", axis=0, tiled=False)
+    last, first_part = together(by_aux[cut:], first_part)
+    last_part = over_x(last)
+
+    def sent(part, k):
+        return to_other_half(transformed(part, k, orbitals, place, 1 - zh))
+
+    def kept(part, k):
+        return transformed(part, k, orbitals, place, zh)
+
+    def neighbours(own):
+        return fetched(own, other_core), fetched(own, next_row), fetched(own, previous_row)
+
+    arrived_0, arrived_1 = sent(first_part, 0), sent(first_part, 1)
+    own_0 = kept(first_part, 0) + arrived_0
+    own_1 = kept(first_part, 1) + arrived_1
+    other_0, below_0, above_0 = neighbours(own_0)
+    arrived_2 = sent(last_part, 0)
+    own_2 = kept(last_part, 0) + arrived_2
+    other_0, below_0, above_0, own_1 = together(other_0, below_0, above_0, own_1)
+    across_0 = fetched(below_0, over_to_across)
+    other_1, below_1, above_1 = neighbours(own_1)
+    other_1, below_1, above_1, across_0, own_2 = together(other_1, below_1, above_1, across_0, own_2)
+    across_1 = fetched(below_1, over_to_across)
+    other_2, below_2, above_2 = neighbours(own_2)
+    known = [(own_0, own_1), (other_0, other_1), (below_0, below_1), (above_0, above_1)]
+    early = gram(known, EARLY, shares)
+    other_2, below_2, above_2, across_1, early = together(other_2, below_2, above_2, across_1, early)
+    across_2 = fetched(below_2, over_to_across)
+    known_2 = [(own_2,), (other_2,), (below_2,), (above_2,)]
+    early = gram(known_2, EARLY, shares, early)
+    late = gram(known + [(across_0, across_1)], LATE, shares)
+    across_2, late = together(across_2, late)
+    late = gram(known_2 + [(across_2,)], LATE, shares, late)
 
     def sent_home(tiles, pairs):
         summed = lax.all_to_all(tiles, "col", split_axis=0, concat_axis=0, tiled=True).sum(0)

time: 307 us -> 271 us (0.88)
  waiting for transfers between devices: 140 us -> 111 us
  local copies, waits for them, and re-layouts: 21.8 us -> 15.6 us
    ppermute x12, waiting for transfers between devices: 49.2 us -> 33.9 us  [fetched(): return lax.ppermute(value, 'blk', route)]
    pallas_call x6 -> x4, Pallas kernels: 44.6 us -> 32 us  [gram(): pl.pallas_call(functools.partial(gram_kernel, len(flat), more), grid_spec...]
    pallas_call x6, Pallas kernels: 25.1 us -> 36.6 us  [transformed(): pl.pallas_call(transform_kernel, grid_spec=pltpu.PrefetchScalarGridSpec(n...]
    all_to_all x2, waiting for transfers between devices: 54.8 us -> 45.2 us  [over_x(): lax.all_to_all(part, 'col', split_axis=0, concat_axis=0, tiled=True, axis...]
    ppermute x6, waiting for transfers between devices: 7.8 us -> 0.2 us  [the longest x3 0.19 us: on_device(): ring.append(lax.ppermute(ring[0], 'col', route))]
    unnamed x60 -> x42, local copies, waits for them, and re-layouts: 11.6 us -> 5.4 us
  transfers between devices with their start and end apart: 30 -> 30, of which waited for: 15 -> 9; matrix products, arithmetic and copies ran while one was open for 5% -> 6% of each run, Pallas kernels for 20% -> 23%
where the time goes in v3:
time: 271 us; the launch traced here: 270 us
  waiting for transfers between devices  111 us (41%)
  Pallas kernels  70.6 us (26%)
  starting transfers between devices  51.4 us (19%)
  local copies, waits for them, and re-layouts  15.6 us (6%)
  between operations  13.6 us (5%)
  other arithmetic  7.57 us (3%)
    all_to_all x2, waiting for transfers between devices, over_x(): lax.all_to_all(part, 'col', split_axis=0, concat_axis=0, tiled=True, axis...  45.2 us
    pallas_call x6, Pallas kernels, transformed(): pl.pallas_call(transform_kernel, grid_spec=pltpu.PrefetchScalarGridSpec(n...  36.6 us
    ppermute x12, waiting for transfers between devices, fetched(): return lax.ppermute(value, 'blk', route)  33.9 us
    pallas_call x4, Pallas kernels, gram(): pl.pallas_call(functools.partial(gram_kernel, len(flat), more), grid_spec...  32 us
    all_to_all x2, waiting for transfers between devices, sent_home(): lax.all_to_all(tiles, 'col', split_axis=0, concat_axis=0, tiled=True).sum(0)  28.6 us
    all_to_all x2, starting transfers between devices, sent_home(): lax.all_to_all(tiles, 'col', split_axis=0, concat_axis=0, tiled=True).sum(0)  12.4 us
    ppermute x12, starting transfers between devices, fetched(): return lax.ppermute(value, 'blk', route)  11.2 us
    all_to_all x2, starting transfers between devices, over_x(): lax.all_to_all(part, 'col', split_axis=0, concat_axis=0, tiled=True, axis...  8.45 us
  transfers between devices with their start and end apart: 30, of which 9 were waited for; matrix products, arithmetic and copies ran while one was open for 6% of the time, Pallas kernels for 23%

profile of v3, /device:TPU:0, one launch (start us, length us, event | category | flops | bytes accessed | tf_op | source)
XLA Modules:
  0.0 269.5 jit_solution(17323448258228052309)
XLA Ops:
  6.5 1.6 collective-permute-start.2
  8.1 2.7 %collective-permute-start.1 = (f32[64,512]{1,0:T(8,128)}, f32[64,512]{1,0:T(8,128)S(1)}, u32[]{:S(2)}, u32[]{:S(2)}) collective-permute-start(f32[64,512]{1,0:T(8,128)} %bitcast.25), channel_id=1, source_target_pairs={{4,0},{5,1},{6,2},{7,3},{0,4},{1,5},{2,6},{3,7},{12,8},{13,9},{14,... | collective-permute-start | bytes 393224 | tf_op jit(solution)/shard_map/ppermute | solution.py:242
  10.8 1.4 collective-permute-start
  12.3 4.6 %slice.45 = f32[8,256,512]{2,1,0:T(8,128)} slice(f32[12,256,512]{2,1,0:T(8,128)} %bitcast.22), slice={[0:8], [0:256], [0:512]} | slice | bytes 8388608 | tf_op jit(solution)/shard_map/slice | solution.py:243
  17.1 0.8 pad_maximum_fusion
  17.9 4.8 %all-to-all-start = ((f32[8,256,512]{2,1,0:T(8,128)}), f32[8,256,512]{2,1,0:T(8,128)}, u32[]{:S(2)}, u32[]{:S(2)}) async-start(f32[8,256,512]{2,1,0:T(8,128)} %slice.45), calls=%async_computation | async-start | bytes 8388608 | tf_op jit(solution)/shard_map/all_to_all | solution.py:230
  22.8 3.1 %slice.44 = f32[4,256,512]{2,1,0:T(8,128)} slice(f32[12,256,512]{2,1,0:T(8,128)} %bitcast.23), slice={[8:12], [0:256], [0:512]} | slice | bytes 4194304 | tf_op jit(solution)/shard_map/slice | solution.py:247
  25.9 45.2 %all-to-all-done = f32[8,256,512]{2,1,0:T(8,128)} async-done(((f32[8,256,512]{2,1,0:T(8,128)}), f32[8,256,512]{2,1,0:T(8,128)}, u32[]{:S(2)}, u32[]{:S(2)}) %all-to-all-start) | async-done | bytes 4194336 | tf_op jit(solution)/shard_map/all_to_all | solution.py:230
  71.1 3.6 %all-to-all-start.1 = ((f32[4,256,512]{2,1,0:T(8,128)}), f32[4,256,512]{2,1,0:T(8,128)S(1)}, u32[]{:S(2)}, u32[]{:S(2)}) async-start(f32[4,256,512]{2,1,0:T(8,128)} %slice.44), calls=%async_computation.1 | async-start | bytes 4194304 | tf_op jit(solution)/shard_map/all_to_all | solution.py:230
  75.4 6.1 %transform.7 = f32[256,512]{1,0:T(8,128)} custom-call(s32[2]{0:T(128)} %pad_add_fusion.1.place, f32[4,2,256,512]{3,2,1,0:T(8,128)} %bitcast.5.part, f32[16,4,64,512]{3,2,1,0:T(8,128)} %bitcast.14), custom_call_target="tpu_custom_call" | custom-call | flops 1610612736 | bytes 8388608 | tf_op jit(solution)/shard_map/transform/pallas_call | solution.py:121
  81.5 3.9 %collective-permute-start.3 = (f32[256,512]{1,0:T(8,128)}, f32[256,512]{1,0:T(8,128)}, u32[]{:S(2)}, u32[]{:S(2)}) collective-permute-start(f32[256,512]{1,0:T(8,128)} %transform.7), channel_id=1, source_target_pairs={{1,0},{0,1},{3,2},{2,3},{5,4},{4,5},{7,6},{6,7},{9,8},{8,9},{11,10... | collective-permute-start | bytes 1572872 | tf_op jit(solution)/shard_map/ppermute | solution.py:236
  86.0 6.1 %transform.9 = f32[256,512]{1,0:T(8,128)} custom-call(s32[2]{0:T(128)} %pad_add_fusion.1.place, f32[4,2,256,512]{3,2,1,0:T(8,128)} %bitcast.5.part, f32[16,4,64,512]{3,2,1,0:T(8,128)} %bitcast.15), custom_call_target="tpu_custom_call" | custom-call | flops 1610612736 | bytes 8388608 | tf_op jit(solution)/shard_map/transform/pallas_call | solution.py:121
  92.1 6.1 %transform.6 = f32[256,512]{1,0:T(8,128)} custom-call(s32[2]{0:T(128)} %pad_add_fusion.place, f32[4,2,256,512]{3,2,1,0:T(8,128)} %bitcast.5.part, f32[16,4,64,512]{3,2,1,0:T(8,128)} %bitcast.16), custom_call_target="tpu_custom_call" | custom-call | flops 1610612736 | bytes 8388608 | tf_op jit(solution)/shard_map/transform/pallas_call | solution.py:121
  98.2 1.3 add.19.refs_0_
  99.5 1.6 collective-permute-start.6
  101.1 1.7 collective-permute-start.5
  102.8 1.3 copy-done
  104.1 6.1 %transform.11 = f32[256,512]{1,0:T(8,128)} custom-call(s32[2]{0:T(128)} %pad_add_fusion.1.place, f32[4,1,256,512]{3,2,1,0:T(8,128)} %bitcast.20, f32[16,4,64,512]{3,2,1,0:T(8,128)} %bitcast.17), custom_call_target="tpu_custom_call" | custom-call | flops 1610612736 | bytes 8388608 | tf_op jit(solution)/shard_map/transform/pallas_call | solution.py:121
  110.2 3.8 %collective-permute-start.12 = (f32[256,512]{1,0:T(8,128)}, f32[256,512]{1,0:T(8,128)S(1)}, u32[]{:S(2)}, u32[]{:S(2)}) collective-permute-start(f32[256,512]{1,0:T(8,128)} %transform.11), channel_id=1, source_target_pairs={{1,0},{0,1},{3,2},{2,3},{5,4},{4,5},{7,6},{6,7},{9,8},{8,9},{11,10... | collective-permute-start | bytes 1572872 | tf_op jit(solution)/shard_map/ppermute | solution.py:236
  114.1 6.1 %transform.8 = f32[256,512]{1,0:T(8,128)} custom-call(s32[2]{0:T(128)} %pad_add_fusion.place, f32[4,2,256,512]{3,2,1,0:T(8,128)} %bitcast.5.part, f32[16,4,64,512]{3,2,1,0:T(8,128)} %bitcast.18), custom_call_target="tpu_custom_call" | custom-call | flops 1610612736 | bytes 8388608 | tf_op jit(solution)/shard_map/transform/pallas_call | solution.py:121
  120.2 1.1 add.20.refs_1_
  121.4 0.9 collective-permute-start.11
  122.6 2.9 %collective-permute-start.9 = (f32[256,512]{1,0:T(8,128)S(1)}, f32[256,512]{1,0:T(8,128)}, u32[]{:S(2)}, u32[]{:S(2)}) collective-permute-start(f32[256,512]{1,0:T(8,128)S(1)} %add.20.refs_1_), channel_id=1, source_target_pairs={{32,0},{40,8},{48,16},{56,24},{64,32},{72,40},{80,48},{88,56},{96,... | collective-permute-start | bytes 1572872 | tf_op jit(solution)/shard_map/ppermute | solution.py:61
  125.5 6.1 %transform.10 = f32[256,512]{1,0:T(8,128)} custom-call(s32[2]{0:T(128)} %pad_add_fusion.place, f32[4,1,256,512]{3,2,1,0:T(8,128)} %bitcast.21, f32[16,4,64,512]{3,2,1,0:T(8,128)} %bitcast.19), custom_call_target="tpu_custom_call" | custom-call | flops 1610612736 | bytes 8388608 | tf_op jit(solution)/shard_map/transform/pallas_call | solution.py:121
  131.6 1.1 add.21.refs_0_
  132.7 6.1 %collective-permute-done.11.refs_8_ = f32[256,512]{1,0:T(8,128)S(1)} collective-permute-done((f32[256,512]{1,0:T(8,128)}, f32[256,512]{1,0:T(8,128)S(1)}, u32[]{:S(2)}, u32[]{:S(2)}) %collective-permute-start.11) | collective-permute-done | bytes 524320 | tf_op jit(solution)/shard_map/ppermute | solution.py:61
  138.9 0.8 copy-done.19
  140.5 2.9 %collective-permute-start.14 = (f32[256,512]{1,0:T(8,128)S(1)}, f32[256,512]{1,0:T(8,128)S(1)}, u32[]{:S(2)}, u32[]{:S(2)}) collective-permute-start(f32[256,512]{1,0:T(8,128)S(1)} %add.21.refs_0_), channel_id=1, source_target_pairs={{32,0},{40,8},{48,16},{56,24},{64,32},{72,40},{80,48},{88,56},{96,... | collective-permute-start | bytes 1572872 | tf_op jit(solution)/shard_map/ppermute | solution.py:61
  143.4 8.7 %gram.4.refs_4_ = f32[8,8,32,256]{3,2,1,0:T(8,128)} custom-call(s32[8]{0:T(128)} %constant.49.clone.left_of, s32[8]{0:T(128)} %constant.50.clone.right_of, f32[256,512]{1,0:T(8,128)} %copy-done.6, f32[256,512]{1,0:T(8,128)} %copy-done.7, f32[256,512]{1,0:T(8,128)} %collective-permute-done.4.refs_2_, f32[256,512]{1,0:T(8,128)} %copy-done.19, ...), custom_call_target="tpu_custom_call" | custom-call | flops 3221225472 | bytes 6291456 | tf_op jit(solution)/shard_map/gram/pallas_call | solution.py:176
  152.2 1.3 collective-permute-done.16.refs_9_
  153.5 2.0 collective-permute-done.15.refs_3_
  155.5 0.8 copy-done.2
  156.5 0.8 copy-done.5
  157.3 6.8 %gram.5 = f32[8,8,32,256]{3,2,1,0:T(8,128)} custom-call(s32[8]{0:T(128)} %constant.49.clone.left_of, s32[8]{0:T(128)} %constant.50.clone.right_of, f32[256,512]{1,0:T(8,128)} %copy-done.1, f32[256,512]{1,0:T(8,128)} %copy-done.5, f32[256,512]{1,0:T(8,128)} %copy-done.3, f32[256,512]{1,0:T(8,128)} %copy-done.2, ...), custom_call_target="tpu_custom_call", output_to_operand_aliasing={{}: (6, {})} | custom-call | flops 1610612736 | bytes 6291456 | tf_op jit(solution)/shard_map/gram/pallas_call | solution.py:176
  164.1 4.9 %all-to-all-start.2 = ((f32[8,8,32,256]{3,2,1,0:T(8,128)}), f32[8,8,32,256]{3,2,1,0:T(8,128)S(1)}, u32[]{:S(2)}, u32[]{:S(2)}) async-start(f32[8,8,32,256]{3,2,1,0:T(8,128)} %gram.5), calls=%async_computation.2 | async-start | bytes 4194304 | tf_op jit(solution)/shard_map/all_to_all | solution.py:282
  169.1 9.4 %gram.6.refs_5_ = f32[8,8,32,256]{3,2,1,0:T(8,128)} custom-call(s32[8]{0:T(128)} %constant.51.clone.left_of, s32[8]{0:T(128)} %constant.52.clone.right_of, f32[256,512]{1,0:T(8,128)} %copy-done.6, f32[256,512]{1,0:T(8,128)} %copy-done.7, f32[256,512]{1,0:T(8,128)} %collective-permute-done.4.refs_2_, f32[256,512]{1,0:T(8,128)} %copy-done.19, ...), custom_call_target="tpu_custom_call" | custom-call | flops 3221225472 | bytes 6291456 | tf_op jit(solution)/shard_map/gram/pallas_call | solution.py:176
  178.4 24.4 %collective-permute-done.20.refs_4_ = f32[256,512]{1,0:T(8,128)S(1)} collective-permute-done((f32[256,512]{1,0:T(8,128)S(1)}, f32[256,512]{1,0:T(8,128)S(1)}, u32[]{:S(2)}, u32[]{:S(2)}) %collective-permute-start.20) | collective-permute-done | bytes 524320 | tf_op jit(solution)/shard_map/ppermute | solution.py:61
  202.9 0.8 copy-done.8
  203.7 7.1 %gram.7 = f32[8,8,32,256]{3,2,1,0:T(8,128)} custom-call(s32[8]{0:T(128)} %constant.51.clone.left_of, s32[8]{0:T(128)} %constant.52.clone.right_of, f32[256,512]{1,0:T(8,128)} %copy-done.1, f32[256,512]{1,0:T(8,128)} %copy-done.5, f32[256,512]{1,0:T(8,128)} %copy-done.3, f32[256,512]{1,0:T(8,128)} %copy-done.2, ...), custom_call_target="tpu_custom_call", output_to_operand_aliasing={{}: (7, {})} | custom-call | flops 1610612736 | bytes 6291456 | tf_op jit(solution)/shard_map/gram/pallas_call | solution.py:176
  210.8 7.5 %all-to-all-start.3 = ((f32[8,8,32,256]{3,2,1,0:T(8,128)}), f32[8,8,32,256]{3,2,1,0:T(8,128)}, u32[]{:S(2)}, u32[]{:S(2)}) async-start(f32[8,8,32,256]{3,2,1,0:T(8,128)} %gram.7), calls=%async_computation.3 | async-start | bytes 4194304 | tf_op jit(solution)/shard_map/all_to_all | solution.py:282
  218.5 2.2 collective-permute-start.19
  221.4 28.6 %all-to-all-done.3 = f32[8,8,32,256]{3,2,1,0:T(8,128)} async-done(((f32[8,8,32,256]{3,2,1,0:T(8,128)}), f32[8,8,32,256]{3,2,1,0:T(8,128)}, u32[]{:S(2)}, u32[]{:S(2)}) %all-to-all-start.3) | async-done | bytes 2097184 | tf_op jit(solution)/shard_map/all_to_all | solution.py:282
  249.9 1.8 reduce_sum.19
  251.7 1.1 collective-permute-start.24
  253.4 1.3 collective-permute-start.23
  256.0 1.2 dynamic-slice_bitcast_fusion.table
  257.3 2.7 %collective-permute-done.22.refs_6_ = f32[1,32,256]{2,1,0:T(8,128)S(1)} collective-permute-done((f32[1,32,256]{2,1,0:T(8,128)S(1)}, f32[1,32,256]{2,1,0:T(8,128)S(1)}, u32[]{:S(2)}, u32[]{:S(2)}) %collective-permute-start.22) | collective-permute-done | bytes 32800 | tf_op jit(solution)/shard_map/ppermute | solution.py:66
  260.7 2.0 assemble.1
  (81 shorter events, 6.5 us)
Async XLA Ops:
  6.5 68.8 %all-gather.3.cloned.1.call-start = ((), (), s32[]{:S(2)}) async-start(), calls=%async_computation.4 | async-start | bytes 8912896 | tf_op jit(solution)/shard_map/all_gather | solution.py:246
  6.5 10.3 %collective-permute-start.2 = (f32[64,512]{1,0:T(8,128)}, f32[64,512]{1,0:T(8,128)S(1)}, u32[]{:S(2)}, u32[]{:S(2)}) collective-permute-start(f32[64,512]{1,0:T(8,128)} %bitcast.24), channel_id=1, source_target_pairs={{6,0},{7,1},{0,2},{1,3},{2,4},{3,5},{4,6},{5,7},{14,8},{15,9},{8,1... | collective-permute-start | bytes 393224 | tf_op jit(solution)/shard_map/ppermute | solution.py:242
  8.1 9.0 %collective-permute-start.1 = (f32[64,512]{1,0:T(8,128)}, f32[64,512]{1,0:T(8,128)S(1)}, u32[]{:S(2)}, u32[]{:S(2)}) collective-permute-start(f32[64,512]{1,0:T(8,128)} %bitcast.25), channel_id=1, source_target_pairs={{4,0},{5,1},{6,2},{7,3},{0,4},{1,5},{2,6},{3,7},{12,8},{13,9},{14,... | collective-permute-start | bytes 393224 | tf_op jit(solution)/shard_map/ppermute | solution.py:242
  10.8 6.2 %collective-permute-start = (f32[64,512]{1,0:T(8,128)}, f32[64,512]{1,0:T(8,128)S(1)}, u32[]{:S(2)}, u32[]{:S(2)}) collective-permute-start(f32[64,512]{1,0:T(8,128)} %bitcast.26), channel_id=1, source_target_pairs={{2,0},{3,1},{4,2},{5,3},{6,4},{7,5},{0,6},{1,7},{10,8},{11,9},{12,... | collective-permute-start | bytes 393224 | tf_op jit(solution)/shard_map/ppermute | solution.py:242
  12.3 4.8 %copy-start.9 = (f32[512,64]{0,1:T(8,128)S(1)}, f32[512,64]{0,1:T(8,128)}, u32[]{:S(2)}) copy-start(f32[512,64]{0,1:T(8,128)} %param.12) | copy-start | bytes 393220
  17.9 53.1 %all-to-all-start = ((f32[8,256,512]{2,1,0:T(8,128)}), f32[8,256,512]{2,1,0:T(8,128)}, u32[]{:S(2)}, u32[]{:S(2)}) async-start(f32[8,256,512]{2,1,0:T(8,128)} %slice.45), calls=%async_computation | async-start | bytes 8388608 | tf_op jit(solution)/shard_map/all_to_all | solution.py:230
  71.1 31.7 %all-to-all-start.1 = ((f32[4,256,512]{2,1,0:T(8,128)}), f32[4,256,512]{2,1,0:T(8,128)S(1)}, u32[]{:S(2)}, u32[]{:S(2)}) async-start(f32[4,256,512]{2,1,0:T(8,128)} %slice.44), calls=%async_computation.1 | async-start | bytes 4194304 | tf_op jit(solution)/shard_map/all_to_all | solution.py:230
  81.5 16.7 %collective-permute-start.3 = (f32[256,512]{1,0:T(8,128)}, f32[256,512]{1,0:T(8,128)}, u32[]{:S(2)}, u32[]{:S(2)}) collective-permute-start(f32[256,512]{1,0:T(8,128)} %transform.7), channel_id=1, source_target_pairs={{1,0},{0,1},{3,2},{2,3},{5,4},{4,5},{7,6},{6,7},{9,8},{8,9},{11,10... | collective-permute-start | bytes 1572872 | tf_op jit(solution)/shard_map/ppermute | solution.py:236
  92.1 28.1 %collective-permute-start.7 = (f32[256,512]{1,0:T(8,128)}, f32[256,512]{1,0:T(8,128)S(1)}, u32[]{:S(2)}, u32[]{:S(2)}) collective-permute-start(f32[256,512]{1,0:T(8,128)} %transform.9), channel_id=1, source_target_pairs={{1,0},{0,1},{3,2},{2,3},{5,4},{4,5},{7,6},{6,7},{9,8},{8,9},{11,10... | collective-permute-start | bytes 1572872 | tf_op jit(solution)/shard_map/ppermute | solution.py:236
  99.5 20.7 %copy-start.6 = (f32[256,512]{1,0:T(8,128)}, f32[256,512]{1,0:T(8,128)S(1)}, u32[]{:S(2)}) copy-start(f32[256,512]{1,0:T(8,128)S(1)} %add.19.refs_0_) | copy-start | bytes 1572868
  99.5 21.8 %collective-permute-start.6 = (f32[256,512]{1,0:T(8,128)S(1)}, f32[256,512]{1,0:T(8,128)}, u32[]{:S(2)}, u32[]{:S(2)}) collective-permute-start(f32[256,512]{1,0:T(8,128)S(1)} %add.19.refs_0_), channel_id=1, source_target_pairs={{96,0},{104,8},{112,16},{120,24},{0,32},{8,40},{16,48},{24,56},{40... | collective-permute-start | bytes 1572872 | tf_op jit(solution)/shard_map/ppermute | solution.py:61
  101.1 20.2 %collective-permute-start.5 = (f32[256,512]{1,0:T(8,128)S(1)}, f32[256,512]{1,0:T(8,128)}, u32[]{:S(2)}, u32[]{:S(2)}) collective-permute-start(f32[256,512]{1,0:T(8,128)S(1)} %add.19.refs_0_), channel_id=1, source_target_pairs={{32,0},{40,8},{48,16},{56,24},{64,32},{72,40},{80,48},{88,56},{96,... | collective-permute-start | bytes 1572872 | tf_op jit(solution)/shard_map/ppermute | solution.py:61
  102.8 18.6 %collective-permute-start.4 = (f32[256,512]{1,0:T(8,128)S(1)}, f32[256,512]{1,0:T(8,128)}, u32[]{:S(2)}, u32[]{:S(2)}) collective-permute-start(f32[256,512]{1,0:T(8,128)S(1)} %add.19.refs_0_), channel_id=1, source_target_pairs={{8,0},{0,8},{24,16},{16,24},{40,32},{32,40},{56,48},{48,56},{72,64... | collective-permute-start | bytes 1572872 | tf_op jit(solution)/shard_map/ppermute | solution.py:61
  102.8 1.3 copy-start
  110.2 21.3 %collective-permute-start.12 = (f32[256,512]{1,0:T(8,128)}, f32[256,512]{1,0:T(8,128)S(1)}, u32[]{:S(2)}, u32[]{:S(2)}) collective-permute-start(f32[256,512]{1,0:T(8,128)} %transform.11), channel_id=1, source_target_pairs={{1,0},{0,1},{3,2},{2,3},{5,4},{4,5},{7,6},{6,7},{9,8},{8,9},{11,10... | collective-permute-start | bytes 1572872 | tf_op jit(solution)/shard_map/ppermute | solution.py:236
  121.3 10.3 %copy-start.7 = (f32[256,512]{1,0:T(8,128)}, f32[256,512]{1,0:T(8,128)S(1)}, u32[]{:S(2)}) copy-start(f32[256,512]{1,0:T(8,128)S(1)} %add.20.refs_1_) | copy-start | bytes 1572868
  121.4 17.5 %collective-permute-start.11 = (f32[256,512]{1,0:T(8,128)}, f32[256,512]{1,0:T(8,128)S(1)}, u32[]{:S(2)}, u32[]{:S(2)}) collective-permute-start(f32[256,512]{1,0:T(8,128)} %collective-permute-done.5.refs_4_), channel_id=1, source_target_pairs={{16,0},{24,8},{8,16},{0,24},{48,32},{56,40},{40,48},{32,56},{88,64... | collective-permute-start | bytes 1572872 | tf_op jit(solution)/shard_map/ppermute | solution.py:61
  122.3 16.6 %collective-permute-start.10 = (f32[256,512]{1,0:T(8,128)S(1)}, f32[256,512]{1,0:T(8,128)S(1)}, u32[]{:S(2)}, u32[]{:S(2)}) collective-permute-start(f32[256,512]{1,0:T(8,128)S(1)} %add.20.refs_1_), channel_id=1, source_target_pairs={{96,0},{104,8},{112,16},{120,24},{0,32},{8,40},{16,48},{24,56},{40... | collective-permute-start | bytes 1572872 | tf_op jit(solution)/shard_map/ppermute | solution.py:61
  122.6 16.2 %collective-permute-start.9 = (f32[256,512]{1,0:T(8,128)S(1)}, f32[256,512]{1,0:T(8,128)}, u32[]{:S(2)}, u32[]{:S(2)}) collective-permute-start(f32[256,512]{1,0:T(8,128)S(1)} %add.20.refs_1_), channel_id=1, source_target_pairs={{32,0},{40,8},{48,16},{56,24},{64,32},{72,40},{80,48},{88,56},{96,... | collective-permute-start | bytes 1572872 | tf_op jit(solution)/shard_map/ppermute | solution.py:61
  125.5 13.4 %collective-permute-start.8 = (f32[256,512]{1,0:T(8,128)S(1)}, f32[256,512]{1,0:T(8,128)S(1)}, u32[]{:S(2)}, u32[]{:S(2)}) collective-permute-start(f32[256,512]{1,0:T(8,128)S(1)} %add.20.refs_1_), channel_id=1, source_target_pairs={{8,0},{0,8},{24,16},{16,24},{40,32},{32,40},{56,48},{48,56},{72,64... | collective-permute-start | bytes 1572872 | tf_op jit(solution)/shard_map/ppermute | solution.py:61
  132.7 19.4 %copy-start.1 = (f32[256,512]{1,0:T(8,128)}, f32[256,512]{1,0:T(8,128)S(1)}, u32[]{:S(2)}) copy-start(f32[256,512]{1,0:T(8,128)S(1)} %add.21.refs_0_) | copy-start | bytes 1572868
  138.9 1.3 copy-start.17
  138.9 1.7 copy-start.18
  138.9 0.8 copy-start.19
  139.7 13.8 %collective-permute-start.16 = (f32[256,512]{1,0:T(8,128)}, f32[256,512]{1,0:T(8,128)S(1)}, u32[]{:S(2)}, u32[]{:S(2)}) collective-permute-start(f32[256,512]{1,0:T(8,128)} %collective-permute-done.9.refs_5_), channel_id=1, source_target_pairs={{16,0},{24,8},{8,16},{0,24},{48,32},{56,40},{40,48},{32,56},{88,64... | collective-permute-start | bytes 1572872 | tf_op jit(solution)/shard_map/ppermute | solution.py:61
  140.2 15.3 %collective-permute-start.15 = (f32[256,512]{1,0:T(8,128)S(1)}, f32[256,512]{1,0:T(8,128)S(1)}, u32[]{:S(2)}, u32[]{:S(2)}) collective-permute-start(f32[256,512]{1,0:T(8,128)S(1)} %add.21.refs_0_), channel_id=1, source_target_pairs={{96,0},{104,8},{112,16},{120,24},{0,32},{8,40},{16,48},{24,56},{40... | collective-permute-start | bytes 1572872 | tf_op jit(solution)/shard_map/ppermute | solution.py:61
  140.5 15.0 %collective-permute-start.14 = (f32[256,512]{1,0:T(8,128)S(1)}, f32[256,512]{1,0:T(8,128)S(1)}, u32[]{:S(2)}, u32[]{:S(2)}) collective-permute-start(f32[256,512]{1,0:T(8,128)S(1)} %add.21.refs_0_), channel_id=1, source_target_pairs={{32,0},{40,8},{48,16},{56,24},{64,32},{72,40},{80,48},{88,56},{96,... | collective-permute-start | bytes 1572872 | tf_op jit(solution)/shard_map/ppermute | solution.py:61
  143.4 12.1 %collective-permute-start.13 = (f32[256,512]{1,0:T(8,128)S(1)}, f32[256,512]{1,0:T(8,128)S(1)}, u32[]{:S(2)}, u32[]{:S(2)}) collective-permute-start(f32[256,512]{1,0:T(8,128)S(1)} %add.21.refs_0_), channel_id=1, source_target_pairs={{8,0},{0,8},{24,16},{16,24},{40,32},{32,40},{56,48},{48,56},{72,64... | collective-permute-start | bytes 1572872 | tf_op jit(solution)/shard_map/ppermute | solution.py:61
  153.5 10.6 %copy-start.20 = (f32[256,512]{1,0:T(8,128)}, f32[256,512]{1,0:T(8,128)S(1)}, u32[]{:S(2)}) copy-start(f32[256,512]{1,0:T(8,128)S(1)} %collective-permute-done.16.refs_9_) | copy-start | bytes 1572868
  155.5 0.8 copy-start.2
  155.5 1.0 copy-start.3
  156.5 0.8 copy-start.5
  164.1 4.9 %copy-start.4 = (f32[256,512]{1,0:T(8,128)S(1)}, f32[256,512]{1,0:T(8,128)}, u32[]{:S(2)}) copy-start(f32[256,512]{1,0:T(8,128)} %copy-done.3) | copy-start | bytes 1572868
  164.1 46.7 %all-to-all-start.2 = ((f32[8,8,32,256]{3,2,1,0:T(8,128)}), f32[8,8,32,256]{3,2,1,0:T(8,128)S(1)}, u32[]{:S(2)}, u32[]{:S(2)}) async-start(f32[8,8,32,256]{3,2,1,0:T(8,128)} %gram.5), calls=%async_computation.2 | async-start | bytes 4194304 | tf_op jit(solution)/shard_map/all_to_all | solution.py:282
  169.0 33.9 %collective-permute-start.20 = (f32[256,512]{1,0:T(8,128)S(1)}, f32[256,512]{1,0:T(8,128)S(1)}, u32[]{:S(2)}, u32[]{:S(2)}) collective-permute-start(f32[256,512]{1,0:T(8,128)S(1)} %copy-done.4), channel_id=1, source_target_pairs={{16,0},{24,8},{8,16},{0,24},{48,32},{56,40},{40,48},{32,56},{88,64... | collective-permute-start | bytes 1572872 | tf_op jit(solution)/shard_map/ppermute | solution.py:61
  202.9 0.8 copy-start.8
  210.8 39.1 %all-to-all-start.3 = ((f32[8,8,32,256]{3,2,1,0:T(8,128)}), f32[8,8,32,256]{3,2,1,0:T(8,128)}, u32[]{:S(2)}, u32[]{:S(2)}) async-start(f32[8,8,32,256]{3,2,1,0:T(8,128)} %gram.7), calls=%async_computation.3 | async-start | bytes 4194304 | tf_op jit(solution)/shard_map/all_to_all | solution.py:282
  218.5 36.2 %collective-permute-start.19 = (f32[1,32,256]{2,1,0:T(8,128)S(1)}, f32[1,32,256]{2,1,0:T(8,128)S(1)}, u32[]{:S(2)}, u32[]{:S(2)}) collective-permute-start(f32[1,32,256]{2,1,0:T(8,128)S(1)} %get-tuple-element.55), channel_id=1, source_target_pairs={{0,96},{8,104},{16,112},{24,120},{32,0},{40,8},{48,16},{56,24},{64... | collective-permute-start | bytes 98312 | tf_op jit(solution)/shard_map/ppermute | solution.py:66
  220.7 34.7 %collective-permute-start.17 = (f32[1,32,256]{2,1,0:T(8,128)S(1)}, f32[1,32,256]{2,1,0:T(8,128)S(1)}, u32[]{:S(2)}, u32[]{:S(2)}) collective-permute-start(f32[1,32,256]{2,1,0:T(8,128)S(1)} %get-tuple-element.56), channel_id=1, source_target_pairs={{0,8},{8,0},{16,24},{24,16},{32,40},{40,32},{48,56},{56,48},{64,72... | collective-permute-start | bytes 98312 | tf_op jit(solution)/shard_map/ppermute | solution.py:66
  221.4 35.8 %collective-permute-start.18 = (f32[3,32,256]{2,1,0:T(8,128)S(1)}, f32[3,32,256]{2,1,0:T(8,128)S(1)}, u32[]{:S(2)}, u32[]{:S(2)}) collective-permute-start(f32[3,32,256]{2,1,0:T(8,128)S(1)} %get-tuple-element.57), channel_id=1, source_target_pairs={{0,32},{8,40},{16,48},{24,56},{32,64},{40,72},{48,80},{56,88},{64,... | collective-permute-start | bytes 294920 | tf_op jit(solution)/shard_map/ppermute | solution.py:66
  251.7 8.3 %collective-permute-start.24 = (f32[4,32,256]{2,1,0:T(8,128)S(1)}, f32[4,32,256]{2,1,0:T(8,128)S(1)}, u32[]{:S(2)}, u32[]{:S(2)}) collective-permute-start(f32[4,32,256]{2,1,0:T(8,128)S(1)} %slice.54), channel_id=1, source_target_pairs={{0,48},{8,56},{16,40},{24,32},{32,80},{40,88},{48,72},{56,64},{64,... | collective-permute-start | bytes 393224 | tf_op jit(solution)/shard_map/ppermute | solution.py:66
  253.4 3.9 %collective-permute-start.23 = (f32[1,32,256]{2,1,0:T(8,128)S(1)}, f32[1,32,256]{2,1,0:T(8,128)S(1)}, u32[]{:S(2)}, u32[]{:S(2)}) collective-permute-start(f32[1,32,256]{2,1,0:T(8,128)S(1)} %get-tuple-element.51), channel_id=1, source_target_pairs={{0,96},{8,104},{16,112},{24,120},{32,0},{40,8},{48,16},{56,24},{64... | collective-permute-start | bytes 98312 | tf_op jit(solution)/shard_map/ppermute | solution.py:66
  254.7 5.3 %copy-start.12 = (f32[1,32,256]{2,1,0:T(8,128)}, f32[1,32,256]{2,1,0:T(8,128)S(1)}, u32[]{:S(2)}) copy-start(f32[1,32,256]{2,1,0:T(8,128)S(1)} %collective-permute-done.19.refs_3_) | copy-start | bytes 98308
  254.7 5.3 %collective-permute-start.22 = (f32[1,32,256]{2,1,0:T(8,128)S(1)}, f32[1,32,256]{2,1,0:T(8,128)S(1)}, u32[]{:S(2)}, u32[]{:S(2)}) collective-permute-start(f32[1,32,256]{2,1,0:T(8,128)S(1)} %get-tuple-element.52), channel_id=1, source_target_pairs={{0,32},{8,40},{16,48},{24,56},{32,64},{40,72},{48,80},{56,88},{64,... | collective-permute-start | bytes 98312 | tf_op jit(solution)/shard_map/ppermute | solution.py:66
  255.4 4.6 %copy-start.13 = (f32[1,32,256]{2,1,0:T(8,128)}, f32[1,32,256]{2,1,0:T(8,128)S(1)}, u32[]{:S(2)}) copy-start(f32[1,32,256]{2,1,0:T(8,128)S(1)} %collective-permute-done.17.refs_1_) | copy-start | bytes 98308
  255.4 4.6 %collective-permute-start.21 = (f32[1,32,256]{2,1,0:T(8,128)S(1)}, f32[1,32,256]{2,1,0:T(8,128)S(1)}, u32[]{:S(2)}, u32[]{:S(2)}) collective-permute-start(f32[1,32,256]{2,1,0:T(8,128)S(1)} %get-tuple-element.53), channel_id=1, source_target_pairs={{0,8},{8,0},{16,24},{24,16},{32,40},{40,32},{48,56},{56,48},{64,72... | collective-permute-start | bytes 98312 | tf_op jit(solution)/shard_map/ppermute | solution.py:66
  257.2 2.9 %copy-start.11 = (f32[3,32,256]{2,1,0:T(8,128)}, f32[3,32,256]{2,1,0:T(8,128)S(1)}, u32[]{:S(2)}) copy-start(f32[3,32,256]{2,1,0:T(8,128)S(1)} %collective-permute-done.18.refs_2_) | copy-start | bytes 294916
  257.3 2.8 %copy-start.14 = (f32[1,32,256]{2,1,0:T(8,128)}, f32[1,32,256]{2,1,0:T(8,128)S(1)}, u32[]{:S(2)}) copy-start(f32[1,32,256]{2,1,0:T(8,128)S(1)} %collective-permute-done.23.refs_7_) | copy-start | bytes 98308
  (3 other events, 1.9 us)
Sparse Core Ops, SparseCore 0:
  18.1 54.1 all-gather.2

commit v4 on v3

--- a/solution.py
+++ b/solution.py
@@ -11,10 +11,11 @@
 Y, ZL, CORES, X, ZH = 4, 2, 2, 4, 2
 X_GROUPS = [[x * ZH + zh for x in range(X)] for zh in range(ZH)]
 OWN, OTHER, BELOW, ABOVE, ACROSS = range(5)
-EARLY = [(OWN, OWN), (OWN, OTHER), (OWN, BELOW), (OTHER, BELOW),
-         (BELOW, OWN), (BELOW, OTHER), (BELOW, ABOVE), (ABOVE, BELOW)]
-LATE = [(OWN, ACROSS), (OTHER, ACROSS), (BELOW, ACROSS), (ABOVE, ACROSS),
-        (ACROSS, OWN), (ACROSS, OTHER), (ACROSS, BELOW), (ACROSS, ABOVE)]
+EARLY = [(OWN, OWN), (OWN, OTHER), (OWN, BELOW), (OTHER, BELOW), (BELOW, ABOVE)]
+LATE = [(OWN, ACROSS), (OTHER, ACROSS), (BELOW, ACROSS), (ABOVE, ACROSS)]
+EARLY_ROUTES = [(OWN, [0, 1, 2], []), (OTHER, [3], []), (BELOW, [4], [2, 3]), (ABOVE, [], [4])]
+LATE_ROUTES = [(OWN, [0], []), (OTHER, [1], []), (BELOW, [2], []), (ABOVE, [3], []),
+               (ACROSS, [], [0, 1, 2, 3])]
 
 
 def block_of(y, zl, core):
@@ -67,17 +68,15 @@
 
 
 def column_table():
-    table = np.zeros((len(places()), len(EARLY) + len(LATE)), np.int32)
-    slot = 0
-    for tiles in (EARLY, LATE):
-        for row in range(5):
-            for left, right in tiles:
-                if left != row:
-                    continue
-                for at in places():
-                    target = block_of(*RELATED[row](*at))
-                    table[target, slot] = block_of(*RELATED[right](*at))
-                slot += 1
+    straight, turned = [], []
+    for tiles, routes in ((EARLY, EARLY_ROUTES), (LATE, LATE_ROUTES)):
+        for target, as_is, to_turn in routes:
+            straight += [(target, tiles[k][1]) for k in as_is]
+            turned += [(target, tiles[k][0]) for k in to_turn]
+    table = np.zeros((len(places()), len(straight + turned)), np.int32)
+    for slot, (target, column) in enumerate(straight + turned):
+        for at in places():
+            table[block_of(*RELATED[target](*at)), slot] = block_of(*RELATED[column](*at))
     return table
 
 
@@ -138,80 +137,113 @@
     )(jnp.stack([place, half]), part, orbitals)
 
 
-def gram_kernel(count, more, left_of, right_of, *refs):
+def gram_kernel(pairs, chunks, more, left_of, right_of, *refs):
+    left_rows, right_rows = sides(pairs)
+    count = (1 + max(left_rows + right_rows)) * chunks
     blocks, refs = refs[:count], refs[count:]
     if more:
         so_far, refs = refs[0], refs[1:]
     out, lefts, rights = refs
     depth = blocks[0].shape[1]
-    chunks = count // lefts.shape[0]
-    step = pl.program_id(0)
-
-    @pl.when(step == 0)
-    def _():
-        for k, block in enumerate(blocks):
-            high, low = high_and_low(block[...])
-            at, first = k // chunks, k % chunks * 3
-            for ref, order in ((lefts, (high, high, low)), (rights, (high, low, high))):
+    for k, block in enumerate(blocks):
+        high, low = high_and_low(block[...])
+        row, first = k // chunks, k % chunks * 3
+        for ref, rows, order in (
+            (lefts, left_rows, (high, high, low)), (rights, right_rows, (high, low, high))
+        ):
+            if row in rows:
                 for piece, value in enumerate(order, first):
-                    ref[at, :, piece * depth : (piece + 1) * depth] = value
-
-    shares, together, part, width = out.shape
-    for k in range(together):
-        at = step * together + k
-        tile = dot(lefts[left_of[at]], rights[right_of[at]]).reshape(shares, part, width)
-        out[:, k] = so_far[:, k] + tile if more else tile
+                    ref[rows.index(row), :, piece * depth : (piece + 1) * depth] = value
+
+    shares, tiles, part, width = out.shape
+
+    @pl.loop(0, tiles)
+    def _(t):
+        tile = dot(lefts[left_of[t]], rights[right_of[t]]).reshape(shares, part, width)
+        out[:, t] = so_far[:, t] + tile if more else tile
+
+
+def sides(pairs):
+    return sorted({left for left, _ in pairs}), sorted({right for _, right in pairs})
 
 
 def gram(blocks, pairs, shares, so_far=None):
     rows, depth = blocks[0][0].shape
     chunks = len(blocks[0])
     flat = [chunk for block in blocks for chunk in block]
-    tiles, together = len(pairs), 2
+    tiles = len(pairs)
     more = so_far is not None
-    whole = pl.BlockSpec((rows, depth), lambda t, *s: (0, 0))
-    tile = pl.BlockSpec((shares, together, rows // shares, rows), lambda t, *s: (0, t, 0, 0))
-    shape = jax.ShapeDtypeStruct((shares, tiles, rows // shares, rows), jnp.float32)
-    order = np.array(pairs, np.int32)
+    left_rows, right_rows = sides(pairs)
+    inputs = flat + ([so_far] if more else [])
     return pl.pallas_call(
-        functools.partial(gram_kernel, len(flat), more),
-        grid_spec=pltpu.PrefetchScalarGridSpec(
-            num_scalar_prefetch=2,
-            grid=(tiles // together,),
-            in_specs=[whole] * len(flat) + [tile] * more,
-            out_specs=tile,
-            scratch_shapes=[pltpu.VMEM((len(blocks), rows, 3 * chunks * depth), jnp.bfloat16)] * 2,
-        ),
-        out_shape=shape,
-        input_output_aliases={2 + len(flat): 0} if more else {},
+        functools.partial(gram_kernel, pairs, chunks, more),
+        in_specs=[pl.BlockSpec(memory_space=pltpu.SMEM)] * 2
+        + [pl.BlockSpec(memory_space=pltpu.VMEM)] * len(inputs),
+        out_specs=pl.BlockSpec(memory_space=pltpu.VMEM),
+        scratch_shapes=[
+            pltpu.VMEM((len(side), rows, 3 * chunks * depth), jnp.bfloat16)
+            for side in (left_rows, right_rows)
+        ],
+        out_shape=jax.ShapeDtypeStruct((shares, tiles, rows // shares, rows), jnp.float32),
         cost_estimate=pl.CostEstimate(
             flops=6 * tiles * rows * rows * chunks * depth, bytes_accessed=6 << 20, transcendentals=0
         ),
         name="gram",
-    )(order[:, 0], order[:, 1], *flat, *([so_far] if more else []))
-
-
-def assemble_kernel(table, *refs):
-    *groups, out = refs
-    slot = 0
-    for group in groups:
-        for k in range(group.shape[0]):
-            width = group.shape[2]
-            at = pl.multiple_of(table[slot] * width, width)
-            out[:, pl.ds(at, width)] = group[k]
-            slot += 1
-
-
-def assembled(table, groups, columns):
+    )(
+        np.array([left_rows.index(left) for left, _ in pairs], np.int32),
+        np.array([right_rows.index(right) for _, right in pairs], np.int32),
+        *inputs,
+    )
+
+
+def in_vmem(kernel, inputs, outputs, name, tables=()):
     return pl.pallas_call(
-        assemble_kernel,
-        in_specs=[pl.BlockSpec(memory_space=pltpu.SMEM)]
-        + [pl.BlockSpec(memory_space=pltpu.VMEM)] * len(groups),
-        out_specs=pl.BlockSpec(memory_space=pltpu.VMEM),
-        out_shape=jax.ShapeDtypeStruct((groups[0].shape[1], columns), jnp.float32),
+        kernel,
+        in_specs=[pl.BlockSpec(memory_space=pltpu.SMEM)] * len(tables)
+        + [pl.BlockSpec(memory_space=pltpu.VMEM)] * len(inputs),
+        out_specs=[pl.BlockSpec(memory_space=pltpu.VMEM)] * len(outputs),
+        out_shape=[jax.ShapeDtypeStruct(shape, jnp.float32) for shape in outputs],
         cost_estimate=pl.CostEstimate(flops=0, bytes_accessed=1 << 20, transcendentals=0),
-        name="assemble",
-    )(table, *groups)
+        name=name,
+    )(*tables, *inputs)
+
+
+def summed(moved, routes):
+    def kernel(moved_ref, *outs):
+        for out, (_, as_is, to_turn) in zip(outs, routes):
+            for k, tile in enumerate(as_is + to_turn):
+                out[k] = moved_ref[:, tile].sum(0)
+
+    shape = moved.shape[2:]
+    outputs = [(len(as_is + to_turn),) + shape for _, as_is, to_turn in routes]
+    return in_vmem(kernel, [moved], outputs, "sum")
+
+
+def turned(slabs, picks, shares):
+    part, width = slabs[0].shape[1:]
+
+    def kernel(*refs):
+        *ins, out = refs
+        rows = [ref[k] for ref, ks in zip(ins, picks) for k in ks]
+        rows += [jnp.zeros((part, width), jnp.float32)] * (width // part - len(rows))
+        out[...] = jnp.concatenate(rows, axis=0).T.reshape(out.shape)
+
+    return in_vmem(kernel, slabs, [(shares, width // shares, width)], "turn")[0]
+
+
+def assembled(table, slabs, picks, crossed, columns):
+    shares, part, width = crossed.shape
+
+    def kernel(table_ref, *refs):
+        *ins, crossed_ref, out = refs
+        pieces = [ref[k] for ref, ks in zip(ins, picks) for k in ks]
+        for k in range(columns // width - len(pieces)):
+            lanes = slice(k * part, (k + 1) * part)
+            pieces.append(jnp.concatenate([crossed_ref[s, :, lanes] for s in range(shares)], axis=1))
+        for slot, piece in enumerate(pieces):
+            out[:, pl.ds(pl.multiple_of(table_ref[slot] * width, width), width)] = piece
+
+    return in_vmem(kernel, [*slabs, crossed], [(part, columns)], "assemble", [table])[0]
 
 
 def together(*values):
@@ -234,6 +266,9 @@
 
     def to_other_half(value):
         return lax.ppermute(value, "col", swap_zh)
+
+    def over_col(tiles):
+        return lax.all_to_all(tiles, "col", split_axis=0, concat_axis=0, tiled=True)
 
     cut = aux - X
     ring = [coefficients.T]
@@ -275,24 +310,28 @@
     known_2 = [(own_2,), (other_2,), (below_2,), (above_2,)]
     early = gram(known_2, EARLY, shares, early)
     late = gram(known + [(across_0, across_1)], LATE, shares)
-    across_2, late = together(across_2, late)
+    across_2, late, early_moved = together(across_2, late, over_col(early))
     late = gram(known_2 + [(across_2,)], LATE, shares, late)
 
-    def sent_home(tiles, pairs):
-        summed = lax.all_to_all(tiles, "col", split_axis=0, concat_axis=0, tiled=True).sum(0)
-        groups = []
-        first = 0
-        for row, target_of in enumerate(RELATED):
-            count = sum(left == row for left, _ in pairs)
-            if count:
-                group = summed[first : first + count]
-                groups.append(delivered(group, target_of) if row else group)
-            first += count
-        return groups
-
-    groups = sent_home(early, EARLY) + sent_home(late, LATE)
+    def sent_home(moved, routes):
+        groups = summed(moved, routes)
+        return [
+            delivered(group, RELATED[target]) if target else group
+            for group, (target, _, _) in zip(groups, routes)
+        ]
+
+    late_moved, *early_slabs = together(over_col(late), *sent_home(early_moved, EARLY_ROUTES))
+    slabs = early_slabs + sent_home(late_moved, LATE_ROUTES)
+    routes = EARLY_ROUTES + LATE_ROUTES
+    straight = [range(len(as_is)) for _, as_is, _ in routes]
+    to_turn = [range(len(as_is), len(as_is + to_turn)) for _, as_is, to_turn in routes]
+
+    def chosen(picks):
+        return [slab for slab, ks in zip(slabs, picks) if len(ks)], [ks for ks in picks if len(ks)]
+
+    crossed = over_col(turned(*chosen(to_turn), shares))
     table = lax.dynamic_slice(jnp.asarray(column_table()), (blk, 0), (1, 16))[0]
-    return assembled(table, groups, rows * lax.axis_size("blk"))
+    return assembled(table, *chosen(straight), crossed, rows * lax.axis_size("blk"))
 
 
 def solution(mesh):

time: 271 us -> 259 us (0.956)
  waiting for transfers between devices: 111 us -> 93 us
  starting transfers between devices: 51.4 us -> 58.1 us
    all_to_all x2 -> x3, waiting for transfers between devices: 28.6 us -> 10.1 us  [over_col(): return lax.all_to_all(tiles, 'col', split_axis=0, concat_axis=0, tiled=True)]
    ppermute x7, waiting for transfers between devices: 2.83 us -> 9.08 us  [delivered(): return lax.ppermute(value, 'blk', route)]
    ppermute x12, waiting for transfers between devices: 33.9 us -> 28.4 us  [fetched(): return lax.ppermute(value, 'blk', route)]
    all_to_all x2 -> x3, starting transfers between devices: 12.4 us -> 16.6 us  [over_col(): return lax.all_to_all(tiles, 'col', split_axis=0, concat_axis=0, tiled=True)]
    unnamed x42 -> x48, local copies, waits for them, and re-layouts: 5.4 us -> 7.11 us
    pallas_call x5 -> x8, Pallas kernels: 33.9 us -> 33.2 us  [the longest x4 25.3 us: gram(): pl.pallas_call(functools.partial(gram_kernel, pairs, chunks, more), in_sp...]
  transfers between devices with their start and end apart: 30 -> 31, of which waited for: 9 -> 12; matrix products, arithmetic and copies ran while one was open for 6% -> 6% of each run, Pallas kernels for 23% -> 20%
where the time goes in v4:
time: 259 us; the launch traced here: 257 us
  waiting for transfers between devices  93 us (36%)
  Pallas kernels  69.9 us (27%)
  starting transfers between devices  58.1 us (22%)
  local copies, waits for them, and re-layouts  17.2 us (7%)
  between operations  13.6 us (5%)
  other arithmetic  5.61 us (2%)
    all_to_all x2, waiting for transfers between devices, over_x(): lax.all_to_all(part, 'col', split_axis=0, concat_axis=0, tiled=True, axis...  45.2 us
    pallas_call x6, Pallas kernels, transformed(): pl.pallas_call(transform_kernel, grid_spec=pltpu.PrefetchScalarGridSpec(n...  36.6 us
    ppermute x12, waiting for transfers between devices, fetched(): return lax.ppermute(value, 'blk', route)  28.4 us
    pallas_call x4, Pallas kernels, gram(): pl.pallas_call(functools.partial(gram_kernel, pairs, chunks, more), in_sp...  25.3 us
    all_to_all x3, starting transfers between devices, over_col(): return lax.all_to_all(tiles, 'col', split_axis=0, concat_axis=0, tiled=True)  16.6 us
    ppermute x12, starting transfers between devices, fetched(): return lax.ppermute(value, 'blk', route)  11.2 us
    all_to_all x3, waiting for transfers between devices, over_col(): return lax.all_to_all(tiles, 'col', split_axis=0, concat_axis=0, tiled=True)  10.1 us
    ppermute x7, waiting for transfers between devices, delivered(): return lax.ppermute(value, 'blk', route)  9.08 us
  transfers between devices with their start and end apart: 31, of which 12 were waited for; matrix products, arithmetic and copies ran while one was open for 6% of the time, Pallas kernels for 20%

profile of v4, /device:TPU:0, one launch (start us, length us, event | category | flops | bytes accessed | tf_op | source)
XLA Modules:
  0.0 257.4 jit_solution(10693908410846957088)
XLA Ops:
  6.5 1.6 collective-permute-start.2
  8.1 2.7 %collective-permute-start.1 = (f32[64,512]{1,0:T(8,128)}, f32[64,512]{1,0:T(8,128)S(1)}, u32[]{:S(2)}, u32[]{:S(2)}) collective-permute-start(f32[64,512]{1,0:T(8,128)} %bitcast.25), channel_id=1, source_target_pairs={{4,0},{5,1},{6,2},{7,3},{0,4},{1,5},{2,6},{3,7},{12,8},{13,9},{14,... | collective-permute-start | bytes 393224 | tf_op jit(solution)/shard_map/ppermute | solution.py:277
  10.8 1.4 collective-permute-start
  12.3 4.6 %slice.9 = f32[8,256,512]{2,1,0:T(8,128)} slice(f32[12,256,512]{2,1,0:T(8,128)} %bitcast.22), slice={[0:8], [0:256], [0:512]} | slice | bytes 8388608 | tf_op jit(solution)/shard_map/slice | solution.py:278
  17.9 4.9 %all-to-all-start = ((f32[8,256,512]{2,1,0:T(8,128)}), f32[8,256,512]{2,1,0:T(8,128)}, u32[]{:S(2)}, u32[]{:S(2)}) async-start(f32[8,256,512]{2,1,0:T(8,128)} %slice.9), calls=%async_computation | async-start | bytes 8388608 | tf_op jit(solution)/shard_map/all_to_all | solution.py:262
  22.8 3.1 %slice.8 = f32[4,256,512]{2,1,0:T(8,128)} slice(f32[12,256,512]{2,1,0:T(8,128)} %bitcast.23), slice={[8:12], [0:256], [0:512]} | slice | bytes 4194304 | tf_op jit(solution)/shard_map/slice | solution.py:282
  25.9 45.2 %all-to-all-done = f32[8,256,512]{2,1,0:T(8,128)} async-done(((f32[8,256,512]{2,1,0:T(8,128)}), f32[8,256,512]{2,1,0:T(8,128)}, u32[]{:S(2)}, u32[]{:S(2)}) %all-to-all-start) | async-done | bytes 4194336 | tf_op jit(solution)/shard_map/all_to_all | solution.py:262
  71.1 3.6 %all-to-all-start.1 = ((f32[4,256,512]{2,1,0:T(8,128)}), f32[4,256,512]{2,1,0:T(8,128)S(1)}, u32[]{:S(2)}, u32[]{:S(2)}) async-start(f32[4,256,512]{2,1,0:T(8,128)} %slice.8), calls=%async_computation.1 | async-start | bytes 4194304 | tf_op jit(solution)/shard_map/all_to_all | solution.py:262
  75.3 6.1 %transform.7 = f32[256,512]{1,0:T(8,128)} custom-call(s32[2]{0:T(128)} %pad_add_fusion.1.place, f32[4,2,256,512]{3,2,1,0:T(8,128)} %bitcast.5.part, f32[16,4,64,512]{3,2,1,0:T(8,128)} %bitcast.14), custom_call_target="tpu_custom_call" | custom-call | flops 1610612736 | bytes 8388608 | tf_op jit(solution)/shard_map/transform/pallas_call | solution.py:120
  81.4 3.9 %collective-permute-start.3 = (f32[256,512]{1,0:T(8,128)}, f32[256,512]{1,0:T(8,128)}, u32[]{:S(2)}, u32[]{:S(2)}) collective-permute-start(f32[256,512]{1,0:T(8,128)} %transform.7), channel_id=1, source_target_pairs={{1,0},{0,1},{3,2},{2,3},{5,4},{4,5},{7,6},{6,7},{9,8},{8,9},{11,10... | collective-permute-start | bytes 1572872 | tf_op jit(solution)/shard_map/ppermute | solution.py:268
  85.9 6.1 %transform.9 = f32[256,512]{1,0:T(8,128)} custom-call(s32[2]{0:T(128)} %pad_add_fusion.1.place, f32[4,2,256,512]{3,2,1,0:T(8,128)} %bitcast.5.part, f32[16,4,64,512]{3,2,1,0:T(8,128)} %bitcast.15), custom_call_target="tpu_custom_call" | custom-call | flops 1610612736 | bytes 8388608 | tf_op jit(solution)/shard_map/transform/pallas_call | solution.py:120
  92.1 6.1 %transform.6 = f32[256,512]{1,0:T(8,128)} custom-call(s32[2]{0:T(128)} %pad_add_fusion.place, f32[4,2,256,512]{3,2,1,0:T(8,128)} %bitcast.5.part, f32[16,4,64,512]{3,2,1,0:T(8,128)} %bitcast.16), custom_call_target="tpu_custom_call" | custom-call | flops 1610612736 | bytes 8388608 | tf_op jit(solution)/shard_map/transform/pallas_call | solution.py:120
  98.2 1.3 add.19.refs_0_
  99.4 1.7 collective-permute-start.6
  101.1 1.7 collective-permute-start.5
  102.8 1.3 copy-done
  104.1 6.2 %transform.11 = f32[256,512]{1,0:T(8,128)} custom-call(s32[2]{0:T(128)} %pad_add_fusion.1.place, f32[4,1,256,512]{3,2,1,0:T(8,128)} %bitcast.20, f32[16,4,64,512]{3,2,1,0:T(8,128)} %bitcast.17), custom_call_target="tpu_custom_call" | custom-call | flops 1610612736 | bytes 8388608 | tf_op jit(solution)/shard_map/transform/pallas_call | solution.py:120
  110.2 3.8 %collective-permute-start.12 = (f32[256,512]{1,0:T(8,128)}, f32[256,512]{1,0:T(8,128)S(1)}, u32[]{:S(2)}, u32[]{:S(2)}) collective-permute-start(f32[256,512]{1,0:T(8,128)} %transform.11), channel_id=1, source_target_pairs={{1,0},{0,1},{3,2},{2,3},{5,4},{4,5},{7,6},{6,7},{9,8},{8,9},{11,10... | collective-permute-start | bytes 1572872 | tf_op jit(solution)/shard_map/ppermute | solution.py:268
  114.0 6.1 %transform.8 = f32[256,512]{1,0:T(8,128)} custom-call(s32[2]{0:T(128)} %pad_add_fusion.place, f32[4,2,256,512]{3,2,1,0:T(8,128)} %bitcast.5.part, f32[16,4,64,512]{3,2,1,0:T(8,128)} %bitcast.18), custom_call_target="tpu_custom_call" | custom-call | flops 1610612736 | bytes 8388608 | tf_op jit(solution)/shard_map/transform/pallas_call | solution.py:120
  120.1 1.1 add.20.refs_1_
  122.6 2.9 %collective-permute-start.9 = (f32[256,512]{1,0:T(8,128)S(1)}, f32[256,512]{1,0:T(8,128)}, u32[]{:S(2)}, u32[]{:S(2)}) collective-permute-start(f32[256,512]{1,0:T(8,128)S(1)} %add.20.refs_1_), channel_id=1, source_target_pairs={{32,0},{40,8},{48,16},{56,24},{64,32},{72,40},{80,48},{88,56},{96,... | collective-permute-start | bytes 1572872 | tf_op jit(solution)/shard_map/ppermute | solution.py:62
  125.4 6.1 %transform.10 = f32[256,512]{1,0:T(8,128)} custom-call(s32[2]{0:T(128)} %pad_add_fusion.place, f32[4,1,256,512]{3,2,1,0:T(8,128)} %bitcast.21, f32[16,4,64,512]{3,2,1,0:T(8,128)} %bitcast.19), custom_call_target="tpu_custom_call" | custom-call | flops 1610612736 | bytes 8388608 | tf_op jit(solution)/shard_map/transform/pallas_call | solution.py:120
  131.5 1.1 add.21.refs_0_
  132.7 6.1 %collective-permute-done.11.refs_8_ = f32[256,512]{1,0:T(8,128)S(1)} collective-permute-done((f32[256,512]{1,0:T(8,128)}, f32[256,512]{1,0:T(8,128)S(1)}, u32[]{:S(2)}, u32[]{:S(2)}) %collective-permute-start.11) | collective-permute-done | bytes 524320 | tf_op jit(solution)/shard_map/ppermute | solution.py:62
  140.4 2.9 %collective-permute-start.14 = (f32[256,512]{1,0:T(8,128)S(1)}, f32[256,512]{1,0:T(8,128)S(1)}, u32[]{:S(2)}, u32[]{:S(2)}) collective-permute-start(f32[256,512]{1,0:T(8,128)S(1)} %add.21.refs_0_), channel_id=1, source_target_pairs={{32,0},{40,8},{48,16},{56,24},{64,32},{72,40},{80,48},{88,56},{96,... | collective-permute-start | bytes 1572872 | tf_op jit(solution)/shard_map/ppermute | solution.py:62
  143.3 7.2 %gram.4.refs_4_ = f32[8,5,32,256]{3,2,1,0:T(8,128)} custom-call(s32[5]{0:T(128)} %constant.47.clone.left_of, s32[5]{0:T(128)} %constant.48.clone.right_of, f32[256,512]{1,0:T(8,128)} %copy-done.8, f32[256,512]{1,0:T(8,128)} %copy-done.9, f32[256,512]{1,0:T(8,128)} %collective-permute-done.4.refs_2_, f32[256,512]{1,0:T(8,128)} %copy-done.14, ...), custom_call_target="tpu_custom_call" | custom-call | flops 2013265920 | bytes 6291456 | tf_op jit(solution)/shard_map/gram/pallas_call | solution.py:178
  150.5 2.9 %collective-permute-done.16.refs_9_ = f32[256,512]{1,0:T(8,128)S(1)} collective-permute-done((f32[256,512]{1,0:T(8,128)}, f32[256,512]{1,0:T(8,128)S(1)}, u32[]{:S(2)}, u32[]{:S(2)}) %collective-permute-start.16) | collective-permute-done | bytes 524320 | tf_op jit(solution)/shard_map/ppermute | solution.py:62
  153.4 2.0 collective-permute-done.15.refs_3_
  157.2 5.5 %gram.6 = f32[8,5,32,256]{3,2,1,0:T(8,128)} custom-call(s32[5]{0:T(128)} %constant.47.clone.left_of, s32[5]{0:T(128)} %constant.48.clone.right_of, f32[256,512]{1,0:T(8,128)} %copy-done.2, f32[256,512]{1,0:T(8,128)} %copy-done.7, f32[256,512]{1,0:T(8,128)} %copy-done.5, f32[256,512]{1,0:T(8,128)} %copy-done.4, f32[8,5,32,256]{3,2,1,0:T(8,128)} %gram.4.refs_4_), custom_call_target="tpu_custom_call" | custom-call | flops 1006632960 | bytes 6291456 | tf_op jit(solution)/shard_map/gram/pallas_call | solution.py:178
  162.7 4.9 %all-to-all-start.2 = ((f32[8,5,32,256]{3,2,1,0:T(8,128)}), f32[8,5,32,256]{3,2,1,0:T(8,128)S(1)}, u32[]{:S(2)}, u32[]{:S(2)}) async-start(f32[8,5,32,256]{3,2,1,0:T(8,128)} %gram.6), calls=%async_computation.2 | async-start | bytes 2621440 | tf_op jit(solution)/shard_map/all_to_all | solution.py:271
  168.8 6.9 %gram.5.refs_5_ = f32[8,4,32,256]{3,2,1,0:T(8,128)} custom-call(s32[4]{0:T(128)} %call_exported.2.left_of, s32[4]{0:T(128)} %call_exported.8.right_of, f32[256,512]{1,0:T(8,128)} %copy-done.8, f32[256,512]{1,0:T(8,128)} %copy-done.9, f32[256,512]{1,0:T(8,128)} %collective-permute-done.4.refs_2_, f32[256,512]{1,0:T(8,128)} %copy-done.14, ...), custom_call_target="tpu_custom_call" | custom-call | flops 1610612736 | bytes 6291456 | tf_op jit(solution)/shard_map/gram/pallas_call | solution.py:178
  175.8 17.3 %collective-permute-done.17.refs_4_ = f32[256,512]{1,0:T(8,128)S(1)} collective-permute-done((f32[256,512]{1,0:T(8,128)S(1)}, f32[256,512]{1,0:T(8,128)S(1)}, u32[]{:S(2)}, u32[]{:S(2)}) %collective-permute-start.17) | collective-permute-done | bytes 524320 | tf_op jit(solution)/shard_map/ppermute | solution.py:62
  193.9 5.6 %gram.7 = f32[8,4,32,256]{3,2,1,0:T(8,128)} custom-call(s32[4]{0:T(128)} %call_exported.2.left_of, s32[4]{0:T(128)} %call_exported.8.right_of, f32[256,512]{1,0:T(8,128)} %copy-done.2, f32[256,512]{1,0:T(8,128)} %copy-done.7, f32[256,512]{1,0:T(8,128)} %copy-done.5, f32[256,512]{1,0:T(8,128)} %copy-done.4, f32[256,512]{1,0:T(8,128)} %copy-done.11, ...), custom_call_target="tpu_custom_call" | custom-call | flops 805306368 | bytes 6291456 | tf_op jit(solution)/shard_map/gram/pallas_call | solution.py:178
  199.5 7.5 %all-to-all-start.3 = ((f32[8,4,32,256]{3,2,1,0:T(8,128)}), f32[8,4,32,256]{3,2,1,0:T(8,128)S(1)}, u32[]{:S(2)}, u32[]{:S(2)}) async-start(f32[8,4,32,256]{3,2,1,0:T(8,128)} %gram.7), calls=%async_computation.3 | async-start | bytes 2097152 | tf_op jit(solution)/shard_map/all_to_all | solution.py:271
  207.0 2.1 sum.2
  209.9 2.4 collective-permute-start.20
  212.3 1.9 collective-permute-done.20.refs_1_
  215.1 7.1 %all-to-all-done.3.moved_ref = f32[8,4,32,256]{3,2,1,0:T(8,128)S(1)} async-done(((f32[8,4,32,256]{3,2,1,0:T(8,128)}), f32[8,4,32,256]{3,2,1,0:T(8,128)S(1)}, u32[]{:S(2)}, u32[]{:S(2)}) %all-to-all-start.3) | async-done | bytes 1048608 | tf_op jit(solution)/shard_map/all_to_all | solution.py:271
  223.3 2.0 sum.3
  225.2 1.9 collective-permute-start.24
  227.1 5.4 %collective-permute-done.24.refs_2_ = f32[4,32,256]{2,1,0:T(8,128)S(1)} collective-permute-done((f32[4,32,256]{2,1,0:T(8,128)}, f32[4,32,256]{2,1,0:T(8,128)S(1)}, u32[]{:S(2)}, u32[]{:S(2)}) %collective-permute-start.24) | collective-permute-done | bytes 131104 | tf_op jit(solution)/shard_map/ppermute | solution.py:67
  233.2 1.8 turn.1
  235.0 4.2 %all-to-all-start.4 = ((f32[8,32,256]{2,1,0:T(8,128)}), f32[8,32,256]{2,1,0:T(8,128)S(1)}, u32[]{:S(2)}, u32[]{:S(2)}) async-start(f32[8,32,256]{2,1,0:T(8,128)} %turn.1), calls=%async_computation.4 | async-start | bytes 524288 | tf_op jit(solution)/shard_map/all_to_all | solution.py:271
  239.2 1.1 collective-permute-start.22
  240.3 2.2 collective-permute-start.23
  242.5 1.2 dynamic-slice_bitcast_fusion.table_ref
  244.6 3.0 %all-to-all-done.4.refs_7_ = f32[8,32,256]{2,1,0:T(8,128)S(1)} async-done(((f32[8,32,256]{2,1,0:T(8,128)}), f32[8,32,256]{2,1,0:T(8,128)S(1)}, u32[]{:S(2)}, u32[]{:S(2)}) %all-to-all-start.4) | async-done | bytes 262176 | tf_op jit(solution)/shard_map/all_to_all | solution.py:271
  248.3 2.2 assemble.1
  (88 shorter events, 14.0 us)
Async XLA Ops:
  6.5 68.8 %all-gather.3.cloned.1.call-start = ((), (), s32[]{:S(2)}) async-start(), calls=%async_computation.5 | async-start | bytes 8912896 | tf_op jit(solution)/shard_map/all_gather | solution.py:281
  6.5 10.3 %collective-permute-start.2 = (f32[64,512]{1,0:T(8,128)}, f32[64,512]{1,0:T(8,128)S(1)}, u32[]{:S(2)}, u32[]{:S(2)}) collective-permute-start(f32[64,512]{1,0:T(8,128)} %bitcast.24), channel_id=1, source_target_pairs={{6,0},{7,1},{0,2},{1,3},{2,4},{3,5},{4,6},{5,7},{14,8},{15,9},{8,1... | collective-permute-start | bytes 393224 | tf_op jit(solution)/shard_map/ppermute | solution.py:277
  8.1 9.0 %collective-permute-start.1 = (f32[64,512]{1,0:T(8,128)}, f32[64,512]{1,0:T(8,128)S(1)}, u32[]{:S(2)}, u32[]{:S(2)}) collective-permute-start(f32[64,512]{1,0:T(8,128)} %bitcast.25), channel_id=1, source_target_pairs={{4,0},{5,1},{6,2},{7,3},{0,4},{1,5},{2,6},{3,7},{12,8},{13,9},{14,... | collective-permute-start | bytes 393224 | tf_op jit(solution)/shard_map/ppermute | solution.py:277
  10.8 6.2 %collective-permute-start = (f32[64,512]{1,0:T(8,128)}, f32[64,512]{1,0:T(8,128)S(1)}, u32[]{:S(2)}, u32[]{:S(2)}) collective-permute-start(f32[64,512]{1,0:T(8,128)} %bitcast.26), channel_id=1, source_target_pairs={{2,0},{3,1},{4,2},{5,3},{6,4},{7,5},{0,6},{1,7},{10,8},{11,9},{12,... | collective-permute-start | bytes 393224 | tf_op jit(solution)/shard_map/ppermute | solution.py:277
  12.3 4.8 %copy-start.18 = (f32[512,64]{0,1:T(8,128)S(1)}, f32[512,64]{0,1:T(8,128)}, u32[]{:S(2)}) copy-start(f32[512,64]{0,1:T(8,128)} %param.12) | copy-start | bytes 393220
  17.9 53.1 %all-to-all-start = ((f32[8,256,512]{2,1,0:T(8,128)}), f32[8,256,512]{2,1,0:T(8,128)}, u32[]{:S(2)}, u32[]{:S(2)}) async-start(f32[8,256,512]{2,1,0:T(8,128)} %slice.9), calls=%async_computation | async-start | bytes 8388608 | tf_op jit(solution)/shard_map/all_to_all | solution.py:262
  71.1 31.7 %all-to-all-start.1 = ((f32[4,256,512]{2,1,0:T(8,128)}), f32[4,256,512]{2,1,0:T(8,128)S(1)}, u32[]{:S(2)}, u32[]{:S(2)}) async-start(f32[4,256,512]{2,1,0:T(8,128)} %slice.8), calls=%async_computation.1 | async-start | bytes 4194304 | tf_op jit(solution)/shard_map/all_to_all | solution.py:262
  81.4 16.8 %collective-permute-start.3 = (f32[256,512]{1,0:T(8,128)}, f32[256,512]{1,0:T(8,128)}, u32[]{:S(2)}, u32[]{:S(2)}) collective-permute-start(f32[256,512]{1,0:T(8,128)} %transform.7), channel_id=1, source_target_pairs={{1,0},{0,1},{3,2},{2,3},{5,4},{4,5},{7,6},{6,7},{9,8},{8,9},{11,10... | collective-permute-start | bytes 1572872 | tf_op jit(solution)/shard_map/ppermute | solution.py:268
  92.1 28.1 %collective-permute-start.7 = (f32[256,512]{1,0:T(8,128)}, f32[256,512]{1,0:T(8,128)S(1)}, u32[]{:S(2)}, u32[]{:S(2)}) collective-permute-start(f32[256,512]{1,0:T(8,128)} %transform.9), channel_id=1, source_target_pairs={{1,0},{0,1},{3,2},{2,3},{5,4},{4,5},{7,6},{6,7},{9,8},{8,9},{11,10... | collective-permute-start | bytes 1572872 | tf_op jit(solution)/shard_map/ppermute | solution.py:268
  99.4 20.7 %copy-start.8 = (f32[256,512]{1,0:T(8,128)}, f32[256,512]{1,0:T(8,128)S(1)}, u32[]{:S(2)}) copy-start(f32[256,512]{1,0:T(8,128)S(1)} %add.19.refs_0_) | copy-start | bytes 1572868
  99.4 21.8 %collective-permute-start.6 = (f32[256,512]{1,0:T(8,128)S(1)}, f32[256,512]{1,0:T(8,128)}, u32[]{:S(2)}, u32[]{:S(2)}) collective-permute-start(f32[256,512]{1,0:T(8,128)S(1)} %add.19.refs_0_), channel_id=1, source_target_pairs={{96,0},{104,8},{112,16},{120,24},{0,32},{8,40},{16,48},{24,56},{40... | collective-permute-start | bytes 1572872 | tf_op jit(solution)/shard_map/ppermute | solution.py:62
  101.1 20.2 %collective-permute-start.5 = (f32[256,512]{1,0:T(8,128)S(1)}, f32[256,512]{1,0:T(8,128)}, u32[]{:S(2)}, u32[]{:S(2)}) collective-permute-start(f32[256,512]{1,0:T(8,128)S(1)} %add.19.refs_0_), channel_id=1, source_target_pairs={{32,0},{40,8},{48,16},{56,24},{64,32},{72,40},{80,48},{88,56},{96,... | collective-permute-start | bytes 1572872 | tf_op jit(solution)/shard_map/ppermute | solution.py:62
  102.8 18.5 %collective-permute-start.4 = (f32[256,512]{1,0:T(8,128)S(1)}, f32[256,512]{1,0:T(8,128)}, u32[]{:S(2)}, u32[]{:S(2)}) collective-permute-start(f32[256,512]{1,0:T(8,128)S(1)} %add.19.refs_0_), channel_id=1, source_target_pairs={{8,0},{0,8},{24,16},{16,24},{40,32},{32,40},{56,48},{48,56},{72,64... | collective-permute-start | bytes 1572872 | tf_op jit(solution)/shard_map/ppermute | solution.py:62
  102.8 1.3 copy-start
  110.2 21.3 %collective-permute-start.12 = (f32[256,512]{1,0:T(8,128)}, f32[256,512]{1,0:T(8,128)S(1)}, u32[]{:S(2)}, u32[]{:S(2)}) collective-permute-start(f32[256,512]{1,0:T(8,128)} %transform.11), channel_id=1, source_target_pairs={{1,0},{0,1},{3,2},{2,3},{5,4},{4,5},{7,6},{6,7},{9,8},{8,9},{11,10... | collective-permute-start | bytes 1572872 | tf_op jit(solution)/shard_map/ppermute | solution.py:268
  121.2 10.3 %copy-start.9 = (f32[256,512]{1,0:T(8,128)}, f32[256,512]{1,0:T(8,128)S(1)}, u32[]{:S(2)}) copy-start(f32[256,512]{1,0:T(8,128)S(1)} %add.20.refs_1_) | copy-start | bytes 1572868
  121.3 17.5 %collective-permute-start.11 = (f32[256,512]{1,0:T(8,128)}, f32[256,512]{1,0:T(8,128)S(1)}, u32[]{:S(2)}, u32[]{:S(2)}) collective-permute-start(f32[256,512]{1,0:T(8,128)} %collective-permute-done.5.refs_4_), channel_id=1, source_target_pairs={{16,0},{24,8},{8,16},{0,24},{48,32},{56,40},{40,48},{32,56},{88,64... | collective-permute-start | bytes 1572872 | tf_op jit(solution)/shard_map/ppermute | solution.py:62
  122.2 16.6 %collective-permute-start.10 = (f32[256,512]{1,0:T(8,128)S(1)}, f32[256,512]{1,0:T(8,128)S(1)}, u32[]{:S(2)}, u32[]{:S(2)}) collective-permute-start(f32[256,512]{1,0:T(8,128)S(1)} %add.20.refs_1_), channel_id=1, source_target_pairs={{96,0},{104,8},{112,16},{120,24},{0,32},{8,40},{16,48},{24,56},{40... | collective-permute-start | bytes 1572872 | tf_op jit(solution)/shard_map/ppermute | solution.py:62
  122.6 16.2 %collective-permute-start.9 = (f32[256,512]{1,0:T(8,128)S(1)}, f32[256,512]{1,0:T(8,128)}, u32[]{:S(2)}, u32[]{:S(2)}) collective-permute-start(f32[256,512]{1,0:T(8,128)S(1)} %add.20.refs_1_), channel_id=1, source_target_pairs={{32,0},{40,8},{48,16},{56,24},{64,32},{72,40},{80,48},{88,56},{96,... | collective-permute-start | bytes 1572872 | tf_op jit(solution)/shard_map/ppermute | solution.py:62
  125.4 13.4 %collective-permute-start.8 = (f32[256,512]{1,0:T(8,128)S(1)}, f32[256,512]{1,0:T(8,128)S(1)}, u32[]{:S(2)}, u32[]{:S(2)}) collective-permute-start(f32[256,512]{1,0:T(8,128)S(1)} %add.20.refs_1_), channel_id=1, source_target_pairs={{8,0},{0,8},{24,16},{16,24},{40,32},{32,40},{56,48},{48,56},{72,64... | collective-permute-start | bytes 1572872 | tf_op jit(solution)/shard_map/ppermute | solution.py:62
  132.7 17.8 %copy-start.2 = (f32[256,512]{1,0:T(8,128)}, f32[256,512]{1,0:T(8,128)S(1)}, u32[]{:S(2)}) copy-start(f32[256,512]{1,0:T(8,128)S(1)} %add.21.refs_0_) | copy-start | bytes 1572868
  138.8 1.2 copy-start.13
  139.6 13.8 %collective-permute-start.16 = (f32[256,512]{1,0:T(8,128)}, f32[256,512]{1,0:T(8,128)S(1)}, u32[]{:S(2)}, u32[]{:S(2)}) collective-permute-start(f32[256,512]{1,0:T(8,128)} %collective-permute-done.9.refs_5_), channel_id=1, source_target_pairs={{16,0},{24,8},{8,16},{0,24},{48,32},{56,40},{40,48},{32,56},{88,64... | collective-permute-start | bytes 1572872 | tf_op jit(solution)/shard_map/ppermute | solution.py:62
  140.0 15.3 %collective-permute-start.15 = (f32[256,512]{1,0:T(8,128)S(1)}, f32[256,512]{1,0:T(8,128)S(1)}, u32[]{:S(2)}, u32[]{:S(2)}) collective-permute-start(f32[256,512]{1,0:T(8,128)S(1)} %add.21.refs_0_), channel_id=1, source_target_pairs={{96,0},{104,8},{112,16},{120,24},{0,32},{8,40},{16,48},{24,56},{40... | collective-permute-start | bytes 1572872 | tf_op jit(solution)/shard_map/ppermute | solution.py:62
  140.4 15.0 %collective-permute-start.14 = (f32[256,512]{1,0:T(8,128)S(1)}, f32[256,512]{1,0:T(8,128)S(1)}, u32[]{:S(2)}, u32[]{:S(2)}) collective-permute-start(f32[256,512]{1,0:T(8,128)S(1)} %add.21.refs_0_), channel_id=1, source_target_pairs={{32,0},{40,8},{48,16},{56,24},{64,32},{72,40},{80,48},{88,56},{96,... | collective-permute-start | bytes 1572872 | tf_op jit(solution)/shard_map/ppermute | solution.py:62
  143.3 12.1 %collective-permute-start.13 = (f32[256,512]{1,0:T(8,128)S(1)}, f32[256,512]{1,0:T(8,128)S(1)}, u32[]{:S(2)}, u32[]{:S(2)}) collective-permute-start(f32[256,512]{1,0:T(8,128)S(1)} %add.21.refs_0_), channel_id=1, source_target_pairs={{8,0},{0,8},{24,16},{16,24},{40,32},{32,40},{56,48},{48,56},{72,64... | collective-permute-start | bytes 1572872 | tf_op jit(solution)/shard_map/ppermute | solution.py:62
  153.4 9.4 %copy-start.15 = (f32[256,512]{1,0:T(8,128)}, f32[256,512]{1,0:T(8,128)S(1)}, u32[]{:S(2)}) copy-start(f32[256,512]{1,0:T(8,128)S(1)} %collective-permute-done.16.refs_9_) | copy-start | bytes 1572868
  155.4 1.0 copy-start.5
  162.7 4.9 %copy-start.6 = (f32[256,512]{1,0:T(8,128)S(1)}, f32[256,512]{1,0:T(8,128)}, u32[]{:S(2)}) copy-start(f32[256,512]{1,0:T(8,128)} %copy-done.5) | copy-start | bytes 1572868
  162.7 30.4 %all-to-all-start.2 = ((f32[8,5,32,256]{3,2,1,0:T(8,128)}), f32[8,5,32,256]{3,2,1,0:T(8,128)S(1)}, u32[]{:S(2)}, u32[]{:S(2)}) async-start(f32[8,5,32,256]{3,2,1,0:T(8,128)} %gram.6), calls=%async_computation.2 | async-start | bytes 2621440 | tf_op jit(solution)/shard_map/all_to_all | solution.py:271
  167.6 25.5 %collective-permute-start.17 = (f32[256,512]{1,0:T(8,128)S(1)}, f32[256,512]{1,0:T(8,128)S(1)}, u32[]{:S(2)}, u32[]{:S(2)}) collective-permute-start(f32[256,512]{1,0:T(8,128)S(1)} %copy-done.6), channel_id=1, source_target_pairs={{16,0},{24,8},{8,16},{0,24},{48,32},{56,40},{40,48},{32,56},{88,64... | collective-permute-start | bytes 1572872 | tf_op jit(solution)/shard_map/ppermute | solution.py:62
  193.9 5.6 %copy-start.1 = (f32[8,5,32,256]{3,2,1,0:T(8,128)}, f32[8,5,32,256]{3,2,1,0:T(8,128)S(1)}, u32[]{:S(2)}) copy-start(f32[8,5,32,256]{3,2,1,0:T(8,128)S(1)} %all-to-all-done.2.moved_ref) | copy-start | bytes 3932164
  199.5 22.7 %all-to-all-start.3 = ((f32[8,4,32,256]{3,2,1,0:T(8,128)}), f32[8,4,32,256]{3,2,1,0:T(8,128)S(1)}, u32[]{:S(2)}, u32[]{:S(2)}) async-start(f32[8,4,32,256]{3,2,1,0:T(8,128)} %gram.7), calls=%async_computation.3 | async-start | bytes 2097152 | tf_op jit(solution)/shard_map/all_to_all | solution.py:271
  209.1 6.0 %collective-permute-start.19 = (f32[3,32,256]{2,1,0:T(8,128)}, f32[3,32,256]{2,1,0:T(8,128)S(1)}, u32[]{:S(2)}, u32[]{:S(2)}) collective-permute-start(f32[3,32,256]{2,1,0:T(8,128)} %get-tuple-element.69), channel_id=1, source_target_pairs={{0,32},{8,40},{16,48},{24,56},{32,64},{40,72},{48,80},{56,88},{64,... | collective-permute-start | bytes 294920 | tf_op jit(solution)/shard_map/ppermute | solution.py:67
  209.9 2.4 collective-permute-start.18
  209.9 4.3 %collective-permute-start.20 = (f32[1,32,256]{2,1,0:T(8,128)}, f32[1,32,256]{2,1,0:T(8,128)S(1)}, u32[]{:S(2)}, u32[]{:S(2)}) collective-permute-start(f32[1,32,256]{2,1,0:T(8,128)} %get-tuple-element.70), channel_id=1, source_target_pairs={{0,96},{8,104},{16,112},{24,120},{32,0},{40,8},{48,16},{56,24},{64... | collective-permute-start | bytes 98312 | tf_op jit(solution)/shard_map/ppermute | solution.py:67
  212.3 35.3 %copy-start.19 = (f32[1,32,256]{2,1,0:T(8,128)}, f32[1,32,256]{2,1,0:T(8,128)S(1)}, u32[]{:S(2)}) copy-start(f32[1,32,256]{2,1,0:T(8,128)S(1)} %collective-permute-done.18.refs_1_) | copy-start | bytes 98308
  214.3 18.3 %copy-start.21 = (f32[1,32,256]{2,1,0:T(8,128)}, f32[1,32,256]{2,1,0:T(8,128)S(1)}, u32[]{:S(2)}) copy-start(f32[1,32,256]{2,1,0:T(8,128)S(1)} %collective-permute-done.20.refs_1_) | copy-start | bytes 98308
  215.1 17.4 %copy-start.16 = (f32[3,32,256]{2,1,0:T(8,128)}, f32[3,32,256]{2,1,0:T(8,128)S(1)}, u32[]{:S(2)}) copy-start(f32[3,32,256]{2,1,0:T(8,128)S(1)} %collective-permute-done.19.refs_0_.refs_2_) | copy-start | bytes 294916
  222.2 1.0 copy-start.3
  225.2 7.3 %collective-permute-start.24 = (f32[4,32,256]{2,1,0:T(8,128)}, f32[4,32,256]{2,1,0:T(8,128)S(1)}, u32[]{:S(2)}, u32[]{:S(2)}) collective-permute-start(f32[4,32,256]{2,1,0:T(8,128)} %get-tuple-element.80), channel_id=1, source_target_pairs={{0,48},{8,56},{16,40},{24,32},{32,80},{40,88},{48,72},{56,64},{64,... | collective-permute-start | bytes 393224 | tf_op jit(solution)/shard_map/ppermute | solution.py:67
  235.0 12.6 %all-to-all-start.4 = ((f32[8,32,256]{2,1,0:T(8,128)}), f32[8,32,256]{2,1,0:T(8,128)S(1)}, u32[]{:S(2)}, u32[]{:S(2)}) async-start(f32[8,32,256]{2,1,0:T(8,128)} %turn.1), calls=%async_computation.4 | async-start | bytes 524288 | tf_op jit(solution)/shard_map/all_to_all | solution.py:271
  239.2 4.6 %collective-permute-start.21 = (f32[1,32,256]{2,1,0:T(8,128)}, f32[1,32,256]{2,1,0:T(8,128)S(1)}, u32[]{:S(2)}, u32[]{:S(2)}) collective-permute-start(f32[1,32,256]{2,1,0:T(8,128)} %get-tuple-element.76), channel_id=1, source_target_pairs={{0,8},{8,0},{16,24},{24,16},{32,40},{40,32},{48,56},{56,48},{64,72... | collective-permute-start | bytes 98312 | tf_op jit(solution)/shard_map/ppermute | solution.py:67
  239.2 5.4 %collective-permute-start.22 = (f32[1,32,256]{2,1,0:T(8,128)}, f32[1,32,256]{2,1,0:T(8,128)S(1)}, u32[]{:S(2)}, u32[]{:S(2)}) collective-permute-start(f32[1,32,256]{2,1,0:T(8,128)} %get-tuple-element.77), channel_id=1, source_target_pairs={{0,32},{8,40},{16,48},{24,56},{32,64},{40,72},{48,80},{56,88},{64,... | collective-permute-start | bytes 98312 | tf_op jit(solution)/shard_map/ppermute | solution.py:67
  240.3 4.3 %collective-permute-start.23 = (f32[1,32,256]{2,1,0:T(8,128)}, f32[1,32,256]{2,1,0:T(8,128)S(1)}, u32[]{:S(2)}, u32[]{:S(2)}) collective-permute-start(f32[1,32,256]{2,1,0:T(8,128)} %get-tuple-element.78), channel_id=1, source_target_pairs={{0,96},{8,104},{16,112},{24,120},{32,0},{40,8},{48,16},{56,24},{64... | collective-permute-start | bytes 98312 | tf_op jit(solution)/shard_map/ppermute | solution.py:67
  243.7 3.9 %copy-start.20 = (f32[1,32,256]{2,1,0:T(8,128)}, f32[1,32,256]{2,1,0:T(8,128)S(1)}, u32[]{:S(2)}) copy-start(f32[1,32,256]{2,1,0:T(8,128)S(1)} %collective-permute-done.21.refs_4_) | copy-start | bytes 98308
  244.6 3.0 %copy-start.22 = (f32[1,32,256]{2,1,0:T(8,128)}, f32[1,32,256]{2,1,0:T(8,128)S(1)}, u32[]{:S(2)}) copy-start(f32[1,32,256]{2,1,0:T(8,128)S(1)} %collective-permute-done.22.refs_5_) | copy-start | bytes 98308
  244.6 3.0 %copy-start.23 = (f32[1,32,256]{2,1,0:T(8,128)}, f32[1,32,256]{2,1,0:T(8,128)S(1)}, u32[]{:S(2)}) copy-start(f32[1,32,256]{2,1,0:T(8,128)S(1)} %collective-permute-done.23.refs_6_) | copy-start | bytes 98308
  (7 other events, 5.4 us)
Sparse Core Ops, SparseCore 0:
  18.1 54.1 all-gather.2

commit v5 on v4

--- a/solution.py
+++ b/solution.py
@@ -13,9 +13,8 @@
 OWN, OTHER, BELOW, ABOVE, ACROSS = range(5)
 EARLY = [(OWN, OWN), (OWN, OTHER), (OWN, BELOW), (OTHER, BELOW), (BELOW, ABOVE)]
 LATE = [(OWN, ACROSS), (OTHER, ACROSS), (BELOW, ACROSS), (ABOVE, ACROSS)]
-EARLY_ROUTES = [(OWN, [0, 1, 2], []), (OTHER, [3], []), (BELOW, [4], [2, 3]), (ABOVE, [], [4])]
-LATE_ROUTES = [(OWN, [0], []), (OTHER, [1], []), (BELOW, [2], []), (ABOVE, [3], []),
-               (ACROSS, [], [0, 1, 2, 3])]
+ROUTES = [(OWN, [0, 1, 2, 5], []), (OTHER, [3, 6], []), (BELOW, [4, 7], [2, 3]), (ABOVE, [8], [4]),
+          (ACROSS, [], [5, 6, 7, 8])]
 
 
 def block_of(y, zl, core):
@@ -68,11 +67,9 @@
 
 
 def column_table():
-    straight, turned = [], []
-    for tiles, routes in ((EARLY, EARLY_ROUTES), (LATE, LATE_ROUTES)):
-        for target, as_is, to_turn in routes:
-            straight += [(target, tiles[k][1]) for k in as_is]
-            turned += [(target, tiles[k][0]) for k in to_turn]
+    tiles = EARLY + LATE
+    straight = [(target, tiles[k][1]) for target, as_is, _ in ROUTES for k in as_is]
+    turned = [(target, tiles[k][0]) for target, _, to_turn in ROUTES for k in to_turn]
     table = np.zeros((len(places()), len(straight + turned)), np.int32)
     for slot, (target, column) in enumerate(straight + turned):
         for at in places():
@@ -131,18 +128,20 @@
         ),
         out_shape=jax.ShapeDtypeStruct((rows, steps * columns), jnp.float32),
         cost_estimate=pl.CostEstimate(
-            flops=6 * rows * X * width * steps * columns, bytes_accessed=8 << 20, transcendentals=0
+            flops=0, bytes_accessed=0, transcendentals=0
         ),
         name="transform",
     )(jnp.stack([place, half]), part, orbitals)
 
 
-def gram_kernel(pairs, chunks, more, left_of, right_of, *refs):
+def gram_kernel(pairs, chunks, more, ahead, left_of, right_of, *refs):
     left_rows, right_rows = sides(pairs)
     count = (1 + max(left_rows + right_rows)) * chunks
     blocks, refs = refs[:count], refs[count:]
     if more:
         so_far, refs = refs[0], refs[1:]
+    if ahead:
+        before, refs = refs[0], refs[1:]
     out, lefts, rights = refs
     depth = blocks[0].shape[1]
     for k, block in enumerate(blocks):
@@ -155,28 +154,31 @@
                 for piece, value in enumerate(order, first):
                     ref[rows.index(row), :, piece * depth : (piece + 1) * depth] = value
 
-    shares, tiles, part, width = out.shape
-
-    @pl.loop(0, tiles)
+    shares, _, part, width = out.shape
+    if ahead:
+        out[:, :ahead] = before[...]
+
+    @pl.loop(0, len(pairs))
     def _(t):
         tile = dot(lefts[left_of[t]], rights[right_of[t]]).reshape(shares, part, width)
-        out[:, t] = so_far[:, t] + tile if more else tile
+        out[:, ahead + t] = so_far[:, t] + tile if more else tile
 
 
 def sides(pairs):
     return sorted({left for left, _ in pairs}), sorted({right for _, right in pairs})
 
 
-def gram(blocks, pairs, shares, so_far=None):
+def gram(blocks, pairs, shares, so_far=None, before=None):
     rows, depth = blocks[0][0].shape
     chunks = len(blocks[0])
     flat = [chunk for block in blocks for chunk in block]
-    tiles = len(pairs)
     more = so_far is not None
+    ahead = 0 if before is None else before.shape[1]
+    tiles = ahead + len(pairs)
     left_rows, right_rows = sides(pairs)
-    inputs = flat + ([so_far] if more else [])
+    inputs = flat + ([so_far] if more else []) + ([before] if ahead else [])
     return pl.pallas_call(
-        functools.partial(gram_kernel, pairs, chunks, more),
+        functools.partial(gram_kernel, pairs, chunks, more, ahead),
         in_specs=[pl.BlockSpec(memory_space=pltpu.SMEM)] * 2
         + [pl.BlockSpec(memory_space=pltpu.VMEM)] * len(inputs),
         out_specs=pl.BlockSpec(memory_space=pltpu.VMEM),
@@ -186,7 +188,7 @@
         ],
         out_shape=jax.ShapeDtypeStruct((shares, tiles, rows // shares, rows), jnp.float32),
         cost_estimate=pl.CostEstimate(
-            flops=6 * tiles * rows * rows * chunks * depth, bytes_accessed=6 << 20, transcendentals=0
+            flops=0, bytes_accessed=0, transcendentals=0
         ),
         name="gram",
     )(
@@ -208,14 +210,14 @@
     )(*tables, *inputs)
 
 
-def summed(moved, routes):
+def summed(moved):
     def kernel(moved_ref, *outs):
-        for out, (_, as_is, to_turn) in zip(outs, routes):
+        for out, (_, as_is, to_turn) in zip(outs, ROUTES):
             for k, tile in enumerate(as_is + to_turn):
                 out[k] = moved_ref[:, tile].sum(0)
 
     shape = moved.shape[2:]
-    outputs = [(len(as_is + to_turn),) + shape for _, as_is, to_turn in routes]
+    outputs = [(len(as_is + to_turn),) + shape for _, as_is, to_turn in ROUTES]
     return in_vmem(kernel, [moved], outputs, "sum")
 
 
@@ -294,6 +296,7 @@
     arrived_0, arrived_1 = sent(first_part, 0), sent(first_part, 1)
     own_0 = kept(first_part, 0) + arrived_0
     own_1 = kept(first_part, 1) + arrived_1
+    own_1, last_part = together(own_1, last_part)
     other_0, below_0, above_0 = neighbours(own_0)
     arrived_2 = sent(last_part, 0)
     own_2 = kept(last_part, 0) + arrived_2
@@ -310,21 +313,15 @@
     known_2 = [(own_2,), (other_2,), (below_2,), (above_2,)]
     early = gram(known_2, EARLY, shares, early)
     late = gram(known + [(across_0, across_1)], LATE, shares)
-    across_2, late, early_moved = together(across_2, late, over_col(early))
-    late = gram(known_2 + [(across_2,)], LATE, shares, late)
-
-    def sent_home(moved, routes):
-        groups = summed(moved, routes)
-        return [
-            delivered(group, RELATED[target]) if target else group
-            for group, (target, _, _) in zip(groups, routes)
-        ]
-
-    late_moved, *early_slabs = together(over_col(late), *sent_home(early_moved, EARLY_ROUTES))
-    slabs = early_slabs + sent_home(late_moved, LATE_ROUTES)
-    routes = EARLY_ROUTES + LATE_ROUTES
-    straight = [range(len(as_is)) for _, as_is, _ in routes]
-    to_turn = [range(len(as_is), len(as_is + to_turn)) for _, as_is, to_turn in routes]
+    across_2, late, early = together(across_2, late, early)
+    tiles = gram(known_2 + [(across_2,)], LATE, shares, late, early)
+
+    slabs = [
+        delivered(slab, RELATED[target]) if target else slab
+        for slab, (target, _, _) in zip(summed(over_col(tiles)), ROUTES)
+    ]
+    straight = [range(len(as_is)) for _, as_is, _ in ROUTES]
+    to_turn = [range(len(as_is), len(as_is + to_turn)) for _, as_is, to_turn in ROUTES]
 
     def chosen(picks):
         return [slab for slab, ks in zip(slabs, picks) if len(ks)], [ks for ks in picks if len(ks)]

time: 259 us -> 257 us (level)
  blocking collectives: 0 us -> 36.2 us
  starting transfers between devices: 58.1 us -> 40.1 us
  waiting for transfers between devices: 93 us -> 76.7 us
    all_to_all x0 -> x1, blocking collectives: none -> 36.2 us  [over_col(): return lax.all_to_all(tiles, 'col', split_axis=0, concat_axis=0, tiled=True)]
    ppermute x12, waiting for transfers between devices: 28.4 us -> 15.3 us  [fetched(): return lax.ppermute(value, 'blk', route)]
    all_to_all x3 -> x1, starting transfers between devices: 16.6 us -> 3.78 us  [over_col(): return lax.all_to_all(tiles, 'col', split_axis=0, concat_axis=0, tiled=True)]
    ppermute x7 -> x4, starting transfers between devices: 8.41 us -> 3.24 us  [delivered(): return lax.ppermute(value, 'blk', route)]
    all_to_all x3 -> x1, waiting for transfers between devices: 10.1 us -> 6.97 us  [over_col(): return lax.all_to_all(tiles, 'col', split_axis=0, concat_axis=0, tiled=True)]
    ppermute x7 -> x4, waiting for transfers between devices: 9.08 us -> 6.22 us  [delivered(): return lax.ppermute(value, 'blk', route)]
    ppermute x3, waiting for transfers between devices: 0.01 us -> 2.85 us  [to_other_half(): return lax.ppermute(value, 'col', swap_zh)]
    unnamed x48 -> x34, local copies, waits for them, and re-layouts: 7.11 us -> 5.33 us
  transfers between devices with their start and end apart: 31 -> 26, of which waited for: 12 -> 11; matrix products, arithmetic and copies ran while one was open for 6% -> 6% of each run, Pallas kernels for 20% -> 22%
where the time goes in v5:
time: 257 us
  waiting for transfers between devices  76.7 us (30%)
  Pallas kernels  68.8 us (27%)
  starting transfers between devices  40.1 us (16%)
  blocking collectives  36.2 us (14%)
  local copies, waits for them, and re-layouts  15.4 us (6%)
  between operations  13.6 us (5%)
  other arithmetic  5.82 us (2%)
    all_to_all x2, waiting for transfers between devices, over_x(): lax.all_to_all(part, 'col', split_axis=0, concat_axis=0, tiled=True, axis...  45.2 us
    pallas_call x6, Pallas kernels, transformed(): pl.pallas_call(transform_kernel, grid_spec=pltpu.PrefetchScalarGridSpec(n...  36.6 us
    all_to_all x1, blocking collectives, over_col(): return lax.all_to_all(tiles, 'col', split_axis=0, concat_axis=0, tiled=True)  36.2 us
    pallas_call x4, Pallas kernels, gram(): pl.pallas_call(functools.partial(gram_kernel, pairs, chunks, more, ahead)...  25.7 us
    ppermute x12, waiting for transfers between devices, fetched(): return lax.ppermute(value, 'blk', route)  15.3 us
    ppermute x12, starting transfers between devices, fetched(): return lax.ppermute(value, 'blk', route)  11.2 us
    all_to_all x2, starting transfers between devices, over_x(): lax.all_to_all(part, 'col', split_axis=0, concat_axis=0, tiled=True, axis...  8.47 us
    ppermute x3, starting transfers between devices, to_other_half(): return lax.ppermute(value, 'col', swap_zh)  7.6 us
  transfers between devices with their start and end apart: 26, of which 11 were waited for; matrix products, arithmetic and copies ran while one was open for 6% of the time, Pallas kernels for 22%

profile of v5, /device:TPU:0, one launch (start us, length us, event | category | flops | bytes accessed | tf_op | source)
XLA Modules:
  0.0 256.6 jit_solution(11675446632310772259)
XLA Ops:
  6.5 1.6 collective-permute-start.2
  8.1 2.7 %collective-permute-start.1 = (f32[64,512]{1,0:T(8,128)}, f32[64,512]{1,0:T(8,128)S(1)}, u32[]{:S(2)}, u32[]{:S(2)}) collective-permute-start(f32[64,512]{1,0:T(8,128)} %bitcast.25), channel_id=1, source_target_pairs={{4,0},{5,1},{6,2},{7,3},{0,4},{1,5},{2,6},{3,7},{12,8},{13,9},{14,... | collective-permute-start | bytes 393224 | tf_op jit(solution)/shard_map/ppermute | solution.py:279
  10.8 1.4 collective-permute-start
  12.3 4.6 %slice.9 = f32[8,256,512]{2,1,0:T(8,128)} slice(f32[12,256,512]{2,1,0:T(8,128)} %bitcast.22), slice={[0:8], [0:256], [0:512]} | slice | bytes 8388608 | tf_op jit(solution)/shard_map/slice | solution.py:280
  17.1 0.8 pad_maximum_fusion
  17.9 4.9 %all-to-all-start = ((f32[8,256,512]{2,1,0:T(8,128)}), f32[8,256,512]{2,1,0:T(8,128)}, u32[]{:S(2)}, u32[]{:S(2)}) async-start(f32[8,256,512]{2,1,0:T(8,128)} %slice.9), calls=%async_computation | async-start | bytes 8388608 | tf_op jit(solution)/shard_map/all_to_all | solution.py:264
  22.8 3.1 %slice.8 = f32[4,256,512]{2,1,0:T(8,128)} slice(f32[12,256,512]{2,1,0:T(8,128)} %bitcast.23), slice={[8:12], [0:256], [0:512]} | slice | bytes 4194304 | tf_op jit(solution)/shard_map/slice | solution.py:284
  25.9 45.2 %all-to-all-done = f32[8,256,512]{2,1,0:T(8,128)} async-done(((f32[8,256,512]{2,1,0:T(8,128)}), f32[8,256,512]{2,1,0:T(8,128)}, u32[]{:S(2)}, u32[]{:S(2)}) %all-to-all-start) | async-done | bytes 4194336 | tf_op jit(solution)/shard_map/all_to_all | solution.py:264
  71.1 3.6 %all-to-all-start.1 = ((f32[4,256,512]{2,1,0:T(8,128)}), f32[4,256,512]{2,1,0:T(8,128)S(1)}, u32[]{:S(2)}, u32[]{:S(2)}) async-start(f32[4,256,512]{2,1,0:T(8,128)} %slice.8), calls=%async_computation.1 | async-start | bytes 4194304 | tf_op jit(solution)/shard_map/all_to_all | solution.py:264
  75.4 6.1 %transform.7 = f32[256,512]{1,0:T(8,128)} custom-call(s32[2]{0:T(128)} %pad_add_fusion.1.place, f32[4,2,256,512]{3,2,1,0:T(8,128)} %bitcast.5.part, f32[16,4,64,512]{3,2,1,0:T(8,128)} %bitcast.14), custom_call_target="tpu_custom_call" | custom-call | tf_op jit(solution)/shard_map/transform/pallas_call | solution.py:117
  81.5 3.9 %collective-permute-start.3 = (f32[256,512]{1,0:T(8,128)}, f32[256,512]{1,0:T(8,128)S(1)}, u32[]{:S(2)}, u32[]{:S(2)}) collective-permute-start(f32[256,512]{1,0:T(8,128)} %transform.7), channel_id=1, source_target_pairs={{1,0},{0,1},{3,2},{2,3},{5,4},{4,5},{7,6},{6,7},{9,8},{8,9},{11,10... | collective-permute-start | bytes 1572872 | tf_op jit(solution)/shard_map/ppermute | solution.py:270
  85.4 6.1 %transform.9 = f32[256,512]{1,0:T(8,128)} custom-call(s32[2]{0:T(128)} %pad_add_fusion.1.place, f32[4,2,256,512]{3,2,1,0:T(8,128)} %bitcast.5.part, f32[16,4,64,512]{3,2,1,0:T(8,128)} %bitcast.15), custom_call_target="tpu_custom_call" | custom-call | tf_op jit(solution)/shard_map/transform/pallas_call | solution.py:117
  92.1 6.1 %transform.6 = f32[256,512]{1,0:T(8,128)} custom-call(s32[2]{0:T(128)} %pad_add_fusion.place, f32[4,2,256,512]{3,2,1,0:T(8,128)} %bitcast.5.part, f32[16,4,64,512]{3,2,1,0:T(8,128)} %bitcast.16), custom_call_target="tpu_custom_call" | custom-call | tf_op jit(solution)/shard_map/transform/pallas_call | solution.py:117
  98.2 1.1 add.19.refs_0_
  99.3 1.7 collective-permute-start.6
  101.0 1.7 collective-permute-start.5
  102.7 6.1 %transform.8 = f32[256,512]{1,0:T(8,128)} custom-call(s32[2]{0:T(128)} %pad_add_fusion.place, f32[4,2,256,512]{3,2,1,0:T(8,128)} %bitcast.5.part, f32[16,4,64,512]{3,2,1,0:T(8,128)} %bitcast.17), custom_call_target="tpu_custom_call" | custom-call | tf_op jit(solution)/shard_map/transform/pallas_call | solution.py:117
  108.8 1.3 add.20.refs_1_
  110.1 1.4 copy-done
  111.5 6.1 %transform.11 = f32[256,512]{1,0:T(8,128)} custom-call(s32[2]{0:T(128)} %pad_add_fusion.1.place, f32[4,1,256,512]{3,2,1,0:T(8,128)} %bitcast.20, f32[16,4,64,512]{3,2,1,0:T(8,128)} %bitcast.18), custom_call_target="tpu_custom_call" | custom-call | tf_op jit(solution)/shard_map/transform/pallas_call | solution.py:117
  117.5 3.7 %collective-permute-start.12 = (f32[256,512]{1,0:T(8,128)}, f32[256,512]{1,0:T(8,128)}, u32[]{:S(2)}, u32[]{:S(2)}) collective-permute-start(f32[256,512]{1,0:T(8,128)} %transform.11), channel_id=1, source_target_pairs={{1,0},{0,1},{3,2},{2,3},{5,4},{4,5},{7,6},{6,7},{9,8},{8,9},{11,10... | collective-permute-start | bytes 1572872 | tf_op jit(solution)/shard_map/ppermute | solution.py:270
  121.3 0.9 collective-permute-start.11
  122.6 2.9 %collective-permute-start.9 = (f32[256,512]{1,0:T(8,128)S(1)}, f32[256,512]{1,0:T(8,128)S(1)}, u32[]{:S(2)}, u32[]{:S(2)}) collective-permute-start(f32[256,512]{1,0:T(8,128)S(1)} %add.20.refs_1_), channel_id=1, source_target_pairs={{32,0},{40,8},{48,16},{56,24},{64,32},{72,40},{80,48},{88,56},{96,... | collective-permute-start | bytes 1572872 | tf_op jit(solution)/shard_map/ppermute | solution.py:61
  125.4 6.1 %transform.10 = f32[256,512]{1,0:T(8,128)} custom-call(s32[2]{0:T(128)} %pad_add_fusion.place, f32[4,1,256,512]{3,2,1,0:T(8,128)} %bitcast.21, f32[16,4,64,512]{3,2,1,0:T(8,128)} %bitcast.19), custom_call_target="tpu_custom_call" | custom-call | tf_op jit(solution)/shard_map/transform/pallas_call | solution.py:117
  131.5 2.8 %collective-permute-done.12 = f32[256,512]{1,0:T(8,128)} collective-permute-done((f32[256,512]{1,0:T(8,128)}, f32[256,512]{1,0:T(8,128)}, u32[]{:S(2)}, u32[]{:S(2)}) %collective-permute-start.12) | collective-permute-done | bytes 524320 | tf_op jit(solution)/shard_map/ppermute | solution.py:270
  134.3 1.3 add.21.refs_0_
  135.6 10.4 %collective-permute-done.11.refs_8_ = f32[256,512]{1,0:T(8,128)S(1)} collective-permute-done((f32[256,512]{1,0:T(8,128)}, f32[256,512]{1,0:T(8,128)S(1)}, u32[]{:S(2)}, u32[]{:S(2)}) %collective-permute-start.11) | collective-permute-done | bytes 524320 | tf_op jit(solution)/shard_map/ppermute | solution.py:61
  146.1 0.8 copy-done.11
  147.7 2.9 %collective-permute-start.14 = (f32[256,512]{1,0:T(8,128)S(1)}, f32[256,512]{1,0:T(8,128)S(1)}, u32[]{:S(2)}, u32[]{:S(2)}) collective-permute-start(f32[256,512]{1,0:T(8,128)S(1)} %add.21.refs_0_), channel_id=1, source_target_pairs={{32,0},{40,8},{48,16},{56,24},{64,32},{72,40},{80,48},{88,56},{96,... | collective-permute-start | bytes 1572872 | tf_op jit(solution)/shard_map/ppermute | solution.py:61
  150.5 7.2 %gram.4.refs_4_ = f32[8,5,32,256]{3,2,1,0:T(8,128)} custom-call(s32[5]{0:T(128)} %constant.47.clone.left_of, s32[5]{0:T(128)} %constant.48.clone.right_of, f32[256,512]{1,0:T(8,128)} %copy-done.1, f32[256,512]{1,0:T(8,128)} %copy-done.2, f32[256,512]{1,0:T(8,128)} %collective-permute-done.4.refs_2_, f32[256,512]{1,0:T(8,128)} %copy-done.6, ...), custom_call_target="tpu_custom_call" | custom-call | tf_op jit(solution)/shard_map/gram/pallas_call | solution.py:180
  157.8 2.7 %collective-permute-done.16.refs_9_ = f32[256,512]{1,0:T(8,128)} collective-permute-done((f32[256,512]{1,0:T(8,128)S(1)}, f32[256,512]{1,0:T(8,128)}, u32[]{:S(2)}, u32[]{:S(2)}) %collective-permute-start.16) | collective-permute-done | bytes 524320 | tf_op jit(solution)/shard_map/ppermute | solution.py:61
  160.5 2.1 collective-permute-done.15.refs_3_
  162.7 0.7 copy-done.7
  163.6 5.5 %gram.6.refs_6_ = f32[8,5,32,256]{3,2,1,0:T(8,128)} custom-call(s32[5]{0:T(128)} %constant.47.clone.left_of, s32[5]{0:T(128)} %constant.48.clone.right_of, f32[256,512]{1,0:T(8,128)} %copy-done.3, f32[256,512]{1,0:T(8,128)} %collective-permute-done.13.refs_1_, f32[256,512]{1,0:T(8,128)} %copy-done.8, f32[256,512]{1,0:T(8,128)} %copy-done.7, ...), custom_call_target="tpu_custom_call" | custom-call | tf_op jit(solution)/shard_map/gram/pallas_call | solution.py:180
  170.3 6.9 %gram.5.refs_5_ = f32[8,4,32,256]{3,2,1,0:T(8,128)} custom-call(s32[4]{0:T(128)} %call_exported.2.left_of, s32[4]{0:T(128)} %call_exported.8.right_of, f32[256,512]{1,0:T(8,128)} %copy-done.1, f32[256,512]{1,0:T(8,128)} %copy-done.2, f32[256,512]{1,0:T(8,128)} %collective-permute-done.4.refs_2_, f32[256,512]{1,0:T(8,128)} %copy-done.6, ...), custom_call_target="tpu_custom_call" | custom-call | tf_op jit(solution)/shard_map/gram/pallas_call | solution.py:180
  177.2 0.8 copy-done.12
  178.0 6.0 %gram.7 = f32[8,9,32,256]{3,2,1,0:T(8,128)} custom-call(s32[4]{0:T(128)} %call_exported.2.left_of, s32[4]{0:T(128)} %call_exported.8.right_of, f32[256,512]{1,0:T(8,128)} %copy-done.3, f32[256,512]{1,0:T(8,128)} %collective-permute-done.13.refs_1_, f32[256,512]{1,0:T(8,128)} %copy-done.8, f32[256,512]{1,0:T(8,128)} %copy-done.7, f32[256,512]{1,0:T(8,128)} %copy-done.12, ...), custom_call_target="tpu_custom_call" | custom-call | tf_op jit(solution)/shard_map/gram/pallas_call | solution.py:180
  184.1 36.2 %all_to_all.20.moved_ref = f32[8,9,32,256]{3,2,1,0:T(8,128)} all-to-all(f32[8,9,32,256]{3,2,1,0:T(8,128)} %gram.7), channel_id=1, replica_groups=mesh['blk'=16,'col'=8] {'col'}, dimensions={0} | all-to-all | bytes 4718592 | tf_op jit(solution)/shard_map/all_to_all | solution.py:273
  220.3 2.5 sum.1
  222.9 1.8 collective-permute-start.21
  224.7 1.4 collective-permute-start.20
  226.0 3.8 %collective-permute-done.20.refs_1_.refs_3_ = f32[2,32,256]{2,1,0:T(8,128)S(1)} collective-permute-done((f32[2,32,256]{2,1,0:T(8,128)}, f32[2,32,256]{2,1,0:T(8,128)S(1)}, u32[]{:S(2)}, u32[]{:S(2)}) %collective-permute-start.20) | collective-permute-done | bytes 65568 | tf_op jit(solution)/shard_map/ppermute | solution.py:66
  229.9 2.2 collective-permute-done.21.refs_2_
  232.8 1.8 turn.1
  234.6 3.8 %all-to-all-start.3 = ((f32[8,32,256]{2,1,0:T(8,128)}), f32[8,32,256]{2,1,0:T(8,128)S(1)}, u32[]{:S(2)}, u32[]{:S(2)}) async-start(f32[8,32,256]{2,1,0:T(8,128)} %turn.1), calls=%async_computation.3 | async-start | bytes 524288 | tf_op jit(solution)/shard_map/all_to_all | solution.py:273
  238.4 1.3 dynamic-slice_bitcast_fusion.table_ref
  239.9 7.0 %all-to-all-done.3.refs_4_ = f32[8,32,256]{2,1,0:T(8,128)S(1)} async-done(((f32[8,32,256]{2,1,0:T(8,128)}), f32[8,32,256]{2,1,0:T(8,128)S(1)}, u32[]{:S(2)}, u32[]{:S(2)}) %all-to-all-start.3) | async-done | bytes 262176 | tf_op jit(solution)/shard_map/all_to_all | solution.py:273
  247.5 2.2 assemble.1
  (64 shorter events, 5.8 us)
Async XLA Ops:
  6.5 68.8 %all-gather.3.cloned.1.call-start = ((), (), s32[]{:S(2)}) async-start(), calls=%async_computation.4 | async-start | bytes 8912896 | tf_op jit(solution)/shard_map/all_gather | solution.py:283
  6.5 10.3 %collective-permute-start.2 = (f32[64,512]{1,0:T(8,128)}, f32[64,512]{1,0:T(8,128)S(1)}, u32[]{:S(2)}, u32[]{:S(2)}) collective-permute-start(f32[64,512]{1,0:T(8,128)} %bitcast.24), channel_id=1, source_target_pairs={{6,0},{7,1},{0,2},{1,3},{2,4},{3,5},{4,6},{5,7},{14,8},{15,9},{8,1... | collective-permute-start | bytes 393224 | tf_op jit(solution)/shard_map/ppermute | solution.py:279
  8.1 9.0 %collective-permute-start.1 = (f32[64,512]{1,0:T(8,128)}, f32[64,512]{1,0:T(8,128)S(1)}, u32[]{:S(2)}, u32[]{:S(2)}) collective-permute-start(f32[64,512]{1,0:T(8,128)} %bitcast.25), channel_id=1, source_target_pairs={{4,0},{5,1},{6,2},{7,3},{0,4},{1,5},{2,6},{3,7},{12,8},{13,9},{14,... | collective-permute-start | bytes 393224 | tf_op jit(solution)/shard_map/ppermute | solution.py:279
  10.8 6.2 %collective-permute-start = (f32[64,512]{1,0:T(8,128)}, f32[64,512]{1,0:T(8,128)S(1)}, u32[]{:S(2)}, u32[]{:S(2)}) collective-permute-start(f32[64,512]{1,0:T(8,128)} %bitcast.26), channel_id=1, source_target_pairs={{2,0},{3,1},{4,2},{5,3},{6,4},{7,5},{0,6},{1,7},{10,8},{11,9},{12,... | collective-permute-start | bytes 393224 | tf_op jit(solution)/shard_map/ppermute | solution.py:279
  12.3 4.8 %copy-start.15 = (f32[512,64]{0,1:T(8,128)S(1)}, f32[512,64]{0,1:T(8,128)}, u32[]{:S(2)}) copy-start(f32[512,64]{0,1:T(8,128)} %param.12) | copy-start | bytes 393220
  17.9 53.1 %all-to-all-start = ((f32[8,256,512]{2,1,0:T(8,128)}), f32[8,256,512]{2,1,0:T(8,128)}, u32[]{:S(2)}, u32[]{:S(2)}) async-start(f32[8,256,512]{2,1,0:T(8,128)} %slice.9), calls=%async_computation | async-start | bytes 8388608 | tf_op jit(solution)/shard_map/all_to_all | solution.py:264
  71.1 39.0 %all-to-all-start.1 = ((f32[4,256,512]{2,1,0:T(8,128)}), f32[4,256,512]{2,1,0:T(8,128)S(1)}, u32[]{:S(2)}, u32[]{:S(2)}) async-start(f32[4,256,512]{2,1,0:T(8,128)} %slice.8), calls=%async_computation.1 | async-start | bytes 4194304 | tf_op jit(solution)/shard_map/all_to_all | solution.py:264
  81.5 16.7 %collective-permute-start.3 = (f32[256,512]{1,0:T(8,128)}, f32[256,512]{1,0:T(8,128)S(1)}, u32[]{:S(2)}, u32[]{:S(2)}) collective-permute-start(f32[256,512]{1,0:T(8,128)} %transform.7), channel_id=1, source_target_pairs={{1,0},{0,1},{3,2},{2,3},{5,4},{4,5},{7,6},{6,7},{9,8},{8,9},{11,10... | collective-permute-start | bytes 1572872 | tf_op jit(solution)/shard_map/ppermute | solution.py:270
  91.5 17.3 %collective-permute-start.7 = (f32[256,512]{1,0:T(8,128)}, f32[256,512]{1,0:T(8,128)}, u32[]{:S(2)}, u32[]{:S(2)}) collective-permute-start(f32[256,512]{1,0:T(8,128)} %transform.9), channel_id=1, source_target_pairs={{1,0},{0,1},{3,2},{2,3},{5,4},{4,5},{7,6},{6,7},{9,8},{8,9},{11,10... | collective-permute-start | bytes 1572872 | tf_op jit(solution)/shard_map/ppermute | solution.py:270
  99.3 9.4 %copy-start.1 = (f32[256,512]{1,0:T(8,128)}, f32[256,512]{1,0:T(8,128)S(1)}, u32[]{:S(2)}) copy-start(f32[256,512]{1,0:T(8,128)S(1)} %add.19.refs_0_) | copy-start | bytes 1572868
  99.3 21.9 %collective-permute-start.6 = (f32[256,512]{1,0:T(8,128)S(1)}, f32[256,512]{1,0:T(8,128)}, u32[]{:S(2)}, u32[]{:S(2)}) collective-permute-start(f32[256,512]{1,0:T(8,128)S(1)} %add.19.refs_0_), channel_id=1, source_target_pairs={{96,0},{104,8},{112,16},{120,24},{0,32},{8,40},{16,48},{24,56},{40... | collective-permute-start | bytes 1572872 | tf_op jit(solution)/shard_map/ppermute | solution.py:61
  101.0 20.3 %collective-permute-start.5 = (f32[256,512]{1,0:T(8,128)S(1)}, f32[256,512]{1,0:T(8,128)}, u32[]{:S(2)}, u32[]{:S(2)}) collective-permute-start(f32[256,512]{1,0:T(8,128)S(1)} %add.19.refs_0_), channel_id=1, source_target_pairs={{32,0},{40,8},{48,16},{56,24},{64,32},{72,40},{80,48},{88,56},{96,... | collective-permute-start | bytes 1572872 | tf_op jit(solution)/shard_map/ppermute | solution.py:61
  102.7 18.6 %collective-permute-start.4 = (f32[256,512]{1,0:T(8,128)S(1)}, f32[256,512]{1,0:T(8,128)}, u32[]{:S(2)}, u32[]{:S(2)}) collective-permute-start(f32[256,512]{1,0:T(8,128)S(1)} %add.19.refs_0_), channel_id=1, source_target_pairs={{8,0},{0,8},{24,16},{16,24},{40,32},{32,40},{56,48},{48,56},{72,64... | collective-permute-start | bytes 1572872 | tf_op jit(solution)/shard_map/ppermute | solution.py:61
  110.0 21.5 %copy-start.2 = (f32[256,512]{1,0:T(8,128)}, f32[256,512]{1,0:T(8,128)S(1)}, u32[]{:S(2)}) copy-start(f32[256,512]{1,0:T(8,128)S(1)} %add.20.refs_1_) | copy-start | bytes 1572868
  110.1 1.4 copy-start
  117.5 16.8 %collective-permute-start.12 = (f32[256,512]{1,0:T(8,128)}, f32[256,512]{1,0:T(8,128)}, u32[]{:S(2)}, u32[]{:S(2)}) collective-permute-start(f32[256,512]{1,0:T(8,128)} %transform.11), channel_id=1, source_target_pairs={{1,0},{0,1},{3,2},{2,3},{5,4},{4,5},{7,6},{6,7},{9,8},{8,9},{11,10... | collective-permute-start | bytes 1572872 | tf_op jit(solution)/shard_map/ppermute | solution.py:270
  121.3 24.8 %collective-permute-start.11 = (f32[256,512]{1,0:T(8,128)}, f32[256,512]{1,0:T(8,128)S(1)}, u32[]{:S(2)}, u32[]{:S(2)}) collective-permute-start(f32[256,512]{1,0:T(8,128)} %collective-permute-done.5.refs_4_), channel_id=1, source_target_pairs={{16,0},{24,8},{8,16},{0,24},{48,32},{56,40},{40,48},{32,56},{88,64... | collective-permute-start | bytes 1572872 | tf_op jit(solution)/shard_map/ppermute | solution.py:61
  122.2 23.8 %collective-permute-start.10 = (f32[256,512]{1,0:T(8,128)S(1)}, f32[256,512]{1,0:T(8,128)S(1)}, u32[]{:S(2)}, u32[]{:S(2)}) collective-permute-start(f32[256,512]{1,0:T(8,128)S(1)} %add.20.refs_1_), channel_id=1, source_target_pairs={{96,0},{104,8},{112,16},{120,24},{0,32},{8,40},{16,48},{24,56},{40... | collective-permute-start | bytes 1572872 | tf_op jit(solution)/shard_map/ppermute | solution.py:61
  122.6 23.5 %collective-permute-start.9 = (f32[256,512]{1,0:T(8,128)S(1)}, f32[256,512]{1,0:T(8,128)S(1)}, u32[]{:S(2)}, u32[]{:S(2)}) collective-permute-start(f32[256,512]{1,0:T(8,128)S(1)} %add.20.refs_1_), channel_id=1, source_target_pairs={{32,0},{40,8},{48,16},{56,24},{64,32},{72,40},{80,48},{88,56},{96,... | collective-permute-start | bytes 1572872 | tf_op jit(solution)/shard_map/ppermute | solution.py:61
  125.4 20.6 %collective-permute-start.8 = (f32[256,512]{1,0:T(8,128)S(1)}, f32[256,512]{1,0:T(8,128)S(1)}, u32[]{:S(2)}, u32[]{:S(2)}) collective-permute-start(f32[256,512]{1,0:T(8,128)S(1)} %add.20.refs_1_), channel_id=1, source_target_pairs={{8,0},{0,8},{24,16},{16,24},{40,32},{32,40},{56,48},{48,56},{72,64... | collective-permute-start | bytes 1572872 | tf_op jit(solution)/shard_map/ppermute | solution.py:61
  135.6 22.1 %copy-start.3 = (f32[256,512]{1,0:T(8,128)}, f32[256,512]{1,0:T(8,128)S(1)}, u32[]{:S(2)}) copy-start(f32[256,512]{1,0:T(8,128)S(1)} %add.21.refs_0_) | copy-start | bytes 1572868
  146.0 0.8 copy-start.11
  146.0 4.5 %copy-start.4 = (f32[256,512]{1,0:T(8,128)}, f32[256,512]{1,0:T(8,128)S(1)}, u32[]{:S(2)}) copy-start(f32[256,512]{1,0:T(8,128)S(1)} %collective-permute-done.10.refs_7_) | copy-start | bytes 1572868
  146.0 4.5 %copy-start.5 = (f32[256,512]{1,0:T(8,128)}, f32[256,512]{1,0:T(8,128)S(1)}, u32[]{:S(2)}) copy-start(f32[256,512]{1,0:T(8,128)S(1)} %collective-permute-done.9.refs_5_) | copy-start | bytes 1572868
  146.8 3.7 %copy-start.6 = (f32[256,512]{1,0:T(8,128)}, f32[256,512]{1,0:T(8,128)S(1)}, u32[]{:S(2)}) copy-start(f32[256,512]{1,0:T(8,128)S(1)} %collective-permute-done.8.refs_3_) | copy-start | bytes 1572868
  146.8 13.7 %collective-permute-start.16 = (f32[256,512]{1,0:T(8,128)S(1)}, f32[256,512]{1,0:T(8,128)}, u32[]{:S(2)}, u32[]{:S(2)}) collective-permute-start(f32[256,512]{1,0:T(8,128)S(1)} %collective-permute-done.9.refs_5_), channel_id=1, source_target_pairs={{16,0},{24,8},{8,16},{0,24},{48,32},{56,40},{40,48},{32,56},{88,64... | collective-permute-start | bytes 1572872 | tf_op jit(solution)/shard_map/ppermute | solution.py:61
  147.3 15.3 %collective-permute-start.15 = (f32[256,512]{1,0:T(8,128)S(1)}, f32[256,512]{1,0:T(8,128)S(1)}, u32[]{:S(2)}, u32[]{:S(2)}) collective-permute-start(f32[256,512]{1,0:T(8,128)S(1)} %add.21.refs_0_), channel_id=1, source_target_pairs={{96,0},{104,8},{112,16},{120,24},{0,32},{8,40},{16,48},{24,56},{40... | collective-permute-start | bytes 1572872 | tf_op jit(solution)/shard_map/ppermute | solution.py:61
  147.7 15.0 %collective-permute-start.14 = (f32[256,512]{1,0:T(8,128)S(1)}, f32[256,512]{1,0:T(8,128)S(1)}, u32[]{:S(2)}, u32[]{:S(2)}) collective-permute-start(f32[256,512]{1,0:T(8,128)S(1)} %add.21.refs_0_), channel_id=1, source_target_pairs={{32,0},{40,8},{48,16},{56,24},{64,32},{72,40},{80,48},{88,56},{96,... | collective-permute-start | bytes 1572872 | tf_op jit(solution)/shard_map/ppermute | solution.py:61
  150.5 12.1 %collective-permute-start.13 = (f32[256,512]{1,0:T(8,128)S(1)}, f32[256,512]{1,0:T(8,128)}, u32[]{:S(2)}, u32[]{:S(2)}) collective-permute-start(f32[256,512]{1,0:T(8,128)S(1)} %add.21.refs_0_), channel_id=1, source_target_pairs={{8,0},{0,8},{24,16},{16,24},{40,32},{32,40},{56,48},{48,56},{72,64... | collective-permute-start | bytes 1572872 | tf_op jit(solution)/shard_map/ppermute | solution.py:61
  162.6 0.8 copy-start.7
  162.6 1.0 copy-start.8
  162.6 14.5 %collective-permute-start.17 = (f32[256,512]{1,0:T(8,128)S(1)}, f32[256,512]{1,0:T(8,128)S(1)}, u32[]{:S(2)}, u32[]{:S(2)}) collective-permute-start(f32[256,512]{1,0:T(8,128)S(1)} %collective-permute-done.14.refs_2_), channel_id=1, source_target_pairs={{16,0},{24,8},{8,16},{0,24},{48,32},{56,40},{40,48},{32,56},{88,64... | collective-permute-start | bytes 1572872 | tf_op jit(solution)/shard_map/ppermute | solution.py:61
  177.2 0.8 copy-start.12
  222.8 7.1 %collective-permute-start.19 = (f32[4,32,256]{2,1,0:T(8,128)}, f32[4,32,256]{2,1,0:T(8,128)S(1)}, u32[]{:S(2)}, u32[]{:S(2)}) collective-permute-start(f32[4,32,256]{2,1,0:T(8,128)} %get-tuple-element.64), channel_id=1, source_target_pairs={{0,32},{8,40},{16,48},{24,56},{32,64},{40,72},{48,80},{56,88},{64,... | collective-permute-start | bytes 393224 | tf_op jit(solution)/shard_map/ppermute | solution.py:66
  222.9 9.2 %collective-permute-start.21 = (f32[4,32,256]{2,1,0:T(8,128)}, f32[4,32,256]{2,1,0:T(8,128)S(1)}, u32[]{:S(2)}, u32[]{:S(2)}) collective-permute-start(f32[4,32,256]{2,1,0:T(8,128)} %get-tuple-element.66), channel_id=1, source_target_pairs={{0,48},{8,56},{16,40},{24,32},{32,80},{40,88},{48,72},{56,64},{64,... | collective-permute-start | bytes 393224 | tf_op jit(solution)/shard_map/ppermute | solution.py:66
  224.7 5.1 %collective-permute-start.20 = (f32[2,32,256]{2,1,0:T(8,128)}, f32[2,32,256]{2,1,0:T(8,128)S(1)}, u32[]{:S(2)}, u32[]{:S(2)}) collective-permute-start(f32[2,32,256]{2,1,0:T(8,128)} %get-tuple-element.65), channel_id=1, source_target_pairs={{0,96},{8,104},{16,112},{24,120},{32,0},{40,8},{48,16},{56,24},{64... | collective-permute-start | bytes 196616 | tf_op jit(solution)/shard_map/ppermute | solution.py:66
  229.8 2.3 copy-start.13
  229.9 2.2 copy-start.10
  232.1 0.7 copy-start.14
  234.6 12.2 %all-to-all-start.3 = ((f32[8,32,256]{2,1,0:T(8,128)}), f32[8,32,256]{2,1,0:T(8,128)S(1)}, u32[]{:S(2)}, u32[]{:S(2)}) async-start(f32[8,32,256]{2,1,0:T(8,128)} %turn.1), calls=%async_computation.3 | async-start | bytes 524288 | tf_op jit(solution)/shard_map/all_to_all | solution.py:273
  238.4 1.5 collective-permute-start.18
  239.9 7.0 %copy-start.16 = (f32[2,32,256]{2,1,0:T(8,128)}, f32[2,32,256]{2,1,0:T(8,128)S(1)}, u32[]{:S(2)}) copy-start(f32[2,32,256]{2,1,0:T(8,128)S(1)} %collective-permute-done.18.refs_1_) | copy-start | bytes 196612
  246.8 0.7 copy-start.9
Sparse Core Ops, SparseCore 0:
  18.1 54.1 all-gather.2

commit v6 on v5

--- a/solution.py
+++ b/solution.py
@@ -88,53 +88,50 @@
     )
 
 
-def transform_kernel(place, part, orbitals, out, high, low):
-    width = part.shape[-1]
-
-    @pl.when(pl.program_id(0) == 0)
-    def _():
-        for x in range(X):
-            high[:, x * width : (x + 1) * width], low[:, x * width : (x + 1) * width] = (
-                high_and_low(part[x, 0])
-            )
-
-    total = jnp.zeros(out.shape, jnp.float32)
-    for x in range(X):
-        slot = lax.rem(x - place[0] + X, X)
-        block = orbitals[:, pl.ds(slot, 1)]
-        c_high, c_low = high_and_low(block.reshape(out.shape[1], width))
-        b_high = high[:, x * width : (x + 1) * width]
-        b_low = low[:, x * width : (x + 1) * width]
-        total += dot(b_high, c_high) + (dot(b_high, c_low) + dot(b_low, c_high))
-    out[...] = total
+def transform_kernel(index, scalars, part, orbitals, out, rows_in, orbitals_in, sems):
+    place, half = scalars[0], scalars[1]
+    run, each, width = orbitals_in.shape[1:]
+    copies = []
+    for k in range(X):
+        x = lax.rem(place + k, X)
+        copies.append((
+            pltpu.make_async_copy(part.at[x, index], rows_in.at[k], sems.at[0, k]),
+            pltpu.make_async_copy(
+                orbitals.at[pl.ds(half * run, run), k], orbitals_in.at[k], sems.at[1, k]
+            ),
+        ))
+    for of_rows, of_orbitals in copies:
+        of_rows.start()
+        of_orbitals.start()
+    for k, (of_rows, of_orbitals) in enumerate(copies):
+        of_rows.wait()
+        of_orbitals.wait()
+        b_high, b_low = high_and_low(rows_in[k])
+        c_high, c_low = high_and_low(orbitals_in[k].reshape(run * each, width))
+        term = dot(b_high, c_high) + (dot(b_high, c_low) + dot(b_low, c_high))
+        out[...] = out[...] + term if k else term
 
 
 def transformed(part, index, orbitals, place, half):
     rows, width = part.shape[2:]
     blocks, _, each, _ = orbitals.shape
-    steps, run = 2, blocks // 4
-    columns = run * each
+    run = blocks // ZH
     return pl.pallas_call(
-        transform_kernel,
-        grid_spec=pltpu.PrefetchScalarGridSpec(
-            num_scalar_prefetch=1,
-            grid=(steps,),
-            in_specs=[
-                pl.BlockSpec((X, 1, rows, width), lambda j, s: (0, index, 0, 0)),
-                pl.BlockSpec((run, X, each, width), lambda j, s: (s[1] * 2 + j, 0, 0, 0)),
-            ],
-            out_specs=pl.BlockSpec((rows, columns), lambda j, s: (0, j)),
-            scratch_shapes=[pltpu.VMEM((rows, X * width), jnp.bfloat16)] * 2,
-        ),
-        out_shape=jax.ShapeDtypeStruct((rows, steps * columns), jnp.float32),
-        cost_estimate=pl.CostEstimate(
-            flops=0, bytes_accessed=0, transcendentals=0
-        ),
+        functools.partial(transform_kernel, index),
+        in_specs=[pl.BlockSpec(memory_space=pltpu.SMEM)] + [pl.BlockSpec(memory_space=pl.ANY)] * 2,
+        out_specs=pl.BlockSpec(memory_space=pltpu.VMEM),
+        out_shape=jax.ShapeDtypeStruct((rows, run * each), jnp.float32),
+        scratch_shapes=[
+            pltpu.VMEM((X, rows, width), jnp.float32),
+            pltpu.VMEM((X, run, each, width), jnp.float32),
+            pltpu.SemaphoreType.DMA((2, X)),
+        ],
+        cost_estimate=pl.CostEstimate(flops=0, bytes_accessed=0, transcendentals=0),
         name="transform",
     )(jnp.stack([place, half]), part, orbitals)
 
 
-def gram_kernel(pairs, chunks, more, ahead, left_of, right_of, *refs):
+def gram_kernel(pairs, chunks, more, ahead, *refs):
     left_rows, right_rows = sides(pairs)
     count = (1 + max(left_rows + right_rows)) * chunks
     blocks, refs = refs[:count], refs[count:]
@@ -158,9 +155,9 @@
     if ahead:
         out[:, :ahead] = before[...]
 
-    @pl.loop(0, len(pairs))
-    def _(t):
-        tile = dot(lefts[left_of[t]], rights[right_of[t]]).reshape(shares, part, width)
+    for t, (left, right) in enumerate(pairs):
+        tile = dot(lefts[left_rows.index(left)], rights[right_rows.index(right)])
+        tile = tile.reshape(shares, part, width)
         out[:, ahead + t] = so_far[:, t] + tile if more else tile
 
 
@@ -179,8 +176,7 @@
     inputs = flat + ([so_far] if more else []) + ([before] if ahead else [])
     return pl.pallas_call(
         functools.partial(gram_kernel, pairs, chunks, more, ahead),
-        in_specs=[pl.BlockSpec(memory_space=pltpu.SMEM)] * 2
-        + [pl.BlockSpec(memory_space=pltpu.VMEM)] * len(inputs),
+        in_specs=[pl.BlockSpec(memory_space=pltpu.VMEM)] * len(inputs),
         out_specs=pl.BlockSpec(memory_space=pltpu.VMEM),
         scratch_shapes=[
             pltpu.VMEM((len(side), rows, 3 * chunks * depth), jnp.bfloat16)
@@ -191,11 +187,7 @@
             flops=0, bytes_accessed=0, transcendentals=0
         ),
         name="gram",
-    )(
-        np.array([left_rows.index(left) for left, _ in pairs], np.int32),
-        np.array([right_rows.index(right) for _, right in pairs], np.int32),
-        *inputs,
-    )
+    )(*inputs)
 
 
 def in_vmem(kernel, inputs, outputs, name, tables=()):
@@ -284,8 +276,8 @@
     last, first_part = together(by_aux[cut:], first_part)
     last_part = over_x(last)
 
-    def sent(part, k):
-        return to_other_half(transformed(part, k, orbitals, place, 1 - zh))
+    def to_send(part, k):
+        return transformed(part, k, orbitals, place, 1 - zh)
 
     def kept(part, k):
         return transformed(part, k, orbitals, place, zh)
@@ -293,12 +285,13 @@
     def neighbours(own):
         return fetched(own, other_core), fetched(own, next_row), fetched(own, previous_row)
 
-    arrived_0, arrived_1 = sent(first_part, 0), sent(first_part, 1)
+    arrived_0 = to_other_half(to_send(first_part, 0))
+    arrived_1 = to_other_half(to_send(first_part, 1))
     own_0 = kept(first_part, 0) + arrived_0
+    other_0, below_0, above_0 = neighbours(own_0)
+    leaving_2, first_part = together(to_send(last_part, 0), first_part)
+    arrived_2 = to_other_half(leaving_2)
     own_1 = kept(first_part, 1) + arrived_1
-    own_1, last_part = together(own_1, last_part)
-    other_0, below_0, above_0 = neighbours(own_0)
-    arrived_2 = sent(last_part, 0)
     own_2 = kept(last_part, 0) + arrived_2
     other_0, below_0, above_0, own_1 = together(other_0, below_0, above_0, own_1)
     across_0 = fetched(below_0, over_to_across)

time: 257 us -> 248 us (0.965)
  Pallas kernels: 68.8 us -> 57.1 us
  waiting for transfers between devices: 76.7 us -> 79.5 us
  local copies, waits for them, and re-layouts: 15.4 us -> 12.7 us
    pallas_call x6, Pallas kernels: 36.6 us -> 30.4 us  [transformed(): pl.pallas_call(functools.partial(transform_kernel, index), in_specs=[pl.B...]
    pallas_call x4, Pallas kernels: 25.7 us -> 20.1 us  [gram(): pl.pallas_call(functools.partial(gram_kernel, pairs, chunks, more, ahead)...]
    ppermute x12, waiting for transfers between devices: 15.3 us -> 19.5 us  [fetched(): return lax.ppermute(value, 'blk', route)]
    unnamed x34 -> x40, local copies, waits for them, and re-layouts: 5.33 us -> 3.78 us
  transfers between devices with their start and end apart: 26 -> 26, of which waited for: 11 -> 12; matrix products, arithmetic and copies ran while one was open for 6% -> 6% of each run, Pallas kernels for 22% -> 18%
where the time goes in v6:
time: 248 us; the launch traced here: 247 us
  waiting for transfers between devices  79.5 us (32%)
  Pallas kernels  57.1 us (23%)
  starting transfers between devices  42.1 us (17%)
  blocking collectives  36 us (15%)
  between operations  13.7 us (6%)
  local copies, waits for them, and re-layouts  12.7 us (5%)
  other arithmetic  5.77 us (2%)
    all_to_all x2, waiting for transfers between devices, over_x(): lax.all_to_all(part, 'col', split_axis=0, concat_axis=0, tiled=True, axis...  45.2 us
    all_to_all x1, blocking collectives, over_col(): return lax.all_to_all(tiles, 'col', split_axis=0, concat_axis=0, tiled=True)  36 us
    pallas_call x6, Pallas kernels, transformed(): pl.pallas_call(functools.partial(transform_kernel, index), in_specs=[pl.B...  30.4 us
    pallas_call x4, Pallas kernels, gram(): pl.pallas_call(functools.partial(gram_kernel, pairs, chunks, more, ahead)...  20.1 us
    ppermute x12, waiting for transfers between devices, fetched(): return lax.ppermute(value, 'blk', route)  19.5 us
    ppermute x12, starting transfers between devices, fetched(): return lax.ppermute(value, 'blk', route)  11.5 us
    all_to_all x2, starting transfers between devices, over_x(): lax.all_to_all(part, 'col', split_axis=0, concat_axis=0, tiled=True, axis...  8.45 us
    ppermute x3, starting transfers between devices, to_other_half(): return lax.ppermute(value, 'col', swap_zh)  7.83 us
  transfers between devices with their start and end apart: 26, of which 12 were waited for; matrix products, arithmetic and copies ran while one was open for 6% of the time, Pallas kernels for 18%

profile of v6, /device:TPU:0, one launch (start us, length us, event | category | flops | bytes accessed | tf_op | source)
XLA Modules:
  0.0 246.9 jit_solution(7866885916003005189)
XLA Ops:
  6.5 1.6 collective-permute-start.2
  8.1 2.7 %collective-permute-start.1 = (f32[64,512]{1,0:T(8,128)}, f32[64,512]{1,0:T(8,128)S(1)}, u32[]{:S(2)}, u32[]{:S(2)}) collective-permute-start(f32[64,512]{1,0:T(8,128)} %bitcast.25), channel_id=1, source_target_pairs={{4,0},{5,1},{6,2},{7,3},{0,4},{1,5},{2,6},{3,7},{12,8},{13,9},{14,... | collective-permute-start | bytes 393224 | tf_op jit(solution)/shard_map/ppermute | solution.py:271
  10.8 1.4 collective-permute-start
  12.3 4.6 %slice.9 = f32[8,256,512]{2,1,0:T(8,128)} slice(f32[12,256,512]{2,1,0:T(8,128)} %bitcast.22), slice={[0:8], [0:256], [0:512]} | slice | bytes 8388608 | tf_op jit(solution)/shard_map/slice | solution.py:272
  17.1 0.8 pad_maximum_fusion
  17.9 4.8 %all-to-all-start = ((f32[8,256,512]{2,1,0:T(8,128)}), f32[8,256,512]{2,1,0:T(8,128)}, u32[]{:S(2)}, u32[]{:S(2)}) async-start(f32[8,256,512]{2,1,0:T(8,128)} %slice.9), calls=%async_computation | async-start | bytes 8388608 | tf_op jit(solution)/shard_map/all_to_all | solution.py:256
  22.8 3.1 %slice.8 = f32[4,256,512]{2,1,0:T(8,128)} slice(f32[12,256,512]{2,1,0:T(8,128)} %bitcast.23), slice={[8:12], [0:256], [0:512]} | slice | bytes 4194304 | tf_op jit(solution)/shard_map/slice | solution.py:276
  25.9 45.2 %all-to-all-done = f32[8,256,512]{2,1,0:T(8,128)} async-done(((f32[8,256,512]{2,1,0:T(8,128)}), f32[8,256,512]{2,1,0:T(8,128)}, u32[]{:S(2)}, u32[]{:S(2)}) %all-to-all-start) | async-done | bytes 4194336 | tf_op jit(solution)/shard_map/all_to_all | solution.py:256
  71.1 3.6 %all-to-all-start.1 = ((f32[4,256,512]{2,1,0:T(8,128)}), f32[4,256,512]{2,1,0:T(8,128)S(1)}, u32[]{:S(2)}, u32[]{:S(2)}) async-start(f32[4,256,512]{2,1,0:T(8,128)} %slice.8), calls=%async_computation.1 | async-start | bytes 4194304 | tf_op jit(solution)/shard_map/all_to_all | solution.py:256
  75.3 5.0 %transform.7 = f32[256,512]{1,0:T(8,128)} custom-call(s32[2]{0:T(128)} %pad_add_fusion.1.scalars, f32[4,2,256,512]{3,2,1,0:T(8,128)} %bitcast.5.part, f32[16,4,64,512]{3,2,1,0:T(8,128)} %bitcast.14), custom_call_target="tpu_custom_call" | custom-call | tf_op jit(solution)/shard_map/transform/pallas_call | solution.py:119
  80.3 4.0 %collective-permute-start.3 = (f32[256,512]{1,0:T(8,128)}, f32[256,512]{1,0:T(8,128)S(1)}, u32[]{:S(2)}, u32[]{:S(2)}) collective-permute-start(f32[256,512]{1,0:T(8,128)} %transform.7), channel_id=1, source_target_pairs={{1,0},{0,1},{3,2},{2,3},{5,4},{4,5},{7,6},{6,7},{9,8},{8,9},{11,10... | collective-permute-start | bytes 1572872 | tf_op jit(solution)/shard_map/ppermute | solution.py:262
  85.0 5.1 %transform.10 = f32[256,512]{1,0:T(8,128)} custom-call(s32[2]{0:T(128)} %pad_add_fusion.1.scalars, f32[4,2,256,512]{3,2,1,0:T(8,128)} %bitcast.5.part, f32[16,4,64,512]{3,2,1,0:T(8,128)} %bitcast.15), custom_call_target="tpu_custom_call" | custom-call | tf_op jit(solution)/shard_map/transform/pallas_call | solution.py:119
  90.0 5.1 %transform.6 = f32[256,512]{1,0:T(8,128)} custom-call(s32[2]{0:T(128)} %pad_add_fusion.scalars, f32[4,2,256,512]{3,2,1,0:T(8,128)} %bitcast.5.part, f32[16,4,64,512]{3,2,1,0:T(8,128)} %bitcast.16), custom_call_target="tpu_custom_call" | custom-call | tf_op jit(solution)/shard_map/transform/pallas_call | solution.py:119
  95.2 1.1 add.19.refs_0_
  96.3 1.6 collective-permute-start.6
  98.0 1.7 collective-permute-start.5
  99.7 1.3 copy-done
  101.0 5.1 %transform.8 = f32[256,512]{1,0:T(8,128)} custom-call(s32[2]{0:T(128)} %pad_add_fusion.1.scalars, f32[4,1,256,512]{3,2,1,0:T(8,128)} %bitcast.20, f32[16,4,64,512]{3,2,1,0:T(8,128)} %bitcast.17), custom_call_target="tpu_custom_call" | custom-call | tf_op jit(solution)/shard_map/transform/pallas_call | solution.py:119
  106.0 5.2 %transform.9 = f32[256,512]{1,0:T(8,128)} custom-call(s32[2]{0:T(128)} %pad_add_fusion.scalars, f32[4,2,256,512]{3,2,1,0:T(8,128)} %bitcast.5.part, f32[16,4,64,512]{3,2,1,0:T(8,128)} %bitcast.18), custom_call_target="tpu_custom_call" | custom-call | tf_op jit(solution)/shard_map/transform/pallas_call | solution.py:119
  111.3 3.8 %collective-permute-start.12 = (f32[256,512]{1,0:T(8,128)S(1)}, f32[256,512]{1,0:T(8,128)}, u32[]{:S(2)}, u32[]{:S(2)}) collective-permute-start(f32[256,512]{1,0:T(8,128)S(1)} %copy-done.13), channel_id=1, source_target_pairs={{1,0},{0,1},{3,2},{2,3},{5,4},{4,5},{7,6},{6,7},{9,8},{8,9},{11,10... | collective-permute-start | bytes 1572872 | tf_op jit(solution)/shard_map/ppermute | solution.py:262
  115.0 1.3 add.20.refs_1_
  117.1 1.0 collective-permute-start.10
  118.1 2.4 collective-permute-start.9
  120.4 5.1 %transform.11 = f32[256,512]{1,0:T(8,128)} custom-call(s32[2]{0:T(128)} %pad_add_fusion.scalars, f32[4,1,256,512]{3,2,1,0:T(8,128)} %bitcast.21, f32[16,4,64,512]{3,2,1,0:T(8,128)} %bitcast.19), custom_call_target="tpu_custom_call" | custom-call | tf_op jit(solution)/shard_map/transform/pallas_call | solution.py:119
  125.5 2.4 collective-permute-done.12
  127.9 1.3 add.21.refs_0_
  129.2 10.2 %collective-permute-done.11.refs_8_ = f32[256,512]{1,0:T(8,128)S(1)} collective-permute-done((f32[256,512]{1,0:T(8,128)}, f32[256,512]{1,0:T(8,128)S(1)}, u32[]{:S(2)}, u32[]{:S(2)}) %collective-permute-start.11) | collective-permute-done | bytes 524320 | tf_op jit(solution)/shard_map/ppermute | solution.py:61
  140.6 2.9 %collective-permute-start.14 = (f32[256,512]{1,0:T(8,128)S(1)}, f32[256,512]{1,0:T(8,128)S(1)}, u32[]{:S(2)}, u32[]{:S(2)}) collective-permute-start(f32[256,512]{1,0:T(8,128)S(1)} %add.21.refs_0_), channel_id=1, source_target_pairs={{32,0},{40,8},{48,16},{56,24},{64,32},{72,40},{80,48},{88,56},{96,... | collective-permute-start | bytes 1572872 | tf_op jit(solution)/shard_map/ppermute | solution.py:61
  143.5 5.5 %gram.4.refs_4_ = f32[8,5,32,256]{3,2,1,0:T(8,128)} custom-call(f32[256,512]{1,0:T(8,128)} %copy-done.2, f32[256,512]{1,0:T(8,128)} %copy-done.3, f32[256,512]{1,0:T(8,128)} %collective-permute-done.4.refs_2_, f32[256,512]{1,0:T(8,128)} %copy-done.9, f32[256,512]{1,0:T(8,128)} %collective-permute-done.5.refs_4_, f32[256,512]{1,0:T(8,128)} %collective-permute-done.9.refs_5_, ...), custom_call_target="tpu_custom_call" | custom-call | tf_op jit(solution)/shard_map/gram/pallas_call | solution.py:177
  149.0 4.1 %collective-permute-done.16.refs_9_ = f32[256,512]{1,0:T(8,128)S(1)} collective-permute-done((f32[256,512]{1,0:T(8,128)}, f32[256,512]{1,0:T(8,128)S(1)}, u32[]{:S(2)}, u32[]{:S(2)}) %collective-permute-start.16) | collective-permute-done | bytes 524320 | tf_op jit(solution)/shard_map/ppermute | solution.py:61
  153.0 2.1 collective-permute-done.15.refs_3_
  155.5 5.5 %gram.5.refs_5_ = f32[8,4,32,256]{3,2,1,0:T(8,128)} custom-call(f32[256,512]{1,0:T(8,128)} %copy-done.2, f32[256,512]{1,0:T(8,128)} %copy-done.3, f32[256,512]{1,0:T(8,128)} %collective-permute-done.4.refs_2_, f32[256,512]{1,0:T(8,128)} %copy-done.9, f32[256,512]{1,0:T(8,128)} %collective-permute-done.5.refs_4_, f32[256,512]{1,0:T(8,128)} %collective-permute-done.9.refs_5_, ...), custom_call_target="tpu_custom_call" | custom-call | tf_op jit(solution)/shard_map/gram/pallas_call | solution.py:177
  161.0 4.3 %gram.6.refs_6_ = f32[8,5,32,256]{3,2,1,0:T(8,128)} custom-call(f32[256,512]{1,0:T(8,128)} %copy-done.1, f32[256,512]{1,0:T(8,128)} %copy-done.6, f32[256,512]{1,0:T(8,128)} %copy-done.5, f32[256,512]{1,0:T(8,128)} %copy-done.4, f32[8,5,32,256]{3,2,1,0:T(8,128)} %gram.4.refs_4_), custom_call_target="tpu_custom_call" | custom-call | tf_op jit(solution)/shard_map/gram/pallas_call | solution.py:177
  165.2 3.0 %collective-permute-done.17.refs_4_ = f32[256,512]{1,0:T(8,128)S(1)} collective-permute-done((f32[256,512]{1,0:T(8,128)S(1)}, f32[256,512]{1,0:T(8,128)S(1)}, u32[]{:S(2)}, u32[]{:S(2)}) %collective-permute-start.17) | collective-permute-done | bytes 524320 | tf_op jit(solution)/shard_map/ppermute | solution.py:61
  168.3 0.8 copy-done.11
  169.1 4.9 %gram.7 = f32[8,9,32,256]{3,2,1,0:T(8,128)} custom-call(f32[256,512]{1,0:T(8,128)} %copy-done.1, f32[256,512]{1,0:T(8,128)} %copy-done.6, f32[256,512]{1,0:T(8,128)} %copy-done.5, f32[256,512]{1,0:T(8,128)} %copy-done.4, f32[256,512]{1,0:T(8,128)} %copy-done.11, f32[8,4,32,256]{3,2,1,0:T(8,128)} %gram.5.refs_5_, f32[8,5,32,256]{3,2,1,0:T(8,128)} %gram.6.refs_6_), custom_call_target="tpu_custom_call" | custom-call | tf_op jit(solution)/shard_map/gram/pallas_call | solution.py:177
  174.0 36.0 %all_to_all.20.moved_ref = f32[8,9,32,256]{3,2,1,0:T(8,128)} all-to-all(f32[8,9,32,256]{3,2,1,0:T(8,128)} %gram.7), channel_id=1, replica_groups=mesh['blk'=16,'col'=8] {'col'}, dimensions={0} | all-to-all | bytes 4718592 | tf_op jit(solution)/shard_map/all_to_all | solution.py:265
  210.0 2.5 %sum.1 = (f32[4,32,256]{2,1,0:T(8,128)}, f32[2,32,256]{2,1,0:T(8,128)}, f32[4,32,256]{2,1,0:T(8,128)}, f32[2,32,256]{2,1,0:T(8,128)}, f32[4,32,256]{2,1,0:T(8,128)}) custom-call(f32[8,9,32,256]{3,2,1,0:T(8,128)} %all_to_all.20.moved_ref), custom_call_target="tpu_custom_call" | custom-call | bytes 1048576 | tf_op jit(solution)/shard_map/sum/pallas_call | solution.py:194
  213.2 1.4 collective-permute-start.21
  214.6 1.9 collective-permute-start.20
  216.5 2.7 %collective-permute-done.20.refs_1_.refs_3_ = f32[2,32,256]{2,1,0:T(8,128)S(1)} collective-permute-done((f32[2,32,256]{2,1,0:T(8,128)}, f32[2,32,256]{2,1,0:T(8,128)S(1)}, u32[]{:S(2)}, u32[]{:S(2)}) %collective-permute-start.20) | collective-permute-done | bytes 65568 | tf_op jit(solution)/shard_map/ppermute | solution.py:66
  219.2 1.0 collective-permute-done.19.refs_0_.refs_2_
  220.3 1.4 collective-permute-done.21.refs_2_
  222.3 1.8 turn.1
  224.1 4.5 %all-to-all-start.3 = ((f32[8,32,256]{2,1,0:T(8,128)}), f32[8,32,256]{2,1,0:T(8,128)S(1)}, u32[]{:S(2)}, u32[]{:S(2)}) async-start(f32[8,32,256]{2,1,0:T(8,128)} %turn.1), calls=%async_computation.3 | async-start | bytes 524288 | tf_op jit(solution)/shard_map/all_to_all | solution.py:265
  228.7 1.3 dynamic-slice_bitcast_fusion.table_ref
  230.1 7.0 %all-to-all-done.3.refs_4_ = f32[8,32,256]{2,1,0:T(8,128)S(1)} async-done(((f32[8,32,256]{2,1,0:T(8,128)}), f32[8,32,256]{2,1,0:T(8,128)S(1)}, u32[]{:S(2)}, u32[]{:S(2)}) %all-to-all-start.3) | async-done | bytes 262176 | tf_op jit(solution)/shard_map/all_to_all | solution.py:265
  237.8 2.2 assemble.1
  (68 shorter events, 6.2 us)
Async XLA Ops:
  6.5 68.8 %all-gather.3.cloned.1.call-start = ((), (), s32[]{:S(2)}) async-start(), calls=%async_computation.4 | async-start | bytes 8912896 | tf_op jit(solution)/shard_map/all_gather | solution.py:275
  6.5 10.3 %collective-permute-start.2 = (f32[64,512]{1,0:T(8,128)}, f32[64,512]{1,0:T(8,128)S(1)}, u32[]{:S(2)}, u32[]{:S(2)}) collective-permute-start(f32[64,512]{1,0:T(8,128)} %bitcast.24), channel_id=1, source_target_pairs={{6,0},{7,1},{0,2},{1,3},{2,4},{3,5},{4,6},{5,7},{14,8},{15,9},{8,1... | collective-permute-start | bytes 393224 | tf_op jit(solution)/shard_map/ppermute | solution.py:271
  8.1 9.0 %collective-permute-start.1 = (f32[64,512]{1,0:T(8,128)}, f32[64,512]{1,0:T(8,128)S(1)}, u32[]{:S(2)}, u32[]{:S(2)}) collective-permute-start(f32[64,512]{1,0:T(8,128)} %bitcast.25), channel_id=1, source_target_pairs={{4,0},{5,1},{6,2},{7,3},{0,4},{1,5},{2,6},{3,7},{12,8},{13,9},{14,... | collective-permute-start | bytes 393224 | tf_op jit(solution)/shard_map/ppermute | solution.py:271
  10.8 6.2 %collective-permute-start = (f32[64,512]{1,0:T(8,128)}, f32[64,512]{1,0:T(8,128)S(1)}, u32[]{:S(2)}, u32[]{:S(2)}) collective-permute-start(f32[64,512]{1,0:T(8,128)} %bitcast.26), channel_id=1, source_target_pairs={{2,0},{3,1},{4,2},{5,3},{6,4},{7,5},{0,6},{1,7},{10,8},{11,9},{12,... | collective-permute-start | bytes 393224 | tf_op jit(solution)/shard_map/ppermute | solution.py:271
  12.3 4.8 %copy-start.18 = (f32[512,64]{0,1:T(8,128)S(1)}, f32[512,64]{0,1:T(8,128)}, u32[]{:S(2)}) copy-start(f32[512,64]{0,1:T(8,128)} %param.4) | copy-start | bytes 393220
  17.9 53.1 %all-to-all-start = ((f32[8,256,512]{2,1,0:T(8,128)}), f32[8,256,512]{2,1,0:T(8,128)}, u32[]{:S(2)}, u32[]{:S(2)}) async-start(f32[8,256,512]{2,1,0:T(8,128)} %slice.9), calls=%async_computation | async-start | bytes 8388608 | tf_op jit(solution)/shard_map/all_to_all | solution.py:256
  71.1 28.6 %all-to-all-start.1 = ((f32[4,256,512]{2,1,0:T(8,128)}), f32[4,256,512]{2,1,0:T(8,128)S(1)}, u32[]{:S(2)}, u32[]{:S(2)}) async-start(f32[4,256,512]{2,1,0:T(8,128)} %slice.8), calls=%async_computation.1 | async-start | bytes 4194304 | tf_op jit(solution)/shard_map/all_to_all | solution.py:256
  80.3 14.9 %collective-permute-start.3 = (f32[256,512]{1,0:T(8,128)}, f32[256,512]{1,0:T(8,128)S(1)}, u32[]{:S(2)}, u32[]{:S(2)}) collective-permute-start(f32[256,512]{1,0:T(8,128)} %transform.7), channel_id=1, source_target_pairs={{1,0},{0,1},{3,2},{2,3},{5,4},{4,5},{7,6},{6,7},{9,8},{8,9},{11,10... | collective-permute-start | bytes 1572872 | tf_op jit(solution)/shard_map/ppermute | solution.py:262
  95.1 19.9 %collective-permute-start.7 = (f32[256,512]{1,0:T(8,128)}, f32[256,512]{1,0:T(8,128)}, u32[]{:S(2)}, u32[]{:S(2)}) collective-permute-start(f32[256,512]{1,0:T(8,128)} %transform.10), channel_id=1, source_target_pairs={{1,0},{0,1},{3,2},{2,3},{5,4},{4,5},{7,6},{6,7},{9,8},{8,9},{11,10... | collective-permute-start | bytes 1572872 | tf_op jit(solution)/shard_map/ppermute | solution.py:262
  96.3 14.9 %copy-start.2 = (f32[256,512]{1,0:T(8,128)}, f32[256,512]{1,0:T(8,128)S(1)}, u32[]{:S(2)}) copy-start(f32[256,512]{1,0:T(8,128)S(1)} %add.19.refs_0_) | copy-start | bytes 1572868
  96.3 20.0 %collective-permute-start.6 = (f32[256,512]{1,0:T(8,128)S(1)}, f32[256,512]{1,0:T(8,128)S(1)}, u32[]{:S(2)}, u32[]{:S(2)}) collective-permute-start(f32[256,512]{1,0:T(8,128)S(1)} %add.19.refs_0_), channel_id=1, source_target_pairs={{96,0},{104,8},{112,16},{120,24},{0,32},{8,40},{16,48},{24,56},{40... | collective-permute-start | bytes 1572872 | tf_op jit(solution)/shard_map/ppermute | solution.py:61
  98.0 18.4 %collective-permute-start.5 = (f32[256,512]{1,0:T(8,128)S(1)}, f32[256,512]{1,0:T(8,128)}, u32[]{:S(2)}, u32[]{:S(2)}) collective-permute-start(f32[256,512]{1,0:T(8,128)S(1)} %add.19.refs_0_), channel_id=1, source_target_pairs={{32,0},{40,8},{48,16},{56,24},{64,32},{72,40},{80,48},{88,56},{96,... | collective-permute-start | bytes 1572872 | tf_op jit(solution)/shard_map/ppermute | solution.py:61
  99.7 16.7 %collective-permute-start.4 = (f32[256,512]{1,0:T(8,128)S(1)}, f32[256,512]{1,0:T(8,128)}, u32[]{:S(2)}, u32[]{:S(2)}) collective-permute-start(f32[256,512]{1,0:T(8,128)S(1)} %add.19.refs_0_), channel_id=1, source_target_pairs={{8,0},{0,8},{24,16},{16,24},{40,32},{32,40},{56,48},{48,56},{72,64... | collective-permute-start | bytes 1572872 | tf_op jit(solution)/shard_map/ppermute | solution.py:61
  99.7 1.3 copy-start
  106.0 5.2 %copy-start.13 = (f32[256,512]{1,0:T(8,128)S(1)}, f32[256,512]{1,0:T(8,128)}, u32[]{:S(2)}) copy-start(f32[256,512]{1,0:T(8,128)} %transform.8) | copy-start | bytes 1572868
  111.3 16.6 %collective-permute-start.12 = (f32[256,512]{1,0:T(8,128)S(1)}, f32[256,512]{1,0:T(8,128)}, u32[]{:S(2)}, u32[]{:S(2)}) collective-permute-start(f32[256,512]{1,0:T(8,128)S(1)} %copy-done.13), channel_id=1, source_target_pairs={{1,0},{0,1},{3,2},{2,3},{5,4},{4,5},{7,6},{6,7},{9,8},{8,9},{11,10... | collective-permute-start | bytes 1572872 | tf_op jit(solution)/shard_map/ppermute | solution.py:262
  116.3 9.2 %copy-start.3 = (f32[256,512]{1,0:T(8,128)}, f32[256,512]{1,0:T(8,128)S(1)}, u32[]{:S(2)}) copy-start(f32[256,512]{1,0:T(8,128)S(1)} %add.20.refs_1_) | copy-start | bytes 1572868
  116.3 9.2 %copy-start.7 = (f32[256,512]{1,0:T(8,128)}, f32[256,512]{1,0:T(8,128)S(1)}, u32[]{:S(2)}) copy-start(f32[256,512]{1,0:T(8,128)S(1)} %collective-permute-done.6.refs_6_) | copy-start | bytes 1572868
  116.3 23.0 %collective-permute-start.11 = (f32[256,512]{1,0:T(8,128)}, f32[256,512]{1,0:T(8,128)S(1)}, u32[]{:S(2)}, u32[]{:S(2)}) collective-permute-start(f32[256,512]{1,0:T(8,128)} %collective-permute-done.5.refs_4_), channel_id=1, source_target_pairs={{16,0},{24,8},{8,16},{0,24},{48,32},{56,40},{40,48},{32,56},{88,64... | collective-permute-start | bytes 1572872 | tf_op jit(solution)/shard_map/ppermute | solution.py:61
  117.1 22.3 %collective-permute-start.10 = (f32[256,512]{1,0:T(8,128)S(1)}, f32[256,512]{1,0:T(8,128)S(1)}, u32[]{:S(2)}, u32[]{:S(2)}) collective-permute-start(f32[256,512]{1,0:T(8,128)S(1)} %add.20.refs_1_), channel_id=1, source_target_pairs={{96,0},{104,8},{112,16},{120,24},{0,32},{8,40},{16,48},{24,56},{40... | collective-permute-start | bytes 1572872 | tf_op jit(solution)/shard_map/ppermute | solution.py:61
  118.1 21.3 %collective-permute-start.9 = (f32[256,512]{1,0:T(8,128)S(1)}, f32[256,512]{1,0:T(8,128)}, u32[]{:S(2)}, u32[]{:S(2)}) collective-permute-start(f32[256,512]{1,0:T(8,128)S(1)} %add.20.refs_1_), channel_id=1, source_target_pairs={{32,0},{40,8},{48,16},{56,24},{64,32},{72,40},{80,48},{88,56},{96,... | collective-permute-start | bytes 1572872 | tf_op jit(solution)/shard_map/ppermute | solution.py:61
  120.4 19.0 %collective-permute-start.8 = (f32[256,512]{1,0:T(8,128)S(1)}, f32[256,512]{1,0:T(8,128)S(1)}, u32[]{:S(2)}, u32[]{:S(2)}) collective-permute-start(f32[256,512]{1,0:T(8,128)S(1)} %add.20.refs_1_), channel_id=1, source_target_pairs={{8,0},{0,8},{24,16},{16,24},{40,32},{32,40},{56,48},{48,56},{72,64... | collective-permute-start | bytes 1572872 | tf_op jit(solution)/shard_map/ppermute | solution.py:61
  129.2 19.8 %copy-start.1 = (f32[256,512]{1,0:T(8,128)}, f32[256,512]{1,0:T(8,128)S(1)}, u32[]{:S(2)}) copy-start(f32[256,512]{1,0:T(8,128)S(1)} %add.21.refs_0_) | copy-start | bytes 1572868
  139.4 1.2 copy-start.12
  139.4 4.1 %copy-start.8 = (f32[256,512]{1,0:T(8,128)}, f32[256,512]{1,0:T(8,128)S(1)}, u32[]{:S(2)}) copy-start(f32[256,512]{1,0:T(8,128)S(1)} %collective-permute-done.10.refs_7_) | copy-start | bytes 1572868
  139.4 0.8 copy-start.9
  139.4 13.6 %collective-permute-start.16 = (f32[256,512]{1,0:T(8,128)}, f32[256,512]{1,0:T(8,128)S(1)}, u32[]{:S(2)}, u32[]{:S(2)}) collective-permute-start(f32[256,512]{1,0:T(8,128)} %collective-permute-done.9.refs_5_), channel_id=1, source_target_pairs={{16,0},{24,8},{8,16},{0,24},{48,32},{56,40},{40,48},{32,56},{88,64... | collective-permute-start | bytes 1572872 | tf_op jit(solution)/shard_map/ppermute | solution.py:61
  140.2 14.9 %collective-permute-start.15 = (f32[256,512]{1,0:T(8,128)S(1)}, f32[256,512]{1,0:T(8,128)S(1)}, u32[]{:S(2)}, u32[]{:S(2)}) collective-permute-start(f32[256,512]{1,0:T(8,128)S(1)} %add.21.refs_0_), channel_id=1, source_target_pairs={{96,0},{104,8},{112,16},{120,24},{0,32},{8,40},{16,48},{24,56},{40... | collective-permute-start | bytes 1572872 | tf_op jit(solution)/shard_map/ppermute | solution.py:61
  140.6 14.5 %collective-permute-start.14 = (f32[256,512]{1,0:T(8,128)S(1)}, f32[256,512]{1,0:T(8,128)S(1)}, u32[]{:S(2)}, u32[]{:S(2)}) collective-permute-start(f32[256,512]{1,0:T(8,128)S(1)} %add.21.refs_0_), channel_id=1, source_target_pairs={{32,0},{40,8},{48,16},{56,24},{64,32},{72,40},{80,48},{88,56},{96,... | collective-permute-start | bytes 1572872 | tf_op jit(solution)/shard_map/ppermute | solution.py:61
  143.5 11.7 %collective-permute-start.13 = (f32[256,512]{1,0:T(8,128)S(1)}, f32[256,512]{1,0:T(8,128)S(1)}, u32[]{:S(2)}, u32[]{:S(2)}) collective-permute-start(f32[256,512]{1,0:T(8,128)S(1)} %add.21.refs_0_), channel_id=1, source_target_pairs={{8,0},{0,8},{24,16},{16,24},{40,32},{32,40},{56,48},{48,56},{72,64... | collective-permute-start | bytes 1572872 | tf_op jit(solution)/shard_map/ppermute | solution.py:61
  153.0 2.4 copy-start.14
  155.1 5.8 %copy-start.4 = (f32[256,512]{1,0:T(8,128)}, f32[256,512]{1,0:T(8,128)S(1)}, u32[]{:S(2)}) copy-start(f32[256,512]{1,0:T(8,128)S(1)} %collective-permute-done.15.refs_3_) | copy-start | bytes 1572868
  155.2 5.8 %copy-start.5 = (f32[256,512]{1,0:T(8,128)}, f32[256,512]{1,0:T(8,128)S(1)}, u32[]{:S(2)}) copy-start(f32[256,512]{1,0:T(8,128)S(1)} %collective-permute-done.14.refs_2_) | copy-start | bytes 1572868
  155.2 5.8 %copy-start.6 = (f32[256,512]{1,0:T(8,128)}, f32[256,512]{1,0:T(8,128)S(1)}, u32[]{:S(2)}) copy-start(f32[256,512]{1,0:T(8,128)S(1)} %collective-permute-done.13.refs_1_) | copy-start | bytes 1572868
  155.2 13.1 %collective-permute-start.17 = (f32[256,512]{1,0:T(8,128)S(1)}, f32[256,512]{1,0:T(8,128)S(1)}, u32[]{:S(2)}, u32[]{:S(2)}) collective-permute-start(f32[256,512]{1,0:T(8,128)S(1)} %collective-permute-done.14.refs_2_), channel_id=1, source_target_pairs={{16,0},{24,8},{8,16},{0,24},{48,32},{56,40},{40,48},{32,56},{88,64... | collective-permute-start | bytes 1572872 | tf_op jit(solution)/shard_map/ppermute | solution.py:61
  168.3 0.8 copy-start.11
  212.4 7.8 %collective-permute-start.19 = (f32[4,32,256]{2,1,0:T(8,128)}, f32[4,32,256]{2,1,0:T(8,128)S(1)}, u32[]{:S(2)}, u32[]{:S(2)}) collective-permute-start(f32[4,32,256]{2,1,0:T(8,128)} %get-tuple-element.64), channel_id=1, source_target_pairs={{0,32},{8,40},{16,48},{24,56},{32,64},{40,72},{48,80},{56,88},{64,... | collective-permute-start | bytes 393224 | tf_op jit(solution)/shard_map/ppermute | solution.py:66
  213.2 8.4 %collective-permute-start.21 = (f32[4,32,256]{2,1,0:T(8,128)}, f32[4,32,256]{2,1,0:T(8,128)S(1)}, u32[]{:S(2)}, u32[]{:S(2)}) collective-permute-start(f32[4,32,256]{2,1,0:T(8,128)} %get-tuple-element.66), channel_id=1, source_target_pairs={{0,48},{8,56},{16,40},{24,32},{32,80},{40,88},{48,72},{56,64},{64,... | collective-permute-start | bytes 393224 | tf_op jit(solution)/shard_map/ppermute | solution.py:66
  214.6 4.6 %collective-permute-start.20 = (f32[2,32,256]{2,1,0:T(8,128)}, f32[2,32,256]{2,1,0:T(8,128)S(1)}, u32[]{:S(2)}, u32[]{:S(2)}) collective-permute-start(f32[2,32,256]{2,1,0:T(8,128)} %get-tuple-element.65), channel_id=1, source_target_pairs={{0,96},{8,104},{16,112},{24,120},{32,0},{40,8},{48,16},{56,24},{64... | collective-permute-start | bytes 196616 | tf_op jit(solution)/shard_map/ppermute | solution.py:66
  219.2 2.4 copy-start.16
  220.3 1.4 copy-start.15
  221.7 0.6 copy-start.17
  224.1 13.0 %all-to-all-start.3 = ((f32[8,32,256]{2,1,0:T(8,128)}), f32[8,32,256]{2,1,0:T(8,128)S(1)}, u32[]{:S(2)}, u32[]{:S(2)}) async-start(f32[8,32,256]{2,1,0:T(8,128)} %turn.1), calls=%async_computation.3 | async-start | bytes 524288 | tf_op jit(solution)/shard_map/all_to_all | solution.py:265
  228.7 1.5 collective-permute-start.18
  230.1 7.0 %copy-start.19 = (f32[2,32,256]{2,1,0:T(8,128)}, f32[2,32,256]{2,1,0:T(8,128)S(1)}, u32[]{:S(2)}) copy-start(f32[2,32,256]{2,1,0:T(8,128)S(1)} %collective-permute-done.18.refs_1_) | copy-start | bytes 196612
  237.1 0.7 copy-start.10
Sparse Core Ops, SparseCore 0:
  18.1 54.1 all-gather.2

commit v7 on v6

--- a/solution.py
+++ b/solution.py
@@ -13,8 +13,11 @@
 OWN, OTHER, BELOW, ABOVE, ACROSS = range(5)
 EARLY = [(OWN, OWN), (OWN, OTHER), (OWN, BELOW), (OTHER, BELOW), (BELOW, ABOVE)]
 LATE = [(OWN, ACROSS), (OTHER, ACROSS), (BELOW, ACROSS), (ABOVE, ACROSS)]
-ROUTES = [(OWN, [0, 1, 2, 5], []), (OTHER, [3, 6], []), (BELOW, [4, 7], [2, 3]), (ABOVE, [8], [4]),
-          (ACROSS, [], [5, 6, 7, 8])]
+EARLY_ROUTES = [(OWN, [0, 1, 2], []), (OTHER, [3], []), (BELOW, [4], [2, 3]), (ABOVE, [], [4])]
+LATE_ROUTES = [(OWN, [0], []), (OTHER, [1], []), (BELOW, [2], []), (ABOVE, [3], []),
+               (ACROSS, [], [0, 1, 2, 3])]
+ROUTES = EARLY_ROUTES + LATE_ROUTES
+LATE_COST = 20_000_000_000
 
 
 def block_of(y, zl, core):
@@ -67,9 +70,11 @@
 
 
 def column_table():
-    tiles = EARLY + LATE
-    straight = [(target, tiles[k][1]) for target, as_is, _ in ROUTES for k in as_is]
-    turned = [(target, tiles[k][0]) for target, _, to_turn in ROUTES for k in to_turn]
+    straight, turned = [], []
+    for tiles, routes in ((EARLY, EARLY_ROUTES), (LATE, LATE_ROUTES)):
+        for target, as_is, to_turn in routes:
+            straight += [(target, tiles[k][1]) for k in as_is]
+            turned += [(target, tiles[k][0]) for k in to_turn]
     table = np.zeros((len(places()), len(straight + turned)), np.int32)
     for slot, (target, column) in enumerate(straight + turned):
         for at in places():
@@ -131,14 +136,12 @@
     )(jnp.stack([place, half]), part, orbitals)
 
 
-def gram_kernel(pairs, chunks, more, ahead, *refs):
+def gram_kernel(pairs, chunks, more, *refs):
     left_rows, right_rows = sides(pairs)
     count = (1 + max(left_rows + right_rows)) * chunks
     blocks, refs = refs[:count], refs[count:]
     if more:
         so_far, refs = refs[0], refs[1:]
-    if ahead:
-        before, refs = refs[0], refs[1:]
     out, lefts, rights = refs
     depth = blocks[0].shape[1]
     for k, block in enumerate(blocks):
@@ -152,30 +155,26 @@
                     ref[rows.index(row), :, piece * depth : (piece + 1) * depth] = value
 
     shares, _, part, width = out.shape
-    if ahead:
-        out[:, :ahead] = before[...]
-
     for t, (left, right) in enumerate(pairs):
         tile = dot(lefts[left_rows.index(left)], rights[right_rows.index(right)])
         tile = tile.reshape(shares, part, width)
-        out[:, ahead + t] = so_far[:, t] + tile if more else tile
+        out[:, t] = so_far[:, t] + tile if more else tile
 
 
 def sides(pairs):
     return sorted({left for left, _ in pairs}), sorted({right for _, right in pairs})
 
 
-def gram(blocks, pairs, shares, so_far=None, before=None):
+def gram(blocks, pairs, shares, so_far=None, cost=0):
     rows, depth = blocks[0][0].shape
     chunks = len(blocks[0])
     flat = [chunk for block in blocks for chunk in block]
     more = so_far is not None
-    ahead = 0 if before is None else before.shape[1]
-    tiles = ahead + len(pairs)
+    tiles = len(pairs)
     left_rows, right_rows = sides(pairs)
-    inputs = flat + ([so_far] if more else []) + ([before] if ahead else [])
+    inputs = flat + ([so_far] if more else [])
     return pl.pallas_call(
-        functools.partial(gram_kernel, pairs, chunks, more, ahead),
+        functools.partial(gram_kernel, pairs, chunks, more),
         in_specs=[pl.BlockSpec(memory_space=pltpu.VMEM)] * len(inputs),
         out_specs=pl.BlockSpec(memory_space=pltpu.VMEM),
         scratch_shapes=[
@@ -183,9 +182,7 @@
             for side in (left_rows, right_rows)
         ],
         out_shape=jax.ShapeDtypeStruct((shares, tiles, rows // shares, rows), jnp.float32),
-        cost_estimate=pl.CostEstimate(
-            flops=0, bytes_accessed=0, transcendentals=0
-        ),
+        cost_estimate=pl.CostEstimate(flops=cost, bytes_accessed=0, transcendentals=0),
         name="gram",
     )(*inputs)
 
@@ -202,14 +199,14 @@
     )(*tables, *inputs)
 
 
-def summed(moved):
+def summed(moved, routes):
     def kernel(moved_ref, *outs):
-        for out, (_, as_is, to_turn) in zip(outs, ROUTES):
+        for out, (_, as_is, to_turn) in zip(outs, routes):
             for k, tile in enumerate(as_is + to_turn):
                 out[k] = moved_ref[:, tile].sum(0)
 
     shape = moved.shape[2:]
-    outputs = [(len(as_is + to_turn),) + shape for _, as_is, to_turn in ROUTES]
+    outputs = [(len(as_is + to_turn),) + shape for _, as_is, to_turn in routes]
     return in_vmem(kernel, [moved], outputs, "sum")
 
 
@@ -306,13 +303,19 @@
     known_2 = [(own_2,), (other_2,), (below_2,), (above_2,)]
     early = gram(known_2, EARLY, shares, early)
     late = gram(known + [(across_0, across_1)], LATE, shares)
+    early_moved = over_col(early)
     across_2, late, early = together(across_2, late, early)
-    tiles = gram(known_2 + [(across_2,)], LATE, shares, late, early)
-
-    slabs = [
-        delivered(slab, RELATED[target]) if target else slab
-        for slab, (target, _, _) in zip(summed(over_col(tiles)), ROUTES)
-    ]
+    late = gram(known_2 + [(across_2,)], LATE, shares, late, LATE_COST)
+    early_moved, late = together(early_moved, late)
+
+    def sent_home(moved, routes):
+        return [
+            delivered(slab, RELATED[target]) if target else slab
+            for slab, (target, _, _) in zip(summed(moved, routes), routes)
+        ]
+
+    late_moved, *slabs = together(over_col(late), *sent_home(early_moved, EARLY_ROUTES))
+    slabs += sent_home(late_moved, LATE_ROUTES)
     straight = [range(len(as_is)) for _, as_is, _ in ROUTES]
     to_turn = [range(len(as_is), len(as_is + to_turn)) for _, as_is, to_turn in ROUTES]
 

time: 248 us -> 242 us (0.976)
  blocking collectives: 36 us -> 0 us
  waiting for transfers between devices: 79.5 us -> 97.1 us
  starting transfers between devices: 42.1 us -> 52.9 us
    all_to_all x1 -> x0, blocking collectives: 36 us -> none  [over_col(): return lax.all_to_all(tiles, 'col', split_axis=0, concat_axis=0, tiled=True)]
    all_to_all x1 -> x3, starting transfers between devices: 4.53 us -> 13.1 us  [over_col(): return lax.all_to_all(tiles, 'col', split_axis=0, concat_axis=0, tiled=True)]
    all_to_all x1 -> x3, waiting for transfers between devices: 6.97 us -> 15.1 us  [over_col(): return lax.all_to_all(tiles, 'col', split_axis=0, concat_axis=0, tiled=True)]
    ppermute x4 -> x7, waiting for transfers between devices: 5.28 us -> 10.9 us  [delivered(): return lax.ppermute(value, 'blk', route)]
    ppermute x12, waiting for transfers between devices: 19.5 us -> 23.2 us  [fetched(): return lax.ppermute(value, 'blk', route)]
    ppermute x4 -> x7, starting transfers between devices: 4.1 us -> 6.54 us  [delivered(): return lax.ppermute(value, 'blk', route)]
    unnamed x40 -> x44, local copies, waits for them, and re-layouts: 3.78 us -> 5.41 us
    pallas_call x3 -> x4, Pallas kernels: 6.53 us -> 8 us  [in_vmem(): pl.pallas_call(kernel, in_specs=[pl.BlockSpec(memory_space=pltpu.SMEM)] *...]
  transfers between devices with their start and end apart: 26 -> 31, of which waited for: 12 -> 14; matrix products, arithmetic and copies ran while one was open for 6% -> 6% of each run, Pallas kernels for 18% -> 21%
where the time goes in v7:
time: 242 us; the launch traced here: 241 us
  waiting for transfers between devices  97.1 us (40%)
  Pallas kernels  57.3 us (24%)
  starting transfers between devices  52.9 us (22%)
  local copies, waits for them, and re-layouts  14.4 us (6%)
  between operations  13.7 us (6%)
  other arithmetic  5.72 us (2%)
    all_to_all x2, waiting for transfers between devices, over_x(): lax.all_to_all(part, 'col', split_axis=0, concat_axis=0, tiled=True, axis...  45.1 us
    pallas_call x6, Pallas kernels, transformed(): pl.pallas_call(functools.partial(transform_kernel, index), in_specs=[pl.B...  30.3 us
    ppermute x12, waiting for transfers between devices, fetched(): return lax.ppermute(value, 'blk', route)  23.2 us
    pallas_call x4, Pallas kernels, gram(): pl.pallas_call(functools.partial(gram_kernel, pairs, chunks, more), in_sp...  19 us
    all_to_all x3, waiting for transfers between devices, over_col(): return lax.all_to_all(tiles, 'col', split_axis=0, concat_axis=0, tiled=True)  15.1 us
    all_to_all x3, starting transfers between devices, over_col(): return lax.all_to_all(tiles, 'col', split_axis=0, concat_axis=0, tiled=True)  13.1 us
    ppermute x12, starting transfers between devices, fetched(): return lax.ppermute(value, 'blk', route)  11.2 us
    ppermute x7, waiting for transfers between devices, delivered(): return lax.ppermute(value, 'blk', route)  10.9 us
  transfers between devices with their start and end apart: 31, of which 14 were waited for; matrix products, arithmetic and copies ran while one was open for 6% of the time, Pallas kernels for 21%

profile of v7, /device:TPU:0, one launch (start us, length us, event | category | flops | bytes accessed | tf_op | source)
XLA Modules:
  0.0 241.1 jit_solution(10890013739285306279)
XLA Ops:
  6.5 1.6 collective-permute-start.2
  8.1 2.7 %collective-permute-start.1 = (f32[64,512]{1,0:T(8,128)}, f32[64,512]{1,0:T(8,128)S(1)}, u32[]{:S(2)}, u32[]{:S(2)}) collective-permute-start(f32[64,512]{1,0:T(8,128)} %bitcast.25), channel_id=1, source_target_pairs={{4,0},{5,1},{6,2},{7,3},{0,4},{1,5},{2,6},{3,7},{12,8},{13,9},{14,... | collective-permute-start | bytes 393224 | tf_op jit(solution)/shard_map/ppermute | solution.py:268
  10.8 1.4 collective-permute-start
  12.3 4.6 %slice.9 = f32[8,256,512]{2,1,0:T(8,128)} slice(f32[12,256,512]{2,1,0:T(8,128)} %bitcast.22), slice={[0:8], [0:256], [0:512]} | slice | bytes 8388608 | tf_op jit(solution)/shard_map/slice | solution.py:269
  17.9 4.8 %all-to-all-start = ((f32[8,256,512]{2,1,0:T(8,128)}), f32[8,256,512]{2,1,0:T(8,128)}, u32[]{:S(2)}, u32[]{:S(2)}) async-start(f32[8,256,512]{2,1,0:T(8,128)} %slice.9), calls=%async_computation | async-start | bytes 8388608 | tf_op jit(solution)/shard_map/all_to_all | solution.py:253
  22.8 3.1 %slice.8 = f32[4,256,512]{2,1,0:T(8,128)} slice(f32[12,256,512]{2,1,0:T(8,128)} %bitcast.23), slice={[8:12], [0:256], [0:512]} | slice | bytes 4194304 | tf_op jit(solution)/shard_map/slice | solution.py:273
  25.9 45.1 %all-to-all-done = f32[8,256,512]{2,1,0:T(8,128)} async-done(((f32[8,256,512]{2,1,0:T(8,128)}), f32[8,256,512]{2,1,0:T(8,128)}, u32[]{:S(2)}, u32[]{:S(2)}) %all-to-all-start) | async-done | bytes 4194336 | tf_op jit(solution)/shard_map/all_to_all | solution.py:253
  71.1 3.6 %all-to-all-start.1 = ((f32[4,256,512]{2,1,0:T(8,128)}), f32[4,256,512]{2,1,0:T(8,128)S(1)}, u32[]{:S(2)}, u32[]{:S(2)}) async-start(f32[4,256,512]{2,1,0:T(8,128)} %slice.8), calls=%async_computation.1 | async-start | bytes 4194304 | tf_op jit(solution)/shard_map/all_to_all | solution.py:253
  75.3 5.1 %transform.7 = f32[256,512]{1,0:T(8,128)} custom-call(s32[2]{0:T(128)} %pad_add_fusion.1.scalars, f32[4,2,256,512]{3,2,1,0:T(8,128)} %bitcast.5.part, f32[16,4,64,512]{3,2,1,0:T(8,128)} %bitcast.14), custom_call_target="tpu_custom_call" | custom-call | tf_op jit(solution)/shard_map/transform/pallas_call | solution.py:124
  80.4 3.9 %collective-permute-start.3 = (f32[256,512]{1,0:T(8,128)}, f32[256,512]{1,0:T(8,128)S(1)}, u32[]{:S(2)}, u32[]{:S(2)}) collective-permute-start(f32[256,512]{1,0:T(8,128)} %transform.7), channel_id=1, source_target_pairs={{1,0},{0,1},{3,2},{2,3},{5,4},{4,5},{7,6},{6,7},{9,8},{8,9},{11,10... | collective-permute-start | bytes 1572872 | tf_op jit(solution)/shard_map/ppermute | solution.py:259
  84.9 5.0 %transform.10 = f32[256,512]{1,0:T(8,128)} custom-call(s32[2]{0:T(128)} %pad_add_fusion.1.scalars, f32[4,2,256,512]{3,2,1,0:T(8,128)} %bitcast.5.part, f32[16,4,64,512]{3,2,1,0:T(8,128)} %bitcast.15), custom_call_target="tpu_custom_call" | custom-call | tf_op jit(solution)/shard_map/transform/pallas_call | solution.py:124
  89.9 5.0 %transform.6 = f32[256,512]{1,0:T(8,128)} custom-call(s32[2]{0:T(128)} %pad_add_fusion.scalars, f32[4,2,256,512]{3,2,1,0:T(8,128)} %bitcast.5.part, f32[16,4,64,512]{3,2,1,0:T(8,128)} %bitcast.16), custom_call_target="tpu_custom_call" | custom-call | tf_op jit(solution)/shard_map/transform/pallas_call | solution.py:124
  95.1 1.1 add.19.refs_0_
  96.3 1.7 collective-permute-start.6
  97.9 1.6 collective-permute-start.5
  99.6 1.3 copy-done
  100.9 5.1 %transform.8 = f32[256,512]{1,0:T(8,128)} custom-call(s32[2]{0:T(128)} %pad_add_fusion.1.scalars, f32[4,1,256,512]{3,2,1,0:T(8,128)} %bitcast.20, f32[16,4,64,512]{3,2,1,0:T(8,128)} %bitcast.17), custom_call_target="tpu_custom_call" | custom-call | tf_op jit(solution)/shard_map/transform/pallas_call | solution.py:124
  105.9 5.1 %transform.9 = f32[256,512]{1,0:T(8,128)} custom-call(s32[2]{0:T(128)} %pad_add_fusion.scalars, f32[4,2,256,512]{3,2,1,0:T(8,128)} %bitcast.5.part, f32[16,4,64,512]{3,2,1,0:T(8,128)} %bitcast.18), custom_call_target="tpu_custom_call" | custom-call | tf_op jit(solution)/shard_map/transform/pallas_call | solution.py:124
  111.0 3.8 %collective-permute-start.12 = (f32[256,512]{1,0:T(8,128)}, f32[256,512]{1,0:T(8,128)}, u32[]{:S(2)}, u32[]{:S(2)}) collective-permute-start(f32[256,512]{1,0:T(8,128)} %transform.8), channel_id=1, source_target_pairs={{1,0},{0,1},{3,2},{2,3},{5,4},{4,5},{7,6},{6,7},{9,8},{8,9},{11,10... | collective-permute-start | bytes 1572872 | tf_op jit(solution)/shard_map/ppermute | solution.py:259
  114.8 1.3 add.20.refs_1_
  117.9 2.4 collective-permute-start.9
  120.3 5.0 %transform.11 = f32[256,512]{1,0:T(8,128)} custom-call(s32[2]{0:T(128)} %pad_add_fusion.scalars, f32[4,1,256,512]{3,2,1,0:T(8,128)} %bitcast.21, f32[16,4,64,512]{3,2,1,0:T(8,128)} %bitcast.19), custom_call_target="tpu_custom_call" | custom-call | tf_op jit(solution)/shard_map/transform/pallas_call | solution.py:124
  125.4 2.5 %collective-permute-done.12 = f32[256,512]{1,0:T(8,128)} collective-permute-done((f32[256,512]{1,0:T(8,128)}, f32[256,512]{1,0:T(8,128)}, u32[]{:S(2)}, u32[]{:S(2)}) %collective-permute-start.12) | collective-permute-done | bytes 524320 | tf_op jit(solution)/shard_map/ppermute | solution.py:259
  127.8 1.3 add.21.refs_0_
  129.1 10.3 %collective-permute-done.11.refs_8_ = f32[256,512]{1,0:T(8,128)} collective-permute-done((f32[256,512]{1,0:T(8,128)}, f32[256,512]{1,0:T(8,128)}, u32[]{:S(2)}, u32[]{:S(2)}) %collective-permute-start.11) | collective-permute-done | bytes 524320 | tf_op jit(solution)/shard_map/ppermute | solution.py:64
  140.4 2.8 %collective-permute-start.14 = (f32[256,512]{1,0:T(8,128)S(1)}, f32[256,512]{1,0:T(8,128)S(1)}, u32[]{:S(2)}, u32[]{:S(2)}) collective-permute-start(f32[256,512]{1,0:T(8,128)S(1)} %add.21.refs_0_), channel_id=1, source_target_pairs={{32,0},{40,8},{48,16},{56,24},{64,32},{72,40},{80,48},{88,56},{96,... | collective-permute-start | bytes 1572872 | tf_op jit(solution)/shard_map/ppermute | solution.py:64
  143.2 5.4 %gram.4.refs_4_ = f32[8,5,32,256]{3,2,1,0:T(8,128)} custom-call(f32[256,512]{1,0:T(8,128)} %copy-done.2, f32[256,512]{1,0:T(8,128)} %copy-done.3, f32[256,512]{1,0:T(8,128)} %collective-permute-done.4.refs_2_, f32[256,512]{1,0:T(8,128)} %collective-permute-done.8.refs_3_, f32[256,512]{1,0:T(8,128)} %collective-permute-done.5.refs_4_, f32[256,512]{1,0:T(8,128)} %copy-done.8, ...), custom_call_target="tpu_custom_call" | custom-call | tf_op jit(solution)/shard_map/gram/pallas_call | solution.py:176
  148.7 4.2 %collective-permute-done.16.refs_9_ = f32[256,512]{1,0:T(8,128)S(1)} collective-permute-done((f32[256,512]{1,0:T(8,128)S(1)}, f32[256,512]{1,0:T(8,128)S(1)}, u32[]{:S(2)}, u32[]{:S(2)}) %collective-permute-start.16) | collective-permute-done | bytes 524320 | tf_op jit(solution)/shard_map/ppermute | solution.py:64
  152.8 2.2 collective-permute-done.15.refs_3_
  156.0 4.3 %gram.5 = f32[8,5,32,256]{3,2,1,0:T(8,128)} custom-call(f32[256,512]{1,0:T(8,128)} %copy-done.5, f32[256,512]{1,0:T(8,128)} %collective-permute-done.13.refs_1_, f32[256,512]{1,0:T(8,128)} %copy-done.12, f32[256,512]{1,0:T(8,128)} %copy-done.10, f32[8,5,32,256]{3,2,1,0:T(8,128)} %gram.4.refs_4_), custom_call_target="tpu_custom_call" | custom-call | tf_op jit(solution)/shard_map/gram/pallas_call | solution.py:176
  160.3 5.1 %all-to-all-start.2 = ((f32[8,5,32,256]{3,2,1,0:T(8,128)}), f32[8,5,32,256]{3,2,1,0:T(8,128)S(1)}, u32[]{:S(2)}, u32[]{:S(2)}) async-start(f32[8,5,32,256]{3,2,1,0:T(8,128)} %gram.5), calls=%async_computation.2 | async-start | bytes 2621440 | tf_op jit(solution)/shard_map/all_to_all | solution.py:262
  165.4 5.3 %gram.6.refs_5_ = f32[8,4,32,256]{3,2,1,0:T(8,128)} custom-call(f32[256,512]{1,0:T(8,128)} %copy-done.2, f32[256,512]{1,0:T(8,128)} %copy-done.3, f32[256,512]{1,0:T(8,128)} %collective-permute-done.4.refs_2_, f32[256,512]{1,0:T(8,128)} %collective-permute-done.8.refs_3_, f32[256,512]{1,0:T(8,128)} %collective-permute-done.5.refs_4_, f32[256,512]{1,0:T(8,128)} %copy-done.8, ...), custom_call_target="tpu_custom_call" | custom-call | tf_op jit(solution)/shard_map/gram/pallas_call | solution.py:176
  170.7 6.5 %collective-permute-done.17.refs_4_ = f32[256,512]{1,0:T(8,128)S(1)} collective-permute-done((f32[256,512]{1,0:T(8,128)S(1)}, f32[256,512]{1,0:T(8,128)S(1)}, u32[]{:S(2)}, u32[]{:S(2)}) %collective-permute-start.17) | collective-permute-done | bytes 524320 | tf_op jit(solution)/shard_map/ppermute | solution.py:64
  178.0 4.0 %gram.7 = f32[8,4,32,256]{3,2,1,0:T(8,128)} custom-call(f32[256,512]{1,0:T(8,128)} %copy-done.5, f32[256,512]{1,0:T(8,128)} %collective-permute-done.13.refs_1_, f32[256,512]{1,0:T(8,128)} %copy-done.12, f32[256,512]{1,0:T(8,128)} %copy-done.10, f32[256,512]{1,0:T(8,128)} %copy-done.21, f32[8,4,32,256]{3,2,1,0:T(8,128)} %gram.6.refs_5_), custom_call_target="tpu_custom_call" | custom-call | flops 20000000000 | tf_op jit(solution)/shard_map/gram/pallas_call | solution.py:176
  182.0 4.6 %all-to-all-done.2.moved_ref = f32[8,5,32,256]{3,2,1,0:T(8,128)S(1)} async-done(((f32[8,5,32,256]{3,2,1,0:T(8,128)}), f32[8,5,32,256]{3,2,1,0:T(8,128)S(1)}, u32[]{:S(2)}, u32[]{:S(2)}) %all-to-all-start.2) | async-done | bytes 1310752 | tf_op jit(solution)/shard_map/all_to_all | solution.py:262
  186.7 3.8 %all-to-all-start.3 = ((f32[8,4,32,256]{3,2,1,0:T(8,128)}), f32[8,4,32,256]{3,2,1,0:T(8,128)S(1)}, u32[]{:S(2)}, u32[]{:S(2)}) async-start(f32[8,4,32,256]{3,2,1,0:T(8,128)} %gram.7), calls=%async_computation.3 | async-start | bytes 2097152 | tf_op jit(solution)/shard_map/all_to_all | solution.py:262
  190.4 2.1 sum.2
  192.8 3.0 %collective-permute-start.20 = (f32[1,32,256]{2,1,0:T(8,128)}, f32[1,32,256]{2,1,0:T(8,128)S(1)}, u32[]{:S(2)}, u32[]{:S(2)}) collective-permute-start(f32[1,32,256]{2,1,0:T(8,128)} %get-tuple-element.76), channel_id=1, source_target_pairs={{0,96},{8,104},{16,112},{24,120},{32,0},{40,8},{48,16},{56,24},{64... | collective-permute-start | bytes 98312 | tf_op jit(solution)/shard_map/ppermute | solution.py:69
  195.7 1.9 collective-permute-done.20.refs_1_
  198.5 7.5 %all-to-all-done.3.moved_ref = f32[8,4,32,256]{3,2,1,0:T(8,128)S(1)} async-done(((f32[8,4,32,256]{3,2,1,0:T(8,128)}), f32[8,4,32,256]{3,2,1,0:T(8,128)S(1)}, u32[]{:S(2)}, u32[]{:S(2)}) %all-to-all-start.3) | async-done | bytes 1048608 | tf_op jit(solution)/shard_map/all_to_all | solution.py:262
  207.0 2.0 sum.3
  209.0 7.3 %collective-permute-done.24.refs_2_ = f32[4,32,256]{2,1,0:T(8,128)S(1)} collective-permute-done((f32[4,32,256]{2,1,0:T(8,128)}, f32[4,32,256]{2,1,0:T(8,128)S(1)}, u32[]{:S(2)}, u32[]{:S(2)}) %collective-permute-start.24) | collective-permute-done | bytes 131104 | tf_op jit(solution)/shard_map/ppermute | solution.py:69
  217.0 1.8 turn.1
  218.8 4.2 %all-to-all-start.4 = ((f32[8,32,256]{2,1,0:T(8,128)}), f32[8,32,256]{2,1,0:T(8,128)S(1)}, u32[]{:S(2)}, u32[]{:S(2)}) async-start(f32[8,32,256]{2,1,0:T(8,128)} %turn.1), calls=%async_computation.4 | async-start | bytes 524288 | tf_op jit(solution)/shard_map/all_to_all | solution.py:262
  223.0 3.2 %collective-permute-start.23 = (f32[1,32,256]{2,1,0:T(8,128)}, f32[1,32,256]{2,1,0:T(8,128)S(1)}, u32[]{:S(2)}, u32[]{:S(2)}) collective-permute-start(f32[1,32,256]{2,1,0:T(8,128)} %get-tuple-element.84), channel_id=1, source_target_pairs={{0,96},{8,104},{16,112},{24,120},{32,0},{40,8},{48,16},{56,24},{64... | collective-permute-start | bytes 98312 | tf_op jit(solution)/shard_map/ppermute | solution.py:69
  226.3 1.3 dynamic-slice_bitcast_fusion.table_ref
  228.4 3.0 %all-to-all-done.4.refs_7_ = f32[8,32,256]{2,1,0:T(8,128)S(1)} async-done(((f32[8,32,256]{2,1,0:T(8,128)}), f32[8,32,256]{2,1,0:T(8,128)S(1)}, u32[]{:S(2)}, u32[]{:S(2)}) %all-to-all-start.4) | async-done | bytes 262176 | tf_op jit(solution)/shard_map/all_to_all | solution.py:262
  232.1 2.2 assemble.1
  (82 shorter events, 11.3 us)
Async XLA Ops:
  6.5 68.8 %all-gather.3.cloned.1.call-start = ((), (), s32[]{:S(2)}) async-start(), calls=%async_computation.5 | async-start | bytes 8912896 | tf_op jit(solution)/shard_map/all_gather | solution.py:272
  6.5 10.3 %collective-permute-start.2 = (f32[64,512]{1,0:T(8,128)}, f32[64,512]{1,0:T(8,128)S(1)}, u32[]{:S(2)}, u32[]{:S(2)}) collective-permute-start(f32[64,512]{1,0:T(8,128)} %bitcast.24), channel_id=1, source_target_pairs={{6,0},{7,1},{0,2},{1,3},{2,4},{3,5},{4,6},{5,7},{14,8},{15,9},{8,1... | collective-permute-start | bytes 393224 | tf_op jit(solution)/shard_map/ppermute | solution.py:268
  8.1 9.0 %collective-permute-start.1 = (f32[64,512]{1,0:T(8,128)}, f32[64,512]{1,0:T(8,128)S(1)}, u32[]{:S(2)}, u32[]{:S(2)}) collective-permute-start(f32[64,512]{1,0:T(8,128)} %bitcast.25), channel_id=1, source_target_pairs={{4,0},{5,1},{6,2},{7,3},{0,4},{1,5},{2,6},{3,7},{12,8},{13,9},{14,... | collective-permute-start | bytes 393224 | tf_op jit(solution)/shard_map/ppermute | solution.py:268
  10.8 6.2 %collective-permute-start = (f32[64,512]{1,0:T(8,128)}, f32[64,512]{1,0:T(8,128)S(1)}, u32[]{:S(2)}, u32[]{:S(2)}) collective-permute-start(f32[64,512]{1,0:T(8,128)} %bitcast.26), channel_id=1, source_target_pairs={{2,0},{3,1},{4,2},{5,3},{6,4},{7,5},{0,6},{1,7},{10,8},{11,9},{12,... | collective-permute-start | bytes 393224 | tf_op jit(solution)/shard_map/ppermute | solution.py:268
  12.3 4.8 %copy-start.15 = (f32[512,64]{0,1:T(8,128)S(1)}, f32[512,64]{0,1:T(8,128)}, u32[]{:S(2)}) copy-start(f32[512,64]{0,1:T(8,128)} %param.4) | copy-start | bytes 393220
  17.9 53.1 %all-to-all-start = ((f32[8,256,512]{2,1,0:T(8,128)}), f32[8,256,512]{2,1,0:T(8,128)}, u32[]{:S(2)}, u32[]{:S(2)}) async-start(f32[8,256,512]{2,1,0:T(8,128)} %slice.9), calls=%async_computation | async-start | bytes 8388608 | tf_op jit(solution)/shard_map/all_to_all | solution.py:253
  71.1 28.5 %all-to-all-start.1 = ((f32[4,256,512]{2,1,0:T(8,128)}), f32[4,256,512]{2,1,0:T(8,128)S(1)}, u32[]{:S(2)}, u32[]{:S(2)}) async-start(f32[4,256,512]{2,1,0:T(8,128)} %slice.8), calls=%async_computation.1 | async-start | bytes 4194304 | tf_op jit(solution)/shard_map/all_to_all | solution.py:253
  80.4 14.7 %collective-permute-start.3 = (f32[256,512]{1,0:T(8,128)}, f32[256,512]{1,0:T(8,128)S(1)}, u32[]{:S(2)}, u32[]{:S(2)}) collective-permute-start(f32[256,512]{1,0:T(8,128)} %transform.7), channel_id=1, source_target_pairs={{1,0},{0,1},{3,2},{2,3},{5,4},{4,5},{7,6},{6,7},{9,8},{8,9},{11,10... | collective-permute-start | bytes 1572872 | tf_op jit(solution)/shard_map/ppermute | solution.py:259
  95.0 19.8 %collective-permute-start.7 = (f32[256,512]{1,0:T(8,128)}, f32[256,512]{1,0:T(8,128)}, u32[]{:S(2)}, u32[]{:S(2)}) collective-permute-start(f32[256,512]{1,0:T(8,128)} %transform.10), channel_id=1, source_target_pairs={{1,0},{0,1},{3,2},{2,3},{5,4},{4,5},{7,6},{6,7},{9,8},{8,9},{11,10... | collective-permute-start | bytes 1572872 | tf_op jit(solution)/shard_map/ppermute | solution.py:259
  96.2 14.7 %copy-start.2 = (f32[256,512]{1,0:T(8,128)}, f32[256,512]{1,0:T(8,128)S(1)}, u32[]{:S(2)}) copy-start(f32[256,512]{1,0:T(8,128)S(1)} %add.19.refs_0_) | copy-start | bytes 1572868
  96.3 19.9 %collective-permute-start.6 = (f32[256,512]{1,0:T(8,128)S(1)}, f32[256,512]{1,0:T(8,128)S(1)}, u32[]{:S(2)}, u32[]{:S(2)}) collective-permute-start(f32[256,512]{1,0:T(8,128)S(1)} %add.19.refs_0_), channel_id=1, source_target_pairs={{96,0},{104,8},{112,16},{120,24},{0,32},{8,40},{16,48},{24,56},{40... | collective-permute-start | bytes 1572872 | tf_op jit(solution)/shard_map/ppermute | solution.py:64
  97.9 18.2 %collective-permute-start.5 = (f32[256,512]{1,0:T(8,128)S(1)}, f32[256,512]{1,0:T(8,128)}, u32[]{:S(2)}, u32[]{:S(2)}) collective-permute-start(f32[256,512]{1,0:T(8,128)S(1)} %add.19.refs_0_), channel_id=1, source_target_pairs={{32,0},{40,8},{48,16},{56,24},{64,32},{72,40},{80,48},{88,56},{96,... | collective-permute-start | bytes 1572872 | tf_op jit(solution)/shard_map/ppermute | solution.py:64
  99.6 16.6 %collective-permute-start.4 = (f32[256,512]{1,0:T(8,128)S(1)}, f32[256,512]{1,0:T(8,128)}, u32[]{:S(2)}, u32[]{:S(2)}) collective-permute-start(f32[256,512]{1,0:T(8,128)S(1)} %add.19.refs_0_), channel_id=1, source_target_pairs={{8,0},{0,8},{24,16},{16,24},{40,32},{32,40},{56,48},{48,56},{72,64... | collective-permute-start | bytes 1572872 | tf_op jit(solution)/shard_map/ppermute | solution.py:64
  99.6 1.3 copy-start
  111.0 16.8 %collective-permute-start.12 = (f32[256,512]{1,0:T(8,128)}, f32[256,512]{1,0:T(8,128)}, u32[]{:S(2)}, u32[]{:S(2)}) collective-permute-start(f32[256,512]{1,0:T(8,128)} %transform.8), channel_id=1, source_target_pairs={{1,0},{0,1},{3,2},{2,3},{5,4},{4,5},{7,6},{6,7},{9,8},{8,9},{11,10... | collective-permute-start | bytes 1572872 | tf_op jit(solution)/shard_map/ppermute | solution.py:259
  116.1 9.2 %copy-start.3 = (f32[256,512]{1,0:T(8,128)}, f32[256,512]{1,0:T(8,128)S(1)}, u32[]{:S(2)}) copy-start(f32[256,512]{1,0:T(8,128)S(1)} %add.20.refs_1_) | copy-start | bytes 1572868
  116.1 9.2 %copy-start.6 = (f32[256,512]{1,0:T(8,128)}, f32[256,512]{1,0:T(8,128)S(1)}, u32[]{:S(2)}) copy-start(f32[256,512]{1,0:T(8,128)S(1)} %collective-permute-done.6.refs_6_) | copy-start | bytes 1572868
  116.2 23.3 %collective-permute-start.11 = (f32[256,512]{1,0:T(8,128)}, f32[256,512]{1,0:T(8,128)}, u32[]{:S(2)}, u32[]{:S(2)}) collective-permute-start(f32[256,512]{1,0:T(8,128)} %collective-permute-done.5.refs_4_), channel_id=1, source_target_pairs={{16,0},{24,8},{8,16},{0,24},{48,32},{56,40},{40,48},{32,56},{88,64... | collective-permute-start | bytes 1572872 | tf_op jit(solution)/shard_map/ppermute | solution.py:64
  116.8 22.6 %collective-permute-start.10 = (f32[256,512]{1,0:T(8,128)S(1)}, f32[256,512]{1,0:T(8,128)S(1)}, u32[]{:S(2)}, u32[]{:S(2)}) collective-permute-start(f32[256,512]{1,0:T(8,128)S(1)} %add.20.refs_1_), channel_id=1, source_target_pairs={{96,0},{104,8},{112,16},{120,24},{0,32},{8,40},{16,48},{24,56},{40... | collective-permute-start | bytes 1572872 | tf_op jit(solution)/shard_map/ppermute | solution.py:64
  117.9 21.6 %collective-permute-start.9 = (f32[256,512]{1,0:T(8,128)S(1)}, f32[256,512]{1,0:T(8,128)S(1)}, u32[]{:S(2)}, u32[]{:S(2)}) collective-permute-start(f32[256,512]{1,0:T(8,128)S(1)} %add.20.refs_1_), channel_id=1, source_target_pairs={{32,0},{40,8},{48,16},{56,24},{64,32},{72,40},{80,48},{88,56},{96,... | collective-permute-start | bytes 1572872 | tf_op jit(solution)/shard_map/ppermute | solution.py:64
  120.3 19.2 %collective-permute-start.8 = (f32[256,512]{1,0:T(8,128)S(1)}, f32[256,512]{1,0:T(8,128)}, u32[]{:S(2)}, u32[]{:S(2)}) collective-permute-start(f32[256,512]{1,0:T(8,128)S(1)} %add.20.refs_1_), channel_id=1, source_target_pairs={{8,0},{0,8},{24,16},{16,24},{40,32},{32,40},{56,48},{48,56},{72,64... | collective-permute-start | bytes 1572872 | tf_op jit(solution)/shard_map/ppermute | solution.py:64
  129.1 19.6 %copy-start.5 = (f32[256,512]{1,0:T(8,128)}, f32[256,512]{1,0:T(8,128)S(1)}, u32[]{:S(2)}) copy-start(f32[256,512]{1,0:T(8,128)S(1)} %add.21.refs_0_) | copy-start | bytes 1572868
  139.5 3.8 %copy-start.7 = (f32[256,512]{1,0:T(8,128)}, f32[256,512]{1,0:T(8,128)S(1)}, u32[]{:S(2)}) copy-start(f32[256,512]{1,0:T(8,128)S(1)} %collective-permute-done.10.refs_7_) | copy-start | bytes 1572868
  139.5 3.8 %copy-start.8 = (f32[256,512]{1,0:T(8,128)}, f32[256,512]{1,0:T(8,128)S(1)}, u32[]{:S(2)}) copy-start(f32[256,512]{1,0:T(8,128)S(1)} %collective-permute-done.9.refs_5_) | copy-start | bytes 1572868
  139.5 13.3 %collective-permute-start.16 = (f32[256,512]{1,0:T(8,128)S(1)}, f32[256,512]{1,0:T(8,128)S(1)}, u32[]{:S(2)}, u32[]{:S(2)}) collective-permute-start(f32[256,512]{1,0:T(8,128)S(1)} %collective-permute-done.9.refs_5_), channel_id=1, source_target_pairs={{16,0},{24,8},{8,16},{0,24},{48,32},{56,40},{40,48},{32,56},{88,64... | collective-permute-start | bytes 1572872 | tf_op jit(solution)/shard_map/ppermute | solution.py:64
  140.0 15.0 %collective-permute-start.15 = (f32[256,512]{1,0:T(8,128)S(1)}, f32[256,512]{1,0:T(8,128)S(1)}, u32[]{:S(2)}, u32[]{:S(2)}) collective-permute-start(f32[256,512]{1,0:T(8,128)S(1)} %add.21.refs_0_), channel_id=1, source_target_pairs={{96,0},{104,8},{112,16},{120,24},{0,32},{8,40},{16,48},{24,56},{40... | collective-permute-start | bytes 1572872 | tf_op jit(solution)/shard_map/ppermute | solution.py:64
  140.4 14.7 %collective-permute-start.14 = (f32[256,512]{1,0:T(8,128)S(1)}, f32[256,512]{1,0:T(8,128)S(1)}, u32[]{:S(2)}, u32[]{:S(2)}) collective-permute-start(f32[256,512]{1,0:T(8,128)S(1)} %add.21.refs_0_), channel_id=1, source_target_pairs={{32,0},{40,8},{48,16},{56,24},{64,32},{72,40},{80,48},{88,56},{96,... | collective-permute-start | bytes 1572872 | tf_op jit(solution)/shard_map/ppermute | solution.py:64
  143.2 11.8 %collective-permute-start.13 = (f32[256,512]{1,0:T(8,128)S(1)}, f32[256,512]{1,0:T(8,128)}, u32[]{:S(2)}, u32[]{:S(2)}) collective-permute-start(f32[256,512]{1,0:T(8,128)S(1)} %add.21.refs_0_), channel_id=1, source_target_pairs={{8,0},{0,8},{24,16},{16,24},{40,32},{32,40},{56,48},{48,56},{72,64... | collective-permute-start | bytes 1572872 | tf_op jit(solution)/shard_map/ppermute | solution.py:64
  152.8 12.6 %copy-start.11 = (f32[256,512]{1,0:T(8,128)}, f32[256,512]{1,0:T(8,128)S(1)}, u32[]{:S(2)}) copy-start(f32[256,512]{1,0:T(8,128)S(1)} %collective-permute-done.16.refs_9_) | copy-start | bytes 1572868
  155.1 22.2 %collective-permute-start.17 = (f32[256,512]{1,0:T(8,128)S(1)}, f32[256,512]{1,0:T(8,128)S(1)}, u32[]{:S(2)}, u32[]{:S(2)}) collective-permute-start(f32[256,512]{1,0:T(8,128)S(1)} %collective-permute-done.14.refs_2_), channel_id=1, source_target_pairs={{16,0},{24,8},{8,16},{0,24},{48,32},{56,40},{40,48},{32,56},{88,64... | collective-permute-start | bytes 1572872 | tf_op jit(solution)/shard_map/ppermute | solution.py:64
  160.3 26.3 %all-to-all-start.2 = ((f32[8,5,32,256]{3,2,1,0:T(8,128)}), f32[8,5,32,256]{3,2,1,0:T(8,128)S(1)}, u32[]{:S(2)}, u32[]{:S(2)}) async-start(f32[8,5,32,256]{3,2,1,0:T(8,128)} %gram.5), calls=%async_computation.2 | async-start | bytes 2621440 | tf_op jit(solution)/shard_map/all_to_all | solution.py:262
  186.7 3.8 %copy-start.1 = (f32[8,5,32,256]{3,2,1,0:T(8,128)}, f32[8,5,32,256]{3,2,1,0:T(8,128)S(1)}, u32[]{:S(2)}) copy-start(f32[8,5,32,256]{3,2,1,0:T(8,128)S(1)} %all-to-all-done.2.moved_ref) | copy-start | bytes 3932164
  186.7 19.4 %all-to-all-start.3 = ((f32[8,4,32,256]{3,2,1,0:T(8,128)}), f32[8,4,32,256]{3,2,1,0:T(8,128)S(1)}, u32[]{:S(2)}, u32[]{:S(2)}) async-start(f32[8,4,32,256]{3,2,1,0:T(8,128)} %gram.7), calls=%async_computation.3 | async-start | bytes 2097152 | tf_op jit(solution)/shard_map/all_to_all | solution.py:262
  192.5 6.0 %collective-permute-start.19 = (f32[3,32,256]{2,1,0:T(8,128)}, f32[3,32,256]{2,1,0:T(8,128)S(1)}, u32[]{:S(2)}, u32[]{:S(2)}) collective-permute-start(f32[3,32,256]{2,1,0:T(8,128)} %get-tuple-element.75), channel_id=1, source_target_pairs={{0,32},{8,40},{16,48},{24,56},{32,64},{40,72},{48,80},{56,88},{64,... | collective-permute-start | bytes 294920 | tf_op jit(solution)/shard_map/ppermute | solution.py:69
  192.8 3.0 %collective-permute-start.18 = (f32[1,32,256]{2,1,0:T(8,128)}, f32[1,32,256]{2,1,0:T(8,128)S(1)}, u32[]{:S(2)}, u32[]{:S(2)}) collective-permute-start(f32[1,32,256]{2,1,0:T(8,128)} %get-tuple-element.74), channel_id=1, source_target_pairs={{0,8},{8,0},{16,24},{24,16},{32,40},{40,32},{48,56},{56,48},{64,72... | collective-permute-start | bytes 98312 | tf_op jit(solution)/shard_map/ppermute | solution.py:69
  192.8 4.9 %collective-permute-start.20 = (f32[1,32,256]{2,1,0:T(8,128)}, f32[1,32,256]{2,1,0:T(8,128)S(1)}, u32[]{:S(2)}, u32[]{:S(2)}) collective-permute-start(f32[1,32,256]{2,1,0:T(8,128)} %get-tuple-element.76), channel_id=1, source_target_pairs={{0,96},{8,104},{16,112},{24,120},{32,0},{40,8},{48,16},{56,24},{64... | collective-permute-start | bytes 98312 | tf_op jit(solution)/shard_map/ppermute | solution.py:69
  195.7 35.7 %copy-start.16 = (f32[1,32,256]{2,1,0:T(8,128)}, f32[1,32,256]{2,1,0:T(8,128)S(1)}, u32[]{:S(2)}) copy-start(f32[1,32,256]{2,1,0:T(8,128)S(1)} %collective-permute-done.18.refs_1_) | copy-start | bytes 98308
  197.6 18.6 %copy-start.18 = (f32[1,32,256]{2,1,0:T(8,128)}, f32[1,32,256]{2,1,0:T(8,128)S(1)}, u32[]{:S(2)}) copy-start(f32[1,32,256]{2,1,0:T(8,128)S(1)} %collective-permute-done.20.refs_1_) | copy-start | bytes 98308
  198.5 17.8 %copy-start.13 = (f32[3,32,256]{2,1,0:T(8,128)}, f32[3,32,256]{2,1,0:T(8,128)S(1)}, u32[]{:S(2)}) copy-start(f32[3,32,256]{2,1,0:T(8,128)S(1)} %collective-permute-done.19.refs_0_.refs_2_) | copy-start | bytes 294916
  206.0 1.0 copy-start.4
  209.0 7.3 %collective-permute-start.24 = (f32[4,32,256]{2,1,0:T(8,128)}, f32[4,32,256]{2,1,0:T(8,128)S(1)}, u32[]{:S(2)}, u32[]{:S(2)}) collective-permute-start(f32[4,32,256]{2,1,0:T(8,128)} %get-tuple-element.86), channel_id=1, source_target_pairs={{0,48},{8,56},{16,40},{24,32},{32,80},{40,88},{48,72},{56,64},{64,... | collective-permute-start | bytes 393224 | tf_op jit(solution)/shard_map/ppermute | solution.py:69
  218.8 12.6 %all-to-all-start.4 = ((f32[8,32,256]{2,1,0:T(8,128)}), f32[8,32,256]{2,1,0:T(8,128)S(1)}, u32[]{:S(2)}, u32[]{:S(2)}) async-start(f32[8,32,256]{2,1,0:T(8,128)} %turn.1), calls=%async_computation.4 | async-start | bytes 524288 | tf_op jit(solution)/shard_map/all_to_all | solution.py:262
  222.9 4.6 %collective-permute-start.21 = (f32[1,32,256]{2,1,0:T(8,128)}, f32[1,32,256]{2,1,0:T(8,128)S(1)}, u32[]{:S(2)}, u32[]{:S(2)}) collective-permute-start(f32[1,32,256]{2,1,0:T(8,128)} %get-tuple-element.82), channel_id=1, source_target_pairs={{0,8},{8,0},{16,24},{24,16},{32,40},{40,32},{48,56},{56,48},{64,72... | collective-permute-start | bytes 98312 | tf_op jit(solution)/shard_map/ppermute | solution.py:69
  223.0 5.4 %collective-permute-start.22 = (f32[1,32,256]{2,1,0:T(8,128)}, f32[1,32,256]{2,1,0:T(8,128)S(1)}, u32[]{:S(2)}, u32[]{:S(2)}) collective-permute-start(f32[1,32,256]{2,1,0:T(8,128)} %get-tuple-element.83), channel_id=1, source_target_pairs={{0,32},{8,40},{16,48},{24,56},{32,64},{40,72},{48,80},{56,88},{64,... | collective-permute-start | bytes 98312 | tf_op jit(solution)/shard_map/ppermute | solution.py:69
  223.0 5.3 %collective-permute-start.23 = (f32[1,32,256]{2,1,0:T(8,128)}, f32[1,32,256]{2,1,0:T(8,128)S(1)}, u32[]{:S(2)}, u32[]{:S(2)}) collective-permute-start(f32[1,32,256]{2,1,0:T(8,128)} %get-tuple-element.84), channel_id=1, source_target_pairs={{0,96},{8,104},{16,112},{24,120},{32,0},{40,8},{48,16},{56,24},{64... | collective-permute-start | bytes 98312 | tf_op jit(solution)/shard_map/ppermute | solution.py:69
  227.5 3.9 %copy-start.17 = (f32[1,32,256]{2,1,0:T(8,128)}, f32[1,32,256]{2,1,0:T(8,128)S(1)}, u32[]{:S(2)}) copy-start(f32[1,32,256]{2,1,0:T(8,128)S(1)} %collective-permute-done.21.refs_4_) | copy-start | bytes 98308
  228.4 3.0 %copy-start.19 = (f32[1,32,256]{2,1,0:T(8,128)}, f32[1,32,256]{2,1,0:T(8,128)S(1)}, u32[]{:S(2)}) copy-start(f32[1,32,256]{2,1,0:T(8,128)S(1)} %collective-permute-done.22.refs_5_) | copy-start | bytes 98308
  228.4 3.0 %copy-start.20 = (f32[1,32,256]{2,1,0:T(8,128)}, f32[1,32,256]{2,1,0:T(8,128)S(1)}, u32[]{:S(2)}) copy-start(f32[1,32,256]{2,1,0:T(8,128)S(1)} %collective-permute-done.23.refs_6_) | copy-start | bytes 98308
  (5 other events, 4.0 us)
Sparse Core Ops, SparseCore 0:
  18.1 54.1 all-gather.2

commit v8 on v7

--- a/solution.py
+++ b/solution.py
@@ -18,6 +18,7 @@
                (ACROSS, [], [0, 1, 2, 3])]
 ROUTES = EARLY_ROUTES + LATE_ROUTES
 LATE_COST = 20_000_000_000
+SENT_COST = KEPT_COST = 5_000_000_000
 
 
 def block_of(y, zl, core):
@@ -117,7 +118,7 @@
         out[...] = out[...] + term if k else term
 
 
-def transformed(part, index, orbitals, place, half):
+def transformed(part, index, orbitals, place, half, cost=0):
     rows, width = part.shape[2:]
     blocks, _, each, _ = orbitals.shape
     run = blocks // ZH
@@ -131,7 +132,7 @@
             pltpu.VMEM((X, run, each, width), jnp.float32),
             pltpu.SemaphoreType.DMA((2, X)),
         ],
-        cost_estimate=pl.CostEstimate(flops=0, bytes_accessed=0, transcendentals=0),
+        cost_estimate=pl.CostEstimate(flops=cost, bytes_accessed=0, transcendentals=0),
         name="transform",
     )(jnp.stack([place, half]), part, orbitals)
 
@@ -274,10 +275,10 @@
     last_part = over_x(last)
 
     def to_send(part, k):
-        return transformed(part, k, orbitals, place, 1 - zh)
+        return transformed(part, k, orbitals, place, 1 - zh, SENT_COST)
 
     def kept(part, k):
-        return transformed(part, k, orbitals, place, zh)
+        return transformed(part, k, orbitals, place, zh, KEPT_COST)
 
     def neighbours(own):
         return fetched(own, other_core), fetched(own, next_row), fetched(own, previous_row)
@@ -293,12 +294,12 @@
     other_0, below_0, above_0, own_1 = together(other_0, below_0, above_0, own_1)
     across_0 = fetched(below_0, over_to_across)
     other_1, below_1, above_1 = neighbours(own_1)
-    other_1, below_1, above_1, across_0, own_2 = together(other_1, below_1, above_1, across_0, own_2)
+    other_1, below_1, above_1, own_2 = together(other_1, below_1, above_1, own_2)
     across_1 = fetched(below_1, over_to_across)
     other_2, below_2, above_2 = neighbours(own_2)
     known = [(own_0, own_1), (other_0, other_1), (below_0, below_1), (above_0, above_1)]
     early = gram(known, EARLY, shares)
-    other_2, below_2, above_2, across_1, early = together(other_2, below_2, above_2, across_1, early)
+    other_2, below_2, above_2, across_0, early = together(other_2, below_2, above_2, across_0, early)
     across_2 = fetched(below_2, over_to_across)
     known_2 = [(own_2,), (other_2,), (below_2,), (above_2,)]
     early = gram(known_2, EARLY, shares, early)

time: 242 us -> 237 us (0.979)
  waiting for transfers between devices: 97.1 us -> 90.5 us
  starting transfers between devices: 52.9 us -> 56 us
    all_to_all x3, waiting for transfers between devices: 15.1 us -> 10 us  [over_col(): return lax.all_to_all(tiles, 'col', split_axis=0, concat_axis=0, tiled=True)]
  transfers between devices with their start and end apart: 31 -> 31, of which waited for: 14 -> 12; matrix products, arithmetic and copies ran while one was open for 6% -> 6% of each run, Pallas kernels for 21% -> 22%
where the time goes in v8:
time: 237 us; the launch traced here: 236 us
  waiting for transfers between devices  90.5 us (38%)
  Pallas kernels  57.3 us (24%)
  starting transfers between devices  56 us (24%)
  between operations  13.7 us (6%)
  local copies, waits for them, and re-layouts  13.1 us (6%)
  other arithmetic  5.66 us (2%)
    all_to_all x2, waiting for transfers between devices, over_x(): lax.all_to_all(part, 'col', split_axis=0, concat_axis=0, tiled=True, axis...  45.1 us
    pallas_call x6, Pallas kernels, transformed(): pl.pallas_call(functools.partial(transform_kernel, index), in_specs=[pl.B...  30.3 us
    ppermute x12, waiting for transfers between devices, fetched(): return lax.ppermute(value, 'blk', route)  21.4 us
    pallas_call x4, Pallas kernels, gram(): pl.pallas_call(functools.partial(gram_kernel, pairs, chunks, more), in_sp...  19 us
    all_to_all x3, starting transfers between devices, over_col(): return lax.all_to_all(tiles, 'col', split_axis=0, concat_axis=0, tiled=True)  14.2 us
    ppermute x12, starting transfers between devices, fetched(): return lax.ppermute(value, 'blk', route)  12.3 us
    ppermute x7, waiting for transfers between devices, delivered(): return lax.ppermute(value, 'blk', route)  10.9 us
    all_to_all x3, waiting for transfers between devices, over_col(): return lax.all_to_all(tiles, 'col', split_axis=0, concat_axis=0, tiled=True)  10 us
  transfers between devices with their start and end apart: 31, of which 12 were waited for; matrix products, arithmetic and copies ran while one was open for 6% of the time, Pallas kernels for 22%

profile of v8, /device:TPU:0, one launch (start us, length us, event | category | flops | bytes accessed | tf_op | source)
XLA Modules:
  0.0 236.3 jit_solution(15293887572093602832)
XLA Ops:
  6.5 1.6 collective-permute-start.2
  8.1 2.7 %collective-permute-start.1 = (f32[64,512]{1,0:T(8,128)}, f32[64,512]{1,0:T(8,128)S(1)}, u32[]{:S(2)}, u32[]{:S(2)}) collective-permute-start(f32[64,512]{1,0:T(8,128)} %bitcast.17), channel_id=1, source_target_pairs={{4,0},{5,1},{6,2},{7,3},{0,4},{1,5},{2,6},{3,7},{12,8},{13,9},{14,... | collective-permute-start | bytes 393224 | tf_op jit(solution)/shard_map/ppermute | solution.py:269
  10.8 1.4 collective-permute-start
  12.3 4.6 %slice.9 = f32[8,256,512]{2,1,0:T(8,128)} slice(f32[12,256,512]{2,1,0:T(8,128)} %bitcast.14), slice={[0:8], [0:256], [0:512]} | slice | bytes 8388608 | tf_op jit(solution)/shard_map/slice | solution.py:270
  17.9 4.8 %all-to-all-start = ((f32[8,256,512]{2,1,0:T(8,128)}), f32[8,256,512]{2,1,0:T(8,128)}, u32[]{:S(2)}, u32[]{:S(2)}) async-start(f32[8,256,512]{2,1,0:T(8,128)} %slice.9), calls=%async_computation | async-start | bytes 8388608 | tf_op jit(solution)/shard_map/all_to_all | solution.py:254
  22.8 3.1 %slice.8 = f32[4,256,512]{2,1,0:T(8,128)} slice(f32[12,256,512]{2,1,0:T(8,128)} %bitcast.15), slice={[8:12], [0:256], [0:512]} | slice | bytes 4194304 | tf_op jit(solution)/shard_map/slice | solution.py:274
  25.9 45.1 %all-to-all-done = f32[8,256,512]{2,1,0:T(8,128)} async-done(((f32[8,256,512]{2,1,0:T(8,128)}), f32[8,256,512]{2,1,0:T(8,128)}, u32[]{:S(2)}, u32[]{:S(2)}) %all-to-all-start) | async-done | bytes 4194336 | tf_op jit(solution)/shard_map/all_to_all | solution.py:254
  71.1 4.4 %all-to-all-start.1 = ((f32[4,256,512]{2,1,0:T(8,128)}), f32[4,256,512]{2,1,0:T(8,128)}, u32[]{:S(2)}, u32[]{:S(2)}) async-start(f32[4,256,512]{2,1,0:T(8,128)} %slice.8), calls=%async_computation.1 | async-start | bytes 4194304 | tf_op jit(solution)/shard_map/all_to_all | solution.py:254
  76.8 5.0 %transform.7 = f32[256,512]{1,0:T(8,128)} custom-call(s32[2]{0:T(128)} %pad_add_fusion.1.scalars, f32[4,2,256,512]{3,2,1,0:T(8,128)} %bitcast.5.part, f32[16,4,64,512]{3,2,1,0:T(8,128)} %bitcast.23), custom_call_target="tpu_custom_call" | custom-call | flops 5000000000 | tf_op jit(solution)/shard_map/transform/pallas_call | solution.py:125
  81.8 4.0 %collective-permute-start.3 = (f32[256,512]{1,0:T(8,128)}, f32[256,512]{1,0:T(8,128)S(1)}, u32[]{:S(2)}, u32[]{:S(2)}) collective-permute-start(f32[256,512]{1,0:T(8,128)} %transform.7), channel_id=1, source_target_pairs={{1,0},{0,1},{3,2},{2,3},{5,4},{4,5},{7,6},{6,7},{9,8},{8,9},{11,10... | collective-permute-start | bytes 1572872 | tf_op jit(solution)/shard_map/ppermute | solution.py:260
  85.8 5.0 %transform.10 = f32[256,512]{1,0:T(8,128)} custom-call(s32[2]{0:T(128)} %pad_add_fusion.1.scalars, f32[4,2,256,512]{3,2,1,0:T(8,128)} %bitcast.5.part, f32[16,4,64,512]{3,2,1,0:T(8,128)} %bitcast.24), custom_call_target="tpu_custom_call" | custom-call | flops 5000000000 | tf_op jit(solution)/shard_map/transform/pallas_call | solution.py:125
  91.0 5.1 %transform.6 = f32[256,512]{1,0:T(8,128)} custom-call(s32[2]{0:T(128)} %pad_add_fusion.scalars, f32[4,2,256,512]{3,2,1,0:T(8,128)} %bitcast.5.part, f32[16,4,64,512]{3,2,1,0:T(8,128)} %bitcast.25), custom_call_target="tpu_custom_call" | custom-call | flops 5000000000 | tf_op jit(solution)/shard_map/transform/pallas_call | solution.py:125
  96.0 2.8 %collective-permute-done.3 = f32[256,512]{1,0:T(8,128)S(1)} collective-permute-done((f32[256,512]{1,0:T(8,128)}, f32[256,512]{1,0:T(8,128)S(1)}, u32[]{:S(2)}, u32[]{:S(2)}) %collective-permute-start.3) | collective-permute-done | bytes 524320 | tf_op jit(solution)/shard_map/ppermute | solution.py:260
  98.9 1.1 add.19.refs_0_
  100.0 1.6 collective-permute-start.6
  101.6 1.7 collective-permute-start.5
  103.3 5.1 %transform.8 = f32[256,512]{1,0:T(8,128)} custom-call(s32[2]{0:T(128)} %pad_add_fusion.1.scalars, f32[4,1,256,512]{3,2,1,0:T(8,128)} %bitcast.12.part, f32[16,4,64,512]{3,2,1,0:T(8,128)} %bitcast.26), custom_call_target="tpu_custom_call" | custom-call | flops 5000000000 | tf_op jit(solution)/shard_map/transform/pallas_call | solution.py:125
  108.4 3.8 %collective-permute-start.11 = (f32[256,512]{1,0:T(8,128)}, f32[256,512]{1,0:T(8,128)S(1)}, u32[]{:S(2)}, u32[]{:S(2)}) collective-permute-start(f32[256,512]{1,0:T(8,128)} %transform.8), channel_id=1, source_target_pairs={{1,0},{0,1},{3,2},{2,3},{5,4},{4,5},{7,6},{6,7},{9,8},{8,9},{11,10... | collective-permute-start | bytes 1572872 | tf_op jit(solution)/shard_map/ppermute | solution.py:260
  112.2 5.0 %transform.9 = f32[256,512]{1,0:T(8,128)} custom-call(s32[2]{0:T(128)} %pad_add_fusion.scalars, f32[4,2,256,512]{3,2,1,0:T(8,128)} %bitcast.5.part, f32[16,4,64,512]{3,2,1,0:T(8,128)} %bitcast.27), custom_call_target="tpu_custom_call" | custom-call | flops 5000000000 | tf_op jit(solution)/shard_map/transform/pallas_call | solution.py:125
  117.2 1.3 add.20.refs_1_
  119.0 2.9 %collective-permute-start.9 = (f32[256,512]{1,0:T(8,128)S(1)}, f32[256,512]{1,0:T(8,128)}, u32[]{:S(2)}, u32[]{:S(2)}) collective-permute-start(f32[256,512]{1,0:T(8,128)S(1)} %add.20.refs_1_), channel_id=1, source_target_pairs={{32,0},{40,8},{48,16},{56,24},{64,32},{72,40},{80,48},{88,56},{96,... | collective-permute-start | bytes 1572872 | tf_op jit(solution)/shard_map/ppermute | solution.py:65
  121.9 5.1 %transform.11 = f32[256,512]{1,0:T(8,128)} custom-call(s32[2]{0:T(128)} %pad_add_fusion.scalars, f32[4,1,256,512]{3,2,1,0:T(8,128)} %bitcast.12.part, f32[16,4,64,512]{3,2,1,0:T(8,128)} %bitcast.28), custom_call_target="tpu_custom_call" | custom-call | flops 5000000000 | tf_op jit(solution)/shard_map/transform/pallas_call | solution.py:125
  127.0 1.1 add.21.refs_0_
  128.2 1.2 collective-permute-start.15
  129.3 4.6 %collective-permute-done.10.refs_7_ = f32[256,512]{1,0:T(8,128)S(1)} collective-permute-done((f32[256,512]{1,0:T(8,128)S(1)}, f32[256,512]{1,0:T(8,128)S(1)}, u32[]{:S(2)}, u32[]{:S(2)}) %collective-permute-start.10) | collective-permute-done | bytes 524320 | tf_op jit(solution)/shard_map/ppermute | solution.py:65
  134.5 2.7 %collective-permute-start.13 = (f32[256,512]{1,0:T(8,128)S(1)}, f32[256,512]{1,0:T(8,128)}, u32[]{:S(2)}, u32[]{:S(2)}) collective-permute-start(f32[256,512]{1,0:T(8,128)S(1)} %add.21.refs_0_), channel_id=1, source_target_pairs={{32,0},{40,8},{48,16},{56,24},{64,32},{72,40},{80,48},{88,56},{96,... | collective-permute-start | bytes 1572872 | tf_op jit(solution)/shard_map/ppermute | solution.py:65
  137.3 1.1 collective-permute-start.17
  138.4 5.4 %gram.4.refs_4_ = f32[8,5,32,256]{3,2,1,0:T(8,128)} custom-call(f32[256,512]{1,0:T(8,128)} %copy-done.1, f32[256,512]{1,0:T(8,128)} %copy-done.2, f32[256,512]{1,0:T(8,128)} %copy-done.7, f32[256,512]{1,0:T(8,128)} %collective-permute-done.8.refs_3_, f32[256,512]{1,0:T(8,128)} %copy-done.6, f32[256,512]{1,0:T(8,128)} %collective-permute-done.9.refs_5_, ...), custom_call_target="tpu_custom_call" | custom-call | tf_op jit(solution)/shard_map/gram/pallas_call | solution.py:177
  143.8 4.6 %collective-permute-done.14.refs_3_ = f32[256,512]{1,0:T(8,128)S(1)} collective-permute-done((f32[256,512]{1,0:T(8,128)S(1)}, f32[256,512]{1,0:T(8,128)S(1)}, u32[]{:S(2)}, u32[]{:S(2)}) %collective-permute-start.14) | collective-permute-done | bytes 524320 | tf_op jit(solution)/shard_map/ppermute | solution.py:65
  149.5 4.3 %gram.5 = f32[8,5,32,256]{3,2,1,0:T(8,128)} custom-call(f32[256,512]{1,0:T(8,128)} %copy-done.4, f32[256,512]{1,0:T(8,128)} %copy-done.12, f32[256,512]{1,0:T(8,128)} %collective-permute-done.13.refs_2_, f32[256,512]{1,0:T(8,128)} %copy-done.11, f32[8,5,32,256]{3,2,1,0:T(8,128)} %gram.4.refs_4_), custom_call_target="tpu_custom_call" | custom-call | tf_op jit(solution)/shard_map/gram/pallas_call | solution.py:177
  153.8 4.8 %all-to-all-start.2 = ((f32[8,5,32,256]{3,2,1,0:T(8,128)}), f32[8,5,32,256]{3,2,1,0:T(8,128)S(1)}, u32[]{:S(2)}, u32[]{:S(2)}) async-start(f32[8,5,32,256]{3,2,1,0:T(8,128)} %gram.5), calls=%async_computation.2 | async-start | bytes 2621440 | tf_op jit(solution)/shard_map/all_to_all | solution.py:263
  158.6 5.3 %gram.6.refs_5_ = f32[8,4,32,256]{3,2,1,0:T(8,128)} custom-call(f32[256,512]{1,0:T(8,128)} %copy-done.1, f32[256,512]{1,0:T(8,128)} %copy-done.2, f32[256,512]{1,0:T(8,128)} %copy-done.7, f32[256,512]{1,0:T(8,128)} %collective-permute-done.8.refs_3_, f32[256,512]{1,0:T(8,128)} %copy-done.6, f32[256,512]{1,0:T(8,128)} %collective-permute-done.9.refs_5_, ...), custom_call_target="tpu_custom_call" | custom-call | tf_op jit(solution)/shard_map/gram/pallas_call | solution.py:177
  163.9 12.1 %collective-permute-done.16.refs_4_ = f32[256,512]{1,0:T(8,128)S(1)} collective-permute-done((f32[256,512]{1,0:T(8,128)}, f32[256,512]{1,0:T(8,128)S(1)}, u32[]{:S(2)}, u32[]{:S(2)}) %collective-permute-start.16) | collective-permute-done | bytes 524320 | tf_op jit(solution)/shard_map/ppermute | solution.py:65
  176.8 4.0 %gram.7 = f32[8,4,32,256]{3,2,1,0:T(8,128)} custom-call(f32[256,512]{1,0:T(8,128)} %copy-done.4, f32[256,512]{1,0:T(8,128)} %copy-done.12, f32[256,512]{1,0:T(8,128)} %collective-permute-done.13.refs_2_, f32[256,512]{1,0:T(8,128)} %copy-done.11, f32[256,512]{1,0:T(8,128)} %copy-done.21, f32[8,4,32,256]{3,2,1,0:T(8,128)} %gram.6.refs_5_), custom_call_target="tpu_custom_call" | custom-call | flops 20000000000 | tf_op jit(solution)/shard_map/gram/pallas_call | solution.py:177
  180.8 5.5 %all-to-all-start.3 = ((f32[8,4,32,256]{3,2,1,0:T(8,128)}), f32[8,4,32,256]{3,2,1,0:T(8,128)S(1)}, u32[]{:S(2)}, u32[]{:S(2)}) async-start(f32[8,4,32,256]{3,2,1,0:T(8,128)} %gram.7), calls=%async_computation.3 | async-start | bytes 2097152 | tf_op jit(solution)/shard_map/all_to_all | solution.py:263
  186.3 2.1 sum.2
  188.4 3.2 %collective-permute-start.20 = (f32[1,32,256]{2,1,0:T(8,128)}, f32[1,32,256]{2,1,0:T(8,128)S(1)}, u32[]{:S(2)}, u32[]{:S(2)}) collective-permute-start(f32[1,32,256]{2,1,0:T(8,128)} %get-tuple-element.74), channel_id=1, source_target_pairs={{0,96},{8,104},{16,112},{24,120},{32,0},{40,8},{48,16},{56,24},{64... | collective-permute-start | bytes 98312 | tf_op jit(solution)/shard_map/ppermute | solution.py:70
  191.6 1.9 collective-permute-done.20.refs_1_
  194.4 7.0 %all-to-all-done.3.moved_ref = f32[8,4,32,256]{3,2,1,0:T(8,128)S(1)} async-done(((f32[8,4,32,256]{3,2,1,0:T(8,128)}), f32[8,4,32,256]{3,2,1,0:T(8,128)S(1)}, u32[]{:S(2)}, u32[]{:S(2)}) %all-to-all-start.3) | async-done | bytes 1048608 | tf_op jit(solution)/shard_map/all_to_all | solution.py:263
  201.4 1.0 copy-done.3
  202.4 2.0 sum.3
  204.4 7.3 %collective-permute-done.24.refs_2_ = f32[4,32,256]{2,1,0:T(8,128)S(1)} collective-permute-done((f32[4,32,256]{2,1,0:T(8,128)}, f32[4,32,256]{2,1,0:T(8,128)S(1)}, u32[]{:S(2)}, u32[]{:S(2)}) %collective-permute-start.24) | collective-permute-done | bytes 131104 | tf_op jit(solution)/shard_map/ppermute | solution.py:70
  212.3 1.8 turn.1
  214.1 3.9 %all-to-all-start.4 = ((f32[8,32,256]{2,1,0:T(8,128)}), f32[8,32,256]{2,1,0:T(8,128)S(1)}, u32[]{:S(2)}, u32[]{:S(2)}) async-start(f32[8,32,256]{2,1,0:T(8,128)} %turn.1), calls=%async_computation.4 | async-start | bytes 524288 | tf_op jit(solution)/shard_map/all_to_all | solution.py:263
  218.2 3.2 %collective-permute-start.23 = (f32[1,32,256]{2,1,0:T(8,128)}, f32[1,32,256]{2,1,0:T(8,128)S(1)}, u32[]{:S(2)}, u32[]{:S(2)}) collective-permute-start(f32[1,32,256]{2,1,0:T(8,128)} %get-tuple-element.82), channel_id=1, source_target_pairs={{0,96},{8,104},{16,112},{24,120},{32,0},{40,8},{48,16},{56,24},{64... | collective-permute-start | bytes 98312 | tf_op jit(solution)/shard_map/ppermute | solution.py:70
  221.4 1.3 dynamic-slice_bitcast_fusion.table_ref
  223.5 3.0 %all-to-all-done.4.refs_7_ = f32[8,32,256]{2,1,0:T(8,128)S(1)} async-done(((f32[8,32,256]{2,1,0:T(8,128)}), f32[8,32,256]{2,1,0:T(8,128)S(1)}, u32[]{:S(2)}, u32[]{:S(2)}) %all-to-all-start.4) | async-done | bytes 262176 | tf_op jit(solution)/shard_map/all_to_all | solution.py:263
  227.2 2.2 assemble.1
  (82 shorter events, 8.5 us)
Async XLA Ops:
  6.5 70.3 %all-gather.3.cloned.1.call-start = ((), (), s32[]{:S(2)}) async-start(), calls=%async_computation.5 | async-start | bytes 8912896 | tf_op jit(solution)/shard_map/all_gather | solution.py:273
  6.5 10.3 %collective-permute-start.2 = (f32[64,512]{1,0:T(8,128)}, f32[64,512]{1,0:T(8,128)S(1)}, u32[]{:S(2)}, u32[]{:S(2)}) collective-permute-start(f32[64,512]{1,0:T(8,128)} %bitcast.16), channel_id=1, source_target_pairs={{6,0},{7,1},{0,2},{1,3},{2,4},{3,5},{4,6},{5,7},{14,8},{15,9},{8,1... | collective-permute-start | bytes 393224 | tf_op jit(solution)/shard_map/ppermute | solution.py:269
  8.1 9.0 %collective-permute-start.1 = (f32[64,512]{1,0:T(8,128)}, f32[64,512]{1,0:T(8,128)S(1)}, u32[]{:S(2)}, u32[]{:S(2)}) collective-permute-start(f32[64,512]{1,0:T(8,128)} %bitcast.17), channel_id=1, source_target_pairs={{4,0},{5,1},{6,2},{7,3},{0,4},{1,5},{2,6},{3,7},{12,8},{13,9},{14,... | collective-permute-start | bytes 393224 | tf_op jit(solution)/shard_map/ppermute | solution.py:269
  10.8 6.2 %collective-permute-start = (f32[64,512]{1,0:T(8,128)}, f32[64,512]{1,0:T(8,128)S(1)}, u32[]{:S(2)}, u32[]{:S(2)}) collective-permute-start(f32[64,512]{1,0:T(8,128)} %bitcast.18), channel_id=1, source_target_pairs={{2,0},{3,1},{4,2},{5,3},{6,4},{7,5},{0,6},{1,7},{10,8},{11,9},{12,... | collective-permute-start | bytes 393224 | tf_op jit(solution)/shard_map/ppermute | solution.py:269
  12.3 4.8 %copy-start.15 = (f32[512,64]{0,1:T(8,128)S(1)}, f32[512,64]{0,1:T(8,128)}, u32[]{:S(2)}) copy-start(f32[512,64]{0,1:T(8,128)} %param.4) | copy-start | bytes 393220
  17.9 53.1 %all-to-all-start = ((f32[8,256,512]{2,1,0:T(8,128)}), f32[8,256,512]{2,1,0:T(8,128)}, u32[]{:S(2)}, u32[]{:S(2)}) async-start(f32[8,256,512]{2,1,0:T(8,128)} %slice.9), calls=%async_computation | async-start | bytes 8388608 | tf_op jit(solution)/shard_map/all_to_all | solution.py:254
  71.1 32.3 %all-to-all-start.1 = ((f32[4,256,512]{2,1,0:T(8,128)}), f32[4,256,512]{2,1,0:T(8,128)}, u32[]{:S(2)}, u32[]{:S(2)}) async-start(f32[4,256,512]{2,1,0:T(8,128)} %slice.8), calls=%async_computation.1 | async-start | bytes 4194304 | tf_op jit(solution)/shard_map/all_to_all | solution.py:254
  81.8 17.0 %collective-permute-start.3 = (f32[256,512]{1,0:T(8,128)}, f32[256,512]{1,0:T(8,128)S(1)}, u32[]{:S(2)}, u32[]{:S(2)}) collective-permute-start(f32[256,512]{1,0:T(8,128)} %transform.7), channel_id=1, source_target_pairs={{1,0},{0,1},{3,2},{2,3},{5,4},{4,5},{7,6},{6,7},{9,8},{8,9},{11,10... | collective-permute-start | bytes 1572872 | tf_op jit(solution)/shard_map/ppermute | solution.py:260
  90.9 26.4 %collective-permute-start.7 = (f32[256,512]{1,0:T(8,128)}, f32[256,512]{1,0:T(8,128)}, u32[]{:S(2)}, u32[]{:S(2)}) collective-permute-start(f32[256,512]{1,0:T(8,128)} %transform.10), channel_id=1, source_target_pairs={{1,0},{0,1},{3,2},{2,3},{5,4},{4,5},{7,6},{6,7},{9,8},{8,9},{11,10... | collective-permute-start | bytes 1572872 | tf_op jit(solution)/shard_map/ppermute | solution.py:260
  100.0 8.4 %copy-start.1 = (f32[256,512]{1,0:T(8,128)}, f32[256,512]{1,0:T(8,128)S(1)}, u32[]{:S(2)}) copy-start(f32[256,512]{1,0:T(8,128)S(1)} %add.19.refs_0_) | copy-start | bytes 1572868
  100.0 18.5 %collective-permute-start.6 = (f32[256,512]{1,0:T(8,128)S(1)}, f32[256,512]{1,0:T(8,128)S(1)}, u32[]{:S(2)}, u32[]{:S(2)}) collective-permute-start(f32[256,512]{1,0:T(8,128)S(1)} %add.19.refs_0_), channel_id=1, source_target_pairs={{96,0},{104,8},{112,16},{120,24},{0,32},{8,40},{16,48},{24,56},{40... | collective-permute-start | bytes 1572872 | tf_op jit(solution)/shard_map/ppermute | solution.py:65
  101.6 16.9 %collective-permute-start.5 = (f32[256,512]{1,0:T(8,128)S(1)}, f32[256,512]{1,0:T(8,128)S(1)}, u32[]{:S(2)}, u32[]{:S(2)}) collective-permute-start(f32[256,512]{1,0:T(8,128)S(1)} %add.19.refs_0_), channel_id=1, source_target_pairs={{32,0},{40,8},{48,16},{56,24},{64,32},{72,40},{80,48},{88,56},{96,... | collective-permute-start | bytes 1572872 | tf_op jit(solution)/shard_map/ppermute | solution.py:65
  103.3 15.3 %collective-permute-start.4 = (f32[256,512]{1,0:T(8,128)S(1)}, f32[256,512]{1,0:T(8,128)S(1)}, u32[]{:S(2)}, u32[]{:S(2)}) collective-permute-start(f32[256,512]{1,0:T(8,128)S(1)} %add.19.refs_0_), channel_id=1, source_target_pairs={{8,0},{0,8},{24,16},{16,24},{40,32},{32,40},{56,48},{48,56},{72,64... | collective-permute-start | bytes 1572872 | tf_op jit(solution)/shard_map/ppermute | solution.py:65
  108.4 18.6 %collective-permute-start.11 = (f32[256,512]{1,0:T(8,128)}, f32[256,512]{1,0:T(8,128)S(1)}, u32[]{:S(2)}, u32[]{:S(2)}) collective-permute-start(f32[256,512]{1,0:T(8,128)} %transform.8), channel_id=1, source_target_pairs={{1,0},{0,1},{3,2},{2,3},{5,4},{4,5},{7,6},{6,7},{9,8},{8,9},{11,10... | collective-permute-start | bytes 1572872 | tf_op jit(solution)/shard_map/ppermute | solution.py:260
  118.5 8.5 %copy-start.2 = (f32[256,512]{1,0:T(8,128)}, f32[256,512]{1,0:T(8,128)S(1)}, u32[]{:S(2)}) copy-start(f32[256,512]{1,0:T(8,128)S(1)} %add.20.refs_1_) | copy-start | bytes 1572868
  118.5 8.4 %copy-start.5 = (f32[256,512]{1,0:T(8,128)}, f32[256,512]{1,0:T(8,128)S(1)}, u32[]{:S(2)}) copy-start(f32[256,512]{1,0:T(8,128)S(1)} %collective-permute-done.6.refs_6_) | copy-start | bytes 1572868
  118.6 9.6 %copy-start.6 = (f32[256,512]{1,0:T(8,128)}, f32[256,512]{1,0:T(8,128)S(1)}, u32[]{:S(2)}) copy-start(f32[256,512]{1,0:T(8,128)S(1)} %collective-permute-done.5.refs_4_) | copy-start | bytes 1572868
  118.6 8.4 %copy-start.7 = (f32[256,512]{1,0:T(8,128)}, f32[256,512]{1,0:T(8,128)S(1)}, u32[]{:S(2)}) copy-start(f32[256,512]{1,0:T(8,128)S(1)} %collective-permute-done.4.refs_2_) | copy-start | bytes 1572868
  118.6 15.3 %collective-permute-start.10 = (f32[256,512]{1,0:T(8,128)S(1)}, f32[256,512]{1,0:T(8,128)S(1)}, u32[]{:S(2)}, u32[]{:S(2)}) collective-permute-start(f32[256,512]{1,0:T(8,128)S(1)} %add.20.refs_1_), channel_id=1, source_target_pairs={{96,0},{104,8},{112,16},{120,24},{0,32},{8,40},{16,48},{24,56},{40... | collective-permute-start | bytes 1572872 | tf_op jit(solution)/shard_map/ppermute | solution.py:65
  119.0 14.9 %collective-permute-start.9 = (f32[256,512]{1,0:T(8,128)S(1)}, f32[256,512]{1,0:T(8,128)}, u32[]{:S(2)}, u32[]{:S(2)}) collective-permute-start(f32[256,512]{1,0:T(8,128)S(1)} %add.20.refs_1_), channel_id=1, source_target_pairs={{32,0},{40,8},{48,16},{56,24},{64,32},{72,40},{80,48},{88,56},{96,... | collective-permute-start | bytes 1572872 | tf_op jit(solution)/shard_map/ppermute | solution.py:65
  121.9 12.0 %collective-permute-start.8 = (f32[256,512]{1,0:T(8,128)S(1)}, f32[256,512]{1,0:T(8,128)}, u32[]{:S(2)}, u32[]{:S(2)}) collective-permute-start(f32[256,512]{1,0:T(8,128)S(1)} %add.20.refs_1_), channel_id=1, source_target_pairs={{8,0},{0,8},{24,16},{16,24},{40,32},{32,40},{56,48},{48,56},{72,64... | collective-permute-start | bytes 1572872 | tf_op jit(solution)/shard_map/ppermute | solution.py:65
  128.2 15.7 %copy-start.4 = (f32[256,512]{1,0:T(8,128)}, f32[256,512]{1,0:T(8,128)S(1)}, u32[]{:S(2)}) copy-start(f32[256,512]{1,0:T(8,128)S(1)} %add.21.refs_0_) | copy-start | bytes 1572868
  128.2 15.7 %collective-permute-start.15 = (f32[256,512]{1,0:T(8,128)S(1)}, f32[256,512]{1,0:T(8,128)S(1)}, u32[]{:S(2)}, u32[]{:S(2)}) collective-permute-start(f32[256,512]{1,0:T(8,128)S(1)} %collective-permute-done.5.refs_4_), channel_id=1, source_target_pairs={{16,0},{24,8},{8,16},{0,24},{48,32},{56,40},{40,48},{32,56},{88,64... | collective-permute-start | bytes 1572872 | tf_op jit(solution)/shard_map/ppermute | solution.py:65
  133.9 4.4 %copy-start.8 = (f32[256,512]{1,0:T(8,128)}, f32[256,512]{1,0:T(8,128)S(1)}, u32[]{:S(2)}) copy-start(f32[256,512]{1,0:T(8,128)S(1)} %collective-permute-done.10.refs_7_) | copy-start | bytes 1572868
  134.0 14.5 %collective-permute-start.14 = (f32[256,512]{1,0:T(8,128)S(1)}, f32[256,512]{1,0:T(8,128)S(1)}, u32[]{:S(2)}, u32[]{:S(2)}) collective-permute-start(f32[256,512]{1,0:T(8,128)S(1)} %add.21.refs_0_), channel_id=1, source_target_pairs={{96,0},{104,8},{112,16},{120,24},{0,32},{8,40},{16,48},{24,56},{40... | collective-permute-start | bytes 1572872 | tf_op jit(solution)/shard_map/ppermute | solution.py:65
  134.5 14.0 %collective-permute-start.13 = (f32[256,512]{1,0:T(8,128)S(1)}, f32[256,512]{1,0:T(8,128)}, u32[]{:S(2)}, u32[]{:S(2)}) collective-permute-start(f32[256,512]{1,0:T(8,128)S(1)} %add.21.refs_0_), channel_id=1, source_target_pairs={{32,0},{40,8},{48,16},{56,24},{64,32},{72,40},{80,48},{88,56},{96,... | collective-permute-start | bytes 1572872 | tf_op jit(solution)/shard_map/ppermute | solution.py:65
  137.3 11.2 %collective-permute-start.12 = (f32[256,512]{1,0:T(8,128)S(1)}, f32[256,512]{1,0:T(8,128)S(1)}, u32[]{:S(2)}, u32[]{:S(2)}) collective-permute-start(f32[256,512]{1,0:T(8,128)S(1)} %add.21.refs_0_), channel_id=1, source_target_pairs={{8,0},{0,8},{24,16},{16,24},{40,32},{32,40},{56,48},{48,56},{72,64... | collective-permute-start | bytes 1572872 | tf_op jit(solution)/shard_map/ppermute | solution.py:65
  137.3 21.3 %collective-permute-start.17 = (f32[256,512]{1,0:T(8,128)}, f32[256,512]{1,0:T(8,128)}, u32[]{:S(2)}, u32[]{:S(2)}) collective-permute-start(f32[256,512]{1,0:T(8,128)} %collective-permute-done.9.refs_5_), channel_id=1, source_target_pairs={{16,0},{24,8},{8,16},{0,24},{48,32},{56,40},{40,48},{32,56},{88,64... | collective-permute-start | bytes 1572872 | tf_op jit(solution)/shard_map/ppermute | solution.py:65
  143.8 10.0 %copy-start.10 = (f32[256,512]{1,0:T(8,128)}, f32[256,512]{1,0:T(8,128)S(1)}, u32[]{:S(2)}) copy-start(f32[256,512]{1,0:T(8,128)S(1)} %collective-permute-done.15.refs_8_) | copy-start | bytes 1572868
  148.5 27.5 %collective-permute-start.16 = (f32[256,512]{1,0:T(8,128)}, f32[256,512]{1,0:T(8,128)S(1)}, u32[]{:S(2)}, u32[]{:S(2)}) collective-permute-start(f32[256,512]{1,0:T(8,128)} %collective-permute-done.13.refs_2_), channel_id=1, source_target_pairs={{16,0},{24,8},{8,16},{0,24},{48,32},{56,40},{40,48},{32,56},{88,64... | collective-permute-start | bytes 1572872 | tf_op jit(solution)/shard_map/ppermute | solution.py:65
  153.8 27.0 %all-to-all-start.2 = ((f32[8,5,32,256]{3,2,1,0:T(8,128)}), f32[8,5,32,256]{3,2,1,0:T(8,128)S(1)}, u32[]{:S(2)}, u32[]{:S(2)}) async-start(f32[8,5,32,256]{3,2,1,0:T(8,128)} %gram.5), calls=%async_computation.2 | async-start | bytes 2621440 | tf_op jit(solution)/shard_map/all_to_all | solution.py:263
  180.8 5.5 %copy-start = (f32[8,5,32,256]{3,2,1,0:T(8,128)}, f32[8,5,32,256]{3,2,1,0:T(8,128)S(1)}, u32[]{:S(2)}) copy-start(f32[8,5,32,256]{3,2,1,0:T(8,128)S(1)} %all-to-all-done.2.moved_ref) | copy-start | bytes 3932164
  180.8 20.6 %all-to-all-start.3 = ((f32[8,4,32,256]{3,2,1,0:T(8,128)}), f32[8,4,32,256]{3,2,1,0:T(8,128)S(1)}, u32[]{:S(2)}, u32[]{:S(2)}) async-start(f32[8,4,32,256]{3,2,1,0:T(8,128)} %gram.7), calls=%async_computation.3 | async-start | bytes 2097152 | tf_op jit(solution)/shard_map/all_to_all | solution.py:263
  188.4 6.0 %collective-permute-start.19 = (f32[3,32,256]{2,1,0:T(8,128)}, f32[3,32,256]{2,1,0:T(8,128)S(1)}, u32[]{:S(2)}, u32[]{:S(2)}) collective-permute-start(f32[3,32,256]{2,1,0:T(8,128)} %get-tuple-element.73), channel_id=1, source_target_pairs={{0,32},{8,40},{16,48},{24,56},{32,64},{40,72},{48,80},{56,88},{64,... | collective-permute-start | bytes 294920 | tf_op jit(solution)/shard_map/ppermute | solution.py:70
  188.4 3.2 %collective-permute-start.18 = (f32[1,32,256]{2,1,0:T(8,128)}, f32[1,32,256]{2,1,0:T(8,128)S(1)}, u32[]{:S(2)}, u32[]{:S(2)}) collective-permute-start(f32[1,32,256]{2,1,0:T(8,128)} %get-tuple-element.72), channel_id=1, source_target_pairs={{0,8},{8,0},{16,24},{24,16},{32,40},{40,32},{48,56},{56,48},{64,72... | collective-permute-start | bytes 98312 | tf_op jit(solution)/shard_map/ppermute | solution.py:70
  188.4 5.1 %collective-permute-start.20 = (f32[1,32,256]{2,1,0:T(8,128)}, f32[1,32,256]{2,1,0:T(8,128)S(1)}, u32[]{:S(2)}, u32[]{:S(2)}) collective-permute-start(f32[1,32,256]{2,1,0:T(8,128)} %get-tuple-element.74), channel_id=1, source_target_pairs={{0,96},{8,104},{16,112},{24,120},{32,0},{40,8},{48,16},{56,24},{64... | collective-permute-start | bytes 98312 | tf_op jit(solution)/shard_map/ppermute | solution.py:70
  191.6 34.9 %copy-start.16 = (f32[1,32,256]{2,1,0:T(8,128)}, f32[1,32,256]{2,1,0:T(8,128)S(1)}, u32[]{:S(2)}) copy-start(f32[1,32,256]{2,1,0:T(8,128)S(1)} %collective-permute-done.18.refs_1_) | copy-start | bytes 98308
  193.5 18.2 %copy-start.18 = (f32[1,32,256]{2,1,0:T(8,128)}, f32[1,32,256]{2,1,0:T(8,128)S(1)}, u32[]{:S(2)}) copy-start(f32[1,32,256]{2,1,0:T(8,128)S(1)} %collective-permute-done.20.refs_1_) | copy-start | bytes 98308
  194.4 17.3 %copy-start.13 = (f32[3,32,256]{2,1,0:T(8,128)}, f32[3,32,256]{2,1,0:T(8,128)S(1)}, u32[]{:S(2)}) copy-start(f32[3,32,256]{2,1,0:T(8,128)S(1)} %collective-permute-done.19.refs_0_.refs_2_) | copy-start | bytes 294916
  201.4 1.0 copy-start.3
  204.4 7.3 %collective-permute-start.24 = (f32[4,32,256]{2,1,0:T(8,128)}, f32[4,32,256]{2,1,0:T(8,128)S(1)}, u32[]{:S(2)}, u32[]{:S(2)}) collective-permute-start(f32[4,32,256]{2,1,0:T(8,128)} %get-tuple-element.84), channel_id=1, source_target_pairs={{0,48},{8,56},{16,40},{24,32},{32,80},{40,88},{48,72},{56,64},{64,... | collective-permute-start | bytes 393224 | tf_op jit(solution)/shard_map/ppermute | solution.py:70
  214.1 12.4 %all-to-all-start.4 = ((f32[8,32,256]{2,1,0:T(8,128)}), f32[8,32,256]{2,1,0:T(8,128)S(1)}, u32[]{:S(2)}, u32[]{:S(2)}) async-start(f32[8,32,256]{2,1,0:T(8,128)} %turn.1), calls=%async_computation.4 | async-start | bytes 524288 | tf_op jit(solution)/shard_map/all_to_all | solution.py:263
  218.1 4.6 %collective-permute-start.21 = (f32[1,32,256]{2,1,0:T(8,128)}, f32[1,32,256]{2,1,0:T(8,128)S(1)}, u32[]{:S(2)}, u32[]{:S(2)}) collective-permute-start(f32[1,32,256]{2,1,0:T(8,128)} %get-tuple-element.80), channel_id=1, source_target_pairs={{0,8},{8,0},{16,24},{24,16},{32,40},{40,32},{48,56},{56,48},{64,72... | collective-permute-start | bytes 98312 | tf_op jit(solution)/shard_map/ppermute | solution.py:70
  218.1 5.4 %collective-permute-start.22 = (f32[1,32,256]{2,1,0:T(8,128)}, f32[1,32,256]{2,1,0:T(8,128)S(1)}, u32[]{:S(2)}, u32[]{:S(2)}) collective-permute-start(f32[1,32,256]{2,1,0:T(8,128)} %get-tuple-element.81), channel_id=1, source_target_pairs={{0,32},{8,40},{16,48},{24,56},{32,64},{40,72},{48,80},{56,88},{64,... | collective-permute-start | bytes 98312 | tf_op jit(solution)/shard_map/ppermute | solution.py:70
  218.2 5.3 %collective-permute-start.23 = (f32[1,32,256]{2,1,0:T(8,128)}, f32[1,32,256]{2,1,0:T(8,128)S(1)}, u32[]{:S(2)}, u32[]{:S(2)}) collective-permute-start(f32[1,32,256]{2,1,0:T(8,128)} %get-tuple-element.82), channel_id=1, source_target_pairs={{0,96},{8,104},{16,112},{24,120},{32,0},{40,8},{48,16},{56,24},{64... | collective-permute-start | bytes 98312 | tf_op jit(solution)/shard_map/ppermute | solution.py:70
  222.7 3.9 %copy-start.17 = (f32[1,32,256]{2,1,0:T(8,128)}, f32[1,32,256]{2,1,0:T(8,128)S(1)}, u32[]{:S(2)}) copy-start(f32[1,32,256]{2,1,0:T(8,128)S(1)} %collective-permute-done.21.refs_4_) | copy-start | bytes 98308
  223.5 3.0 %copy-start.19 = (f32[1,32,256]{2,1,0:T(8,128)}, f32[1,32,256]{2,1,0:T(8,128)S(1)}, u32[]{:S(2)}) copy-start(f32[1,32,256]{2,1,0:T(8,128)S(1)} %collective-permute-done.22.refs_5_) | copy-start | bytes 98308
  223.5 3.0 %copy-start.20 = (f32[1,32,256]{2,1,0:T(8,128)}, f32[1,32,256]{2,1,0:T(8,128)S(1)}, u32[]{:S(2)}) copy-start(f32[1,32,256]{2,1,0:T(8,128)S(1)} %collective-permute-done.23.refs_6_) | copy-start | bytes 98308
  (5 other events, 4.0 us)
Sparse Core Ops, SparseCore 0:
  18.1 54.1 all-gather.2

commit v9 on v8

--- a/solution.py
+++ b/solution.py
@@ -94,8 +94,9 @@
     )
 
 
-def transform_kernel(index, scalars, part, orbitals, out, rows_in, orbitals_in, sems):
-    place, half = scalars[0], scalars[1]
+def transform_kernel(index, keeps, part, orbitals, out, rows_in, orbitals_in, sems):
+    col = lax.axis_index("col")
+    place, half = col // ZH, lax.rem(col + (0 if keeps else 1), ZH)
     run, each, width = orbitals_in.shape[1:]
     copies = []
     for k in range(X):
@@ -118,13 +119,13 @@
         out[...] = out[...] + term if k else term
 
 
-def transformed(part, index, orbitals, place, half, cost=0):
+def transformed(part, index, orbitals, keeps, cost):
     rows, width = part.shape[2:]
     blocks, _, each, _ = orbitals.shape
     run = blocks // ZH
     return pl.pallas_call(
-        functools.partial(transform_kernel, index),
-        in_specs=[pl.BlockSpec(memory_space=pltpu.SMEM)] + [pl.BlockSpec(memory_space=pl.ANY)] * 2,
+        functools.partial(transform_kernel, index, keeps),
+        in_specs=[pl.BlockSpec(memory_space=pl.ANY)] * 2,
         out_specs=pl.BlockSpec(memory_space=pltpu.VMEM),
         out_shape=jax.ShapeDtypeStruct((rows, run * each), jnp.float32),
         scratch_shapes=[
@@ -134,7 +135,7 @@
         ],
         cost_estimate=pl.CostEstimate(flops=cost, bytes_accessed=0, transcendentals=0),
         name="transform",
-    )(jnp.stack([place, half]), part, orbitals)
+    )(part, orbitals)
 
 
 def gram_kernel(pairs, chunks, more, *refs):
@@ -245,8 +246,7 @@
 def on_device(three_index, coefficients):
     rows, aux, width = three_index.shape
     by_aux = three_index.transpose(1, 0, 2)
-    blk, col = lax.axis_index("blk"), lax.axis_index("col")
-    place, zh = col // ZH, col % ZH
+    blk = lax.axis_index("blk")
     swap_zh = [(x * ZH + 1 - h, x * ZH + h) for x in range(X) for h in range(ZH)]
     shares = lax.axis_size("col")
 
@@ -275,10 +275,10 @@
     last_part = over_x(last)
 
     def to_send(part, k):
-        return transformed(part, k, orbitals, place, 1 - zh, SENT_COST)
+        return transformed(part, k, orbitals, False, SENT_COST)
 
     def kept(part, k):
-        return transformed(part, k, orbitals, place, zh, KEPT_COST)
+        return transformed(part, k, orbitals, True, KEPT_COST)
 
     def neighbours(own):
         return fetched(own, other_core), fetched(own, next_row), fetched(own, previous_row)
@@ -295,6 +295,7 @@
     across_0 = fetched(below_0, over_to_across)
     other_1, below_1, above_1 = neighbours(own_1)
     other_1, below_1, above_1, own_2 = together(other_1, below_1, above_1, own_2)
+    across_0, below_1 = together(across_0, below_1)
     across_1 = fetched(below_1, over_to_across)
     other_2, below_2, above_2 = neighbours(own_2)
     known = [(own_0, own_1), (other_0, other_1), (below_0, below_1), (above_0, above_1)]

time: 237 us -> 234 us (0.987)
  Pallas kernels: 57.3 us -> 53.3 us
    all_to_all x3, waiting for transfers between devices: 10 us -> 14.6 us  [over_col(): return lax.all_to_all(tiles, 'col', split_axis=0, concat_axis=0, tiled=True)]
    ppermute x12, waiting for transfers between devices: 21.4 us -> 17.2 us  [fetched(): return lax.ppermute(value, 'blk', route)]
    pallas_call x6, Pallas kernels: 30.3 us -> 26.3 us  [transformed(): pl.pallas_call(functools.partial(transform_kernel, index, keeps), in_spec...]
    unnamed x44 -> x46, local copies, waits for them, and re-layouts: 4.16 us -> 4.98 us
  transfers between devices with their start and end apart: 31 -> 31, of which waited for: 12 -> 14; matrix products, arithmetic and copies ran while one was open for 6% -> 5% of each run, Pallas kernels for 22% -> 20%
where the time goes in v9:
time: 234 us; the launch traced here: 233 us
  waiting for transfers between devices  92.2 us (39%)
  starting transfers between devices  55.5 us (24%)
  Pallas kernels  53.3 us (23%)
  local copies, waits for them, and re-layouts  13.9 us (6%)
  between operations  13.7 us (6%)
  other arithmetic  4.36 us (2%)
    all_to_all x2, waiting for transfers between devices, over_x(): lax.all_to_all(part, 'col', split_axis=0, concat_axis=0, tiled=True, axis...  45.1 us
    pallas_call x6, Pallas kernels, transformed(): pl.pallas_call(functools.partial(transform_kernel, index, keeps), in_spec...  26.3 us
    pallas_call x4, Pallas kernels, gram(): pl.pallas_call(functools.partial(gram_kernel, pairs, chunks, more), in_sp...  19 us
    ppermute x12, waiting for transfers between devices, fetched(): return lax.ppermute(value, 'blk', route)  17.2 us
    all_to_all x3, waiting for transfers between devices, over_col(): return lax.all_to_all(tiles, 'col', split_axis=0, concat_axis=0, tiled=True)  14.6 us
    all_to_all x3, starting transfers between devices, over_col(): return lax.all_to_all(tiles, 'col', split_axis=0, concat_axis=0, tiled=True)  14.3 us
    ppermute x12, starting transfers between devices, fetched(): return lax.ppermute(value, 'blk', route)  11.8 us
    ppermute x7, waiting for transfers between devices, delivered(): return lax.ppermute(value, 'blk', route)  11 us
  transfers between devices with their start and end apart: 31, of which 14 were waited for; matrix products, arithmetic and copies ran while one was open for 5% of the time, Pallas kernels for 20%

profile of v9, /device:TPU:0, one launch (start us, length us, event | category | flops | bytes accessed | tf_op | source)
XLA Modules:
  0.0 233.0 jit_solution(11969723493629431368)
XLA Ops:
  6.5 1.6 collective-permute-start.2
  8.1 2.7 %collective-permute-start.1 = (f32[64,512]{1,0:T(8,128)}, f32[64,512]{1,0:T(8,128)S(1)}, u32[]{:S(2)}, u32[]{:S(2)}) collective-permute-start(f32[64,512]{1,0:T(8,128)} %bitcast.14), channel_id=1, source_target_pairs={{4,0},{5,1},{6,2},{7,3},{0,4},{1,5},{2,6},{3,7},{12,8},{13,9},{14,... | collective-permute-start | bytes 393224 | tf_op jit(solution)/shard_map/ppermute | solution.py:269
  10.8 1.4 collective-permute-start
  12.3 4.6 %slice.9 = f32[8,256,512]{2,1,0:T(8,128)} slice(f32[12,256,512]{2,1,0:T(8,128)} %bitcast.11), slice={[0:8], [0:256], [0:512]} | slice | bytes 8388608 | tf_op jit(solution)/shard_map/slice | solution.py:270
  17.9 4.9 %all-to-all-start = ((f32[8,256,512]{2,1,0:T(8,128)}), f32[8,256,512]{2,1,0:T(8,128)}, u32[]{:S(2)}, u32[]{:S(2)}) async-start(f32[8,256,512]{2,1,0:T(8,128)} %slice.9), calls=%async_computation | async-start | bytes 8388608 | tf_op jit(solution)/shard_map/all_to_all | solution.py:254
  22.8 3.1 %slice.8 = f32[4,256,512]{2,1,0:T(8,128)} slice(f32[12,256,512]{2,1,0:T(8,128)} %bitcast.12), slice={[8:12], [0:256], [0:512]} | slice | bytes 4194304 | tf_op jit(solution)/shard_map/slice | solution.py:274
  25.9 45.1 %all-to-all-done = f32[8,256,512]{2,1,0:T(8,128)} async-done(((f32[8,256,512]{2,1,0:T(8,128)}), f32[8,256,512]{2,1,0:T(8,128)}, u32[]{:S(2)}, u32[]{:S(2)}) %all-to-all-start) | async-done | bytes 4194336 | tf_op jit(solution)/shard_map/all_to_all | solution.py:254
  71.1 4.4 %all-to-all-start.1 = ((f32[4,256,512]{2,1,0:T(8,128)}), f32[4,256,512]{2,1,0:T(8,128)}, u32[]{:S(2)}, u32[]{:S(2)}) async-start(f32[4,256,512]{2,1,0:T(8,128)} %slice.8), calls=%async_computation.1 | async-start | bytes 4194304 | tf_op jit(solution)/shard_map/all_to_all | solution.py:254
  75.6 4.4 %transform.7 = f32[256,512]{1,0:T(8,128)} custom-call(f32[4,2,256,512]{3,2,1,0:T(8,128)} %bitcast.3.part, f32[16,4,64,512]{3,2,1,0:T(8,128)} %bitcast.20), custom_call_target="tpu_custom_call" | custom-call | flops 5000000000 | tf_op jit(solution)/shard_map/transform/pallas_call | solution.py:126
  79.9 4.0 %collective-permute-start.3 = (f32[256,512]{1,0:T(8,128)}, f32[256,512]{1,0:T(8,128)S(1)}, u32[]{:S(2)}, u32[]{:S(2)}) collective-permute-start(f32[256,512]{1,0:T(8,128)} %transform.7), channel_id=1, source_target_pairs={{1,0},{0,1},{3,2},{2,3},{5,4},{4,5},{7,6},{6,7},{9,8},{8,9},{11,10... | collective-permute-start | bytes 1572872 | tf_op jit(solution)/shard_map/ppermute | solution.py:260
  83.9 4.4 %transform.10 = f32[256,512]{1,0:T(8,128)} custom-call(f32[4,2,256,512]{3,2,1,0:T(8,128)} %bitcast.3.part, f32[16,4,64,512]{3,2,1,0:T(8,128)} %bitcast.21), custom_call_target="tpu_custom_call" | custom-call | flops 5000000000 | tf_op jit(solution)/shard_map/transform/pallas_call | solution.py:126
  88.4 4.4 %transform.6 = f32[256,512]{1,0:T(8,128)} custom-call(f32[4,2,256,512]{3,2,1,0:T(8,128)} %bitcast.3.part, f32[16,4,64,512]{3,2,1,0:T(8,128)} %bitcast.22), custom_call_target="tpu_custom_call" | custom-call | flops 5000000000 | tf_op jit(solution)/shard_map/transform/pallas_call | solution.py:126
  92.8 4.1 %collective-permute-done.3 = f32[256,512]{1,0:T(8,128)S(1)} collective-permute-done((f32[256,512]{1,0:T(8,128)}, f32[256,512]{1,0:T(8,128)S(1)}, u32[]{:S(2)}, u32[]{:S(2)}) %collective-permute-start.3) | collective-permute-done | bytes 524320 | tf_op jit(solution)/shard_map/ppermute | solution.py:260
  97.0 1.1 add.13.refs_0_
  98.1 1.6 collective-permute-start.6
  99.7 1.7 collective-permute-start.5
  101.4 4.4 %transform.8 = f32[256,512]{1,0:T(8,128)} custom-call(f32[4,1,256,512]{3,2,1,0:T(8,128)} %bitcast.9.part, f32[16,4,64,512]{3,2,1,0:T(8,128)} %bitcast.23), custom_call_target="tpu_custom_call" | custom-call | flops 5000000000 | tf_op jit(solution)/shard_map/transform/pallas_call | solution.py:126
  105.8 3.8 %collective-permute-start.11 = (f32[256,512]{1,0:T(8,128)}, f32[256,512]{1,0:T(8,128)}, u32[]{:S(2)}, u32[]{:S(2)}) collective-permute-start(f32[256,512]{1,0:T(8,128)} %transform.8), channel_id=1, source_target_pairs={{1,0},{0,1},{3,2},{2,3},{5,4},{4,5},{7,6},{6,7},{9,8},{8,9},{11,10... | collective-permute-start | bytes 1572872 | tf_op jit(solution)/shard_map/ppermute | solution.py:260
  109.6 4.4 %transform.9 = f32[256,512]{1,0:T(8,128)} custom-call(f32[4,2,256,512]{3,2,1,0:T(8,128)} %bitcast.3.part, f32[16,4,64,512]{3,2,1,0:T(8,128)} %bitcast.24), custom_call_target="tpu_custom_call" | custom-call | flops 5000000000 | tf_op jit(solution)/shard_map/transform/pallas_call | solution.py:126
  114.0 1.1 add.14.refs_1_
  116.2 2.3 collective-permute-start.9
  118.5 1.1 collective-permute-start.15
  119.7 4.4 %transform.11 = f32[256,512]{1,0:T(8,128)} custom-call(f32[4,1,256,512]{3,2,1,0:T(8,128)} %bitcast.9.part, f32[16,4,64,512]{3,2,1,0:T(8,128)} %bitcast.25), custom_call_target="tpu_custom_call" | custom-call | flops 5000000000 | tf_op jit(solution)/shard_map/transform/pallas_call | solution.py:126
  124.1 1.3 add.15.refs_0_
  125.4 5.1 %collective-permute-done.10.refs_7_ = f32[256,512]{1,0:T(8,128)S(1)} collective-permute-done((f32[256,512]{1,0:T(8,128)S(1)}, f32[256,512]{1,0:T(8,128)S(1)}, u32[]{:S(2)}, u32[]{:S(2)}) %collective-permute-start.10) | collective-permute-done | bytes 524320 | tf_op jit(solution)/shard_map/ppermute | solution.py:65
  130.8 3.0 %collective-permute-start.13 = (f32[256,512]{1,0:T(8,128)S(1)}, f32[256,512]{1,0:T(8,128)}, u32[]{:S(2)}, u32[]{:S(2)}) collective-permute-start(f32[256,512]{1,0:T(8,128)S(1)} %add.15.refs_0_), channel_id=1, source_target_pairs={{32,0},{40,8},{48,16},{56,24},{64,32},{72,40},{80,48},{88,56},{96,... | collective-permute-start | bytes 1572872 | tf_op jit(solution)/shard_map/ppermute | solution.py:65
  135.0 5.4 %gram.4.refs_4_ = f32[8,5,32,256]{3,2,1,0:T(8,128)} custom-call(f32[256,512]{1,0:T(8,128)} %copy-done.1, f32[256,512]{1,0:T(8,128)} %copy-done.2, f32[256,512]{1,0:T(8,128)} %copy-done.7, f32[256,512]{1,0:T(8,128)} %collective-permute-done.8.refs_3_, f32[256,512]{1,0:T(8,128)} %copy-done.6, f32[256,512]{1,0:T(8,128)} %collective-permute-done.9.refs_5_, ...), custom_call_target="tpu_custom_call" | custom-call | tf_op jit(solution)/shard_map/gram/pallas_call | solution.py:178
  140.5 4.6 %collective-permute-done.14.refs_3_ = f32[256,512]{1,0:T(8,128)S(1)} collective-permute-done((f32[256,512]{1,0:T(8,128)S(1)}, f32[256,512]{1,0:T(8,128)S(1)}, u32[]{:S(2)}, u32[]{:S(2)}) %collective-permute-start.14) | collective-permute-done | bytes 524320 | tf_op jit(solution)/shard_map/ppermute | solution.py:65
  146.1 4.3 %gram.5 = f32[8,5,32,256]{3,2,1,0:T(8,128)} custom-call(f32[256,512]{1,0:T(8,128)} %copy-done.4, f32[256,512]{1,0:T(8,128)} %copy-done.12, f32[256,512]{1,0:T(8,128)} %collective-permute-done.13.refs_2_, f32[256,512]{1,0:T(8,128)} %copy-done.11, f32[8,5,32,256]{3,2,1,0:T(8,128)} %gram.4.refs_4_), custom_call_target="tpu_custom_call" | custom-call | tf_op jit(solution)/shard_map/gram/pallas_call | solution.py:178
  150.4 6.0 %all-to-all-start.2 = ((f32[8,5,32,256]{3,2,1,0:T(8,128)}), f32[8,5,32,256]{3,2,1,0:T(8,128)S(1)}, u32[]{:S(2)}, u32[]{:S(2)}) async-start(f32[8,5,32,256]{3,2,1,0:T(8,128)} %gram.5), calls=%async_computation.2 | async-start | bytes 2621440 | tf_op jit(solution)/shard_map/all_to_all | solution.py:263
  157.2 5.3 %gram.6.refs_5_ = f32[8,4,32,256]{3,2,1,0:T(8,128)} custom-call(f32[256,512]{1,0:T(8,128)} %copy-done.1, f32[256,512]{1,0:T(8,128)} %copy-done.2, f32[256,512]{1,0:T(8,128)} %copy-done.7, f32[256,512]{1,0:T(8,128)} %collective-permute-done.8.refs_3_, f32[256,512]{1,0:T(8,128)} %copy-done.6, f32[256,512]{1,0:T(8,128)} %collective-permute-done.9.refs_5_, ...), custom_call_target="tpu_custom_call" | custom-call | tf_op jit(solution)/shard_map/gram/pallas_call | solution.py:178
  162.5 6.9 %collective-permute-done.16.refs_4_ = f32[256,512]{1,0:T(8,128)S(1)} collective-permute-done((f32[256,512]{1,0:T(8,128)}, f32[256,512]{1,0:T(8,128)S(1)}, u32[]{:S(2)}, u32[]{:S(2)}) %collective-permute-start.16) | collective-permute-done | bytes 524320 | tf_op jit(solution)/shard_map/ppermute | solution.py:65
  170.1 4.0 %gram.7 = f32[8,4,32,256]{3,2,1,0:T(8,128)} custom-call(f32[256,512]{1,0:T(8,128)} %copy-done.4, f32[256,512]{1,0:T(8,128)} %copy-done.12, f32[256,512]{1,0:T(8,128)} %collective-permute-done.13.refs_2_, f32[256,512]{1,0:T(8,128)} %copy-done.11, f32[256,512]{1,0:T(8,128)} %copy-done.22, f32[8,4,32,256]{3,2,1,0:T(8,128)} %gram.6.refs_5_), custom_call_target="tpu_custom_call" | custom-call | flops 20000000000 | tf_op jit(solution)/shard_map/gram/pallas_call | solution.py:178
  174.1 4.0 %all-to-all-done.2.moved_ref = f32[8,5,32,256]{3,2,1,0:T(8,128)S(1)} async-done(((f32[8,5,32,256]{3,2,1,0:T(8,128)}), f32[8,5,32,256]{3,2,1,0:T(8,128)S(1)}, u32[]{:S(2)}, u32[]{:S(2)}) %all-to-all-start.2) | async-done | bytes 1310752 | tf_op jit(solution)/shard_map/all_to_all | solution.py:263
  178.2 4.0 %all-to-all-start.3 = ((f32[8,4,32,256]{3,2,1,0:T(8,128)}), f32[8,4,32,256]{3,2,1,0:T(8,128)S(1)}, u32[]{:S(2)}, u32[]{:S(2)}) async-start(f32[8,4,32,256]{3,2,1,0:T(8,128)} %gram.7), calls=%async_computation.3 | async-start | bytes 2097152 | tf_op jit(solution)/shard_map/all_to_all | solution.py:263
  182.2 2.1 sum.2
  184.3 1.2 collective-permute-start.19
  185.5 2.0 collective-permute-start.20
  187.5 2.1 collective-permute-done.20.refs_1_
  190.3 7.5 %all-to-all-done.3.moved_ref = f32[8,4,32,256]{3,2,1,0:T(8,128)S(1)} async-done(((f32[8,4,32,256]{3,2,1,0:T(8,128)}), f32[8,4,32,256]{3,2,1,0:T(8,128)S(1)}, u32[]{:S(2)}, u32[]{:S(2)}) %all-to-all-start.3) | async-done | bytes 1048608 | tf_op jit(solution)/shard_map/all_to_all | solution.py:263
  198.9 2.0 sum.3
  200.8 7.3 %collective-permute-done.24.refs_2_ = f32[4,32,256]{2,1,0:T(8,128)S(1)} collective-permute-done((f32[4,32,256]{2,1,0:T(8,128)}, f32[4,32,256]{2,1,0:T(8,128)S(1)}, u32[]{:S(2)}, u32[]{:S(2)}) %collective-permute-start.24) | collective-permute-done | bytes 131104 | tf_op jit(solution)/shard_map/ppermute | solution.py:70
  208.8 1.8 turn.1
  210.6 4.2 %all-to-all-start.4 = ((f32[8,32,256]{2,1,0:T(8,128)}), f32[8,32,256]{2,1,0:T(8,128)S(1)}, u32[]{:S(2)}, u32[]{:S(2)}) async-start(f32[8,32,256]{2,1,0:T(8,128)} %turn.1), calls=%async_computation.4 | async-start | bytes 524288 | tf_op jit(solution)/shard_map/all_to_all | solution.py:263
  214.9 3.2 %collective-permute-start.23 = (f32[1,32,256]{2,1,0:T(8,128)}, f32[1,32,256]{2,1,0:T(8,128)S(1)}, u32[]{:S(2)}, u32[]{:S(2)}) collective-permute-start(f32[1,32,256]{2,1,0:T(8,128)} %get-tuple-element.86), channel_id=1, source_target_pairs={{0,96},{8,104},{16,112},{24,120},{32,0},{40,8},{48,16},{56,24},{64... | collective-permute-start | bytes 98312 | tf_op jit(solution)/shard_map/ppermute | solution.py:70
  218.1 1.2 dynamic-slice_bitcast_fusion.table_ref
  220.2 3.0 %all-to-all-done.4.refs_7_ = f32[8,32,256]{2,1,0:T(8,128)S(1)} async-done(((f32[8,32,256]{2,1,0:T(8,128)}), f32[8,32,256]{2,1,0:T(8,128)S(1)}, u32[]{:S(2)}, u32[]{:S(2)}) %all-to-all-start.4) | async-done | bytes 262176 | tf_op jit(solution)/shard_map/all_to_all | solution.py:263
  223.9 2.2 assemble.1
  (82 shorter events, 10.4 us)
Async XLA Ops:
  6.5 69.0 %all-gather.3.cloned.1.call-start = ((), (), s32[]{:S(2)}) async-start(), calls=%async_computation.5 | async-start | bytes 8912896 | tf_op jit(solution)/shard_map/all_gather | solution.py:273
  6.5 10.3 %collective-permute-start.2 = (f32[64,512]{1,0:T(8,128)}, f32[64,512]{1,0:T(8,128)S(1)}, u32[]{:S(2)}, u32[]{:S(2)}) collective-permute-start(f32[64,512]{1,0:T(8,128)} %bitcast.13), channel_id=1, source_target_pairs={{6,0},{7,1},{0,2},{1,3},{2,4},{3,5},{4,6},{5,7},{14,8},{15,9},{8,1... | collective-permute-start | bytes 393224 | tf_op jit(solution)/shard_map/ppermute | solution.py:269
  8.1 9.0 %collective-permute-start.1 = (f32[64,512]{1,0:T(8,128)}, f32[64,512]{1,0:T(8,128)S(1)}, u32[]{:S(2)}, u32[]{:S(2)}) collective-permute-start(f32[64,512]{1,0:T(8,128)} %bitcast.14), channel_id=1, source_target_pairs={{4,0},{5,1},{6,2},{7,3},{0,4},{1,5},{2,6},{3,7},{12,8},{13,9},{14,... | collective-permute-start | bytes 393224 | tf_op jit(solution)/shard_map/ppermute | solution.py:269
  10.8 6.2 %collective-permute-start = (f32[64,512]{1,0:T(8,128)}, f32[64,512]{1,0:T(8,128)S(1)}, u32[]{:S(2)}, u32[]{:S(2)}) collective-permute-start(f32[64,512]{1,0:T(8,128)} %bitcast.15), channel_id=1, source_target_pairs={{2,0},{3,1},{4,2},{5,3},{6,4},{7,5},{0,6},{1,7},{10,8},{11,9},{12,... | collective-permute-start | bytes 393224 | tf_op jit(solution)/shard_map/ppermute | solution.py:269
  12.3 4.8 %copy-start.16 = (f32[512,64]{0,1:T(8,128)S(1)}, f32[512,64]{0,1:T(8,128)}, u32[]{:S(2)}) copy-start(f32[512,64]{0,1:T(8,128)} %param.4) | copy-start | bytes 393220
  17.9 53.1 %all-to-all-start = ((f32[8,256,512]{2,1,0:T(8,128)}), f32[8,256,512]{2,1,0:T(8,128)}, u32[]{:S(2)}, u32[]{:S(2)}) async-start(f32[8,256,512]{2,1,0:T(8,128)} %slice.9), calls=%async_computation | async-start | bytes 8388608 | tf_op jit(solution)/shard_map/all_to_all | solution.py:254
  71.1 30.3 %all-to-all-start.1 = ((f32[4,256,512]{2,1,0:T(8,128)}), f32[4,256,512]{2,1,0:T(8,128)}, u32[]{:S(2)}, u32[]{:S(2)}) async-start(f32[4,256,512]{2,1,0:T(8,128)} %slice.8), calls=%async_computation.1 | async-start | bytes 4194304 | tf_op jit(solution)/shard_map/all_to_all | solution.py:254
  79.9 17.0 %collective-permute-start.3 = (f32[256,512]{1,0:T(8,128)}, f32[256,512]{1,0:T(8,128)S(1)}, u32[]{:S(2)}, u32[]{:S(2)}) collective-permute-start(f32[256,512]{1,0:T(8,128)} %transform.7), channel_id=1, source_target_pairs={{1,0},{0,1},{3,2},{2,3},{5,4},{4,5},{7,6},{6,7},{9,8},{8,9},{11,10... | collective-permute-start | bytes 1572872 | tf_op jit(solution)/shard_map/ppermute | solution.py:260
  88.3 25.7 %collective-permute-start.7 = (f32[256,512]{1,0:T(8,128)}, f32[256,512]{1,0:T(8,128)S(1)}, u32[]{:S(2)}, u32[]{:S(2)}) collective-permute-start(f32[256,512]{1,0:T(8,128)} %transform.10), channel_id=1, source_target_pairs={{1,0},{0,1},{3,2},{2,3},{5,4},{4,5},{7,6},{6,7},{9,8},{8,9},{11,10... | collective-permute-start | bytes 1572872 | tf_op jit(solution)/shard_map/ppermute | solution.py:260
  98.1 7.7 %copy-start.1 = (f32[256,512]{1,0:T(8,128)}, f32[256,512]{1,0:T(8,128)S(1)}, u32[]{:S(2)}) copy-start(f32[256,512]{1,0:T(8,128)S(1)} %add.13.refs_0_) | copy-start | bytes 1572868
  98.1 17.1 %collective-permute-start.6 = (f32[256,512]{1,0:T(8,128)S(1)}, f32[256,512]{1,0:T(8,128)S(1)}, u32[]{:S(2)}, u32[]{:S(2)}) collective-permute-start(f32[256,512]{1,0:T(8,128)S(1)} %add.13.refs_0_), channel_id=1, source_target_pairs={{96,0},{104,8},{112,16},{120,24},{0,32},{8,40},{16,48},{24,56},{40... | collective-permute-start | bytes 1572872 | tf_op jit(solution)/shard_map/ppermute | solution.py:65
  99.7 15.4 %collective-permute-start.5 = (f32[256,512]{1,0:T(8,128)S(1)}, f32[256,512]{1,0:T(8,128)S(1)}, u32[]{:S(2)}, u32[]{:S(2)}) collective-permute-start(f32[256,512]{1,0:T(8,128)S(1)} %add.13.refs_0_), channel_id=1, source_target_pairs={{32,0},{40,8},{48,16},{56,24},{64,32},{72,40},{80,48},{88,56},{96,... | collective-permute-start | bytes 1572872 | tf_op jit(solution)/shard_map/ppermute | solution.py:65
  101.4 13.8 %collective-permute-start.4 = (f32[256,512]{1,0:T(8,128)S(1)}, f32[256,512]{1,0:T(8,128)S(1)}, u32[]{:S(2)}, u32[]{:S(2)}) collective-permute-start(f32[256,512]{1,0:T(8,128)S(1)} %add.13.refs_0_), channel_id=1, source_target_pairs={{8,0},{0,8},{24,16},{16,24},{40,32},{32,40},{56,48},{48,56},{72,64... | collective-permute-start | bytes 1572872 | tf_op jit(solution)/shard_map/ppermute | solution.py:65
  105.8 18.3 %collective-permute-start.11 = (f32[256,512]{1,0:T(8,128)}, f32[256,512]{1,0:T(8,128)}, u32[]{:S(2)}, u32[]{:S(2)}) collective-permute-start(f32[256,512]{1,0:T(8,128)} %transform.8), channel_id=1, source_target_pairs={{1,0},{0,1},{3,2},{2,3},{5,4},{4,5},{7,6},{6,7},{9,8},{8,9},{11,10... | collective-permute-start | bytes 1572872 | tf_op jit(solution)/shard_map/ppermute | solution.py:260
  115.1 8.9 %copy-start.2 = (f32[256,512]{1,0:T(8,128)}, f32[256,512]{1,0:T(8,128)S(1)}, u32[]{:S(2)}) copy-start(f32[256,512]{1,0:T(8,128)S(1)} %add.14.refs_1_) | copy-start | bytes 1572868
  115.2 8.9 %copy-start.5 = (f32[256,512]{1,0:T(8,128)}, f32[256,512]{1,0:T(8,128)S(1)}, u32[]{:S(2)}) copy-start(f32[256,512]{1,0:T(8,128)S(1)} %collective-permute-done.6.refs_6_) | copy-start | bytes 1572868
  115.2 8.9 %copy-start.6 = (f32[256,512]{1,0:T(8,128)}, f32[256,512]{1,0:T(8,128)S(1)}, u32[]{:S(2)}) copy-start(f32[256,512]{1,0:T(8,128)S(1)} %collective-permute-done.5.refs_4_) | copy-start | bytes 1572868
  115.2 8.9 %copy-start.7 = (f32[256,512]{1,0:T(8,128)}, f32[256,512]{1,0:T(8,128)S(1)}, u32[]{:S(2)}) copy-start(f32[256,512]{1,0:T(8,128)S(1)} %collective-permute-done.4.refs_2_) | copy-start | bytes 1572868
  115.2 15.3 %collective-permute-start.10 = (f32[256,512]{1,0:T(8,128)S(1)}, f32[256,512]{1,0:T(8,128)S(1)}, u32[]{:S(2)}, u32[]{:S(2)}) collective-permute-start(f32[256,512]{1,0:T(8,128)S(1)} %add.14.refs_1_), channel_id=1, source_target_pairs={{96,0},{104,8},{112,16},{120,24},{0,32},{8,40},{16,48},{24,56},{40... | collective-permute-start | bytes 1572872 | tf_op jit(solution)/shard_map/ppermute | solution.py:65
  116.2 14.3 %collective-permute-start.9 = (f32[256,512]{1,0:T(8,128)S(1)}, f32[256,512]{1,0:T(8,128)}, u32[]{:S(2)}, u32[]{:S(2)}) collective-permute-start(f32[256,512]{1,0:T(8,128)S(1)} %add.14.refs_1_), channel_id=1, source_target_pairs={{32,0},{40,8},{48,16},{56,24},{64,32},{72,40},{80,48},{88,56},{96,... | collective-permute-start | bytes 1572872 | tf_op jit(solution)/shard_map/ppermute | solution.py:65
  118.5 12.0 %collective-permute-start.8 = (f32[256,512]{1,0:T(8,128)S(1)}, f32[256,512]{1,0:T(8,128)}, u32[]{:S(2)}, u32[]{:S(2)}) collective-permute-start(f32[256,512]{1,0:T(8,128)S(1)} %add.14.refs_1_), channel_id=1, source_target_pairs={{8,0},{0,8},{24,16},{16,24},{40,32},{32,40},{56,48},{48,56},{72,64... | collective-permute-start | bytes 1572872 | tf_op jit(solution)/shard_map/ppermute | solution.py:65
  118.5 15.9 %collective-permute-start.15 = (f32[256,512]{1,0:T(8,128)S(1)}, f32[256,512]{1,0:T(8,128)S(1)}, u32[]{:S(2)}, u32[]{:S(2)}) collective-permute-start(f32[256,512]{1,0:T(8,128)S(1)} %collective-permute-done.5.refs_4_), channel_id=1, source_target_pairs={{16,0},{24,8},{8,16},{0,24},{48,32},{56,40},{40,48},{32,56},{88,64... | collective-permute-start | bytes 1572872 | tf_op jit(solution)/shard_map/ppermute | solution.py:65
  125.4 15.1 %copy-start.4 = (f32[256,512]{1,0:T(8,128)}, f32[256,512]{1,0:T(8,128)S(1)}, u32[]{:S(2)}) copy-start(f32[256,512]{1,0:T(8,128)S(1)} %add.15.refs_0_) | copy-start | bytes 1572868
  130.5 4.5 %copy-start.8 = (f32[256,512]{1,0:T(8,128)}, f32[256,512]{1,0:T(8,128)S(1)}, u32[]{:S(2)}) copy-start(f32[256,512]{1,0:T(8,128)S(1)} %collective-permute-done.10.refs_7_) | copy-start | bytes 1572868
  130.5 14.5 %collective-permute-start.14 = (f32[256,512]{1,0:T(8,128)S(1)}, f32[256,512]{1,0:T(8,128)S(1)}, u32[]{:S(2)}, u32[]{:S(2)}) collective-permute-start(f32[256,512]{1,0:T(8,128)S(1)} %add.15.refs_0_), channel_id=1, source_target_pairs={{96,0},{104,8},{112,16},{120,24},{0,32},{8,40},{16,48},{24,56},{40... | collective-permute-start | bytes 1572872 | tf_op jit(solution)/shard_map/ppermute | solution.py:65
  130.8 14.2 %collective-permute-start.13 = (f32[256,512]{1,0:T(8,128)S(1)}, f32[256,512]{1,0:T(8,128)}, u32[]{:S(2)}, u32[]{:S(2)}) collective-permute-start(f32[256,512]{1,0:T(8,128)S(1)} %add.15.refs_0_), channel_id=1, source_target_pairs={{32,0},{40,8},{48,16},{56,24},{64,32},{72,40},{80,48},{88,56},{96,... | collective-permute-start | bytes 1572872 | tf_op jit(solution)/shard_map/ppermute | solution.py:65
  133.9 11.2 %collective-permute-start.12 = (f32[256,512]{1,0:T(8,128)S(1)}, f32[256,512]{1,0:T(8,128)S(1)}, u32[]{:S(2)}, u32[]{:S(2)}) collective-permute-start(f32[256,512]{1,0:T(8,128)S(1)} %add.15.refs_0_), channel_id=1, source_target_pairs={{8,0},{0,8},{24,16},{16,24},{40,32},{32,40},{56,48},{48,56},{72,64... | collective-permute-start | bytes 1572872 | tf_op jit(solution)/shard_map/ppermute | solution.py:65
  134.4 6.1 %copy-start.10 = (f32[256,512]{1,0:T(8,128)}, f32[256,512]{1,0:T(8,128)S(1)}, u32[]{:S(2)}) copy-start(f32[256,512]{1,0:T(8,128)S(1)} %collective-permute-done.15.refs_8_) | copy-start | bytes 1572868
  134.4 22.0 %collective-permute-start.17 = (f32[256,512]{1,0:T(8,128)}, f32[256,512]{1,0:T(8,128)S(1)}, u32[]{:S(2)}, u32[]{:S(2)}) collective-permute-start(f32[256,512]{1,0:T(8,128)} %collective-permute-done.9.refs_5_), channel_id=1, source_target_pairs={{16,0},{24,8},{8,16},{0,24},{48,32},{56,40},{40,48},{32,56},{88,64... | collective-permute-start | bytes 1572872 | tf_op jit(solution)/shard_map/ppermute | solution.py:65
  145.1 24.3 %collective-permute-start.16 = (f32[256,512]{1,0:T(8,128)}, f32[256,512]{1,0:T(8,128)S(1)}, u32[]{:S(2)}, u32[]{:S(2)}) collective-permute-start(f32[256,512]{1,0:T(8,128)} %collective-permute-done.13.refs_2_), channel_id=1, source_target_pairs={{16,0},{24,8},{8,16},{0,24},{48,32},{56,40},{40,48},{32,56},{88,64... | collective-permute-start | bytes 1572872 | tf_op jit(solution)/shard_map/ppermute | solution.py:65
  150.4 27.8 %all-to-all-start.2 = ((f32[8,5,32,256]{3,2,1,0:T(8,128)}), f32[8,5,32,256]{3,2,1,0:T(8,128)S(1)}, u32[]{:S(2)}, u32[]{:S(2)}) async-start(f32[8,5,32,256]{3,2,1,0:T(8,128)} %gram.5), calls=%async_computation.2 | async-start | bytes 2621440 | tf_op jit(solution)/shard_map/all_to_all | solution.py:263
  178.2 4.0 %copy-start = (f32[8,5,32,256]{3,2,1,0:T(8,128)}, f32[8,5,32,256]{3,2,1,0:T(8,128)S(1)}, u32[]{:S(2)}) copy-start(f32[8,5,32,256]{3,2,1,0:T(8,128)S(1)} %all-to-all-done.2.moved_ref) | copy-start | bytes 3932164
  178.2 19.7 %all-to-all-start.3 = ((f32[8,4,32,256]{3,2,1,0:T(8,128)}), f32[8,4,32,256]{3,2,1,0:T(8,128)S(1)}, u32[]{:S(2)}, u32[]{:S(2)}) async-start(f32[8,4,32,256]{3,2,1,0:T(8,128)} %gram.7), calls=%async_computation.3 | async-start | bytes 2097152 | tf_op jit(solution)/shard_map/all_to_all | solution.py:263
  184.3 6.0 %collective-permute-start.19 = (f32[3,32,256]{2,1,0:T(8,128)}, f32[3,32,256]{2,1,0:T(8,128)S(1)}, u32[]{:S(2)}, u32[]{:S(2)}) collective-permute-start(f32[3,32,256]{2,1,0:T(8,128)} %get-tuple-element.77), channel_id=1, source_target_pairs={{0,32},{8,40},{16,48},{24,56},{32,64},{40,72},{48,80},{56,88},{64,... | collective-permute-start | bytes 294920 | tf_op jit(solution)/shard_map/ppermute | solution.py:70
  185.5 2.0 collective-permute-start.18
  185.5 4.1 %collective-permute-start.20 = (f32[1,32,256]{2,1,0:T(8,128)}, f32[1,32,256]{2,1,0:T(8,128)S(1)}, u32[]{:S(2)}, u32[]{:S(2)}) collective-permute-start(f32[1,32,256]{2,1,0:T(8,128)} %get-tuple-element.78), channel_id=1, source_target_pairs={{0,96},{8,104},{16,112},{24,120},{32,0},{40,8},{48,16},{56,24},{64... | collective-permute-start | bytes 98312 | tf_op jit(solution)/shard_map/ppermute | solution.py:70
  187.5 35.7 %copy-start.17 = (f32[1,32,256]{2,1,0:T(8,128)}, f32[1,32,256]{2,1,0:T(8,128)S(1)}, u32[]{:S(2)}) copy-start(f32[1,32,256]{2,1,0:T(8,128)S(1)} %collective-permute-done.18.refs_1_) | copy-start | bytes 98308
  189.6 18.5 %copy-start.19 = (f32[1,32,256]{2,1,0:T(8,128)}, f32[1,32,256]{2,1,0:T(8,128)S(1)}, u32[]{:S(2)}) copy-start(f32[1,32,256]{2,1,0:T(8,128)S(1)} %collective-permute-done.20.refs_1_) | copy-start | bytes 98308
  190.3 17.8 %copy-start.14 = (f32[3,32,256]{2,1,0:T(8,128)}, f32[3,32,256]{2,1,0:T(8,128)S(1)}, u32[]{:S(2)}) copy-start(f32[3,32,256]{2,1,0:T(8,128)S(1)} %collective-permute-done.19.refs_0_.refs_2_) | copy-start | bytes 294916
  197.8 1.0 copy-start.3
  200.8 7.3 %collective-permute-start.24 = (f32[4,32,256]{2,1,0:T(8,128)}, f32[4,32,256]{2,1,0:T(8,128)S(1)}, u32[]{:S(2)}, u32[]{:S(2)}) collective-permute-start(f32[4,32,256]{2,1,0:T(8,128)} %get-tuple-element.88), channel_id=1, source_target_pairs={{0,48},{8,56},{16,40},{24,32},{32,80},{40,88},{48,72},{56,64},{64,... | collective-permute-start | bytes 393224 | tf_op jit(solution)/shard_map/ppermute | solution.py:70
  210.6 12.6 %all-to-all-start.4 = ((f32[8,32,256]{2,1,0:T(8,128)}), f32[8,32,256]{2,1,0:T(8,128)S(1)}, u32[]{:S(2)}, u32[]{:S(2)}) async-start(f32[8,32,256]{2,1,0:T(8,128)} %turn.1), calls=%async_computation.4 | async-start | bytes 524288 | tf_op jit(solution)/shard_map/all_to_all | solution.py:263
  214.8 4.5 %collective-permute-start.21 = (f32[1,32,256]{2,1,0:T(8,128)}, f32[1,32,256]{2,1,0:T(8,128)S(1)}, u32[]{:S(2)}, u32[]{:S(2)}) collective-permute-start(f32[1,32,256]{2,1,0:T(8,128)} %get-tuple-element.84), channel_id=1, source_target_pairs={{0,8},{8,0},{16,24},{24,16},{32,40},{40,32},{48,56},{56,48},{64,72... | collective-permute-start | bytes 98312 | tf_op jit(solution)/shard_map/ppermute | solution.py:70
  214.8 5.4 %collective-permute-start.22 = (f32[1,32,256]{2,1,0:T(8,128)}, f32[1,32,256]{2,1,0:T(8,128)S(1)}, u32[]{:S(2)}, u32[]{:S(2)}) collective-permute-start(f32[1,32,256]{2,1,0:T(8,128)} %get-tuple-element.85), channel_id=1, source_target_pairs={{0,32},{8,40},{16,48},{24,56},{32,64},{40,72},{48,80},{56,88},{64,... | collective-permute-start | bytes 98312 | tf_op jit(solution)/shard_map/ppermute | solution.py:70
  214.9 5.3 %collective-permute-start.23 = (f32[1,32,256]{2,1,0:T(8,128)}, f32[1,32,256]{2,1,0:T(8,128)S(1)}, u32[]{:S(2)}, u32[]{:S(2)}) collective-permute-start(f32[1,32,256]{2,1,0:T(8,128)} %get-tuple-element.86), channel_id=1, source_target_pairs={{0,96},{8,104},{16,112},{24,120},{32,0},{40,8},{48,16},{56,24},{64... | collective-permute-start | bytes 98312 | tf_op jit(solution)/shard_map/ppermute | solution.py:70
  219.3 4.0 %copy-start.18 = (f32[1,32,256]{2,1,0:T(8,128)}, f32[1,32,256]{2,1,0:T(8,128)S(1)}, u32[]{:S(2)}) copy-start(f32[1,32,256]{2,1,0:T(8,128)S(1)} %collective-permute-done.21.refs_4_) | copy-start | bytes 98308
  220.2 3.0 %copy-start.20 = (f32[1,32,256]{2,1,0:T(8,128)}, f32[1,32,256]{2,1,0:T(8,128)S(1)}, u32[]{:S(2)}) copy-start(f32[1,32,256]{2,1,0:T(8,128)S(1)} %collective-permute-done.22.refs_5_) | copy-start | bytes 98308
  220.2 3.0 %copy-start.21 = (f32[1,32,256]{2,1,0:T(8,128)}, f32[1,32,256]{2,1,0:T(8,128)S(1)}, u32[]{:S(2)}) copy-start(f32[1,32,256]{2,1,0:T(8,128)S(1)} %collective-permute-done.23.refs_6_) | copy-start | bytes 98308
  (6 other events, 4.9 us)
Sparse Core Ops, SparseCore 0:
  18.1 54.1 all-gather.2

commit v10 on v9

--- a/solution.py
+++ b/solution.py
@@ -285,11 +285,11 @@
 
     arrived_0 = to_other_half(to_send(first_part, 0))
     arrived_1 = to_other_half(to_send(first_part, 1))
+    kept_1, arrived_0 = together(kept(first_part, 1), arrived_0)
     own_0 = kept(first_part, 0) + arrived_0
     other_0, below_0, above_0 = neighbours(own_0)
-    leaving_2, first_part = together(to_send(last_part, 0), first_part)
-    arrived_2 = to_other_half(leaving_2)
-    own_1 = kept(first_part, 1) + arrived_1
+    arrived_2 = to_other_half(to_send(last_part, 0))
+    own_1 = kept_1 + arrived_1
     own_2 = kept(last_part, 0) + arrived_2
     other_0, below_0, above_0, own_1 = together(other_0, below_0, above_0, own_1)
     across_0 = fetched(below_0, over_to_across)

time: 234 us -> 234 us (level)
    ppermute x3, waiting for transfers between devices: 4.14 us -> 0.01 us  [to_other_half(): return lax.ppermute(value, 'col', swap_zh)]
    unnamed x46 -> x50, local copies, waits for them, and re-layouts: 4.98 us -> 4.96 us
  transfers between devices with their start and end apart: 31 -> 31, of which waited for: 14 -> 16; matrix products, arithmetic and copies ran while one was open for 5% -> 5% of each run, Pallas kernels for 20% -> 20%
where the time goes in v10:
time: 234 us; the launch traced here: 233 us
  waiting for transfers between devices  90.4 us (39%)
  starting transfers between devices  57.5 us (25%)
  Pallas kernels  53.5 us (23%)
  local copies, waits for them, and re-layouts  13.9 us (6%)
  between operations  13.7 us (6%)
  other arithmetic  4.36 us (2%)
    all_to_all x2, waiting for transfers between devices, over_x(): lax.all_to_all(part, 'col', split_axis=0, concat_axis=0, tiled=True, axis...  45.2 us
    pallas_call x6, Pallas kernels, transformed(): pl.pallas_call(functools.partial(transform_kernel, index, keeps), in_spec...  26.5 us
    ppermute x12, waiting for transfers between devices, fetched(): return lax.ppermute(value, 'blk', route)  19.2 us
    pallas_call x4, Pallas kernels, gram(): pl.pallas_call(functools.partial(gram_kernel, pairs, chunks, more), in_sp...  19 us
    all_to_all x3, starting transfers between devices, over_col(): return lax.all_to_all(tiles, 'col', split_axis=0, concat_axis=0, tiled=True)  15.9 us
    all_to_all x3, waiting for transfers between devices, over_col(): return lax.all_to_all(tiles, 'col', split_axis=0, concat_axis=0, tiled=True)  14.8 us
    ppermute x12, starting transfers between devices, fetched(): return lax.ppermute(value, 'blk', route)  12.4 us
    ppermute x7, waiting for transfers between devices, delivered(): return lax.ppermute(value, 'blk', route)  10.9 us
  transfers between devices with their start and end apart: 31, of which 16 were waited for; matrix products, arithmetic and copies ran while one was open for 5% of the time, Pallas kernels for 20%

profile of v10, /device:TPU:0, one launch (start us, length us, event | category | flops | bytes accessed | tf_op | source)
XLA Modules:
  0.0 233.3 jit_solution(14315583476270631201)
XLA Ops:
  6.5 1.6 collective-permute-start.2
  8.1 2.7 %collective-permute-start.1 = (f32[64,512]{1,0:T(8,128)}, f32[64,512]{1,0:T(8,128)S(1)}, u32[]{:S(2)}, u32[]{:S(2)}) collective-permute-start(f32[64,512]{1,0:T(8,128)} %bitcast.14), channel_id=1, source_target_pairs={{4,0},{5,1},{6,2},{7,3},{0,4},{1,5},{2,6},{3,7},{12,8},{13,9},{14,... | collective-permute-start | bytes 393224 | tf_op jit(solution)/shard_map/ppermute | solution.py:269
  10.8 1.4 collective-permute-start
  12.3 4.6 %slice.9 = f32[8,256,512]{2,1,0:T(8,128)} slice(f32[12,256,512]{2,1,0:T(8,128)} %bitcast.11), slice={[0:8], [0:256], [0:512]} | slice | bytes 8388608 | tf_op jit(solution)/shard_map/slice | solution.py:270
  17.9 4.8 %all-to-all-start = ((f32[8,256,512]{2,1,0:T(8,128)}), f32[8,256,512]{2,1,0:T(8,128)}, u32[]{:S(2)}, u32[]{:S(2)}) async-start(f32[8,256,512]{2,1,0:T(8,128)} %slice.9), calls=%async_computation | async-start | bytes 8388608 | tf_op jit(solution)/shard_map/all_to_all | solution.py:254
  22.8 3.1 %slice.8 = f32[4,256,512]{2,1,0:T(8,128)} slice(f32[12,256,512]{2,1,0:T(8,128)} %bitcast.12), slice={[8:12], [0:256], [0:512]} | slice | bytes 4194304 | tf_op jit(solution)/shard_map/slice | solution.py:274
  25.9 45.2 %all-to-all-done = f32[8,256,512]{2,1,0:T(8,128)} async-done(((f32[8,256,512]{2,1,0:T(8,128)}), f32[8,256,512]{2,1,0:T(8,128)}, u32[]{:S(2)}, u32[]{:S(2)}) %all-to-all-start) | async-done | bytes 4194336 | tf_op jit(solution)/shard_map/all_to_all | solution.py:254
  71.1 4.4 %all-to-all-start.1 = ((f32[4,256,512]{2,1,0:T(8,128)}), f32[4,256,512]{2,1,0:T(8,128)}, u32[]{:S(2)}, u32[]{:S(2)}) async-start(f32[4,256,512]{2,1,0:T(8,128)} %slice.8), calls=%async_computation.1 | async-start | bytes 4194304 | tf_op jit(solution)/shard_map/all_to_all | solution.py:254
  75.5 4.4 %transform.8 = f32[256,512]{1,0:T(8,128)} custom-call(f32[4,2,256,512]{3,2,1,0:T(8,128)} %bitcast.3.part, f32[16,4,64,512]{3,2,1,0:T(8,128)} %bitcast.20), custom_call_target="tpu_custom_call" | custom-call | flops 5000000000 | tf_op jit(solution)/shard_map/transform/pallas_call | solution.py:126
  79.9 3.9 %collective-permute-start.3 = (f32[256,512]{1,0:T(8,128)}, f32[256,512]{1,0:T(8,128)S(1)}, u32[]{:S(2)}, u32[]{:S(2)}) collective-permute-start(f32[256,512]{1,0:T(8,128)} %transform.8), channel_id=1, source_target_pairs={{1,0},{0,1},{3,2},{2,3},{5,4},{4,5},{7,6},{6,7},{9,8},{8,9},{11,10... | collective-permute-start | bytes 1572872 | tf_op jit(solution)/shard_map/ppermute | solution.py:260
  83.9 4.4 %transform.9 = f32[256,512]{1,0:T(8,128)} custom-call(f32[4,2,256,512]{3,2,1,0:T(8,128)} %bitcast.3.part, f32[16,4,64,512]{3,2,1,0:T(8,128)} %bitcast.21), custom_call_target="tpu_custom_call" | custom-call | flops 5000000000 | tf_op jit(solution)/shard_map/transform/pallas_call | solution.py:126
  88.3 4.5 %transform.7 = f32[256,512]{1,0:T(8,128)} custom-call(f32[4,2,256,512]{3,2,1,0:T(8,128)} %bitcast.3.part, f32[16,4,64,512]{3,2,1,0:T(8,128)} %bitcast.22), custom_call_target="tpu_custom_call" | custom-call | flops 5000000000 | tf_op jit(solution)/shard_map/transform/pallas_call | solution.py:126
  92.9 4.4 %transform.6 = f32[256,512]{1,0:T(8,128)} custom-call(f32[4,2,256,512]{3,2,1,0:T(8,128)} %bitcast.3.part, f32[16,4,64,512]{3,2,1,0:T(8,128)} %bitcast.23), custom_call_target="tpu_custom_call" | custom-call | flops 5000000000 | tf_op jit(solution)/shard_map/transform/pallas_call | solution.py:126
  97.3 1.1 add.13.refs_0_
  98.4 1.7 collective-permute-start.6
  100.1 1.6 collective-permute-start.5
  101.7 4.5 %transform.11 = f32[256,512]{1,0:T(8,128)} custom-call(f32[4,1,256,512]{3,2,1,0:T(8,128)} %bitcast.9.part, f32[16,4,64,512]{3,2,1,0:T(8,128)} %bitcast.24), custom_call_target="tpu_custom_call" | custom-call | flops 5000000000 | tf_op jit(solution)/shard_map/transform/pallas_call | solution.py:126
  106.2 3.6 %collective-permute-start.11 = (f32[256,512]{1,0:T(8,128)}, f32[256,512]{1,0:T(8,128)}, u32[]{:S(2)}, u32[]{:S(2)}) collective-permute-start(f32[256,512]{1,0:T(8,128)} %transform.11), channel_id=1, source_target_pairs={{1,0},{0,1},{3,2},{2,3},{5,4},{4,5},{7,6},{6,7},{9,8},{8,9},{11,10... | collective-permute-start | bytes 1572872 | tf_op jit(solution)/shard_map/ppermute | solution.py:260
  111.3 2.5 %collective-permute-done.5.refs_4_ = f32[256,512]{1,0:T(8,128)S(1)} collective-permute-done((f32[256,512]{1,0:T(8,128)S(1)}, f32[256,512]{1,0:T(8,128)S(1)}, u32[]{:S(2)}, u32[]{:S(2)}) %collective-permute-start.5) | collective-permute-done | bytes 524320 | tf_op jit(solution)/shard_map/ppermute | solution.py:65
  114.4 2.7 %collective-permute-start.9 = (f32[256,512]{1,0:T(8,128)S(1)}, f32[256,512]{1,0:T(8,128)}, u32[]{:S(2)}, u32[]{:S(2)}) collective-permute-start(f32[256,512]{1,0:T(8,128)S(1)} %add.14.refs_1_), channel_id=1, source_target_pairs={{32,0},{40,8},{48,16},{56,24},{64,32},{72,40},{80,48},{88,56},{96,... | collective-permute-start | bytes 1572872 | tf_op jit(solution)/shard_map/ppermute | solution.py:65
  117.2 1.7 collective-permute-start.15
  118.8 4.4 %transform.10 = f32[256,512]{1,0:T(8,128)} custom-call(f32[4,1,256,512]{3,2,1,0:T(8,128)} %bitcast.9.part, f32[16,4,64,512]{3,2,1,0:T(8,128)} %bitcast.25), custom_call_target="tpu_custom_call" | custom-call | flops 5000000000 | tf_op jit(solution)/shard_map/transform/pallas_call | solution.py:126
  123.3 1.3 add.15.refs_0_
  124.6 3.6 %collective-permute-done.10.refs_7_ = f32[256,512]{1,0:T(8,128)S(1)} collective-permute-done((f32[256,512]{1,0:T(8,128)S(1)}, f32[256,512]{1,0:T(8,128)S(1)}, u32[]{:S(2)}, u32[]{:S(2)}) %collective-permute-start.10) | collective-permute-done | bytes 524320 | tf_op jit(solution)/shard_map/ppermute | solution.py:65
  128.9 1.5 collective-permute-start.14
  130.4 1.7 collective-permute-start.13
  132.1 2.4 %collective-permute-done.15.refs_8_ = f32[256,512]{1,0:T(8,128)S(1)} collective-permute-done((f32[256,512]{1,0:T(8,128)S(1)}, f32[256,512]{1,0:T(8,128)S(1)}, u32[]{:S(2)}, u32[]{:S(2)}) %collective-permute-start.15) | collective-permute-done | bytes 524320 | tf_op jit(solution)/shard_map/ppermute | solution.py:65
  135.3 5.4 %gram.4.refs_4_ = f32[8,5,32,256]{3,2,1,0:T(8,128)} custom-call(f32[256,512]{1,0:T(8,128)} %copy-done.1, f32[256,512]{1,0:T(8,128)} %copy-done.2, f32[256,512]{1,0:T(8,128)} %copy-done.7, f32[256,512]{1,0:T(8,128)} %collective-permute-done.8.refs_3_, f32[256,512]{1,0:T(8,128)} %copy-done.6, f32[256,512]{1,0:T(8,128)} %collective-permute-done.9.refs_5_, ...), custom_call_target="tpu_custom_call" | custom-call | tf_op jit(solution)/shard_map/gram/pallas_call | solution.py:178
  140.7 3.0 %collective-permute-done.14.refs_3_ = f32[256,512]{1,0:T(8,128)S(1)} collective-permute-done((f32[256,512]{1,0:T(8,128)S(1)}, f32[256,512]{1,0:T(8,128)S(1)}, u32[]{:S(2)}, u32[]{:S(2)}) %collective-permute-start.14) | collective-permute-done | bytes 524320 | tf_op jit(solution)/shard_map/ppermute | solution.py:65
  144.7 4.3 %gram.5 = f32[8,5,32,256]{3,2,1,0:T(8,128)} custom-call(f32[256,512]{1,0:T(8,128)} %copy-done.4, f32[256,512]{1,0:T(8,128)} %copy-done.12, f32[256,512]{1,0:T(8,128)} %collective-permute-done.13.refs_2_, f32[256,512]{1,0:T(8,128)} %copy-done.11, f32[8,5,32,256]{3,2,1,0:T(8,128)} %gram.4.refs_4_), custom_call_target="tpu_custom_call" | custom-call | tf_op jit(solution)/shard_map/gram/pallas_call | solution.py:178
  149.0 7.7 %all-to-all-start.2 = ((f32[8,5,32,256]{3,2,1,0:T(8,128)}), f32[8,5,32,256]{3,2,1,0:T(8,128)S(1)}, u32[]{:S(2)}, u32[]{:S(2)}) async-start(f32[8,5,32,256]{3,2,1,0:T(8,128)} %gram.5), calls=%async_computation.2 | async-start | bytes 2621440 | tf_op jit(solution)/shard_map/all_to_all | solution.py:263
  157.5 5.3 %gram.6.refs_5_ = f32[8,4,32,256]{3,2,1,0:T(8,128)} custom-call(f32[256,512]{1,0:T(8,128)} %copy-done.1, f32[256,512]{1,0:T(8,128)} %copy-done.2, f32[256,512]{1,0:T(8,128)} %copy-done.7, f32[256,512]{1,0:T(8,128)} %collective-permute-done.8.refs_3_, f32[256,512]{1,0:T(8,128)} %copy-done.6, f32[256,512]{1,0:T(8,128)} %collective-permute-done.9.refs_5_, ...), custom_call_target="tpu_custom_call" | custom-call | tf_op jit(solution)/shard_map/gram/pallas_call | solution.py:178
  162.8 6.6 %collective-permute-done.16.refs_4_ = f32[256,512]{1,0:T(8,128)S(1)} collective-permute-done((f32[256,512]{1,0:T(8,128)}, f32[256,512]{1,0:T(8,128)S(1)}, u32[]{:S(2)}, u32[]{:S(2)}) %collective-permute-start.16) | collective-permute-done | bytes 524320 | tf_op jit(solution)/shard_map/ppermute | solution.py:65
  170.2 4.0 %gram.7 = f32[8,4,32,256]{3,2,1,0:T(8,128)} custom-call(f32[256,512]{1,0:T(8,128)} %copy-done.4, f32[256,512]{1,0:T(8,128)} %copy-done.12, f32[256,512]{1,0:T(8,128)} %collective-permute-done.13.refs_2_, f32[256,512]{1,0:T(8,128)} %copy-done.11, f32[256,512]{1,0:T(8,128)} %copy-done.24, f32[8,4,32,256]{3,2,1,0:T(8,128)} %gram.6.refs_5_), custom_call_target="tpu_custom_call" | custom-call | flops 20000000000 | tf_op jit(solution)/shard_map/gram/pallas_call | solution.py:178
  174.2 4.3 %all-to-all-done.2.moved_ref = f32[8,5,32,256]{3,2,1,0:T(8,128)S(1)} async-done(((f32[8,5,32,256]{3,2,1,0:T(8,128)}), f32[8,5,32,256]{3,2,1,0:T(8,128)S(1)}, u32[]{:S(2)}, u32[]{:S(2)}) %all-to-all-start.2) | async-done | bytes 1310752 | tf_op jit(solution)/shard_map/all_to_all | solution.py:263
  178.5 4.1 %all-to-all-start.3 = ((f32[8,4,32,256]{3,2,1,0:T(8,128)}), f32[8,4,32,256]{3,2,1,0:T(8,128)S(1)}, u32[]{:S(2)}, u32[]{:S(2)}) async-start(f32[8,4,32,256]{3,2,1,0:T(8,128)} %gram.7), calls=%async_computation.3 | async-start | bytes 2097152 | tf_op jit(solution)/shard_map/all_to_all | solution.py:263
  182.5 2.1 sum.2
  185.7 2.1 collective-permute-start.20
  187.8 2.0 collective-permute-done.20.refs_1_
  190.6 7.5 %all-to-all-done.3.moved_ref = f32[8,4,32,256]{3,2,1,0:T(8,128)S(1)} async-done(((f32[8,4,32,256]{3,2,1,0:T(8,128)}), f32[8,4,32,256]{3,2,1,0:T(8,128)S(1)}, u32[]{:S(2)}, u32[]{:S(2)}) %all-to-all-start.3) | async-done | bytes 1048608 | tf_op jit(solution)/shard_map/all_to_all | solution.py:263
  199.2 2.0 sum.3
  201.1 7.3 %collective-permute-done.24.refs_2_ = f32[4,32,256]{2,1,0:T(8,128)S(1)} collective-permute-done((f32[4,32,256]{2,1,0:T(8,128)}, f32[4,32,256]{2,1,0:T(8,128)S(1)}, u32[]{:S(2)}, u32[]{:S(2)}) %collective-permute-start.24) | collective-permute-done | bytes 131104 | tf_op jit(solution)/shard_map/ppermute | solution.py:70
  209.1 1.8 turn.1
  210.9 4.2 %all-to-all-start.4 = ((f32[8,32,256]{2,1,0:T(8,128)}), f32[8,32,256]{2,1,0:T(8,128)S(1)}, u32[]{:S(2)}, u32[]{:S(2)}) async-start(f32[8,32,256]{2,1,0:T(8,128)} %turn.1), calls=%async_computation.4 | async-start | bytes 524288 | tf_op jit(solution)/shard_map/all_to_all | solution.py:263
  215.2 3.2 %collective-permute-start.23 = (f32[1,32,256]{2,1,0:T(8,128)}, f32[1,32,256]{2,1,0:T(8,128)S(1)}, u32[]{:S(2)}, u32[]{:S(2)}) collective-permute-start(f32[1,32,256]{2,1,0:T(8,128)} %get-tuple-element.86), channel_id=1, source_target_pairs={{0,96},{8,104},{16,112},{24,120},{32,0},{40,8},{48,16},{56,24},{64... | collective-permute-start | bytes 98312 | tf_op jit(solution)/shard_map/ppermute | solution.py:70
  218.4 1.2 dynamic-slice_bitcast_fusion.table_ref
  220.5 3.0 %all-to-all-done.4.refs_7_ = f32[8,32,256]{2,1,0:T(8,128)S(1)} async-done(((f32[8,32,256]{2,1,0:T(8,128)}), f32[8,32,256]{2,1,0:T(8,128)S(1)}, u32[]{:S(2)}, u32[]{:S(2)}) %all-to-all-start.4) | async-done | bytes 262176 | tf_op jit(solution)/shard_map/all_to_all | solution.py:263
  224.2 2.2 assemble.1
  (86 shorter events, 12.7 us)
Async XLA Ops:
  6.5 69.0 %all-gather.3.cloned.1.call-start = ((), (), s32[]{:S(2)}) async-start(), calls=%async_computation.5 | async-start | bytes 8912896 | tf_op jit(solution)/shard_map/all_gather | solution.py:273
  6.5 10.3 %collective-permute-start.2 = (f32[64,512]{1,0:T(8,128)}, f32[64,512]{1,0:T(8,128)S(1)}, u32[]{:S(2)}, u32[]{:S(2)}) collective-permute-start(f32[64,512]{1,0:T(8,128)} %bitcast.13), channel_id=1, source_target_pairs={{6,0},{7,1},{0,2},{1,3},{2,4},{3,5},{4,6},{5,7},{14,8},{15,9},{8,1... | collective-permute-start | bytes 393224 | tf_op jit(solution)/shard_map/ppermute | solution.py:269
  8.1 9.0 %collective-permute-start.1 = (f32[64,512]{1,0:T(8,128)}, f32[64,512]{1,0:T(8,128)S(1)}, u32[]{:S(2)}, u32[]{:S(2)}) collective-permute-start(f32[64,512]{1,0:T(8,128)} %bitcast.14), channel_id=1, source_target_pairs={{4,0},{5,1},{6,2},{7,3},{0,4},{1,5},{2,6},{3,7},{12,8},{13,9},{14,... | collective-permute-start | bytes 393224 | tf_op jit(solution)/shard_map/ppermute | solution.py:269
  10.8 6.2 %collective-permute-start = (f32[64,512]{1,0:T(8,128)}, f32[64,512]{1,0:T(8,128)S(1)}, u32[]{:S(2)}, u32[]{:S(2)}) collective-permute-start(f32[64,512]{1,0:T(8,128)} %bitcast.15), channel_id=1, source_target_pairs={{2,0},{3,1},{4,2},{5,3},{6,4},{7,5},{0,6},{1,7},{10,8},{11,9},{12,... | collective-permute-start | bytes 393224 | tf_op jit(solution)/shard_map/ppermute | solution.py:269
  12.3 4.8 %copy-start.17 = (f32[512,64]{0,1:T(8,128)S(1)}, f32[512,64]{0,1:T(8,128)}, u32[]{:S(2)}) copy-start(f32[512,64]{0,1:T(8,128)} %param.4) | copy-start | bytes 393220
  17.9 53.1 %all-to-all-start = ((f32[8,256,512]{2,1,0:T(8,128)}), f32[8,256,512]{2,1,0:T(8,128)}, u32[]{:S(2)}, u32[]{:S(2)}) async-start(f32[8,256,512]{2,1,0:T(8,128)} %slice.9), calls=%async_computation | async-start | bytes 8388608 | tf_op jit(solution)/shard_map/all_to_all | solution.py:254
  71.1 30.6 %all-to-all-start.1 = ((f32[4,256,512]{2,1,0:T(8,128)}), f32[4,256,512]{2,1,0:T(8,128)}, u32[]{:S(2)}, u32[]{:S(2)}) async-start(f32[4,256,512]{2,1,0:T(8,128)} %slice.8), calls=%async_computation.1 | async-start | bytes 4194304 | tf_op jit(solution)/shard_map/all_to_all | solution.py:254
  79.9 17.3 %collective-permute-start.3 = (f32[256,512]{1,0:T(8,128)}, f32[256,512]{1,0:T(8,128)S(1)}, u32[]{:S(2)}, u32[]{:S(2)}) collective-permute-start(f32[256,512]{1,0:T(8,128)} %transform.8), channel_id=1, source_target_pairs={{1,0},{0,1},{3,2},{2,3},{5,4},{4,5},{7,6},{6,7},{9,8},{8,9},{11,10... | collective-permute-start | bytes 1572872 | tf_op jit(solution)/shard_map/ppermute | solution.py:260
  88.3 4.5 %copy-start.23 = (f32[256,512]{1,0:T(8,128)S(1)}, f32[256,512]{1,0:T(8,128)}, u32[]{:S(2)}) copy-start(f32[256,512]{1,0:T(8,128)} %transform.9) | copy-start | bytes 1572868
  92.8 17.0 %collective-permute-start.7 = (f32[256,512]{1,0:T(8,128)S(1)}, f32[256,512]{1,0:T(8,128)}, u32[]{:S(2)}, u32[]{:S(2)}) collective-permute-start(f32[256,512]{1,0:T(8,128)S(1)} %copy-done.23), channel_id=1, source_target_pairs={{1,0},{0,1},{3,2},{2,3},{5,4},{4,5},{7,6},{6,7},{9,8},{8,9},{11,10... | collective-permute-start | bytes 1572872 | tf_op jit(solution)/shard_map/ppermute | solution.py:260
  98.4 7.8 %copy-start.1 = (f32[256,512]{1,0:T(8,128)}, f32[256,512]{1,0:T(8,128)S(1)}, u32[]{:S(2)}) copy-start(f32[256,512]{1,0:T(8,128)S(1)} %add.13.refs_0_) | copy-start | bytes 1572868
  98.4 13.0 %collective-permute-start.6 = (f32[256,512]{1,0:T(8,128)S(1)}, f32[256,512]{1,0:T(8,128)S(1)}, u32[]{:S(2)}, u32[]{:S(2)}) collective-permute-start(f32[256,512]{1,0:T(8,128)S(1)} %add.13.refs_0_), channel_id=1, source_target_pairs={{96,0},{104,8},{112,16},{120,24},{0,32},{8,40},{16,48},{24,56},{40... | collective-permute-start | bytes 1572872 | tf_op jit(solution)/shard_map/ppermute | solution.py:65
  100.1 13.8 %collective-permute-start.5 = (f32[256,512]{1,0:T(8,128)S(1)}, f32[256,512]{1,0:T(8,128)S(1)}, u32[]{:S(2)}, u32[]{:S(2)}) collective-permute-start(f32[256,512]{1,0:T(8,128)S(1)} %add.13.refs_0_), channel_id=1, source_target_pairs={{32,0},{40,8},{48,16},{56,24},{64,32},{72,40},{80,48},{88,56},{96,... | collective-permute-start | bytes 1572872 | tf_op jit(solution)/shard_map/ppermute | solution.py:65
  101.7 12.1 %collective-permute-start.4 = (f32[256,512]{1,0:T(8,128)S(1)}, f32[256,512]{1,0:T(8,128)S(1)}, u32[]{:S(2)}, u32[]{:S(2)}) collective-permute-start(f32[256,512]{1,0:T(8,128)S(1)} %add.13.refs_0_), channel_id=1, source_target_pairs={{8,0},{0,8},{24,16},{16,24},{40,32},{32,40},{56,48},{48,56},{72,64... | collective-permute-start | bytes 1572872 | tf_op jit(solution)/shard_map/ppermute | solution.py:65
  101.7 8.1 %copy-start.13 = (f32[256,512]{1,0:T(8,128)S(1)}, f32[256,512]{1,0:T(8,128)}, u32[]{:S(2)}) copy-start(f32[256,512]{1,0:T(8,128)} %transform.7) | copy-start | bytes 1572868
  106.2 17.1 %collective-permute-start.11 = (f32[256,512]{1,0:T(8,128)}, f32[256,512]{1,0:T(8,128)}, u32[]{:S(2)}, u32[]{:S(2)}) collective-permute-start(f32[256,512]{1,0:T(8,128)} %transform.11), channel_id=1, source_target_pairs={{1,0},{0,1},{3,2},{2,3},{5,4},{4,5},{7,6},{6,7},{9,8},{8,9},{11,10... | collective-permute-start | bytes 1572872 | tf_op jit(solution)/shard_map/ppermute | solution.py:260
  110.9 12.3 %copy-start.2 = (f32[256,512]{1,0:T(8,128)}, f32[256,512]{1,0:T(8,128)S(1)}, u32[]{:S(2)}) copy-start(f32[256,512]{1,0:T(8,128)S(1)} %add.14.refs_1_) | copy-start | bytes 1572868
  111.3 11.9 %copy-start.5 = (f32[256,512]{1,0:T(8,128)}, f32[256,512]{1,0:T(8,128)S(1)}, u32[]{:S(2)}) copy-start(f32[256,512]{1,0:T(8,128)S(1)} %collective-permute-done.6.refs_6_) | copy-start | bytes 1572868
  113.8 9.4 %copy-start.6 = (f32[256,512]{1,0:T(8,128)}, f32[256,512]{1,0:T(8,128)S(1)}, u32[]{:S(2)}) copy-start(f32[256,512]{1,0:T(8,128)S(1)} %collective-permute-done.5.refs_4_) | copy-start | bytes 1572868
  113.9 9.4 %copy-start.7 = (f32[256,512]{1,0:T(8,128)}, f32[256,512]{1,0:T(8,128)S(1)}, u32[]{:S(2)}) copy-start(f32[256,512]{1,0:T(8,128)S(1)} %collective-permute-done.4.refs_2_) | copy-start | bytes 1572868
  113.9 14.3 %collective-permute-start.10 = (f32[256,512]{1,0:T(8,128)S(1)}, f32[256,512]{1,0:T(8,128)S(1)}, u32[]{:S(2)}, u32[]{:S(2)}) collective-permute-start(f32[256,512]{1,0:T(8,128)S(1)} %add.14.refs_1_), channel_id=1, source_target_pairs={{96,0},{104,8},{112,16},{120,24},{0,32},{8,40},{16,48},{24,56},{40... | collective-permute-start | bytes 1572872 | tf_op jit(solution)/shard_map/ppermute | solution.py:65
  114.4 14.5 %collective-permute-start.9 = (f32[256,512]{1,0:T(8,128)S(1)}, f32[256,512]{1,0:T(8,128)}, u32[]{:S(2)}, u32[]{:S(2)}) collective-permute-start(f32[256,512]{1,0:T(8,128)S(1)} %add.14.refs_1_), channel_id=1, source_target_pairs={{32,0},{40,8},{48,16},{56,24},{64,32},{72,40},{80,48},{88,56},{96,... | collective-permute-start | bytes 1572872 | tf_op jit(solution)/shard_map/ppermute | solution.py:65
  117.2 11.7 %collective-permute-start.8 = (f32[256,512]{1,0:T(8,128)S(1)}, f32[256,512]{1,0:T(8,128)}, u32[]{:S(2)}, u32[]{:S(2)}) collective-permute-start(f32[256,512]{1,0:T(8,128)S(1)} %add.14.refs_1_), channel_id=1, source_target_pairs={{8,0},{0,8},{24,16},{16,24},{40,32},{32,40},{56,48},{48,56},{72,64... | collective-permute-start | bytes 1572872 | tf_op jit(solution)/shard_map/ppermute | solution.py:65
  117.2 17.4 %collective-permute-start.15 = (f32[256,512]{1,0:T(8,128)S(1)}, f32[256,512]{1,0:T(8,128)S(1)}, u32[]{:S(2)}, u32[]{:S(2)}) collective-permute-start(f32[256,512]{1,0:T(8,128)S(1)} %collective-permute-done.5.refs_4_), channel_id=1, source_target_pairs={{16,0},{24,8},{8,16},{0,24},{48,32},{56,40},{40,48},{32,56},{88,64... | collective-permute-start | bytes 1572872 | tf_op jit(solution)/shard_map/ppermute | solution.py:65
  124.6 16.2 %copy-start.4 = (f32[256,512]{1,0:T(8,128)}, f32[256,512]{1,0:T(8,128)S(1)}, u32[]{:S(2)}) copy-start(f32[256,512]{1,0:T(8,128)S(1)} %add.15.refs_0_) | copy-start | bytes 1572868
  128.2 7.1 %copy-start.8 = (f32[256,512]{1,0:T(8,128)}, f32[256,512]{1,0:T(8,128)S(1)}, u32[]{:S(2)}) copy-start(f32[256,512]{1,0:T(8,128)S(1)} %collective-permute-done.10.refs_7_) | copy-start | bytes 1572868
  128.9 14.8 %collective-permute-start.14 = (f32[256,512]{1,0:T(8,128)S(1)}, f32[256,512]{1,0:T(8,128)S(1)}, u32[]{:S(2)}, u32[]{:S(2)}) collective-permute-start(f32[256,512]{1,0:T(8,128)S(1)} %add.15.refs_0_), channel_id=1, source_target_pairs={{96,0},{104,8},{112,16},{120,24},{0,32},{8,40},{16,48},{24,56},{40... | collective-permute-start | bytes 1572872 | tf_op jit(solution)/shard_map/ppermute | solution.py:65
  130.4 13.3 %collective-permute-start.13 = (f32[256,512]{1,0:T(8,128)S(1)}, f32[256,512]{1,0:T(8,128)}, u32[]{:S(2)}, u32[]{:S(2)}) collective-permute-start(f32[256,512]{1,0:T(8,128)S(1)} %add.15.refs_0_), channel_id=1, source_target_pairs={{32,0},{40,8},{48,16},{56,24},{64,32},{72,40},{80,48},{88,56},{96,... | collective-permute-start | bytes 1572872 | tf_op jit(solution)/shard_map/ppermute | solution.py:65
  132.1 11.6 %collective-permute-start.12 = (f32[256,512]{1,0:T(8,128)S(1)}, f32[256,512]{1,0:T(8,128)S(1)}, u32[]{:S(2)}, u32[]{:S(2)}) collective-permute-start(f32[256,512]{1,0:T(8,128)S(1)} %add.15.refs_0_), channel_id=1, source_target_pairs={{8,0},{0,8},{24,16},{16,24},{40,32},{32,40},{56,48},{48,56},{72,64... | collective-permute-start | bytes 1572872 | tf_op jit(solution)/shard_map/ppermute | solution.py:65
  134.6 6.2 %copy-start.10 = (f32[256,512]{1,0:T(8,128)}, f32[256,512]{1,0:T(8,128)S(1)}, u32[]{:S(2)}) copy-start(f32[256,512]{1,0:T(8,128)S(1)} %collective-permute-done.15.refs_8_) | copy-start | bytes 1572868
  134.6 22.1 %collective-permute-start.17 = (f32[256,512]{1,0:T(8,128)}, f32[256,512]{1,0:T(8,128)S(1)}, u32[]{:S(2)}, u32[]{:S(2)}) collective-permute-start(f32[256,512]{1,0:T(8,128)} %collective-permute-done.9.refs_5_), channel_id=1, source_target_pairs={{16,0},{24,8},{8,16},{0,24},{48,32},{56,40},{40,48},{32,56},{88,64... | collective-permute-start | bytes 1572872 | tf_op jit(solution)/shard_map/ppermute | solution.py:65
  143.7 25.6 %collective-permute-start.16 = (f32[256,512]{1,0:T(8,128)}, f32[256,512]{1,0:T(8,128)S(1)}, u32[]{:S(2)}, u32[]{:S(2)}) collective-permute-start(f32[256,512]{1,0:T(8,128)} %collective-permute-done.13.refs_2_), channel_id=1, source_target_pairs={{16,0},{24,8},{8,16},{0,24},{48,32},{56,40},{40,48},{32,56},{88,64... | collective-permute-start | bytes 1572872 | tf_op jit(solution)/shard_map/ppermute | solution.py:65
  149.0 29.5 %all-to-all-start.2 = ((f32[8,5,32,256]{3,2,1,0:T(8,128)}), f32[8,5,32,256]{3,2,1,0:T(8,128)S(1)}, u32[]{:S(2)}, u32[]{:S(2)}) async-start(f32[8,5,32,256]{3,2,1,0:T(8,128)} %gram.5), calls=%async_computation.2 | async-start | bytes 2621440 | tf_op jit(solution)/shard_map/all_to_all | solution.py:263
  178.5 4.1 %copy-start = (f32[8,5,32,256]{3,2,1,0:T(8,128)}, f32[8,5,32,256]{3,2,1,0:T(8,128)S(1)}, u32[]{:S(2)}) copy-start(f32[8,5,32,256]{3,2,1,0:T(8,128)S(1)} %all-to-all-done.2.moved_ref) | copy-start | bytes 3932164
  178.5 19.7 %all-to-all-start.3 = ((f32[8,4,32,256]{3,2,1,0:T(8,128)}), f32[8,4,32,256]{3,2,1,0:T(8,128)S(1)}, u32[]{:S(2)}, u32[]{:S(2)}) async-start(f32[8,4,32,256]{3,2,1,0:T(8,128)} %gram.7), calls=%async_computation.3 | async-start | bytes 2097152 | tf_op jit(solution)/shard_map/all_to_all | solution.py:263
  184.6 6.0 %collective-permute-start.19 = (f32[3,32,256]{2,1,0:T(8,128)}, f32[3,32,256]{2,1,0:T(8,128)S(1)}, u32[]{:S(2)}, u32[]{:S(2)}) collective-permute-start(f32[3,32,256]{2,1,0:T(8,128)} %get-tuple-element.77), channel_id=1, source_target_pairs={{0,32},{8,40},{16,48},{24,56},{32,64},{40,72},{48,80},{56,88},{64,... | collective-permute-start | bytes 294920 | tf_op jit(solution)/shard_map/ppermute | solution.py:70
  185.7 2.1 collective-permute-start.18
  185.7 4.1 %collective-permute-start.20 = (f32[1,32,256]{2,1,0:T(8,128)}, f32[1,32,256]{2,1,0:T(8,128)S(1)}, u32[]{:S(2)}, u32[]{:S(2)}) collective-permute-start(f32[1,32,256]{2,1,0:T(8,128)} %get-tuple-element.78), channel_id=1, source_target_pairs={{0,96},{8,104},{16,112},{24,120},{32,0},{40,8},{48,16},{56,24},{64... | collective-permute-start | bytes 98312 | tf_op jit(solution)/shard_map/ppermute | solution.py:70
  187.8 35.7 %copy-start.18 = (f32[1,32,256]{2,1,0:T(8,128)}, f32[1,32,256]{2,1,0:T(8,128)S(1)}, u32[]{:S(2)}) copy-start(f32[1,32,256]{2,1,0:T(8,128)S(1)} %collective-permute-done.18.refs_1_) | copy-start | bytes 98308
  189.8 18.6 %copy-start.20 = (f32[1,32,256]{2,1,0:T(8,128)}, f32[1,32,256]{2,1,0:T(8,128)S(1)}, u32[]{:S(2)}) copy-start(f32[1,32,256]{2,1,0:T(8,128)S(1)} %collective-permute-done.20.refs_1_) | copy-start | bytes 98308
  190.6 17.8 %copy-start.15 = (f32[3,32,256]{2,1,0:T(8,128)}, f32[3,32,256]{2,1,0:T(8,128)S(1)}, u32[]{:S(2)}) copy-start(f32[3,32,256]{2,1,0:T(8,128)S(1)} %collective-permute-done.19.refs_0_.refs_2_) | copy-start | bytes 294916
  201.1 7.3 %collective-permute-start.24 = (f32[4,32,256]{2,1,0:T(8,128)}, f32[4,32,256]{2,1,0:T(8,128)S(1)}, u32[]{:S(2)}, u32[]{:S(2)}) collective-permute-start(f32[4,32,256]{2,1,0:T(8,128)} %get-tuple-element.88), channel_id=1, source_target_pairs={{0,48},{8,56},{16,40},{24,32},{32,80},{40,88},{48,72},{56,64},{64,... | collective-permute-start | bytes 393224 | tf_op jit(solution)/shard_map/ppermute | solution.py:70
  210.9 12.7 %all-to-all-start.4 = ((f32[8,32,256]{2,1,0:T(8,128)}), f32[8,32,256]{2,1,0:T(8,128)S(1)}, u32[]{:S(2)}, u32[]{:S(2)}) async-start(f32[8,32,256]{2,1,0:T(8,128)} %turn.1), calls=%async_computation.4 | async-start | bytes 524288 | tf_op jit(solution)/shard_map/all_to_all | solution.py:263
  215.1 4.5 %collective-permute-start.21 = (f32[1,32,256]{2,1,0:T(8,128)}, f32[1,32,256]{2,1,0:T(8,128)S(1)}, u32[]{:S(2)}, u32[]{:S(2)}) collective-permute-start(f32[1,32,256]{2,1,0:T(8,128)} %get-tuple-element.84), channel_id=1, source_target_pairs={{0,8},{8,0},{16,24},{24,16},{32,40},{40,32},{48,56},{56,48},{64,72... | collective-permute-start | bytes 98312 | tf_op jit(solution)/shard_map/ppermute | solution.py:70
  215.1 5.4 %collective-permute-start.22 = (f32[1,32,256]{2,1,0:T(8,128)}, f32[1,32,256]{2,1,0:T(8,128)S(1)}, u32[]{:S(2)}, u32[]{:S(2)}) collective-permute-start(f32[1,32,256]{2,1,0:T(8,128)} %get-tuple-element.85), channel_id=1, source_target_pairs={{0,32},{8,40},{16,48},{24,56},{32,64},{40,72},{48,80},{56,88},{64,... | collective-permute-start | bytes 98312 | tf_op jit(solution)/shard_map/ppermute | solution.py:70
  215.2 5.3 %collective-permute-start.23 = (f32[1,32,256]{2,1,0:T(8,128)}, f32[1,32,256]{2,1,0:T(8,128)S(1)}, u32[]{:S(2)}, u32[]{:S(2)}) collective-permute-start(f32[1,32,256]{2,1,0:T(8,128)} %get-tuple-element.86), channel_id=1, source_target_pairs={{0,96},{8,104},{16,112},{24,120},{32,0},{40,8},{48,16},{56,24},{64... | collective-permute-start | bytes 98312 | tf_op jit(solution)/shard_map/ppermute | solution.py:70
  219.7 3.9 %copy-start.19 = (f32[1,32,256]{2,1,0:T(8,128)}, f32[1,32,256]{2,1,0:T(8,128)S(1)}, u32[]{:S(2)}) copy-start(f32[1,32,256]{2,1,0:T(8,128)S(1)} %collective-permute-done.21.refs_4_) | copy-start | bytes 98308
  220.5 3.0 %copy-start.22 = (f32[1,32,256]{2,1,0:T(8,128)}, f32[1,32,256]{2,1,0:T(8,128)S(1)}, u32[]{:S(2)}) copy-start(f32[1,32,256]{2,1,0:T(8,128)S(1)} %collective-permute-done.23.refs_6_) | copy-start | bytes 98308
  (8 other events, 8.9 us)
Sparse Core Ops, SparseCore 0:
  18.1 54.1 all-gather.2

commit v11 on v10

--- a/solution.py
+++ b/solution.py
@@ -203,9 +203,10 @@
 
 def summed(moved, routes):
     def kernel(moved_ref, *outs):
+        totals = [moved_ref[:, tile].sum(0) for tile in range(moved_ref.shape[1])]
         for out, (_, as_is, to_turn) in zip(outs, routes):
             for k, tile in enumerate(as_is + to_turn):
-                out[k] = moved_ref[:, tile].sum(0)
+                out[k] = totals[tile]
 
     shape = moved.shape[2:]
     outputs = [(len(as_is + to_turn),) + shape for _, as_is, to_turn in routes]
@@ -291,10 +292,10 @@
     arrived_2 = to_other_half(to_send(last_part, 0))
     own_1 = kept_1 + arrived_1
     own_2 = kept(last_part, 0) + arrived_2
-    other_0, below_0, above_0, own_1 = together(other_0, below_0, above_0, own_1)
+    other_0, above_0, own_1 = together(other_0, above_0, own_1)
     across_0 = fetched(below_0, over_to_across)
     other_1, below_1, above_1 = neighbours(own_1)
-    other_1, below_1, above_1, own_2 = together(other_1, below_1, above_1, own_2)
+    other_1, above_1, own_2 = together(other_1, above_1, own_2)
     across_0, below_1 = together(across_0, below_1)
     across_1 = fetched(below_1, over_to_across)
     other_2, below_2, above_2 = neighbours(own_2)

time: 234 us -> 234 us (level)
  waiting for transfers between devices: 90.4 us -> 84.6 us
  starting transfers between devices: 57.5 us -> 61.3 us
    all_to_all x3, waiting for transfers between devices: 14.8 us -> 10 us  [over_col(): return lax.all_to_all(tiles, 'col', split_axis=0, concat_axis=0, tiled=True)]
    ppermute x7, starting transfers between devices: 6.54 us -> 8.91 us  [delivered(): return lax.ppermute(value, 'blk', route)]
    ppermute x7, waiting for transfers between devices: 10.9 us -> 8.58 us  [delivered(): return lax.ppermute(value, 'blk', route)]
    unnamed x50 -> x48, local copies, waits for them, and re-layouts: 4.96 us -> 4.81 us
  transfers between devices with their start and end apart: 31 -> 31, of which waited for: 16 -> 14; matrix products, arithmetic and copies ran while one was open for 5% -> 5% of each run, Pallas kernels for 20% -> 21%
where the time goes in v11:
time: 234 us; the launch traced here: 231 us
  waiting for transfers between devices  84.6 us (36%)
  starting transfers between devices  61.3 us (26%)
  Pallas kernels  53.4 us (23%)
  local copies, waits for them, and re-layouts  13.7 us (6%)
  between operations  13.7 us (6%)
  other arithmetic  4.36 us (2%)
    all_to_all x2, waiting for transfers between devices, over_x(): lax.all_to_all(part, 'col', split_axis=0, concat_axis=0, tiled=True, axis...  45.2 us
    pallas_call x6, Pallas kernels, transformed(): pl.pallas_call(functools.partial(transform_kernel, index, keeps), in_spec...  26.4 us
    pallas_call x4, Pallas kernels, gram(): pl.pallas_call(functools.partial(gram_kernel, pairs, chunks, more), in_sp...  19 us
    ppermute x12, waiting for transfers between devices, fetched(): return lax.ppermute(value, 'blk', route)  18.7 us
    all_to_all x3, starting transfers between devices, over_col(): return lax.all_to_all(tiles, 'col', split_axis=0, concat_axis=0, tiled=True)  16.9 us
    ppermute x12, starting transfers between devices, fetched(): return lax.ppermute(value, 'blk', route)  12.9 us
    all_to_all x3, waiting for transfers between devices, over_col(): return lax.all_to_all(tiles, 'col', split_axis=0, concat_axis=0, tiled=True)  10 us
    all_to_all x2, starting transfers between devices, over_x(): lax.all_to_all(part, 'col', split_axis=0, concat_axis=0, tiled=True, axis...  9.29 us
  transfers between devices with their start and end apart: 31, of which 14 were waited for; matrix products, arithmetic and copies ran while one was open for 5% of the time, Pallas kernels for 21%

profile of v11, /device:TPU:0, one launch (start us, length us, event | category | flops | bytes accessed | tf_op | source)
XLA Modules:
  0.0 231.1 jit_solution(12809550121191601698)
XLA Ops:
  6.5 1.6 collective-permute-start.2
  8.1 2.7 %collective-permute-start.1 = (f32[64,512]{1,0:T(8,128)}, f32[64,512]{1,0:T(8,128)S(1)}, u32[]{:S(2)}, u32[]{:S(2)}) collective-permute-start(f32[64,512]{1,0:T(8,128)} %bitcast.14), channel_id=1, source_target_pairs={{4,0},{5,1},{6,2},{7,3},{0,4},{1,5},{2,6},{3,7},{12,8},{13,9},{14,... | collective-permute-start | bytes 393224 | tf_op jit(solution)/shard_map/ppermute | solution.py:270
  10.8 1.4 collective-permute-start
  12.3 4.6 %slice.9 = f32[8,256,512]{2,1,0:T(8,128)} slice(f32[12,256,512]{2,1,0:T(8,128)} %bitcast.11), slice={[0:8], [0:256], [0:512]} | slice | bytes 8388608 | tf_op jit(solution)/shard_map/slice | solution.py:271
  17.9 4.9 %all-to-all-start = ((f32[8,256,512]{2,1,0:T(8,128)}), f32[8,256,512]{2,1,0:T(8,128)}, u32[]{:S(2)}, u32[]{:S(2)}) async-start(f32[8,256,512]{2,1,0:T(8,128)} %slice.9), calls=%async_computation | async-start | bytes 8388608 | tf_op jit(solution)/shard_map/all_to_all | solution.py:255
  22.8 3.1 %slice.8 = f32[4,256,512]{2,1,0:T(8,128)} slice(f32[12,256,512]{2,1,0:T(8,128)} %bitcast.12), slice={[8:12], [0:256], [0:512]} | slice | bytes 4194304 | tf_op jit(solution)/shard_map/slice | solution.py:275
  25.9 45.2 %all-to-all-done = f32[8,256,512]{2,1,0:T(8,128)} async-done(((f32[8,256,512]{2,1,0:T(8,128)}), f32[8,256,512]{2,1,0:T(8,128)}, u32[]{:S(2)}, u32[]{:S(2)}) %all-to-all-start) | async-done | bytes 4194336 | tf_op jit(solution)/shard_map/all_to_all | solution.py:255
  71.1 4.4 %all-to-all-start.1 = ((f32[4,256,512]{2,1,0:T(8,128)}), f32[4,256,512]{2,1,0:T(8,128)}, u32[]{:S(2)}, u32[]{:S(2)}) async-start(f32[4,256,512]{2,1,0:T(8,128)} %slice.8), calls=%async_computation.1 | async-start | bytes 4194304 | tf_op jit(solution)/shard_map/all_to_all | solution.py:255
  75.5 4.4 %transform.8 = f32[256,512]{1,0:T(8,128)} custom-call(f32[4,2,256,512]{3,2,1,0:T(8,128)} %bitcast.3.part, f32[16,4,64,512]{3,2,1,0:T(8,128)} %bitcast.20), custom_call_target="tpu_custom_call" | custom-call | flops 5000000000 | tf_op jit(solution)/shard_map/transform/pallas_call | solution.py:126
  79.9 4.0 %collective-permute-start.3 = (f32[256,512]{1,0:T(8,128)}, f32[256,512]{1,0:T(8,128)S(1)}, u32[]{:S(2)}, u32[]{:S(2)}) collective-permute-start(f32[256,512]{1,0:T(8,128)} %transform.8), channel_id=1, source_target_pairs={{1,0},{0,1},{3,2},{2,3},{5,4},{4,5},{7,6},{6,7},{9,8},{8,9},{11,10... | collective-permute-start | bytes 1572872 | tf_op jit(solution)/shard_map/ppermute | solution.py:261
  83.9 4.4 %transform.9 = f32[256,512]{1,0:T(8,128)} custom-call(f32[4,2,256,512]{3,2,1,0:T(8,128)} %bitcast.3.part, f32[16,4,64,512]{3,2,1,0:T(8,128)} %bitcast.21), custom_call_target="tpu_custom_call" | custom-call | flops 5000000000 | tf_op jit(solution)/shard_map/transform/pallas_call | solution.py:126
  88.3 4.5 %transform.7 = f32[256,512]{1,0:T(8,128)} custom-call(f32[4,2,256,512]{3,2,1,0:T(8,128)} %bitcast.3.part, f32[16,4,64,512]{3,2,1,0:T(8,128)} %bitcast.22), custom_call_target="tpu_custom_call" | custom-call | flops 5000000000 | tf_op jit(solution)/shard_map/transform/pallas_call | solution.py:126
  92.9 4.4 %transform.6 = f32[256,512]{1,0:T(8,128)} custom-call(f32[4,2,256,512]{3,2,1,0:T(8,128)} %bitcast.3.part, f32[16,4,64,512]{3,2,1,0:T(8,128)} %bitcast.23), custom_call_target="tpu_custom_call" | custom-call | flops 5000000000 | tf_op jit(solution)/shard_map/transform/pallas_call | solution.py:126
  97.3 1.1 add.13.refs_0_
  98.4 1.6 collective-permute-start.5
  100.1 1.8 collective-permute-start.13
  101.9 4.5 %transform.11 = f32[256,512]{1,0:T(8,128)} custom-call(f32[4,1,256,512]{3,2,1,0:T(8,128)} %bitcast.9.part, f32[16,4,64,512]{3,2,1,0:T(8,128)} %bitcast.24), custom_call_target="tpu_custom_call" | custom-call | flops 5000000000 | tf_op jit(solution)/shard_map/transform/pallas_call | solution.py:126
  106.4 3.5 %collective-permute-start.9 = (f32[256,512]{1,0:T(8,128)}, f32[256,512]{1,0:T(8,128)}, u32[]{:S(2)}, u32[]{:S(2)}) collective-permute-start(f32[256,512]{1,0:T(8,128)} %transform.11), channel_id=1, source_target_pairs={{1,0},{0,1},{3,2},{2,3},{5,4},{4,5},{7,6},{6,7},{9,8},{8,9},{11,10... | collective-permute-start | bytes 1572872 | tf_op jit(solution)/shard_map/ppermute | solution.py:261
  109.9 1.1 add.14.refs_1_
  112.2 3.1 %collective-permute-start.15 = (f32[256,512]{1,0:T(8,128)S(1)}, f32[256,512]{1,0:T(8,128)}, u32[]{:S(2)}, u32[]{:S(2)}) collective-permute-start(f32[256,512]{1,0:T(8,128)S(1)} %add.14.refs_1_), channel_id=1, source_target_pairs={{32,0},{40,8},{48,16},{56,24},{64,32},{72,40},{80,48},{88,56},{96,... | collective-permute-start | bytes 1572872 | tf_op jit(solution)/shard_map/ppermute | solution.py:65
  115.3 1.3 collective-permute-start.14
  116.6 4.4 %transform.10 = f32[256,512]{1,0:T(8,128)} custom-call(f32[4,1,256,512]{3,2,1,0:T(8,128)} %bitcast.9.part, f32[16,4,64,512]{3,2,1,0:T(8,128)} %bitcast.25), custom_call_target="tpu_custom_call" | custom-call | flops 5000000000 | tf_op jit(solution)/shard_map/transform/pallas_call | solution.py:126
  121.0 2.0 collective-permute-done.9
  123.0 1.3 add.15.refs_0_
  124.3 2.4 %collective-permute-done.8.refs_7_ = f32[256,512]{1,0:T(8,128)S(1)} collective-permute-done((f32[256,512]{1,0:T(8,128)S(1)}, f32[256,512]{1,0:T(8,128)S(1)}, u32[]{:S(2)}, u32[]{:S(2)}) %collective-permute-start.8) | collective-permute-done | bytes 524320 | tf_op jit(solution)/shard_map/ppermute | solution.py:65
  126.8 3.2 %collective-permute-start.11 = (f32[256,512]{1,0:T(8,128)S(1)}, f32[256,512]{1,0:T(8,128)}, u32[]{:S(2)}, u32[]{:S(2)}) collective-permute-start(f32[256,512]{1,0:T(8,128)S(1)} %add.15.refs_0_), channel_id=1, source_target_pairs={{32,0},{40,8},{48,16},{56,24},{64,32},{72,40},{80,48},{88,56},{96,... | collective-permute-start | bytes 1572872 | tf_op jit(solution)/shard_map/ppermute | solution.py:65
  130.0 4.2 %collective-permute-done.14.refs_8_ = f32[256,512]{1,0:T(8,128)S(1)} collective-permute-done((f32[256,512]{1,0:T(8,128)S(1)}, f32[256,512]{1,0:T(8,128)S(1)}, u32[]{:S(2)}, u32[]{:S(2)}) %collective-permute-start.14) | collective-permute-done | bytes 524320 | tf_op jit(solution)/shard_map/ppermute | solution.py:65
  135.1 5.4 %gram.4.refs_4_ = f32[8,5,32,256]{3,2,1,0:T(8,128)} custom-call(f32[256,512]{1,0:T(8,128)} %copy-done.1, f32[256,512]{1,0:T(8,128)} %copy-done.2, f32[256,512]{1,0:T(8,128)} %copy-done.6, f32[256,512]{1,0:T(8,128)} %collective-permute-done.7.refs_3_, f32[256,512]{1,0:T(8,128)} %copy-done.7, f32[256,512]{1,0:T(8,128)} %collective-permute-done.15.refs_5_, ...), custom_call_target="tpu_custom_call" | custom-call | tf_op jit(solution)/shard_map/gram/pallas_call | solution.py:178
  141.9 4.3 %gram.5 = f32[8,5,32,256]{3,2,1,0:T(8,128)} custom-call(f32[256,512]{1,0:T(8,128)} %copy-done.4, f32[256,512]{1,0:T(8,128)} %collective-permute-done.10.refs_1_, f32[256,512]{1,0:T(8,128)} %collective-permute-done.11.refs_2_, f32[256,512]{1,0:T(8,128)} %copy-done.11, f32[8,5,32,256]{3,2,1,0:T(8,128)} %gram.4.refs_4_), custom_call_target="tpu_custom_call" | custom-call | tf_op jit(solution)/shard_map/gram/pallas_call | solution.py:178
  146.2 7.7 %all-to-all-start.2 = ((f32[8,5,32,256]{3,2,1,0:T(8,128)}), f32[8,5,32,256]{3,2,1,0:T(8,128)S(1)}, u32[]{:S(2)}, u32[]{:S(2)}) async-start(f32[8,5,32,256]{3,2,1,0:T(8,128)} %gram.5), calls=%async_computation.2 | async-start | bytes 2621440 | tf_op jit(solution)/shard_map/all_to_all | solution.py:264
  154.7 5.3 %gram.6.refs_5_ = f32[8,4,32,256]{3,2,1,0:T(8,128)} custom-call(f32[256,512]{1,0:T(8,128)} %copy-done.1, f32[256,512]{1,0:T(8,128)} %copy-done.2, f32[256,512]{1,0:T(8,128)} %copy-done.6, f32[256,512]{1,0:T(8,128)} %collective-permute-done.7.refs_3_, f32[256,512]{1,0:T(8,128)} %copy-done.7, f32[256,512]{1,0:T(8,128)} %collective-permute-done.15.refs_5_, ...), custom_call_target="tpu_custom_call" | custom-call | tf_op jit(solution)/shard_map/gram/pallas_call | solution.py:178
  160.0 11.1 %collective-permute-done.16.refs_4_ = f32[256,512]{1,0:T(8,128)S(1)} collective-permute-done((f32[256,512]{1,0:T(8,128)}, f32[256,512]{1,0:T(8,128)S(1)}, u32[]{:S(2)}, u32[]{:S(2)}) %collective-permute-start.16) | collective-permute-done | bytes 524320 | tf_op jit(solution)/shard_map/ppermute | solution.py:65
  171.9 4.0 %gram.7 = f32[8,4,32,256]{3,2,1,0:T(8,128)} custom-call(f32[256,512]{1,0:T(8,128)} %copy-done.4, f32[256,512]{1,0:T(8,128)} %collective-permute-done.10.refs_1_, f32[256,512]{1,0:T(8,128)} %collective-permute-done.11.refs_2_, f32[256,512]{1,0:T(8,128)} %copy-done.11, f32[256,512]{1,0:T(8,128)} %copy-done.23, f32[8,4,32,256]{3,2,1,0:T(8,128)} %gram.6.refs_5_), custom_call_target="tpu_custom_call" | custom-call | flops 20000000000 | tf_op jit(solution)/shard_map/gram/pallas_call | solution.py:178
  175.9 5.4 %all-to-all-start.3 = ((f32[8,4,32,256]{3,2,1,0:T(8,128)}), f32[8,4,32,256]{3,2,1,0:T(8,128)S(1)}, u32[]{:S(2)}, u32[]{:S(2)}) async-start(f32[8,4,32,256]{3,2,1,0:T(8,128)} %gram.7), calls=%async_computation.3 | async-start | bytes 2097152 | tf_op jit(solution)/shard_map/all_to_all | solution.py:264
  181.3 2.0 sum.2
  183.3 3.2 %collective-permute-start.20 = (f32[1,32,256]{2,1,0:T(8,128)}, f32[1,32,256]{2,1,0:T(8,128)S(1)}, u32[]{:S(2)}, u32[]{:S(2)}) collective-permute-start(f32[1,32,256]{2,1,0:T(8,128)} %get-tuple-element.74), channel_id=1, source_target_pairs={{0,96},{8,104},{16,112},{24,120},{32,0},{40,8},{48,16},{56,24},{64... | collective-permute-start | bytes 98312 | tf_op jit(solution)/shard_map/ppermute | solution.py:70
  186.6 1.9 collective-permute-done.20.refs_1_
  189.4 7.0 %all-to-all-done.3.moved_ref = f32[8,4,32,256]{3,2,1,0:T(8,128)S(1)} async-done(((f32[8,4,32,256]{3,2,1,0:T(8,128)}), f32[8,4,32,256]{3,2,1,0:T(8,128)S(1)}, u32[]{:S(2)}, u32[]{:S(2)}) %all-to-all-start.3) | async-done | bytes 1048608 | tf_op jit(solution)/shard_map/all_to_all | solution.py:264
  196.4 1.0 copy-done.3
  197.4 1.9 sum.3
  199.4 2.4 %collective-permute-start.24 = (f32[4,32,256]{2,1,0:T(8,128)}, f32[4,32,256]{2,1,0:T(8,128)S(1)}, u32[]{:S(2)}, u32[]{:S(2)}) collective-permute-start(f32[4,32,256]{2,1,0:T(8,128)} %get-tuple-element.84), channel_id=1, source_target_pairs={{0,48},{8,56},{16,40},{24,32},{32,80},{40,88},{48,72},{56,64},{64,... | collective-permute-start | bytes 393224 | tf_op jit(solution)/shard_map/ppermute | solution.py:70
  201.7 4.9 %collective-permute-done.24.refs_2_ = f32[4,32,256]{2,1,0:T(8,128)S(1)} collective-permute-done((f32[4,32,256]{2,1,0:T(8,128)}, f32[4,32,256]{2,1,0:T(8,128)S(1)}, u32[]{:S(2)}, u32[]{:S(2)}) %collective-permute-start.24) | collective-permute-done | bytes 131104 | tf_op jit(solution)/shard_map/ppermute | solution.py:70
  207.3 1.8 turn.1
  209.1 3.8 %all-to-all-start.4 = ((f32[8,32,256]{2,1,0:T(8,128)}), f32[8,32,256]{2,1,0:T(8,128)S(1)}, u32[]{:S(2)}, u32[]{:S(2)}) async-start(f32[8,32,256]{2,1,0:T(8,128)} %turn.1), calls=%async_computation.4 | async-start | bytes 524288 | tf_op jit(solution)/shard_map/all_to_all | solution.py:264
  213.8 2.4 %collective-permute-start.23 = (f32[1,32,256]{2,1,0:T(8,128)}, f32[1,32,256]{2,1,0:T(8,128)S(1)}, u32[]{:S(2)}, u32[]{:S(2)}) collective-permute-start(f32[1,32,256]{2,1,0:T(8,128)} %get-tuple-element.82), channel_id=1, source_target_pairs={{0,96},{8,104},{16,112},{24,120},{32,0},{40,8},{48,16},{56,24},{64... | collective-permute-start | bytes 98312 | tf_op jit(solution)/shard_map/ppermute | solution.py:70
  216.3 1.2 dynamic-slice_bitcast_fusion.table_ref
  218.4 3.0 %all-to-all-done.4.refs_7_ = f32[8,32,256]{2,1,0:T(8,128)S(1)} async-done(((f32[8,32,256]{2,1,0:T(8,128)}), f32[8,32,256]{2,1,0:T(8,128)S(1)}, u32[]{:S(2)}, u32[]{:S(2)}) %all-to-all-start.4) | async-done | bytes 262176 | tf_op jit(solution)/shard_map/all_to_all | solution.py:264
  222.1 2.2 assemble.1
  (84 shorter events, 10.3 us)
Async XLA Ops:
  6.5 69.0 %all-gather.3.cloned.1.call-start = ((), (), s32[]{:S(2)}) async-start(), calls=%async_computation.5 | async-start | bytes 8912896 | tf_op jit(solution)/shard_map/all_gather | solution.py:274
  6.5 10.3 %collective-permute-start.2 = (f32[64,512]{1,0:T(8,128)}, f32[64,512]{1,0:T(8,128)S(1)}, u32[]{:S(2)}, u32[]{:S(2)}) collective-permute-start(f32[64,512]{1,0:T(8,128)} %bitcast.13), channel_id=1, source_target_pairs={{6,0},{7,1},{0,2},{1,3},{2,4},{3,5},{4,6},{5,7},{14,8},{15,9},{8,1... | collective-permute-start | bytes 393224 | tf_op jit(solution)/shard_map/ppermute | solution.py:270
  8.1 9.0 %collective-permute-start.1 = (f32[64,512]{1,0:T(8,128)}, f32[64,512]{1,0:T(8,128)S(1)}, u32[]{:S(2)}, u32[]{:S(2)}) collective-permute-start(f32[64,512]{1,0:T(8,128)} %bitcast.14), channel_id=1, source_target_pairs={{4,0},{5,1},{6,2},{7,3},{0,4},{1,5},{2,6},{3,7},{12,8},{13,9},{14,... | collective-permute-start | bytes 393224 | tf_op jit(solution)/shard_map/ppermute | solution.py:270
  10.8 6.2 %collective-permute-start = (f32[64,512]{1,0:T(8,128)}, f32[64,512]{1,0:T(8,128)S(1)}, u32[]{:S(2)}, u32[]{:S(2)}) collective-permute-start(f32[64,512]{1,0:T(8,128)} %bitcast.15), channel_id=1, source_target_pairs={{2,0},{3,1},{4,2},{5,3},{6,4},{7,5},{0,6},{1,7},{10,8},{11,9},{12,... | collective-permute-start | bytes 393224 | tf_op jit(solution)/shard_map/ppermute | solution.py:270
  12.3 4.8 %copy-start.16 = (f32[512,64]{0,1:T(8,128)S(1)}, f32[512,64]{0,1:T(8,128)}, u32[]{:S(2)}) copy-start(f32[512,64]{0,1:T(8,128)} %param.4) | copy-start | bytes 393220
  17.9 53.1 %all-to-all-start = ((f32[8,256,512]{2,1,0:T(8,128)}), f32[8,256,512]{2,1,0:T(8,128)}, u32[]{:S(2)}, u32[]{:S(2)}) async-start(f32[8,256,512]{2,1,0:T(8,128)} %slice.9), calls=%async_computation | async-start | bytes 8388608 | tf_op jit(solution)/shard_map/all_to_all | solution.py:255
  71.1 30.8 %all-to-all-start.1 = ((f32[4,256,512]{2,1,0:T(8,128)}), f32[4,256,512]{2,1,0:T(8,128)}, u32[]{:S(2)}, u32[]{:S(2)}) async-start(f32[4,256,512]{2,1,0:T(8,128)} %slice.8), calls=%async_computation.1 | async-start | bytes 4194304 | tf_op jit(solution)/shard_map/all_to_all | solution.py:255
  79.9 17.4 %collective-permute-start.3 = (f32[256,512]{1,0:T(8,128)}, f32[256,512]{1,0:T(8,128)S(1)}, u32[]{:S(2)}, u32[]{:S(2)}) collective-permute-start(f32[256,512]{1,0:T(8,128)} %transform.8), channel_id=1, source_target_pairs={{1,0},{0,1},{3,2},{2,3},{5,4},{4,5},{7,6},{6,7},{9,8},{8,9},{11,10... | collective-permute-start | bytes 1572872 | tf_op jit(solution)/shard_map/ppermute | solution.py:261
  88.3 4.5 %copy-start.22 = (f32[256,512]{1,0:T(8,128)S(1)}, f32[256,512]{1,0:T(8,128)}, u32[]{:S(2)}) copy-start(f32[256,512]{1,0:T(8,128)} %transform.9) | copy-start | bytes 1572868
  92.8 17.1 %collective-permute-start.6 = (f32[256,512]{1,0:T(8,128)S(1)}, f32[256,512]{1,0:T(8,128)}, u32[]{:S(2)}, u32[]{:S(2)}) collective-permute-start(f32[256,512]{1,0:T(8,128)S(1)} %copy-done.22), channel_id=1, source_target_pairs={{1,0},{0,1},{3,2},{2,3},{5,4},{4,5},{7,6},{6,7},{9,8},{8,9},{11,10... | collective-permute-start | bytes 1572872 | tf_op jit(solution)/shard_map/ppermute | solution.py:261
  98.4 8.0 %copy-start.1 = (f32[256,512]{1,0:T(8,128)}, f32[256,512]{1,0:T(8,128)S(1)}, u32[]{:S(2)}) copy-start(f32[256,512]{1,0:T(8,128)S(1)} %add.13.refs_0_) | copy-start | bytes 1572868
  98.4 12.9 %collective-permute-start.5 = (f32[256,512]{1,0:T(8,128)S(1)}, f32[256,512]{1,0:T(8,128)S(1)}, u32[]{:S(2)}, u32[]{:S(2)}) collective-permute-start(f32[256,512]{1,0:T(8,128)S(1)} %add.13.refs_0_), channel_id=1, source_target_pairs={{96,0},{104,8},{112,16},{120,24},{0,32},{8,40},{16,48},{24,56},{40... | collective-permute-start | bytes 1572872 | tf_op jit(solution)/shard_map/ppermute | solution.py:65
  100.0 11.3 %collective-permute-start.4 = (f32[256,512]{1,0:T(8,128)S(1)}, f32[256,512]{1,0:T(8,128)S(1)}, u32[]{:S(2)}, u32[]{:S(2)}) collective-permute-start(f32[256,512]{1,0:T(8,128)S(1)} %add.13.refs_0_), channel_id=1, source_target_pairs={{8,0},{0,8},{24,16},{16,24},{40,32},{32,40},{56,48},{48,56},{72,64... | collective-permute-start | bytes 1572872 | tf_op jit(solution)/shard_map/ppermute | solution.py:65
  100.1 15.2 %collective-permute-start.13 = (f32[256,512]{1,0:T(8,128)S(1)}, f32[256,512]{1,0:T(8,128)S(1)}, u32[]{:S(2)}, u32[]{:S(2)}) collective-permute-start(f32[256,512]{1,0:T(8,128)S(1)} %add.13.refs_0_), channel_id=1, source_target_pairs={{32,0},{40,8},{48,16},{56,24},{64,32},{72,40},{80,48},{88,56},{96,... | collective-permute-start | bytes 1572872 | tf_op jit(solution)/shard_map/ppermute | solution.py:65
  101.9 8.0 %copy-start.12 = (f32[256,512]{1,0:T(8,128)S(1)}, f32[256,512]{1,0:T(8,128)}, u32[]{:S(2)}) copy-start(f32[256,512]{1,0:T(8,128)} %transform.7) | copy-start | bytes 1572868
  106.4 16.6 %collective-permute-start.9 = (f32[256,512]{1,0:T(8,128)}, f32[256,512]{1,0:T(8,128)}, u32[]{:S(2)}, u32[]{:S(2)}) collective-permute-start(f32[256,512]{1,0:T(8,128)} %transform.11), channel_id=1, source_target_pairs={{1,0},{0,1},{3,2},{2,3},{5,4},{4,5},{7,6},{6,7},{9,8},{8,9},{11,10... | collective-permute-start | bytes 1572872 | tf_op jit(solution)/shard_map/ppermute | solution.py:261
  111.0 10.0 %copy-start.2 = (f32[256,512]{1,0:T(8,128)}, f32[256,512]{1,0:T(8,128)S(1)}, u32[]{:S(2)}) copy-start(f32[256,512]{1,0:T(8,128)S(1)} %add.14.refs_1_) | copy-start | bytes 1572868
  111.4 9.6 %copy-start.5 = (f32[256,512]{1,0:T(8,128)}, f32[256,512]{1,0:T(8,128)S(1)}, u32[]{:S(2)}) copy-start(f32[256,512]{1,0:T(8,128)S(1)} %collective-permute-done.5.refs_6_) | copy-start | bytes 1572868
  111.4 9.6 %copy-start.6 = (f32[256,512]{1,0:T(8,128)}, f32[256,512]{1,0:T(8,128)S(1)}, u32[]{:S(2)}) copy-start(f32[256,512]{1,0:T(8,128)S(1)} %collective-permute-done.4.refs_2_) | copy-start | bytes 1572868
  111.4 15.4 %collective-permute-start.8 = (f32[256,512]{1,0:T(8,128)S(1)}, f32[256,512]{1,0:T(8,128)S(1)}, u32[]{:S(2)}, u32[]{:S(2)}) collective-permute-start(f32[256,512]{1,0:T(8,128)S(1)} %add.14.refs_1_), channel_id=1, source_target_pairs={{96,0},{104,8},{112,16},{120,24},{0,32},{8,40},{16,48},{24,56},{40... | collective-permute-start | bytes 1572872 | tf_op jit(solution)/shard_map/ppermute | solution.py:65
  111.7 15.0 %collective-permute-start.7 = (f32[256,512]{1,0:T(8,128)S(1)}, f32[256,512]{1,0:T(8,128)}, u32[]{:S(2)}, u32[]{:S(2)}) collective-permute-start(f32[256,512]{1,0:T(8,128)S(1)} %add.14.refs_1_), channel_id=1, source_target_pairs={{8,0},{0,8},{24,16},{16,24},{40,32},{32,40},{56,48},{48,56},{72,64... | collective-permute-start | bytes 1572872 | tf_op jit(solution)/shard_map/ppermute | solution.py:65
  112.2 22.0 %collective-permute-start.15 = (f32[256,512]{1,0:T(8,128)S(1)}, f32[256,512]{1,0:T(8,128)}, u32[]{:S(2)}, u32[]{:S(2)}) collective-permute-start(f32[256,512]{1,0:T(8,128)S(1)} %add.14.refs_1_), channel_id=1, source_target_pairs={{32,0},{40,8},{48,16},{56,24},{64,32},{72,40},{80,48},{88,56},{96,... | collective-permute-start | bytes 1572872 | tf_op jit(solution)/shard_map/ppermute | solution.py:65
  115.3 5.7 %copy-start.7 = (f32[256,512]{1,0:T(8,128)}, f32[256,512]{1,0:T(8,128)S(1)}, u32[]{:S(2)}) copy-start(f32[256,512]{1,0:T(8,128)S(1)} %collective-permute-done.13.refs_4_) | copy-start | bytes 1572868
  115.3 19.0 %collective-permute-start.14 = (f32[256,512]{1,0:T(8,128)S(1)}, f32[256,512]{1,0:T(8,128)S(1)}, u32[]{:S(2)}, u32[]{:S(2)}) collective-permute-start(f32[256,512]{1,0:T(8,128)S(1)} %collective-permute-done.13.refs_4_), channel_id=1, source_target_pairs={{16,0},{24,8},{8,16},{0,24},{48,32},{56,40},{40,48},{32,56},{88,64... | collective-permute-start | bytes 1572872 | tf_op jit(solution)/shard_map/ppermute | solution.py:65
  124.3 16.3 %copy-start.4 = (f32[256,512]{1,0:T(8,128)}, f32[256,512]{1,0:T(8,128)S(1)}, u32[]{:S(2)}) copy-start(f32[256,512]{1,0:T(8,128)S(1)} %add.15.refs_0_) | copy-start | bytes 1572868
  126.7 8.4 %copy-start.8 = (f32[256,512]{1,0:T(8,128)}, f32[256,512]{1,0:T(8,128)S(1)}, u32[]{:S(2)}) copy-start(f32[256,512]{1,0:T(8,128)S(1)} %collective-permute-done.8.refs_7_) | copy-start | bytes 1572868
  126.8 14.4 %collective-permute-start.12 = (f32[256,512]{1,0:T(8,128)S(1)}, f32[256,512]{1,0:T(8,128)S(1)}, u32[]{:S(2)}, u32[]{:S(2)}) collective-permute-start(f32[256,512]{1,0:T(8,128)S(1)} %add.15.refs_0_), channel_id=1, source_target_pairs={{96,0},{104,8},{112,16},{120,24},{0,32},{8,40},{16,48},{24,56},{40... | collective-permute-start | bytes 1572872 | tf_op jit(solution)/shard_map/ppermute | solution.py:65
  126.8 14.4 %collective-permute-start.11 = (f32[256,512]{1,0:T(8,128)S(1)}, f32[256,512]{1,0:T(8,128)}, u32[]{:S(2)}, u32[]{:S(2)}) collective-permute-start(f32[256,512]{1,0:T(8,128)S(1)} %add.15.refs_0_), channel_id=1, source_target_pairs={{32,0},{40,8},{48,16},{56,24},{64,32},{72,40},{80,48},{88,56},{96,... | collective-permute-start | bytes 1572872 | tf_op jit(solution)/shard_map/ppermute | solution.py:65
  130.0 11.1 %collective-permute-start.10 = (f32[256,512]{1,0:T(8,128)S(1)}, f32[256,512]{1,0:T(8,128)}, u32[]{:S(2)}, u32[]{:S(2)}) collective-permute-start(f32[256,512]{1,0:T(8,128)S(1)} %add.15.refs_0_), channel_id=1, source_target_pairs={{8,0},{0,8},{24,16},{16,24},{40,32},{32,40},{56,48},{48,56},{72,64... | collective-permute-start | bytes 1572872 | tf_op jit(solution)/shard_map/ppermute | solution.py:65
  134.2 6.4 %copy-start.10 = (f32[256,512]{1,0:T(8,128)}, f32[256,512]{1,0:T(8,128)S(1)}, u32[]{:S(2)}) copy-start(f32[256,512]{1,0:T(8,128)S(1)} %collective-permute-done.14.refs_8_) | copy-start | bytes 1572868
  134.2 19.6 %collective-permute-start.17 = (f32[256,512]{1,0:T(8,128)}, f32[256,512]{1,0:T(8,128)S(1)}, u32[]{:S(2)}, u32[]{:S(2)}) collective-permute-start(f32[256,512]{1,0:T(8,128)} %collective-permute-done.15.refs_5_), channel_id=1, source_target_pairs={{16,0},{24,8},{8,16},{0,24},{48,32},{56,40},{40,48},{32,56},{88,64... | collective-permute-start | bytes 1572872 | tf_op jit(solution)/shard_map/ppermute | solution.py:65
  141.1 30.0 %collective-permute-start.16 = (f32[256,512]{1,0:T(8,128)}, f32[256,512]{1,0:T(8,128)S(1)}, u32[]{:S(2)}, u32[]{:S(2)}) collective-permute-start(f32[256,512]{1,0:T(8,128)} %collective-permute-done.11.refs_2_), channel_id=1, source_target_pairs={{16,0},{24,8},{8,16},{0,24},{48,32},{56,40},{40,48},{32,56},{88,64... | collective-permute-start | bytes 1572872 | tf_op jit(solution)/shard_map/ppermute | solution.py:65
  146.2 29.7 %all-to-all-start.2 = ((f32[8,5,32,256]{3,2,1,0:T(8,128)}), f32[8,5,32,256]{3,2,1,0:T(8,128)S(1)}, u32[]{:S(2)}, u32[]{:S(2)}) async-start(f32[8,5,32,256]{3,2,1,0:T(8,128)} %gram.5), calls=%async_computation.2 | async-start | bytes 2621440 | tf_op jit(solution)/shard_map/all_to_all | solution.py:264
  175.9 5.4 %copy-start = (f32[8,5,32,256]{3,2,1,0:T(8,128)}, f32[8,5,32,256]{3,2,1,0:T(8,128)S(1)}, u32[]{:S(2)}) copy-start(f32[8,5,32,256]{3,2,1,0:T(8,128)S(1)} %all-to-all-done.2.moved_ref) | copy-start | bytes 3932164
  175.9 20.4 %all-to-all-start.3 = ((f32[8,4,32,256]{3,2,1,0:T(8,128)}), f32[8,4,32,256]{3,2,1,0:T(8,128)S(1)}, u32[]{:S(2)}, u32[]{:S(2)}) async-start(f32[8,4,32,256]{3,2,1,0:T(8,128)} %gram.7), calls=%async_computation.3 | async-start | bytes 2097152 | tf_op jit(solution)/shard_map/all_to_all | solution.py:264
  183.3 6.0 %collective-permute-start.19 = (f32[3,32,256]{2,1,0:T(8,128)}, f32[3,32,256]{2,1,0:T(8,128)S(1)}, u32[]{:S(2)}, u32[]{:S(2)}) collective-permute-start(f32[3,32,256]{2,1,0:T(8,128)} %get-tuple-element.73), channel_id=1, source_target_pairs={{0,32},{8,40},{16,48},{24,56},{32,64},{40,72},{48,80},{56,88},{64,... | collective-permute-start | bytes 294920 | tf_op jit(solution)/shard_map/ppermute | solution.py:70
  183.3 3.2 %collective-permute-start.18 = (f32[1,32,256]{2,1,0:T(8,128)}, f32[1,32,256]{2,1,0:T(8,128)S(1)}, u32[]{:S(2)}, u32[]{:S(2)}) collective-permute-start(f32[1,32,256]{2,1,0:T(8,128)} %get-tuple-element.72), channel_id=1, source_target_pairs={{0,8},{8,0},{16,24},{24,16},{32,40},{40,32},{48,56},{56,48},{64,72... | collective-permute-start | bytes 98312 | tf_op jit(solution)/shard_map/ppermute | solution.py:70
  183.3 5.1 %collective-permute-start.20 = (f32[1,32,256]{2,1,0:T(8,128)}, f32[1,32,256]{2,1,0:T(8,128)S(1)}, u32[]{:S(2)}, u32[]{:S(2)}) collective-permute-start(f32[1,32,256]{2,1,0:T(8,128)} %get-tuple-element.74), channel_id=1, source_target_pairs={{0,96},{8,104},{16,112},{24,120},{32,0},{40,8},{48,16},{56,24},{64... | collective-permute-start | bytes 98312 | tf_op jit(solution)/shard_map/ppermute | solution.py:70
  186.6 34.8 %copy-start.17 = (f32[1,32,256]{2,1,0:T(8,128)}, f32[1,32,256]{2,1,0:T(8,128)S(1)}, u32[]{:S(2)}) copy-start(f32[1,32,256]{2,1,0:T(8,128)S(1)} %collective-permute-done.18.refs_1_) | copy-start | bytes 98308
  188.5 18.2 %copy-start.19 = (f32[1,32,256]{2,1,0:T(8,128)}, f32[1,32,256]{2,1,0:T(8,128)S(1)}, u32[]{:S(2)}) copy-start(f32[1,32,256]{2,1,0:T(8,128)S(1)} %collective-permute-done.20.refs_1_) | copy-start | bytes 98308
  189.4 17.3 %copy-start.14 = (f32[3,32,256]{2,1,0:T(8,128)}, f32[3,32,256]{2,1,0:T(8,128)S(1)}, u32[]{:S(2)}) copy-start(f32[3,32,256]{2,1,0:T(8,128)S(1)} %collective-permute-done.19.refs_0_.refs_2_) | copy-start | bytes 294916
  199.4 7.3 %collective-permute-start.24 = (f32[4,32,256]{2,1,0:T(8,128)}, f32[4,32,256]{2,1,0:T(8,128)S(1)}, u32[]{:S(2)}, u32[]{:S(2)}) collective-permute-start(f32[4,32,256]{2,1,0:T(8,128)} %get-tuple-element.84), channel_id=1, source_target_pairs={{0,48},{8,56},{16,40},{24,32},{32,80},{40,88},{48,72},{56,64},{64,... | collective-permute-start | bytes 393224 | tf_op jit(solution)/shard_map/ppermute | solution.py:70
  209.1 12.3 %all-to-all-start.4 = ((f32[8,32,256]{2,1,0:T(8,128)}), f32[8,32,256]{2,1,0:T(8,128)S(1)}, u32[]{:S(2)}, u32[]{:S(2)}) async-start(f32[8,32,256]{2,1,0:T(8,128)} %turn.1), calls=%async_computation.4 | async-start | bytes 524288 | tf_op jit(solution)/shard_map/all_to_all | solution.py:264
  212.9 4.5 %collective-permute-start.21 = (f32[1,32,256]{2,1,0:T(8,128)}, f32[1,32,256]{2,1,0:T(8,128)S(1)}, u32[]{:S(2)}, u32[]{:S(2)}) collective-permute-start(f32[1,32,256]{2,1,0:T(8,128)} %get-tuple-element.80), channel_id=1, source_target_pairs={{0,8},{8,0},{16,24},{24,16},{32,40},{40,32},{48,56},{56,48},{64,72... | collective-permute-start | bytes 98312 | tf_op jit(solution)/shard_map/ppermute | solution.py:70
  213.0 5.4 %collective-permute-start.22 = (f32[1,32,256]{2,1,0:T(8,128)}, f32[1,32,256]{2,1,0:T(8,128)S(1)}, u32[]{:S(2)}, u32[]{:S(2)}) collective-permute-start(f32[1,32,256]{2,1,0:T(8,128)} %get-tuple-element.81), channel_id=1, source_target_pairs={{0,32},{8,40},{16,48},{24,56},{32,64},{40,72},{48,80},{56,88},{64,... | collective-permute-start | bytes 98312 | tf_op jit(solution)/shard_map/ppermute | solution.py:70
  213.8 4.5 %collective-permute-start.23 = (f32[1,32,256]{2,1,0:T(8,128)}, f32[1,32,256]{2,1,0:T(8,128)S(1)}, u32[]{:S(2)}, u32[]{:S(2)}) collective-permute-start(f32[1,32,256]{2,1,0:T(8,128)} %get-tuple-element.82), channel_id=1, source_target_pairs={{0,96},{8,104},{16,112},{24,120},{32,0},{40,8},{48,16},{56,24},{64... | collective-permute-start | bytes 98312 | tf_op jit(solution)/shard_map/ppermute | solution.py:70
  217.5 3.9 %copy-start.18 = (f32[1,32,256]{2,1,0:T(8,128)}, f32[1,32,256]{2,1,0:T(8,128)S(1)}, u32[]{:S(2)}) copy-start(f32[1,32,256]{2,1,0:T(8,128)S(1)} %collective-permute-done.21.refs_4_) | copy-start | bytes 98308
  218.4 3.0 %copy-start.21 = (f32[1,32,256]{2,1,0:T(8,128)}, f32[1,32,256]{2,1,0:T(8,128)S(1)}, u32[]{:S(2)}) copy-start(f32[1,32,256]{2,1,0:T(8,128)S(1)} %collective-permute-done.23.refs_6_) | copy-start | bytes 98308
  (7 other events, 7.9 us)
Sparse Core Ops, SparseCore 0:
  18.1 54.1 all-gather.2

commit v12 on v9

--- a/solution.py
+++ b/solution.py
@@ -294,7 +294,7 @@
     other_0, below_0, above_0, own_1 = together(other_0, below_0, above_0, own_1)
     across_0 = fetched(below_0, over_to_across)
     other_1, below_1, above_1 = neighbours(own_1)
-    other_1, below_1, above_1, own_2 = together(other_1, below_1, above_1, own_2)
+    other_1, above_1, own_2 = together(other_1, above_1, own_2)
     across_0, below_1 = together(across_0, below_1)
     across_1 = fetched(below_1, over_to_across)
     other_2, below_2, above_2 = neighbours(own_2)

time: 234 us -> 234 us (level)
    ppermute x12, waiting for transfers between devices: 17.2 us -> 20.7 us  [fetched(): return lax.ppermute(value, 'blk', route)]
    all_to_all x3, waiting for transfers between devices: 14.6 us -> 12.1 us  [over_col(): return lax.all_to_all(tiles, 'col', split_axis=0, concat_axis=0, tiled=True)]
    unnamed x46 -> x44, local copies, waits for them, and re-layouts: 4.98 us -> 4.8 us
where the time goes in v12:
time: 234 us; the launch traced here: 233 us
  waiting for transfers between devices  93.2 us (40%)
  starting transfers between devices  54.4 us (23%)
  Pallas kernels  53.3 us (23%)
  local copies, waits for them, and re-layouts  13.8 us (6%)
  between operations  13.7 us (6%)
  other arithmetic  4.36 us (2%)
    all_to_all x2, waiting for transfers between devices, over_x(): lax.all_to_all(part, 'col', split_axis=0, concat_axis=0, tiled=True, axis...  45.1 us
    pallas_call x6, Pallas kernels, transformed(): pl.pallas_call(functools.partial(transform_kernel, index, keeps), in_spec...  26.3 us
    ppermute x12, waiting for transfers between devices, fetched(): return lax.ppermute(value, 'blk', route)  20.7 us
    pallas_call x4, Pallas kernels, gram(): pl.pallas_call(functools.partial(gram_kernel, pairs, chunks, more), in_sp...  19 us
    all_to_all x3, starting transfers between devices, over_col(): return lax.all_to_all(tiles, 'col', split_axis=0, concat_axis=0, tiled=True)  13.4 us
    all_to_all x3, waiting for transfers between devices, over_col(): return lax.all_to_all(tiles, 'col', split_axis=0, concat_axis=0, tiled=True)  12.1 us
    ppermute x12, starting transfers between devices, fetched(): return lax.ppermute(value, 'blk', route)  11.6 us
    ppermute x7, waiting for transfers between devices, delivered(): return lax.ppermute(value, 'blk', route)  10.9 us
  transfers between devices with their start and end apart: 31, of which 14 were waited for; matrix products, arithmetic and copies ran while one was open for 5% of the time, Pallas kernels for 20%

profile of v12, /device:TPU:0, one launch (start us, length us, event | category | flops | bytes accessed | tf_op | source)
XLA Modules:
  0.0 232.7 jit_solution(10739766413405825271)
XLA Ops:
  6.5 1.6 collective-permute-start.2
  8.1 2.7 %collective-permute-start.1 = (f32[64,512]{1,0:T(8,128)}, f32[64,512]{1,0:T(8,128)S(1)}, u32[]{:S(2)}, u32[]{:S(2)}) collective-permute-start(f32[64,512]{1,0:T(8,128)} %bitcast.14), channel_id=1, source_target_pairs={{4,0},{5,1},{6,2},{7,3},{0,4},{1,5},{2,6},{3,7},{12,8},{13,9},{14,... | collective-permute-start | bytes 393224 | tf_op jit(solution)/shard_map/ppermute | solution.py:269
  10.8 1.4 collective-permute-start
  12.3 4.6 %slice.9 = f32[8,256,512]{2,1,0:T(8,128)} slice(f32[12,256,512]{2,1,0:T(8,128)} %bitcast.11), slice={[0:8], [0:256], [0:512]} | slice | bytes 8388608 | tf_op jit(solution)/shard_map/slice | solution.py:270
  17.9 4.8 %all-to-all-start = ((f32[8,256,512]{2,1,0:T(8,128)}), f32[8,256,512]{2,1,0:T(8,128)}, u32[]{:S(2)}, u32[]{:S(2)}) async-start(f32[8,256,512]{2,1,0:T(8,128)} %slice.9), calls=%async_computation | async-start | bytes 8388608 | tf_op jit(solution)/shard_map/all_to_all | solution.py:254
  22.8 3.1 %slice.8 = f32[4,256,512]{2,1,0:T(8,128)} slice(f32[12,256,512]{2,1,0:T(8,128)} %bitcast.12), slice={[8:12], [0:256], [0:512]} | slice | bytes 4194304 | tf_op jit(solution)/shard_map/slice | solution.py:274
  25.9 45.1 %all-to-all-done = f32[8,256,512]{2,1,0:T(8,128)} async-done(((f32[8,256,512]{2,1,0:T(8,128)}), f32[8,256,512]{2,1,0:T(8,128)}, u32[]{:S(2)}, u32[]{:S(2)}) %all-to-all-start) | async-done | bytes 4194336 | tf_op jit(solution)/shard_map/all_to_all | solution.py:254
  71.1 4.4 %all-to-all-start.1 = ((f32[4,256,512]{2,1,0:T(8,128)}), f32[4,256,512]{2,1,0:T(8,128)}, u32[]{:S(2)}, u32[]{:S(2)}) async-start(f32[4,256,512]{2,1,0:T(8,128)} %slice.8), calls=%async_computation.1 | async-start | bytes 4194304 | tf_op jit(solution)/shard_map/all_to_all | solution.py:254
  75.5 4.4 %transform.7 = f32[256,512]{1,0:T(8,128)} custom-call(f32[4,2,256,512]{3,2,1,0:T(8,128)} %bitcast.3.part, f32[16,4,64,512]{3,2,1,0:T(8,128)} %bitcast.20), custom_call_target="tpu_custom_call" | custom-call | flops 5000000000 | tf_op jit(solution)/shard_map/transform/pallas_call | solution.py:126
  79.9 4.0 %collective-permute-start.3 = (f32[256,512]{1,0:T(8,128)}, f32[256,512]{1,0:T(8,128)S(1)}, u32[]{:S(2)}, u32[]{:S(2)}) collective-permute-start(f32[256,512]{1,0:T(8,128)} %transform.7), channel_id=1, source_target_pairs={{1,0},{0,1},{3,2},{2,3},{5,4},{4,5},{7,6},{6,7},{9,8},{8,9},{11,10... | collective-permute-start | bytes 1572872 | tf_op jit(solution)/shard_map/ppermute | solution.py:260
  83.9 4.4 %transform.10 = f32[256,512]{1,0:T(8,128)} custom-call(f32[4,2,256,512]{3,2,1,0:T(8,128)} %bitcast.3.part, f32[16,4,64,512]{3,2,1,0:T(8,128)} %bitcast.21), custom_call_target="tpu_custom_call" | custom-call | flops 5000000000 | tf_op jit(solution)/shard_map/transform/pallas_call | solution.py:126
  88.4 4.4 %transform.6 = f32[256,512]{1,0:T(8,128)} custom-call(f32[4,2,256,512]{3,2,1,0:T(8,128)} %bitcast.3.part, f32[16,4,64,512]{3,2,1,0:T(8,128)} %bitcast.22), custom_call_target="tpu_custom_call" | custom-call | flops 5000000000 | tf_op jit(solution)/shard_map/transform/pallas_call | solution.py:126
  92.8 4.1 %collective-permute-done.3 = f32[256,512]{1,0:T(8,128)S(1)} collective-permute-done((f32[256,512]{1,0:T(8,128)}, f32[256,512]{1,0:T(8,128)S(1)}, u32[]{:S(2)}, u32[]{:S(2)}) %collective-permute-start.3) | collective-permute-done | bytes 524320 | tf_op jit(solution)/shard_map/ppermute | solution.py:260
  97.0 1.1 add.13.refs_0_
  98.1 1.7 collective-permute-start.6
  99.7 1.7 collective-permute-start.5
  101.4 4.4 %transform.8 = f32[256,512]{1,0:T(8,128)} custom-call(f32[4,1,256,512]{3,2,1,0:T(8,128)} %bitcast.9.part, f32[16,4,64,512]{3,2,1,0:T(8,128)} %bitcast.23), custom_call_target="tpu_custom_call" | custom-call | flops 5000000000 | tf_op jit(solution)/shard_map/transform/pallas_call | solution.py:126
  105.8 3.8 %collective-permute-start.10 = (f32[256,512]{1,0:T(8,128)}, f32[256,512]{1,0:T(8,128)}, u32[]{:S(2)}, u32[]{:S(2)}) collective-permute-start(f32[256,512]{1,0:T(8,128)} %transform.8), channel_id=1, source_target_pairs={{1,0},{0,1},{3,2},{2,3},{5,4},{4,5},{7,6},{6,7},{9,8},{8,9},{11,10... | collective-permute-start | bytes 1572872 | tf_op jit(solution)/shard_map/ppermute | solution.py:260
  109.6 4.4 %transform.9 = f32[256,512]{1,0:T(8,128)} custom-call(f32[4,2,256,512]{3,2,1,0:T(8,128)} %bitcast.3.part, f32[16,4,64,512]{3,2,1,0:T(8,128)} %bitcast.24), custom_call_target="tpu_custom_call" | custom-call | flops 5000000000 | tf_op jit(solution)/shard_map/transform/pallas_call | solution.py:126
  114.0 1.1 add.14.refs_1_
  115.2 1.0 collective-permute-start.9
  116.2 2.3 %collective-permute-start.15 = (f32[256,512]{1,0:T(8,128)S(1)}, f32[256,512]{1,0:T(8,128)}, u32[]{:S(2)}, u32[]{:S(2)}) collective-permute-start(f32[256,512]{1,0:T(8,128)S(1)} %add.14.refs_1_), channel_id=1, source_target_pairs={{32,0},{40,8},{48,16},{56,24},{64,32},{72,40},{80,48},{88,56},{96,... | collective-permute-start | bytes 1572872 | tf_op jit(solution)/shard_map/ppermute | solution.py:65
  119.4 4.4 %transform.11 = f32[256,512]{1,0:T(8,128)} custom-call(f32[4,1,256,512]{3,2,1,0:T(8,128)} %bitcast.9.part, f32[16,4,64,512]{3,2,1,0:T(8,128)} %bitcast.25), custom_call_target="tpu_custom_call" | custom-call | flops 5000000000 | tf_op jit(solution)/shard_map/transform/pallas_call | solution.py:126
  123.8 1.3 add.15.refs_0_
  125.1 5.5 %collective-permute-done.9.refs_7_ = f32[256,512]{1,0:T(8,128)S(1)} collective-permute-done((f32[256,512]{1,0:T(8,128)S(1)}, f32[256,512]{1,0:T(8,128)S(1)}, u32[]{:S(2)}, u32[]{:S(2)}) %collective-permute-start.9) | collective-permute-done | bytes 524320 | tf_op jit(solution)/shard_map/ppermute | solution.py:65
  130.6 3.2 %collective-permute-start.12 = (f32[256,512]{1,0:T(8,128)S(1)}, f32[256,512]{1,0:T(8,128)}, u32[]{:S(2)}, u32[]{:S(2)}) collective-permute-start(f32[256,512]{1,0:T(8,128)S(1)} %add.15.refs_0_), channel_id=1, source_target_pairs={{32,0},{40,8},{48,16},{56,24},{64,32},{72,40},{80,48},{88,56},{96,... | collective-permute-start | bytes 1572872 | tf_op jit(solution)/shard_map/ppermute | solution.py:65
  135.2 5.4 %gram.4.refs_4_ = f32[8,5,32,256]{3,2,1,0:T(8,128)} custom-call(f32[256,512]{1,0:T(8,128)} %copy-done.1, f32[256,512]{1,0:T(8,128)} %copy-done.2, f32[256,512]{1,0:T(8,128)} %copy-done.7, f32[256,512]{1,0:T(8,128)} %collective-permute-done.8.refs_3_, f32[256,512]{1,0:T(8,128)} %copy-done.6, f32[256,512]{1,0:T(8,128)} %collective-permute-done.15.refs_5_, ...), custom_call_target="tpu_custom_call" | custom-call | tf_op jit(solution)/shard_map/gram/pallas_call | solution.py:178
  140.7 4.3 %collective-permute-done.13.refs_3_ = f32[256,512]{1,0:T(8,128)S(1)} collective-permute-done((f32[256,512]{1,0:T(8,128)S(1)}, f32[256,512]{1,0:T(8,128)S(1)}, u32[]{:S(2)}, u32[]{:S(2)}) %collective-permute-start.13) | collective-permute-done | bytes 524320 | tf_op jit(solution)/shard_map/ppermute | solution.py:65
  145.8 4.3 %gram.5 = f32[8,5,32,256]{3,2,1,0:T(8,128)} custom-call(f32[256,512]{1,0:T(8,128)} %copy-done.4, f32[256,512]{1,0:T(8,128)} %collective-permute-done.11.refs_1_, f32[256,512]{1,0:T(8,128)} %collective-permute-done.12.refs_2_, f32[256,512]{1,0:T(8,128)} %copy-done.11, f32[8,5,32,256]{3,2,1,0:T(8,128)} %gram.4.refs_4_), custom_call_target="tpu_custom_call" | custom-call | tf_op jit(solution)/shard_map/gram/pallas_call | solution.py:178
  150.1 4.7 %all-to-all-start.2 = ((f32[8,5,32,256]{3,2,1,0:T(8,128)}), f32[8,5,32,256]{3,2,1,0:T(8,128)S(1)}, u32[]{:S(2)}, u32[]{:S(2)}) async-start(f32[8,5,32,256]{3,2,1,0:T(8,128)} %gram.5), calls=%async_computation.2 | async-start | bytes 2621440 | tf_op jit(solution)/shard_map/all_to_all | solution.py:263
  155.6 5.3 %gram.6.refs_5_ = f32[8,4,32,256]{3,2,1,0:T(8,128)} custom-call(f32[256,512]{1,0:T(8,128)} %copy-done.1, f32[256,512]{1,0:T(8,128)} %copy-done.2, f32[256,512]{1,0:T(8,128)} %copy-done.7, f32[256,512]{1,0:T(8,128)} %collective-permute-done.8.refs_3_, f32[256,512]{1,0:T(8,128)} %copy-done.6, f32[256,512]{1,0:T(8,128)} %collective-permute-done.15.refs_5_, ...), custom_call_target="tpu_custom_call" | custom-call | tf_op jit(solution)/shard_map/gram/pallas_call | solution.py:178
  160.9 10.3 %collective-permute-done.16.refs_4_ = f32[256,512]{1,0:T(8,128)S(1)} collective-permute-done((f32[256,512]{1,0:T(8,128)}, f32[256,512]{1,0:T(8,128)S(1)}, u32[]{:S(2)}, u32[]{:S(2)}) %collective-permute-start.16) | collective-permute-done | bytes 524320 | tf_op jit(solution)/shard_map/ppermute | solution.py:65
  172.0 4.0 %gram.7 = f32[8,4,32,256]{3,2,1,0:T(8,128)} custom-call(f32[256,512]{1,0:T(8,128)} %copy-done.4, f32[256,512]{1,0:T(8,128)} %collective-permute-done.11.refs_1_, f32[256,512]{1,0:T(8,128)} %collective-permute-done.12.refs_2_, f32[256,512]{1,0:T(8,128)} %copy-done.11, f32[256,512]{1,0:T(8,128)} %copy-done.21, f32[8,4,32,256]{3,2,1,0:T(8,128)} %gram.6.refs_5_), custom_call_target="tpu_custom_call" | custom-call | flops 20000000000 | tf_op jit(solution)/shard_map/gram/pallas_call | solution.py:178
  176.7 4.8 %all-to-all-start.3 = ((f32[8,4,32,256]{3,2,1,0:T(8,128)}), f32[8,4,32,256]{3,2,1,0:T(8,128)S(1)}, u32[]{:S(2)}, u32[]{:S(2)}) async-start(f32[8,4,32,256]{3,2,1,0:T(8,128)} %gram.7), calls=%async_computation.3 | async-start | bytes 2097152 | tf_op jit(solution)/shard_map/all_to_all | solution.py:263
  181.5 2.1 sum.2
  183.7 3.2 %collective-permute-start.20 = (f32[1,32,256]{2,1,0:T(8,128)}, f32[1,32,256]{2,1,0:T(8,128)S(1)}, u32[]{:S(2)}, u32[]{:S(2)}) collective-permute-start(f32[1,32,256]{2,1,0:T(8,128)} %get-tuple-element.76), channel_id=1, source_target_pairs={{0,96},{8,104},{16,112},{24,120},{32,0},{40,8},{48,16},{56,24},{64... | collective-permute-start | bytes 98312 | tf_op jit(solution)/shard_map/ppermute | solution.py:70
  186.8 1.9 collective-permute-done.20.refs_1_
  188.7 0.9 collective-permute-done.19.refs_0_.refs_2_
  189.6 8.4 %all-to-all-done.3.moved_ref = f32[8,4,32,256]{3,2,1,0:T(8,128)S(1)} async-done(((f32[8,4,32,256]{3,2,1,0:T(8,128)}), f32[8,4,32,256]{3,2,1,0:T(8,128)S(1)}, u32[]{:S(2)}, u32[]{:S(2)}) %all-to-all-start.3) | async-done | bytes 1048608 | tf_op jit(solution)/shard_map/all_to_all | solution.py:263
  198.0 1.0 copy-done.3
  199.0 2.0 sum.3
  201.0 7.3 %collective-permute-done.24.refs_2_ = f32[4,32,256]{2,1,0:T(8,128)S(1)} collective-permute-done((f32[4,32,256]{2,1,0:T(8,128)}, f32[4,32,256]{2,1,0:T(8,128)S(1)}, u32[]{:S(2)}, u32[]{:S(2)}) %collective-permute-start.24) | collective-permute-done | bytes 131104 | tf_op jit(solution)/shard_map/ppermute | solution.py:70
  208.9 1.8 turn.1
  210.7 3.9 %all-to-all-start.4 = ((f32[8,32,256]{2,1,0:T(8,128)}), f32[8,32,256]{2,1,0:T(8,128)S(1)}, u32[]{:S(2)}, u32[]{:S(2)}) async-start(f32[8,32,256]{2,1,0:T(8,128)} %turn.1), calls=%async_computation.4 | async-start | bytes 524288 | tf_op jit(solution)/shard_map/all_to_all | solution.py:263
  214.7 3.2 %collective-permute-start.23 = (f32[1,32,256]{2,1,0:T(8,128)}, f32[1,32,256]{2,1,0:T(8,128)S(1)}, u32[]{:S(2)}, u32[]{:S(2)}) collective-permute-start(f32[1,32,256]{2,1,0:T(8,128)} %get-tuple-element.84), channel_id=1, source_target_pairs={{0,96},{8,104},{16,112},{24,120},{32,0},{40,8},{48,16},{56,24},{64... | collective-permute-start | bytes 98312 | tf_op jit(solution)/shard_map/ppermute | solution.py:70
  217.9 1.3 dynamic-slice_bitcast_fusion.table_ref
  220.0 3.0 %all-to-all-done.4.refs_7_ = f32[8,32,256]{2,1,0:T(8,128)S(1)} async-done(((f32[8,32,256]{2,1,0:T(8,128)}), f32[8,32,256]{2,1,0:T(8,128)S(1)}, u32[]{:S(2)}, u32[]{:S(2)}) %all-to-all-start.4) | async-done | bytes 262176 | tf_op jit(solution)/shard_map/all_to_all | solution.py:263
  223.7 2.2 assemble.1
  (80 shorter events, 9.0 us)
Async XLA Ops:
  6.5 69.0 %all-gather.3.cloned.1.call-start = ((), (), s32[]{:S(2)}) async-start(), calls=%async_computation.5 | async-start | bytes 8912896 | tf_op jit(solution)/shard_map/all_gather | solution.py:273
  6.5 10.3 %collective-permute-start.2 = (f32[64,512]{1,0:T(8,128)}, f32[64,512]{1,0:T(8,128)S(1)}, u32[]{:S(2)}, u32[]{:S(2)}) collective-permute-start(f32[64,512]{1,0:T(8,128)} %bitcast.13), channel_id=1, source_target_pairs={{6,0},{7,1},{0,2},{1,3},{2,4},{3,5},{4,6},{5,7},{14,8},{15,9},{8,1... | collective-permute-start | bytes 393224 | tf_op jit(solution)/shard_map/ppermute | solution.py:269
  8.1 9.0 %collective-permute-start.1 = (f32[64,512]{1,0:T(8,128)}, f32[64,512]{1,0:T(8,128)S(1)}, u32[]{:S(2)}, u32[]{:S(2)}) collective-permute-start(f32[64,512]{1,0:T(8,128)} %bitcast.14), channel_id=1, source_target_pairs={{4,0},{5,1},{6,2},{7,3},{0,4},{1,5},{2,6},{3,7},{12,8},{13,9},{14,... | collective-permute-start | bytes 393224 | tf_op jit(solution)/shard_map/ppermute | solution.py:269
  10.8 6.2 %collective-permute-start = (f32[64,512]{1,0:T(8,128)}, f32[64,512]{1,0:T(8,128)S(1)}, u32[]{:S(2)}, u32[]{:S(2)}) collective-permute-start(f32[64,512]{1,0:T(8,128)} %bitcast.15), channel_id=1, source_target_pairs={{2,0},{3,1},{4,2},{5,3},{6,4},{7,5},{0,6},{1,7},{10,8},{11,9},{12,... | collective-permute-start | bytes 393224 | tf_op jit(solution)/shard_map/ppermute | solution.py:269
  12.3 4.8 %copy-start.15 = (f32[512,64]{0,1:T(8,128)S(1)}, f32[512,64]{0,1:T(8,128)}, u32[]{:S(2)}) copy-start(f32[512,64]{0,1:T(8,128)} %param.4) | copy-start | bytes 393220
  17.9 53.1 %all-to-all-start = ((f32[8,256,512]{2,1,0:T(8,128)}), f32[8,256,512]{2,1,0:T(8,128)}, u32[]{:S(2)}, u32[]{:S(2)}) async-start(f32[8,256,512]{2,1,0:T(8,128)} %slice.9), calls=%async_computation | async-start | bytes 8388608 | tf_op jit(solution)/shard_map/all_to_all | solution.py:254
  71.1 30.3 %all-to-all-start.1 = ((f32[4,256,512]{2,1,0:T(8,128)}), f32[4,256,512]{2,1,0:T(8,128)}, u32[]{:S(2)}, u32[]{:S(2)}) async-start(f32[4,256,512]{2,1,0:T(8,128)} %slice.8), calls=%async_computation.1 | async-start | bytes 4194304 | tf_op jit(solution)/shard_map/all_to_all | solution.py:254
  79.9 17.0 %collective-permute-start.3 = (f32[256,512]{1,0:T(8,128)}, f32[256,512]{1,0:T(8,128)S(1)}, u32[]{:S(2)}, u32[]{:S(2)}) collective-permute-start(f32[256,512]{1,0:T(8,128)} %transform.7), channel_id=1, source_target_pairs={{1,0},{0,1},{3,2},{2,3},{5,4},{4,5},{7,6},{6,7},{9,8},{8,9},{11,10... | collective-permute-start | bytes 1572872 | tf_op jit(solution)/shard_map/ppermute | solution.py:260
  88.3 25.7 %collective-permute-start.7 = (f32[256,512]{1,0:T(8,128)}, f32[256,512]{1,0:T(8,128)S(1)}, u32[]{:S(2)}, u32[]{:S(2)}) collective-permute-start(f32[256,512]{1,0:T(8,128)} %transform.10), channel_id=1, source_target_pairs={{1,0},{0,1},{3,2},{2,3},{5,4},{4,5},{7,6},{6,7},{9,8},{8,9},{11,10... | collective-permute-start | bytes 1572872 | tf_op jit(solution)/shard_map/ppermute | solution.py:260
  98.1 7.7 %copy-start.1 = (f32[256,512]{1,0:T(8,128)}, f32[256,512]{1,0:T(8,128)S(1)}, u32[]{:S(2)}) copy-start(f32[256,512]{1,0:T(8,128)S(1)} %add.13.refs_0_) | copy-start | bytes 1572868
  98.1 17.1 %collective-permute-start.6 = (f32[256,512]{1,0:T(8,128)S(1)}, f32[256,512]{1,0:T(8,128)S(1)}, u32[]{:S(2)}, u32[]{:S(2)}) collective-permute-start(f32[256,512]{1,0:T(8,128)S(1)} %add.13.refs_0_), channel_id=1, source_target_pairs={{96,0},{104,8},{112,16},{120,24},{0,32},{8,40},{16,48},{24,56},{40... | collective-permute-start | bytes 1572872 | tf_op jit(solution)/shard_map/ppermute | solution.py:65
  99.7 15.4 %collective-permute-start.5 = (f32[256,512]{1,0:T(8,128)S(1)}, f32[256,512]{1,0:T(8,128)S(1)}, u32[]{:S(2)}, u32[]{:S(2)}) collective-permute-start(f32[256,512]{1,0:T(8,128)S(1)} %add.13.refs_0_), channel_id=1, source_target_pairs={{32,0},{40,8},{48,16},{56,24},{64,32},{72,40},{80,48},{88,56},{96,... | collective-permute-start | bytes 1572872 | tf_op jit(solution)/shard_map/ppermute | solution.py:65
  101.4 13.8 %collective-permute-start.4 = (f32[256,512]{1,0:T(8,128)S(1)}, f32[256,512]{1,0:T(8,128)S(1)}, u32[]{:S(2)}, u32[]{:S(2)}) collective-permute-start(f32[256,512]{1,0:T(8,128)S(1)} %add.13.refs_0_), channel_id=1, source_target_pairs={{8,0},{0,8},{24,16},{16,24},{40,32},{32,40},{56,48},{48,56},{72,64... | collective-permute-start | bytes 1572872 | tf_op jit(solution)/shard_map/ppermute | solution.py:65
  105.8 18.0 %collective-permute-start.10 = (f32[256,512]{1,0:T(8,128)}, f32[256,512]{1,0:T(8,128)}, u32[]{:S(2)}, u32[]{:S(2)}) collective-permute-start(f32[256,512]{1,0:T(8,128)} %transform.8), channel_id=1, source_target_pairs={{1,0},{0,1},{3,2},{2,3},{5,4},{4,5},{7,6},{6,7},{9,8},{8,9},{11,10... | collective-permute-start | bytes 1572872 | tf_op jit(solution)/shard_map/ppermute | solution.py:260
  115.1 8.6 %copy-start.2 = (f32[256,512]{1,0:T(8,128)}, f32[256,512]{1,0:T(8,128)S(1)}, u32[]{:S(2)}) copy-start(f32[256,512]{1,0:T(8,128)S(1)} %add.14.refs_1_) | copy-start | bytes 1572868
  115.2 8.6 %copy-start.5 = (f32[256,512]{1,0:T(8,128)}, f32[256,512]{1,0:T(8,128)S(1)}, u32[]{:S(2)}) copy-start(f32[256,512]{1,0:T(8,128)S(1)} %collective-permute-done.6.refs_6_) | copy-start | bytes 1572868
  115.2 8.6 %copy-start.6 = (f32[256,512]{1,0:T(8,128)}, f32[256,512]{1,0:T(8,128)S(1)}, u32[]{:S(2)}) copy-start(f32[256,512]{1,0:T(8,128)S(1)} %collective-permute-done.5.refs_4_) | copy-start | bytes 1572868
  115.2 8.6 %copy-start.7 = (f32[256,512]{1,0:T(8,128)}, f32[256,512]{1,0:T(8,128)S(1)}, u32[]{:S(2)}) copy-start(f32[256,512]{1,0:T(8,128)S(1)} %collective-permute-done.4.refs_2_) | copy-start | bytes 1572868
  115.2 15.3 %collective-permute-start.9 = (f32[256,512]{1,0:T(8,128)S(1)}, f32[256,512]{1,0:T(8,128)S(1)}, u32[]{:S(2)}, u32[]{:S(2)}) collective-permute-start(f32[256,512]{1,0:T(8,128)S(1)} %add.14.refs_1_), channel_id=1, source_target_pairs={{96,0},{104,8},{112,16},{120,24},{0,32},{8,40},{16,48},{24,56},{40... | collective-permute-start | bytes 1572872 | tf_op jit(solution)/shard_map/ppermute | solution.py:65
  116.2 14.4 %collective-permute-start.8 = (f32[256,512]{1,0:T(8,128)S(1)}, f32[256,512]{1,0:T(8,128)}, u32[]{:S(2)}, u32[]{:S(2)}) collective-permute-start(f32[256,512]{1,0:T(8,128)S(1)} %add.14.refs_1_), channel_id=1, source_target_pairs={{8,0},{0,8},{24,16},{16,24},{40,32},{32,40},{56,48},{48,56},{72,64... | collective-permute-start | bytes 1572872 | tf_op jit(solution)/shard_map/ppermute | solution.py:65
  116.2 18.2 %collective-permute-start.15 = (f32[256,512]{1,0:T(8,128)S(1)}, f32[256,512]{1,0:T(8,128)}, u32[]{:S(2)}, u32[]{:S(2)}) collective-permute-start(f32[256,512]{1,0:T(8,128)S(1)} %add.14.refs_1_), channel_id=1, source_target_pairs={{32,0},{40,8},{48,16},{56,24},{64,32},{72,40},{80,48},{88,56},{96,... | collective-permute-start | bytes 1572872 | tf_op jit(solution)/shard_map/ppermute | solution.py:65
  118.5 15.9 %collective-permute-start.14 = (f32[256,512]{1,0:T(8,128)S(1)}, f32[256,512]{1,0:T(8,128)S(1)}, u32[]{:S(2)}, u32[]{:S(2)}) collective-permute-start(f32[256,512]{1,0:T(8,128)S(1)} %collective-permute-done.5.refs_4_), channel_id=1, source_target_pairs={{16,0},{24,8},{8,16},{0,24},{48,32},{56,40},{40,48},{32,56},{88,64... | collective-permute-start | bytes 1572872 | tf_op jit(solution)/shard_map/ppermute | solution.py:65
  125.1 15.6 %copy-start.4 = (f32[256,512]{1,0:T(8,128)}, f32[256,512]{1,0:T(8,128)S(1)}, u32[]{:S(2)}) copy-start(f32[256,512]{1,0:T(8,128)S(1)} %add.15.refs_0_) | copy-start | bytes 1572868
  130.5 4.7 %copy-start.8 = (f32[256,512]{1,0:T(8,128)}, f32[256,512]{1,0:T(8,128)S(1)}, u32[]{:S(2)}) copy-start(f32[256,512]{1,0:T(8,128)S(1)} %collective-permute-done.9.refs_7_) | copy-start | bytes 1572868
  130.5 14.4 %collective-permute-start.13 = (f32[256,512]{1,0:T(8,128)S(1)}, f32[256,512]{1,0:T(8,128)S(1)}, u32[]{:S(2)}, u32[]{:S(2)}) collective-permute-start(f32[256,512]{1,0:T(8,128)S(1)} %add.15.refs_0_), channel_id=1, source_target_pairs={{96,0},{104,8},{112,16},{120,24},{0,32},{8,40},{16,48},{24,56},{40... | collective-permute-start | bytes 1572872 | tf_op jit(solution)/shard_map/ppermute | solution.py:65
  130.6 14.4 %collective-permute-start.12 = (f32[256,512]{1,0:T(8,128)S(1)}, f32[256,512]{1,0:T(8,128)}, u32[]{:S(2)}, u32[]{:S(2)}) collective-permute-start(f32[256,512]{1,0:T(8,128)S(1)} %add.15.refs_0_), channel_id=1, source_target_pairs={{32,0},{40,8},{48,16},{56,24},{64,32},{72,40},{80,48},{88,56},{96,... | collective-permute-start | bytes 1572872 | tf_op jit(solution)/shard_map/ppermute | solution.py:65
  133.8 11.2 %collective-permute-start.11 = (f32[256,512]{1,0:T(8,128)S(1)}, f32[256,512]{1,0:T(8,128)}, u32[]{:S(2)}, u32[]{:S(2)}) collective-permute-start(f32[256,512]{1,0:T(8,128)S(1)} %add.15.refs_0_), channel_id=1, source_target_pairs={{8,0},{0,8},{24,16},{16,24},{40,32},{32,40},{56,48},{48,56},{72,64... | collective-permute-start | bytes 1572872 | tf_op jit(solution)/shard_map/ppermute | solution.py:65
  134.4 6.3 %copy-start.10 = (f32[256,512]{1,0:T(8,128)}, f32[256,512]{1,0:T(8,128)S(1)}, u32[]{:S(2)}) copy-start(f32[256,512]{1,0:T(8,128)S(1)} %collective-permute-done.14.refs_8_) | copy-start | bytes 1572868
  134.4 20.4 %collective-permute-start.17 = (f32[256,512]{1,0:T(8,128)}, f32[256,512]{1,0:T(8,128)S(1)}, u32[]{:S(2)}, u32[]{:S(2)}) collective-permute-start(f32[256,512]{1,0:T(8,128)} %collective-permute-done.15.refs_5_), channel_id=1, source_target_pairs={{16,0},{24,8},{8,16},{0,24},{48,32},{56,40},{40,48},{32,56},{88,64... | collective-permute-start | bytes 1572872 | tf_op jit(solution)/shard_map/ppermute | solution.py:65
  145.0 26.2 %collective-permute-start.16 = (f32[256,512]{1,0:T(8,128)}, f32[256,512]{1,0:T(8,128)S(1)}, u32[]{:S(2)}, u32[]{:S(2)}) collective-permute-start(f32[256,512]{1,0:T(8,128)} %collective-permute-done.12.refs_2_), channel_id=1, source_target_pairs={{16,0},{24,8},{8,16},{0,24},{48,32},{56,40},{40,48},{32,56},{88,64... | collective-permute-start | bytes 1572872 | tf_op jit(solution)/shard_map/ppermute | solution.py:65
  150.1 26.6 %all-to-all-start.2 = ((f32[8,5,32,256]{3,2,1,0:T(8,128)}), f32[8,5,32,256]{3,2,1,0:T(8,128)S(1)}, u32[]{:S(2)}, u32[]{:S(2)}) async-start(f32[8,5,32,256]{3,2,1,0:T(8,128)} %gram.5), calls=%async_computation.2 | async-start | bytes 2621440 | tf_op jit(solution)/shard_map/all_to_all | solution.py:263
  176.7 4.8 %copy-start = (f32[8,5,32,256]{3,2,1,0:T(8,128)}, f32[8,5,32,256]{3,2,1,0:T(8,128)S(1)}, u32[]{:S(2)}) copy-start(f32[8,5,32,256]{3,2,1,0:T(8,128)S(1)} %all-to-all-done.2.moved_ref) | copy-start | bytes 3932164
  176.7 21.3 %all-to-all-start.3 = ((f32[8,4,32,256]{3,2,1,0:T(8,128)}), f32[8,4,32,256]{3,2,1,0:T(8,128)S(1)}, u32[]{:S(2)}, u32[]{:S(2)}) async-start(f32[8,4,32,256]{3,2,1,0:T(8,128)} %gram.7), calls=%async_computation.3 | async-start | bytes 2097152 | tf_op jit(solution)/shard_map/all_to_all | solution.py:263
  183.6 6.0 %collective-permute-start.19 = (f32[3,32,256]{2,1,0:T(8,128)}, f32[3,32,256]{2,1,0:T(8,128)S(1)}, u32[]{:S(2)}, u32[]{:S(2)}) collective-permute-start(f32[3,32,256]{2,1,0:T(8,128)} %get-tuple-element.75), channel_id=1, source_target_pairs={{0,32},{8,40},{16,48},{24,56},{32,64},{40,72},{48,80},{56,88},{64,... | collective-permute-start | bytes 294920 | tf_op jit(solution)/shard_map/ppermute | solution.py:70
  183.7 3.2 %collective-permute-start.18 = (f32[1,32,256]{2,1,0:T(8,128)}, f32[1,32,256]{2,1,0:T(8,128)S(1)}, u32[]{:S(2)}, u32[]{:S(2)}) collective-permute-start(f32[1,32,256]{2,1,0:T(8,128)} %get-tuple-element.74), channel_id=1, source_target_pairs={{0,8},{8,0},{16,24},{24,16},{32,40},{40,32},{48,56},{56,48},{64,72... | collective-permute-start | bytes 98312 | tf_op jit(solution)/shard_map/ppermute | solution.py:70
  183.7 5.1 %collective-permute-start.20 = (f32[1,32,256]{2,1,0:T(8,128)}, f32[1,32,256]{2,1,0:T(8,128)S(1)}, u32[]{:S(2)}, u32[]{:S(2)}) collective-permute-start(f32[1,32,256]{2,1,0:T(8,128)} %get-tuple-element.76), channel_id=1, source_target_pairs={{0,96},{8,104},{16,112},{24,120},{32,0},{40,8},{48,16},{56,24},{64... | collective-permute-start | bytes 98312 | tf_op jit(solution)/shard_map/ppermute | solution.py:70
  186.8 36.2 %copy-start.16 = (f32[1,32,256]{2,1,0:T(8,128)}, f32[1,32,256]{2,1,0:T(8,128)S(1)}, u32[]{:S(2)}) copy-start(f32[1,32,256]{2,1,0:T(8,128)S(1)} %collective-permute-done.18.refs_1_) | copy-start | bytes 98308
  188.7 19.5 %copy-start.18 = (f32[1,32,256]{2,1,0:T(8,128)}, f32[1,32,256]{2,1,0:T(8,128)S(1)}, u32[]{:S(2)}) copy-start(f32[1,32,256]{2,1,0:T(8,128)S(1)} %collective-permute-done.20.refs_1_) | copy-start | bytes 98308
  189.6 18.6 %copy-start.13 = (f32[3,32,256]{2,1,0:T(8,128)}, f32[3,32,256]{2,1,0:T(8,128)S(1)}, u32[]{:S(2)}) copy-start(f32[3,32,256]{2,1,0:T(8,128)S(1)} %collective-permute-done.19.refs_0_.refs_2_) | copy-start | bytes 294916
  198.0 1.0 copy-start.3
  201.0 7.3 %collective-permute-start.24 = (f32[4,32,256]{2,1,0:T(8,128)}, f32[4,32,256]{2,1,0:T(8,128)S(1)}, u32[]{:S(2)}, u32[]{:S(2)}) collective-permute-start(f32[4,32,256]{2,1,0:T(8,128)} %get-tuple-element.86), channel_id=1, source_target_pairs={{0,48},{8,56},{16,40},{24,32},{32,80},{40,88},{48,72},{56,64},{64,... | collective-permute-start | bytes 393224 | tf_op jit(solution)/shard_map/ppermute | solution.py:70
  210.7 12.3 %all-to-all-start.4 = ((f32[8,32,256]{2,1,0:T(8,128)}), f32[8,32,256]{2,1,0:T(8,128)S(1)}, u32[]{:S(2)}, u32[]{:S(2)}) async-start(f32[8,32,256]{2,1,0:T(8,128)} %turn.1), calls=%async_computation.4 | async-start | bytes 524288 | tf_op jit(solution)/shard_map/all_to_all | solution.py:263
  214.6 4.6 %collective-permute-start.21 = (f32[1,32,256]{2,1,0:T(8,128)}, f32[1,32,256]{2,1,0:T(8,128)S(1)}, u32[]{:S(2)}, u32[]{:S(2)}) collective-permute-start(f32[1,32,256]{2,1,0:T(8,128)} %get-tuple-element.82), channel_id=1, source_target_pairs={{0,8},{8,0},{16,24},{24,16},{32,40},{40,32},{48,56},{56,48},{64,72... | collective-permute-start | bytes 98312 | tf_op jit(solution)/shard_map/ppermute | solution.py:70
  214.6 5.4 %collective-permute-start.22 = (f32[1,32,256]{2,1,0:T(8,128)}, f32[1,32,256]{2,1,0:T(8,128)S(1)}, u32[]{:S(2)}, u32[]{:S(2)}) collective-permute-start(f32[1,32,256]{2,1,0:T(8,128)} %get-tuple-element.83), channel_id=1, source_target_pairs={{0,32},{8,40},{16,48},{24,56},{32,64},{40,72},{48,80},{56,88},{64,... | collective-permute-start | bytes 98312 | tf_op jit(solution)/shard_map/ppermute | solution.py:70
  214.7 5.3 %collective-permute-start.23 = (f32[1,32,256]{2,1,0:T(8,128)}, f32[1,32,256]{2,1,0:T(8,128)S(1)}, u32[]{:S(2)}, u32[]{:S(2)}) collective-permute-start(f32[1,32,256]{2,1,0:T(8,128)} %get-tuple-element.84), channel_id=1, source_target_pairs={{0,96},{8,104},{16,112},{24,120},{32,0},{40,8},{48,16},{56,24},{64... | collective-permute-start | bytes 98312 | tf_op jit(solution)/shard_map/ppermute | solution.py:70
  219.2 3.9 %copy-start.17 = (f32[1,32,256]{2,1,0:T(8,128)}, f32[1,32,256]{2,1,0:T(8,128)S(1)}, u32[]{:S(2)}) copy-start(f32[1,32,256]{2,1,0:T(8,128)S(1)} %collective-permute-done.21.refs_4_) | copy-start | bytes 98308
  220.0 3.0 %copy-start.19 = (f32[1,32,256]{2,1,0:T(8,128)}, f32[1,32,256]{2,1,0:T(8,128)S(1)}, u32[]{:S(2)}) copy-start(f32[1,32,256]{2,1,0:T(8,128)S(1)} %collective-permute-done.22.refs_5_) | copy-start | bytes 98308
  220.0 3.0 %copy-start.20 = (f32[1,32,256]{2,1,0:T(8,128)}, f32[1,32,256]{2,1,0:T(8,128)S(1)}, u32[]{:S(2)}) copy-start(f32[1,32,256]{2,1,0:T(8,128)S(1)} %collective-permute-done.23.refs_6_) | copy-start | bytes 98308
  (5 other events, 3.8 us)
Sparse Core Ops, SparseCore 0:
  18.1 54.1 all-gather.2
